TPU v7x, 256 devices: a whole 4x4x8 slice. The times are simulated.
256 devices in a mesh: dec: 16 (over x_hi, z), ra: 16 (over y, x_lo, core).
Axes of the slice: x: 4 (x_hi: 2, x_lo: 2; x = x_hi * 2 + x_lo), y: 4, z: 8, core: 2. Of those that a mesh axis runs over, the one named last changes fastest.
Arguments:
- split_maps: bfloat16 [6, 4096, 4096], P(None, 'dec', 'ra'), may hold values from -40 to 40
- white_noise: bfloat16 [8192, 8192], P('dec', 'ra'), may hold values from -6 to 6
Outputs:
- noise_realization: float32 [4096, 4096], P('dec', 'ra')
All inputs are finite; a program needn't handle non-finite values.
Results may differ from a plain program's by a relative error of at most 0.0035.
The roundings to bfloat16 on the way count: a program that leaves them out, or rounds other values in their place, can miss the bound.
Values may be sent and summed in bfloat16 or wider, within the bound.
No kernel may reach another device: no remote copies, remote signals or barrier semaphores. Data moves between devices by JAX's collectives and lax.ppermute only.
A program may use at most 64 MiB of HBM per device.

v0:
```python
import jax
import jax.numpy as jnp
from jax import lax
from jax.sharding import PartitionSpec as P

SMOOTH = 4


def padded(block, sides, width):
    for axis, dim in sides:
        count = lax.axis_size(axis)
        forward = [(i, i + 1) for i in range(count - 1)]
        backward = [(target, source) for source, target in forward]
        low = lax.ppermute(
            lax.slice_in_dim(block, block.shape[dim] - width, None, axis=dim), axis, forward
        )
        high = lax.ppermute(lax.slice_in_dim(block, 0, width, axis=dim), axis, backward)
        block = jnp.concatenate([low, block, high], axis=dim)
    return block


def make_tables(length):
    indices = jnp.arange(length, dtype=jnp.int32)
    phases = indices[:, None] * indices[None, :] % length
    angles = phases.astype(jnp.float32) * (2.0 * jnp.pi / length)
    cos_table = jnp.cos(angles).astype(jnp.bfloat16)
    sin_table = jnp.sin(angles).astype(jnp.bfloat16)
    forward_left = jnp.concatenate([cos_table, sin_table], axis=0)
    forward_right = jnp.concatenate(
        [
            jnp.concatenate([cos_table, -sin_table], axis=1),
            jnp.concatenate([-sin_table, -cos_table], axis=1),
        ],
        axis=0,
    )
    inverse_left = jnp.concatenate(
        [
            jnp.concatenate([cos_table, -sin_table], axis=1),
            jnp.concatenate([sin_table, cos_table], axis=1),
        ],
        axis=0,
    )
    inverse_right = jnp.concatenate([cos_table, -sin_table], axis=0)
    profile = jnp.sin(jnp.pi * (indices.astype(jnp.float32) + 0.5) / length) ** 2
    window = profile[:, None] * profile[None, :]
    distance = jnp.abs(indices[:, None] - indices[None, :])
    distance = jnp.minimum(distance, length - distance)
    smoother = jnp.where(distance <= SMOOTH, 1.0 / (2 * SMOOTH + 1), 0.0).astype(jnp.float32)
    return (forward_left, forward_right, inverse_left, inverse_right, window, smoother)


def forward(tile, forward_left, forward_right):
    length = tile.shape[0]
    halves = jnp.dot(forward_left, tile, preferred_element_type=jnp.float32).astype(jnp.bfloat16)
    joined = jnp.concatenate([halves[:length], halves[length:]], axis=1)
    return jnp.dot(joined, forward_right, preferred_element_type=jnp.float32)


def shape_noise(extended, noise_spectra, tables):
    forward_left, forward_right, inverse_left, inverse_right, window, smoother = tables
    length = extended.shape[1]
    splits = extended.shape[0]
    coadded = jnp.mean(extended.astype(jnp.float32), axis=0)

    def accumulate(number, summed):
        member = lax.dynamic_index_in_dim(extended, number, 0, keepdims=False)
        differ = (window * (member.astype(jnp.float32) - coadded)).astype(jnp.bfloat16)
        spectra = forward(differ, forward_left, forward_right)
        return summed + spectra[:, :length] ** 2 + spectra[:, length:] ** 2

    spectrum_power = lax.fori_loop(0, splits, accumulate, jnp.zeros((length, length), jnp.float32))
    spectrum_power = spectrum_power / ((splits - 1) * jnp.sum(window * window))
    smooth = jnp.dot(
        jnp.dot(smoother, spectrum_power, precision=lax.Precision.HIGHEST),
        smoother,
        precision=lax.Precision.HIGHEST,
    )
    filter_gain = jnp.sqrt(smooth)
    shaped = jnp.concatenate(
        [filter_gain * noise_spectra[:, :length], filter_gain * noise_spectra[:, length:]], axis=0
    ).astype(jnp.bfloat16)
    mixture = jnp.dot(inverse_left, shaped, preferred_element_type=jnp.float32).astype(jnp.bfloat16)
    joined = jnp.concatenate([mixture[:length], mixture[length:]], axis=1)
    real_part = jnp.dot(joined, inverse_right, preferred_element_type=jnp.float32)
    return window * real_part / (length * length)


def fold_rows(values):
    core_side = values.shape[0] // 2
    margin = core_side // 2
    strips = jnp.concatenate([values[:margin], values[values.shape[0] - margin :]], axis=0)
    arrived = padded(strips.astype(jnp.bfloat16), (("dec", 0),), margin).astype(strips.dtype)
    inside = values[margin : margin + core_side]
    return inside + jnp.concatenate([arrived[:margin], arrived[3 * margin :]], axis=0)


def fold_columns(values):
    core_side = values.shape[1] // 2
    margin = core_side // 2
    strips = jnp.concatenate([values[:, :margin], values[:, values.shape[1] - margin :]], axis=1)
    arrived = padded(strips.astype(jnp.bfloat16), (("ra", 1),), margin).astype(strips.dtype)
    inside = values[:, margin : margin + core_side]
    return inside + jnp.concatenate([arrived[:, :margin], arrived[:, 3 * margin :]], axis=1)


def shards(split_maps, white_noise):
    core_side = split_maps.shape[1]
    margin = core_side // 2
    length = 2 * core_side
    tables = make_tables(length)
    noise_spectra = forward(white_noise, tables[0], tables[1])
    extended = padded(split_maps, (("dec", 1), ("ra", 2)), margin)
    realization = shape_noise(extended, noise_spectra, tables)
    folded = fold_columns(fold_rows(realization))
    return folded


def solution(mesh):
    placed = (P(None, "dec", "ra"), P("dec", "ra"))
    return jax.shard_map(
        shards, mesh=mesh, in_specs=placed, out_specs=P("dec", "ra"), check_vma=False
    )
```

profile of v0, /device:TPU:15, one launch (start us, length us, event | category | flops | bytes accessed | tf_op | source)
XLA Modules:
  0.0 125.1 jit_solution(1048737166952794054)
XLA Ops:
  1.2 3.5 %collective-permute-start = (bf16[6,128,256]{2,1,0:T(8,128)(2,1)S(1)}, bf16[6,128,256]{2,1,0:T(8,128)(2,1)S(1)}, u32[]{:S(2)}, u32[]{:S(2)}) collective-permute-start(bf16[6,128,256]{2,1,0:T(8,128)(2,1)S(1)} %get-tuple-element.184), channel_id=1, source_target_pairs={{0,16},{16,32},{32,48},{48,64},{64,80},{80,96},{96,112},{112,128},... | collective-permute-start | bytes 1179656 | tf_op jit(solution)/shard_map/ppermute | solution.py:14
  4.8 6.7 %collective-permute-start.1 = (bf16[6,128,256]{2,1,0:T(8,128)(2,1)S(1)}, bf16[6,128,256]{2,1,0:T(8,128)(2,1)S(1)}, u32[]{:S(2)}, u32[]{:S(2)}) collective-permute-start(bf16[6,128,256]{2,1,0:T(8,128)(2,1)S(1)} %get-tuple-element.183), channel_id=1, source_target_pairs={{16,0},{32,16},{48,32},{64,48},{80,64},{96,80},{112,96},{128,112},... | collective-permute-start | bytes 1179656 | tf_op jit(solution)/shard_map/ppermute | solution.py:17
  11.5 4.3 %sine_convert_fusion = (bf16[512,512]{1,0:T(8,128)(2,1)S(1)}, bf16[512,512]{1,0:T(8,128)(2,1)S(1)}) fusion(), kind=kLoop, calls=%fused_computation.66 | loop fusion | flops 4194304 | bytes 1048576 | tf_op jit(solution)/shard_map/convert_element_type | solution.py:27
  15.8 1.8 %convolution_convert_fusion.1 = bf16[1024,512]{0,1:T(8,128)(2,1)} fusion(bf16[512,512]{1,0:T(8,128)(2,1)S(1)} %copy-done, bf16[512,512]{1,0:T(8,128)(2,1)S(1)} %get-tuple-element.196, bf16[512,512]{1,0:T(8,128)(2,1)S(1)} %get-tuple-element.195), kind=kOutput, calls=%fused_computation.36 | convolution fusion | flops 539492352 | bytes 2621440 | tf_op jit(solution)/shard_map/dot_general | solution.py:54
  17.7 5.2 %fusion.64 = (bf16[512,512]{1,0:T(8,128)(2,1)}, bf16[512,512]{1,0:T(8,128)(2,1)S(1)}) fusion(), kind=kLoop, calls=%fused_computation.79 | loop fusion | flops 5767168 | bytes 1048576 | tf_op jit(solution)/shard_map/neg | solution.py:32
  25.8 3.4 %collective-permute-start.2 = (bf16[6,512,128]{2,1,0:T(8,128)(2,1)}, bf16[6,512,128]{2,1,0:T(8,128)(2,1)}, u32[]{:S(2)}, u32[]{:S(2)}) collective-permute-start(bf16[6,512,128]{2,1,0:T(8,128)(2,1)} %get-tuple-element.177), channel_id=1, source_target_pairs={{0,1},{1,2},{2,3},{3,4},{4,5},{5,6},{6,7},{7,8},{8,9},{9,10},{10,1... | collective-permute-start | bytes 2359304 | tf_op jit(solution)/shard_map/ppermute | solution.py:14
  29.2 2.1 %collective-permute-start.3 = (bf16[6,512,128]{2,1,0:T(8,128)(2,1)}, bf16[6,512,128]{2,1,0:T(8,128)(2,1)}, u32[]{:S(2)}, u32[]{:S(2)}) collective-permute-start(bf16[6,512,128]{2,1,0:T(8,128)(2,1)} %get-tuple-element.178), channel_id=1, source_target_pairs={{1,0},{2,1},{3,2},{4,3},{5,4},{6,5},{7,6},{8,7},{9,8},{10,9},{11,1... | collective-permute-start | bytes 2359304 | tf_op jit(solution)/shard_map/ppermute | solution.py:17
  32.9 2.8 %fusion.23 = bf16[1024,1024]{1,0:T(8,128)(2,1)} fusion(bf16[512,512]{1,0:T(8,128)(2,1)S(1)} %get-tuple-element.198, bf16[512,512]{1,0:T(8,128)(2,1)S(1)} %get-tuple-element.196, bf16[512,512]{1,0:T(8,128)(2,1)} %get-tuple-element.197), kind=kLoop, calls=%fused_computation.28 | loop fusion | flops 8388608 | bytes 3670016 | tf_op jit(solution)/shard_map/concatenate | solution.py:29
  35.8 2.6 %fusion.42 = f32[512,1024]{1,0:T(8,128)} fusion(bf16[512,512]{0,1:T(8,128)(2,1)S(1)} %get-tuple-element.182, bf16[512,512]{0,1:T(8,128)(2,1)S(1)} %get-tuple-element.181, bf16[512,512]{1,0:T(8,128)(2,1)S(1)} %get-tuple-element.198, bf16[512,512]{1,0:T(8,128)(2,1)S(1)} %get-tuple-element.196, bf16[512,512]{1,0:T(8,128)(2,1)S(1)} %copy-done.5), kind=kOutput, calls=%fused_computation.54 | convolution fusion | flops 1084227584 | bytes 4718592 | tf_op jit(solution)/shard_map/dot_general | solution.py:56
  38.5 5.1 %collective-permute-done.2 = bf16[6,512,128]{2,1,0:T(8,128)(2,1)} collective-permute-done((bf16[6,512,128]{2,1,0:T(8,128)(2,1)}, bf16[6,512,128]{2,1,0:T(8,128)(2,1)}, u32[]{:S(2)}, u32[]{:S(2)}) %collective-permute-start.2) | collective-permute-done | bytes 786464 | tf_op jit(solution)/shard_map/ppermute | solution.py:14
  43.5 5.6 %collective-permute-done.3 = bf16[6,512,128]{2,1,0:T(8,128)(2,1)} collective-permute-done((bf16[6,512,128]{2,1,0:T(8,128)(2,1)}, bf16[6,512,128]{2,1,0:T(8,128)(2,1)}, u32[]{:S(2)}, u32[]{:S(2)}) %collective-permute-start.3) | collective-permute-done | bytes 786464 | tf_op jit(solution)/shard_map/ppermute | solution.py:17
  49.1 2.0 %convert_reduce_fusion = f32[512,512]{1,0:T(8,128)S(1)} fusion(bf16[6,512,128]{2,1,0:T(8,128)(2,1)} %collective-permute-done.3, bf16[6,512,256]{2,1,0:T(8,128)(2,1)S(1)} %constant_dynamic-update-slice_fusion, bf16[6,512,128]{2,1,0:T(8,128)(2,1)} %collective-permute-done.2), kind=kLoop, calls=%fused_computation.20 | loop fusion | flops 10747904 | bytes 4194304 | tf_op jit(solution)/shard_map/reduce_sum | solution.py:63
  52.3 3.4 %pad_maximum_fusion = bf16[6,512,512]{2,1,0:T(8,128)(2,1)} fusion(bf16[6,512,128]{2,1,0:T(8,128)(2,1)} %collective-permute-done.3, bf16[6,512,256]{2,1,0:T(8,128)(2,1)S(1)} %constant_dynamic-update-slice_fusion, bf16[6,512,128]{2,1,0:T(8,128)(2,1)} %collective-permute-done.2), kind=kLoop, calls=%fused_computation.21 | loop fusion | flops 9437184 | bytes 6291456 | tf_op jit(solution)/shard_map/concatenate | solution.py:18
  55.7 39.3 %while.14 = (s32[]{:T(128)}, f32[512,512]{1,0:T(8,128)}, bf16[6,512,512]{2,1,0:T(8,128)(2,1)}, f32[512,512]{1,0:T(8,128)}, bf16[1024,512]{1,0:T(8,128)(2,1)}, /*...) while((s32[]{:T(128)}, f32[512,512]{1,0:T(8,128)}, ...), condition=%wide.region_2.3_spmd.clone, body=%wide.region_1.2_spmd.clone.sunk | while | flops 1615855616 | bytes 23597696 | solution.py:71
  55.7 2.8 %fusion.105 = bf16[1024,512]{0,1:T(8,128)(2,1)S(1)} fusion(bf16[1024,512]{1,0:T(8,128)(2,1)} %get-tuple-element.268, f32[512,512]{1,0:T(8,128)} %get-tuple-element.267, f32[512]{0:T(512)S(1)} %get-tuple-element.270, bf16[6,512,512]{2,1,0:T(8,128)(2,1)} %get-tuple-element.266, s32[]{:T(128)} %get-tuple-element.255), kind=kOutput, calls=%fused_computation.2.clone.1 | convolution fusion | flops 538705920 | bytes 3674624 | tf_op jit(solution)/shard_map/while/body/eval_jaxpr/dot_general | solution.py:54
  61.2 2.8 %fusion.105 = bf16[1024,512]{0,1:T(8,128)(2,1)S(1)} fusion(bf16[1024,512]{1,0:T(8,128)(2,1)} %get-tuple-element.268, f32[512,512]{1,0:T(8,128)} %get-tuple-element.267, f32[512]{0:T(512)S(1)} %get-tuple-element.270, bf16[6,512,512]{2,1,0:T(8,128)(2,1)} %get-tuple-element.266, s32[]{:T(128)} %get-tuple-element.255), kind=kOutput, calls=%fused_computation.2.clone.1 | convolution fusion | flops 538705920 | bytes 3674624 | tf_op jit(solution)/shard_map/while/body/eval_jaxpr/dot_general | solution.py:54
  65.3 2.6 %fusion.108 = f32[512,512]{1,0:T(8,128)} fusion(f32[512,1024]{1,0:T(8,128)S(1)} %fusion.107, f32[512,512]{1,0:T(8,128)} %get-tuple-element.256, pred[]{:T(512)S(6)} %compare.4), kind=kLoop, calls=%fused_computation.4.clone.1 | loop fusion | flops 1310720 | bytes 4194305 | tf_op jit(solution)/shard_map/while/body/eval_jaxpr/add | solution.py:69
  67.9 2.8 %fusion.105 = bf16[1024,512]{0,1:T(8,128)(2,1)S(1)} fusion(bf16[1024,512]{1,0:T(8,128)(2,1)} %get-tuple-element.268, f32[512,512]{1,0:T(8,128)} %get-tuple-element.267, f32[512]{0:T(512)S(1)} %get-tuple-element.270, bf16[6,512,512]{2,1,0:T(8,128)(2,1)} %get-tuple-element.266, s32[]{:T(128)} %get-tuple-element.255), kind=kOutput, calls=%fused_computation.2.clone.1 | convolution fusion | flops 538705920 | bytes 3674624 | tf_op jit(solution)/shard_map/while/body/eval_jaxpr/dot_general | solution.py:54
  72.1 2.6 %fusion.108 = f32[512,512]{1,0:T(8,128)} fusion(f32[512,1024]{1,0:T(8,128)S(1)} %fusion.107, f32[512,512]{1,0:T(8,128)} %get-tuple-element.256, pred[]{:T(512)S(6)} %compare.4), kind=kLoop, calls=%fused_computation.4.clone.1 | loop fusion | flops 1310720 | bytes 4194305 | tf_op jit(solution)/shard_map/while/body/eval_jaxpr/add | solution.py:69
  74.7 2.8 %fusion.105 = bf16[1024,512]{0,1:T(8,128)(2,1)S(1)} fusion(bf16[1024,512]{1,0:T(8,128)(2,1)} %get-tuple-element.268, f32[512,512]{1,0:T(8,128)} %get-tuple-element.267, f32[512]{0:T(512)S(1)} %get-tuple-element.270, bf16[6,512,512]{2,1,0:T(8,128)(2,1)} %get-tuple-element.266, s32[]{:T(128)} %get-tuple-element.255), kind=kOutput, calls=%fused_computation.2.clone.1 | convolution fusion | flops 538705920 | bytes 3674624 | tf_op jit(solution)/shard_map/while/body/eval_jaxpr/dot_general | solution.py:54
  78.8 2.6 %fusion.108 = f32[512,512]{1,0:T(8,128)} fusion(f32[512,1024]{1,0:T(8,128)S(1)} %fusion.107, f32[512,512]{1,0:T(8,128)} %get-tuple-element.256, pred[]{:T(512)S(6)} %compare.4), kind=kLoop, calls=%fused_computation.4.clone.1 | loop fusion | flops 1310720 | bytes 4194305 | tf_op jit(solution)/shard_map/while/body/eval_jaxpr/add | solution.py:69
  81.4 2.8 %fusion.105 = bf16[1024,512]{0,1:T(8,128)(2,1)S(1)} fusion(bf16[1024,512]{1,0:T(8,128)(2,1)} %get-tuple-element.268, f32[512,512]{1,0:T(8,128)} %get-tuple-element.267, f32[512]{0:T(512)S(1)} %get-tuple-element.270, bf16[6,512,512]{2,1,0:T(8,128)(2,1)} %get-tuple-element.266, s32[]{:T(128)} %get-tuple-element.255), kind=kOutput, calls=%fused_computation.2.clone.1 | convolution fusion | flops 538705920 | bytes 3674624 | tf_op jit(solution)/shard_map/while/body/eval_jaxpr/dot_general | solution.py:54
  85.6 2.6 %fusion.108 = f32[512,512]{1,0:T(8,128)} fusion(f32[512,1024]{1,0:T(8,128)S(1)} %fusion.107, f32[512,512]{1,0:T(8,128)} %get-tuple-element.256, pred[]{:T(512)S(6)} %compare.4), kind=kLoop, calls=%fused_computation.4.clone.1 | loop fusion | flops 1310720 | bytes 4194305 | tf_op jit(solution)/shard_map/while/body/eval_jaxpr/add | solution.py:69
  88.2 2.8 %fusion.105 = bf16[1024,512]{0,1:T(8,128)(2,1)S(1)} fusion(bf16[1024,512]{1,0:T(8,128)(2,1)} %get-tuple-element.268, f32[512,512]{1,0:T(8,128)} %get-tuple-element.267, f32[512]{0:T(512)S(1)} %get-tuple-element.270, bf16[6,512,512]{2,1,0:T(8,128)(2,1)} %get-tuple-element.266, s32[]{:T(128)} %get-tuple-element.255), kind=kOutput, calls=%fused_computation.2.clone.1 | convolution fusion | flops 538705920 | bytes 3674624 | tf_op jit(solution)/shard_map/while/body/eval_jaxpr/dot_general | solution.py:54
  92.3 2.6 %fusion.108 = f32[512,512]{1,0:T(8,128)} fusion(f32[512,1024]{1,0:T(8,128)S(1)} %fusion.107, f32[512,512]{1,0:T(8,128)} %get-tuple-element.256, pred[]{:T(512)S(6)} %compare.4), kind=kLoop, calls=%fused_computation.4.clone.1 | loop fusion | flops 1310720 | bytes 4194305 | tf_op jit(solution)/shard_map/while/body/eval_jaxpr/add | solution.py:69
  94.9 3.4 %fusion.29 = f32[512,512]{1,0:T(8,128)S(1)} fusion(f32[512,512]{1,0:T(8,128)} %get-tuple-element.129, f32[]{:T(128)S(6)} %mul_shard_map.3), kind=kOutput, calls=%fused_computation.39 | convolution fusion | flops 1612447744 | bytes 2097156 | tf_op jit(solution)/shard_map/dot_general | solution.py:74
  98.4 2.3 %fusion.41 = (bf16[512,512]{1,0:T(8,128)(2,1)S(1)}, bf16[512,512]{1,0:T(8,128)(2,1)S(1)}) fusion(f32[512,1024]{1,0:T(8,128)S(1)} %copy-done.9, f32[512,512]{1,0:T(8,128)S(1)} %fusion.29), kind=kOutput, calls=%fused_computation.53 | convolution fusion | flops 1613234176 | bytes 4194304 | tf_op jit(solution)/shard_map/dot_general | solution.py:73
  102.9 1.9 %collective-permute-start.4 = (bf16[128,512]{1,0:T(8,128)(2,1)S(1)}, bf16[128,512]{1,0:T(8,128)(2,1)S(1)}, u32[]{:S(2)}, u32[]{:S(2)}) collective-permute-start(bf16[128,512]{1,0:T(8,128)(2,1)S(1)} %get-tuple-element.187), channel_id=1, source_target_pairs={{0,16},{16,32},{32,48},{48,64},{64,80},{80,96},{96,112},{112,128},... | collective-permute-start | bytes 393224 | tf_op jit(solution)/shard_map/ppermute | solution.py:14
  104.8 7.0 %collective-permute-start.5 = (bf16[128,512]{1,0:T(8,128)(2,1)S(1)}, bf16[128,512]{1,0:T(8,128)(2,1)S(1)}, u32[]{:S(2)}, u32[]{:S(2)}) collective-permute-start(bf16[128,512]{1,0:T(8,128)(2,1)S(1)} %get-tuple-element.188), channel_id=1, source_target_pairs={{16,0},{32,16},{48,32},{64,48},{80,64},{96,80},{112,96},{128,112},... | collective-permute-start | bytes 393224 | tf_op jit(solution)/shard_map/ppermute | solution.py:17
  114.1 3.7 %collective-permute-start.6 = (bf16[256,128]{1,0:T(8,128)(2,1)S(1)}, bf16[256,128]{1,0:T(8,128)(2,1)S(1)}, u32[]{:S(2)}, u32[]{:S(2)}) collective-permute-start(bf16[256,128]{1,0:T(8,128)(2,1)S(1)} %get-tuple-element.191), channel_id=1, source_target_pairs={{0,1},{1,2},{2,3},{3,4},{4,5},{5,6},{6,7},{7,8},{8,9},{9,10},{10,1... | collective-permute-start | bytes 196616 | tf_op jit(solution)/shard_map/ppermute | solution.py:14
  117.8 1.9 %collective-permute-start.7 = (bf16[256,128]{1,0:T(8,128)(2,1)S(1)}, bf16[256,128]{1,0:T(8,128)(2,1)S(1)}, u32[]{:S(2)}, u32[]{:S(2)}) collective-permute-start(bf16[256,128]{1,0:T(8,128)(2,1)S(1)} %get-tuple-element.192), channel_id=1, source_target_pairs={{1,0},{2,1},{3,2},{4,3},{5,4},{6,5},{7,6},{8,7},{9,8},{10,9},{11,1... | collective-permute-start | bytes 196616 | tf_op jit(solution)/shard_map/ppermute | solution.py:17
  119.8 4.5 %collective-permute-done.7 = bf16[256,128]{1,0:T(8,128)(2,1)S(1)} collective-permute-done((bf16[256,128]{1,0:T(8,128)(2,1)S(1)}, bf16[256,128]{1,0:T(8,128)(2,1)S(1)}, u32[]{:S(2)}, u32[]{:S(2)}) %collective-permute-start.7) | collective-permute-done | bytes 65568 | tf_op jit(solution)/shard_map/ppermute | solution.py:17
  (68 shorter events, 21.1 us)
Async XLA Ops:
  0.0 15.8 %copy-start = (bf16[512,512]{1,0:T(8,128)(2,1)S(1)}, bf16[512,512]{1,0:T(8,128)(2,1)}, u32[]{:S(2)}) copy-start(bf16[512,512]{1,0:T(8,128)(2,1)} %param.5) | copy-start | bytes 1572868
  1.2 22.9 %collective-permute-start = (bf16[6,128,256]{2,1,0:T(8,128)(2,1)S(1)}, bf16[6,128,256]{2,1,0:T(8,128)(2,1)S(1)}, u32[]{:S(2)}, u32[]{:S(2)}) collective-permute-start(bf16[6,128,256]{2,1,0:T(8,128)(2,1)S(1)} %get-tuple-element.184), channel_id=1, source_target_pairs={{0,16},{16,32},{32,48},{48,64},{64,80},{80,96},{96,112},{112,128},... | collective-permute-start | bytes 1179656 | tf_op jit(solution)/shard_map/ppermute | solution.py:14
  4.8 19.4 %collective-permute-start.1 = (bf16[6,128,256]{2,1,0:T(8,128)(2,1)S(1)}, bf16[6,128,256]{2,1,0:T(8,128)(2,1)S(1)}, u32[]{:S(2)}, u32[]{:S(2)}) collective-permute-start(bf16[6,128,256]{2,1,0:T(8,128)(2,1)S(1)} %get-tuple-element.183), channel_id=1, source_target_pairs={{16,0},{32,16},{48,32},{64,48},{80,64},{96,80},{112,96},{128,112},... | collective-permute-start | bytes 1179656 | tf_op jit(solution)/shard_map/ppermute | solution.py:17
  15.8 7.1 %copy-start.6 = (bf16[512,512]{1,0:T(8,128)(2,1)}, bf16[512,512]{1,0:T(8,128)(2,1)S(1)}, u32[]{:S(2)}) copy-start(bf16[512,512]{1,0:T(8,128)(2,1)S(1)} %get-tuple-element.195) | copy-start | bytes 1572868
  17.7 6.5 %copy-start.2 = (bf16[6,256,256]{2,1,0:T(8,128)(2,1)S(1)}, bf16[6,256,256]{2,1,0:T(8,128)(2,1)}, u32[]{:S(2)}) copy-start(bf16[6,256,256]{2,1,0:T(8,128)(2,1)} %param.4) | copy-start | bytes 2359300
  22.9 12.9 %copy-start.3 = (bf16[512,512]{1,0:T(8,128)(2,1)}, bf16[512,512]{1,0:T(8,128)(2,1)S(1)}, u32[]{:S(2)}) copy-start(bf16[512,512]{1,0:T(8,128)(2,1)S(1)} %get-tuple-element.198) | copy-start | bytes 1572868
  25.8 17.7 %collective-permute-start.2 = (bf16[6,512,128]{2,1,0:T(8,128)(2,1)}, bf16[6,512,128]{2,1,0:T(8,128)(2,1)}, u32[]{:S(2)}, u32[]{:S(2)}) collective-permute-start(bf16[6,512,128]{2,1,0:T(8,128)(2,1)} %get-tuple-element.177), channel_id=1, source_target_pairs={{0,1},{1,2},{2,3},{3,4},{4,5},{5,6},{6,7},{7,8},{8,9},{9,10},{10,1... | collective-permute-start | bytes 2359304 | tf_op jit(solution)/shard_map/ppermute | solution.py:14
  29.2 19.9 %collective-permute-start.3 = (bf16[6,512,128]{2,1,0:T(8,128)(2,1)}, bf16[6,512,128]{2,1,0:T(8,128)(2,1)}, u32[]{:S(2)}, u32[]{:S(2)}) collective-permute-start(bf16[6,512,128]{2,1,0:T(8,128)(2,1)} %get-tuple-element.178), channel_id=1, source_target_pairs={{1,0},{2,1},{3,2},{4,3},{5,4},{6,5},{7,6},{8,7},{9,8},{10,9},{11,1... | collective-permute-start | bytes 2359304 | tf_op jit(solution)/shard_map/ppermute | solution.py:17
  32.9 2.8 %copy-start.8 = (bf16[1024,512]{0,1:T(8,128)(2,1)S(1)}, bf16[1024,512]{0,1:T(8,128)(2,1)}, u32[]{:S(2)}) copy-start(bf16[1024,512]{0,1:T(8,128)(2,1)} %convolution_convert_fusion.1) | copy-start | bytes 3145732
  32.9 2.9 %copy-start.5 = (bf16[512,512]{1,0:T(8,128)(2,1)S(1)}, bf16[512,512]{1,0:T(8,128)(2,1)}, u32[]{:S(2)}) copy-start(bf16[512,512]{1,0:T(8,128)(2,1)} %get-tuple-element.197) | copy-start | bytes 1572868
  55.7 2.9 %copy-start.1 = (bf16[1024,1024]{1,0:T(8,128)(2,1)S(1)}, bf16[1024,1024]{1,0:T(8,128)(2,1)}, u32[]{:S(2)}) copy-start(bf16[1024,1024]{1,0:T(8,128)(2,1)} %get-tuple-element.269) | copy-start | bytes 6291460 | tf_op jit(solution)/shard_map/while
  61.2 2.9 %copy-start.1 = (bf16[1024,1024]{1,0:T(8,128)(2,1)S(1)}, bf16[1024,1024]{1,0:T(8,128)(2,1)}, u32[]{:S(2)}) copy-start(bf16[1024,1024]{1,0:T(8,128)(2,1)} %get-tuple-element.269) | copy-start | bytes 6291460 | tf_op jit(solution)/shard_map/while
  67.9 2.9 %copy-start.1 = (bf16[1024,1024]{1,0:T(8,128)(2,1)S(1)}, bf16[1024,1024]{1,0:T(8,128)(2,1)}, u32[]{:S(2)}) copy-start(bf16[1024,1024]{1,0:T(8,128)(2,1)} %get-tuple-element.269) | copy-start | bytes 6291460 | tf_op jit(solution)/shard_map/while
  74.7 2.9 %copy-start.1 = (bf16[1024,1024]{1,0:T(8,128)(2,1)S(1)}, bf16[1024,1024]{1,0:T(8,128)(2,1)}, u32[]{:S(2)}) copy-start(bf16[1024,1024]{1,0:T(8,128)(2,1)} %get-tuple-element.269) | copy-start | bytes 6291460 | tf_op jit(solution)/shard_map/while
  81.4 2.9 %copy-start.1 = (bf16[1024,1024]{1,0:T(8,128)(2,1)S(1)}, bf16[1024,1024]{1,0:T(8,128)(2,1)}, u32[]{:S(2)}) copy-start(bf16[1024,1024]{1,0:T(8,128)(2,1)} %get-tuple-element.269) | copy-start | bytes 6291460 | tf_op jit(solution)/shard_map/while
  88.2 2.9 %copy-start.1 = (bf16[1024,1024]{1,0:T(8,128)(2,1)S(1)}, bf16[1024,1024]{1,0:T(8,128)(2,1)}, u32[]{:S(2)}) copy-start(bf16[1024,1024]{1,0:T(8,128)(2,1)} %get-tuple-element.269) | copy-start | bytes 6291460 | tf_op jit(solution)/shard_map/while
  94.9 3.4 %copy-start.9 = (f32[512,1024]{1,0:T(8,128)S(1)}, f32[512,1024]{1,0:T(8,128)}, u32[]{:S(2)}) copy-start(f32[512,1024]{1,0:T(8,128)} %fusion.42) | copy-start | bytes 6291460
  98.4 2.3 %copy-start.4 = (bf16[512,512]{1,0:T(8,128)(2,1)S(1)}, bf16[512,512]{1,0:T(8,128)(2,1)}, u32[]{:S(2)}) copy-start(bf16[512,512]{1,0:T(8,128)(2,1)} %copy-done.3) | copy-start | bytes 1572868
  98.4 2.3 %copy-start.7 = (bf16[512,512]{1,0:T(8,128)(2,1)S(1)}, bf16[512,512]{1,0:T(8,128)(2,1)}, u32[]{:S(2)}) copy-start(bf16[512,512]{1,0:T(8,128)(2,1)} %copy-done.6) | copy-start | bytes 1572868
  102.9 9.3 %collective-permute-start.4 = (bf16[128,512]{1,0:T(8,128)(2,1)S(1)}, bf16[128,512]{1,0:T(8,128)(2,1)S(1)}, u32[]{:S(2)}, u32[]{:S(2)}) collective-permute-start(bf16[128,512]{1,0:T(8,128)(2,1)S(1)} %get-tuple-element.187), channel_id=1, source_target_pairs={{0,16},{16,32},{32,48},{48,64},{64,80},{80,96},{96,112},{112,128},... | collective-permute-start | bytes 393224 | tf_op jit(solution)/shard_map/ppermute | solution.py:14
  104.8 9.1 %collective-permute-start.5 = (bf16[128,512]{1,0:T(8,128)(2,1)S(1)}, bf16[128,512]{1,0:T(8,128)(2,1)S(1)}, u32[]{:S(2)}, u32[]{:S(2)}) collective-permute-start(bf16[128,512]{1,0:T(8,128)(2,1)S(1)} %get-tuple-element.188), channel_id=1, source_target_pairs={{16,0},{32,16},{48,32},{64,48},{80,64},{96,80},{112,96},{128,112},... | collective-permute-start | bytes 393224 | tf_op jit(solution)/shard_map/ppermute | solution.py:17
  114.1 5.6 %collective-permute-start.6 = (bf16[256,128]{1,0:T(8,128)(2,1)S(1)}, bf16[256,128]{1,0:T(8,128)(2,1)S(1)}, u32[]{:S(2)}, u32[]{:S(2)}) collective-permute-start(bf16[256,128]{1,0:T(8,128)(2,1)S(1)} %get-tuple-element.191), channel_id=1, source_target_pairs={{0,1},{1,2},{2,3},{3,4},{4,5},{5,6},{6,7},{7,8},{8,9},{9,10},{10,1... | collective-permute-start | bytes 196616 | tf_op jit(solution)/shard_map/ppermute | solution.py:14
  117.8 6.5 %collective-permute-start.7 = (bf16[256,128]{1,0:T(8,128)(2,1)S(1)}, bf16[256,128]{1,0:T(8,128)(2,1)S(1)}, u32[]{:S(2)}, u32[]{:S(2)}) collective-permute-start(bf16[256,128]{1,0:T(8,128)(2,1)S(1)} %get-tuple-element.192), channel_id=1, source_target_pairs={{1,0},{2,1},{3,2},{4,3},{5,4},{6,5},{7,6},{8,7},{9,8},{10,9},{11,1... | collective-permute-start | bytes 196616 | tf_op jit(solution)/shard_map/ppermute | solution.py:17
where the time goes:
time: 126 us; the launch traced here: 125 us
  matrix products  36.5 us (29%)
  other arithmetic  36.3 us (29%)
  starting transfers between devices  30.2 us (24%)
  waiting for transfers between devices  17.4 us (14%)
  local copies, waits for them, and re-layouts  3.58 us (3%)
    dot_general x7, matrix products, forward(): jnp.dot(forward_left, tile, preferred_element_type=jnp.float32)  18.5 us
    ppermute x4, starting transfers between devices, padded(): lax.ppermute(lax.slice_in_dim(block, 0, width, axis=dim), axis, backward)  17.7 us
    add x6, other arithmetic, accumulate(): return summed + spectra[:, :length] ** 2 + spectra[:, length:] ** 2  14.4 us
    ppermute x4, starting transfers between devices, padded(): lax.ppermute(lax.slice_in_dim(block, block.shape[dim] - width, None, axis...  12.5 us
    ppermute x4, waiting for transfers between devices, padded(): lax.ppermute(lax.slice_in_dim(block, 0, width, axis=dim), axis, backward)  11.9 us
    dot_general x7, matrix products, forward(): return jnp.dot(joined, forward_right, preferred_element_type=jnp.float32)  10.2 us
    ppermute x4, waiting for transfers between devices, padded(): lax.ppermute(lax.slice_in_dim(block, block.shape[dim] - width, None, axis...  5.48 us
    neg x1, other arithmetic, make_tables(): -cos_table  5.2 us
  transfers between devices with their start and end apart: 8, of which 5 were waited for; matrix products, arithmetic and copies ran while one was open for 15% of the time, Pallas kernels for 0%

commit v1 on v0

v1 whole, which is shorter than its diff:
```python
import functools

import jax
import jax.numpy as jnp
import numpy as np
from jax import lax
from jax.experimental import pallas as pl
from jax.experimental.pallas import tpu as pltpu
from jax.sharding import PartitionSpec as P

import ml_dtypes

SMOOTH = 4
BF16 = jnp.bfloat16
F32 = jnp.float32


def host_tables(length):
    half = length // 2
    index = np.arange(length)
    phase = np.outer(index, index) % length
    cos = np.cos(2 * np.pi * phase / length)
    sin = np.sin(2 * np.pi * phase / length)
    sin[phase % half == 0] = 0.0
    cos = cos.astype(ml_dtypes.bfloat16).astype(np.float64)
    sin = sin.astype(ml_dtypes.bfloat16).astype(np.float64)

    def packed(rows):
        return np.ascontiguousarray(rows).astype(ml_dtypes.bfloat16)

    left = np.zeros((length + 16, length))
    left[:half] = cos[:half]
    left[half:length] = sin[:half]
    left[length] = cos[half]
    right = np.concatenate([cos[:, :half], sin[:, :half]], axis=1)
    right[:, half] = cos[:, half]
    inverse_right = np.concatenate([2 * cos[:half], -2 * sin[:half]], axis=0)
    inverse_right[0] = cos[0]
    inverse_right[half] = cos[half]
    order = np.concatenate([index[:half], [half], -index[1:half]])

    def near(first, second):
        apart = np.abs(first[:, None] - second[None, :]) % length
        return (np.minimum(apart, length - apart) <= SMOOTH).astype(np.float64)

    band_columns = near(order, order)
    band_rows = np.zeros((half + 16, half + 128))
    targets = np.arange(half + 1)
    band_rows[: half + 1, : half + 1] = near(targets, targets)
    first, last = half + 8, half + 16
    band_rows[: half + 1, first + 1 : first + 8] = near(targets, -np.arange(1, 8))
    band_rows[: half + 1, last : last + 8] = near(targets, -np.arange(half - 8, half))
    profile = np.sin(np.pi * (index + 0.5) / length) ** 2
    energy = np.sum(profile**2) ** 2
    return dict(
        left=packed(left),
        right=packed(right),
        inverse_right=packed(inverse_right),
        band_columns=packed(band_columns),
        band_rows=packed(band_rows),
        profile=profile.astype(np.float32),
        energy=float(energy),
    )


def dot(a, b):
    return jnp.dot(a, b, preferred_element_type=F32)


def first_column(shape):
    return lax.broadcasted_iota(jnp.int32, shape, 1) == 0


def three_parts(values):
    high = values.astype(BF16)
    rest = values - high.astype(F32)
    middle = rest.astype(BF16)
    low = (rest - middle.astype(F32)).astype(BF16)
    return high, middle, low


def quarters(spectra, half):
    length = 2 * half
    return (
        spectra[:half, :half],
        spectra[:half, half:],
        spectra[half:length, :half],
        spectra[half:length, half:],
        spectra[length : length + 8, :half],
        spectra[length : length + 8, half:],
    )


def noise_kernel(half, noise_ref, left_ref, right_ref, re_ref, im_ref):
    halves = dot(left_ref[...], noise_ref[...]).astype(BF16)
    spectra = dot(halves, right_ref[...])
    cc, cs, sc, ss, nc, ns = quarters(spectra, half)
    edge = first_column((half, half))
    re_ref[:half, :half] = jnp.where(edge, cc, cc - ss)
    re_ref[:half, half:] = jnp.where(edge, cs, cc + ss)
    im_ref[:half, :half] = -jnp.where(edge, sc, cs + sc)
    im_ref[:half, half:] = jnp.where(edge, -ss, cs - sc)
    edge = first_column((8, half))
    re_ref[half : half + 8, :half] = nc
    re_ref[half : half + 8, half:] = jnp.where(edge, ns, nc)
    im_ref[half : half + 8, :half] = jnp.where(edge, 0.0, -ns)
    im_ref[half : half + 8, half:] = jnp.where(edge, 0.0, ns)


def main_kernel(
    half, scale,
    core_ref, up_ref, down_ref, before_ref, after_ref, re_ref, im_ref,
    rows_ref, cols_ref, left_ref, right_ref, band_rows_ref, band_columns_ref,
    inverse_right_ref,
    top_ref, inside_ref, bottom_ref,
    tile, power, stacked,
):
    length = 2 * half
    margin = half // 2
    splits = core_ref.shape[0]

    def fill(source, row, col):
        height, width = source.shape[1:]
        step = 32
        pc = cols_ref[:1, col : col + width]

        def strip(number, carry):
            start = pl.multiple_of(number * step, step)
            target = pl.multiple_of(row + start, step)
            members = [source[s, pl.ds(start, step), :].astype(F32) for s in range(splits)]
            mean = functools.reduce(lambda a, b: a + b, members) * (1.0 / splits)
            weights = rows_ref[pl.ds(target, step), :1] * pc
            for s in range(splits):
                tile[s, pl.ds(target, step), col : col + width] = (
                    weights * (members[s] - mean)
                ).astype(BF16)
            return carry

        lax.fori_loop(0, height // step, strip, 0)

    fill(up_ref, 0, margin)
    fill(core_ref, margin, margin)
    fill(down_ref, margin + half, margin)
    fill(before_ref, 0, 0)
    fill(after_ref, 0, margin + half)

    power[...] = jnp.zeros_like(power)
    edge = first_column((half, half))
    edge8 = first_column((8, half))

    def accumulate(s, carry):
        halves = dot(left_ref[...], tile[s]).astype(BF16)
        spectra = dot(halves, right_ref[...])
        cc, cs, sc, ss, nc, ns = quarters(spectra, half)
        e = jnp.where(edge, cc, cc - ss)
        f = jnp.where(edge, sc, cs + sc)
        g = jnp.where(edge, cs, cc + ss)
        h = jnp.where(edge, ss, cs - sc)
        power[:half, :half] += e * e + f * f
        power[:half, half:] += g * g + h * h
        nc, ns = nc * nc, ns * ns
        power[half : half + 8, :half] += jnp.where(edge8, nc, nc + ns)
        power[half : half + 8, half:] += jnp.where(edge8, ns, nc + ns)
        return carry

    lax.fori_loop(0, splits, accumulate, 0)

    stack_rows = half + 128
    stacked[...] = jnp.zeros_like(stacked)
    for part, values in enumerate(three_parts(power[...])):
        stacked[part, : half + 8, :] = values
    for place, start in ((half + 8, 0), (half + 16, half - 8)):
        a = power[start : start + 8, :half]
        b = power[start : start + 8, half:]
        mirrored = jnp.concatenate(
            [jnp.where(edge8, a, b), jnp.where(edge8, b, a)], axis=1
        )
        for part, values in enumerate(three_parts(mirrored)):
            stacked[part, place : place + 8, :] = values
    smooth = (
        dot(band_rows_ref[...], stacked[2])
        + dot(band_rows_ref[...], stacked[1])
        + dot(band_rows_ref[...], stacked[0])
    )
    high, middle, low = three_parts(smooth)
    smooth = (
        dot(low, band_columns_ref[...])
        + dot(middle, band_columns_ref[...])
        + dot(high, band_columns_ref[...])
    )
    gain = jnp.sqrt(jnp.maximum(smooth[: half + 8], 0.0) * scale)
    gr = (gain * re_ref[...]).astype(BF16)
    gi = (gain * im_ref[...]).astype(BF16)
    er, fr = gr[:half, :half], gr[:half, half:]
    ei, fi = gi[:half, :half], gi[:half, half:]
    start = lax.broadcasted_iota(jnp.int32, (half, half), 0) == 0
    nyquist_u = gr[half : half + 1, :half]
    nyquist_v = jnp.where(edge8[:1], gr[half : half + 1, half:], gi[half : half + 1, :half])
    zero = jnp.zeros((), BF16)
    near_u = jnp.concatenate([er, jnp.where(start, nyquist_u, -ei)], axis=0)
    far_u = jnp.concatenate(
        [jnp.where(edge, er, fr), -jnp.where(edge, ei, fi)], axis=0
    )
    near_v = jnp.concatenate(
        [jnp.where(edge, fr, ei), jnp.where(start, nyquist_v, jnp.where(edge, -fi, er))], axis=0
    )
    far_v = jnp.concatenate(
        [jnp.where(edge, fr, -fi), -jnp.where(edge, fi, fr)], axis=0
    )
    start = lax.broadcasted_iota(jnp.int32, (length, half), 0) % half == 0
    far_u, far_v = jnp.where(start, zero, far_u), jnp.where(start, zero, far_v)
    u = dot(right_ref[...], near_u) + dot(right_ref[...], far_u)
    v = dot(right_ref[...], near_v) + dot(right_ref[...], far_v)
    joined = jnp.concatenate([u.astype(BF16), v.astype(BF16)], axis=1)
    real_part = dot(joined, inverse_right_ref[...])
    window = rows_ref[:, :1] * cols_ref[:1, :]
    values = window * real_part * (1.0 / (length * length))
    top_ref[...] = values[:margin].astype(BF16)
    bottom_ref[...] = values[margin + half :].astype(BF16)
    inside_ref[...] = values[margin : margin + half]


def steps(axis):
    count = lax.axis_size(axis)
    forward = [(i, i + 1) for i in range(count - 1)]
    backward = [(target, source) for source, target in forward]
    return forward, backward


def exchange(last, first, axis):
    forward, backward = steps(axis)
    return lax.ppermute(last, axis, forward), lax.ppermute(first, axis, backward)


def whole(count):
    return [pl.BlockSpec(memory_space=pltpu.VMEM)] * count


def shards(tables, split_maps, white_noise):
    splits, core_side, _ = split_maps.shape
    half = core_side
    margin = core_side // 2
    length = 2 * core_side
    constant = {k: jnp.asarray(v) for k, v in tables.items() if k != "energy"}
    profile = tables["profile"]
    rows = jnp.asarray(np.ascontiguousarray(np.broadcast_to(profile[:, None], (length, 128))))
    cols = jnp.asarray(np.ascontiguousarray(np.broadcast_to(profile[None, :], (8, length))))
    scale = 1.0 / ((2 * SMOOTH + 1) ** 2 * (splits - 1) * tables["energy"])

    spectrum = jax.ShapeDtypeStruct((half + 8, length), F32)
    re, im = pl.pallas_call(
        functools.partial(noise_kernel, half),
        out_shape=(spectrum, spectrum),
        in_specs=whole(3),
        out_specs=tuple(whole(2)),
        cost_estimate=pl.CostEstimate(flops=4 * length**3, bytes_accessed=6 * length**2, transcendentals=0),
        name="noise_spectrum",
    )(white_noise, constant["left"], constant["right"])

    up, down = exchange(split_maps[:, core_side - margin :], split_maps[:, :margin], "dec")
    tall = jnp.concatenate([up, split_maps, down], axis=1)
    before, after = exchange(tall[:, :, core_side - margin :], tall[:, :, :margin], "ra")

    strip = jax.ShapeDtypeStruct((margin, length), BF16)
    top, inside, bottom = pl.pallas_call(
        functools.partial(main_kernel, half, scale),
        out_shape=(strip, jax.ShapeDtypeStruct((half, length), F32), strip),
        in_specs=whole(14),
        out_specs=tuple(whole(3)),
        scratch_shapes=[
            pltpu.VMEM((splits, length, length), BF16),
            pltpu.VMEM((half + 8, length), F32),
            pltpu.VMEM((3, half + 128, length), BF16),
        ],
        cost_estimate=pl.CostEstimate(flops=36 * length**3, bytes_accessed=20 * length**2, transcendentals=0),
        name="tile_model",
    )(
        split_maps, up, down, before, after, re, im, rows, cols,
        constant["left"], constant["right"], constant["band_rows"], constant["band_columns"],
        constant["inverse_right"],
    )

    from_up, from_down = exchange(bottom, top, "dec")
    inside = inside + jnp.concatenate([from_up, from_down], axis=0).astype(F32)
    from_before, from_after = exchange(
        inside[:, length - margin :].astype(BF16), inside[:, :margin].astype(BF16), "ra"
    )
    return inside[:, margin : margin + core_side] + jnp.concatenate(
        [from_before, from_after], axis=1
    ).astype(F32)


def solution(mesh):
    tables = host_tables(512)
    placed = (P(None, "dec", "ra"), P("dec", "ra"))
    return jax.shard_map(
        functools.partial(shards, tables), mesh=mesh, in_specs=placed, out_specs=P("dec", "ra"), check_vma=False
    )
```

time: 126 us -> 83 us (0.66)
  matrix products: 36.5 us -> 0 us
  other arithmetic: 36.3 us -> 1.86 us
  Pallas kernels: 0 us -> 17.8 us
  waiting for transfers between devices: 17.4 us -> 29.6 us
    dot_general x18 -> x0, matrix products: 36.5 us -> none  [the longest x7 18.5 us: forward(): jnp.dot(forward_left, tile, preferred_element_type=jnp.float32)]
    pallas_call x0 -> x2, Pallas kernels: none -> 17.8 us  [the longest x1 14.7 us: shards(): pl.pallas_call(functools.partial(main_kernel, half, scale), out_shape=(st...]
    add x7 -> x1, other arithmetic: 15.1 us -> 0.74 us  [shards(): inside[:, margin:margin + core_side]]
    ppermute x8, waiting for transfers between devices: 17.4 us -> 29.6 us  [the longest x4 16.8 us: exchange(): lax.ppermute(last, axis, forward)]
    concatenate x3 -> x0, other arithmetic: 7.32 us -> none  [the longest x1 3.37 us: padded(): block = jnp.concatenate([low, block, high], axis=dim)]
    neg x1 -> x0, other arithmetic: 5.2 us -> none  [make_tables(): -cos_table]
    convert_element_type x1 -> x0, other arithmetic: 4.31 us -> none  [make_tables(): sin_table = jnp.sin(angles).astype(jnp.bfloat16)]
    reduce_sum x2 -> x0, other arithmetic: 2.94 us -> none  [the longest x1 1.97 us: shape_noise(): coadded = jnp.mean(extended.astype(jnp.float32), axis=0)]
  transfers between devices with their start and end apart: 8 -> 8, of which waited for: 5 -> 7; matrix products, arithmetic and copies ran while one was open for 15% -> 0% of each run, Pallas kernels for 0% -> 4%
where the time goes in v1:
time: 83 us; the launch traced here: 82.6 us
  starting transfers between devices  30.3 us (37%)
  waiting for transfers between devices  29.6 us (36%)
  Pallas kernels  17.8 us (21%)
  local copies, waits for them, and re-layouts  2.97 us (4%)
  other arithmetic  1.86 us (2%)
    ppermute x4, starting transfers between devices, exchange(): lax.ppermute(first, axis, backward)  18.3 us
    ppermute x4, waiting for transfers between devices, exchange(): lax.ppermute(last, axis, forward)  16.8 us
    pallas_call x1, Pallas kernels, shards(): pl.pallas_call(functools.partial(main_kernel, half, scale), out_shape=(st...  14.7 us
    ppermute x4, waiting for transfers between devices, exchange(): lax.ppermute(first, axis, backward)  12.8 us
    ppermute x4, starting transfers between devices, exchange(): lax.ppermute(last, axis, forward)  12 us
    pallas_call x1, Pallas kernels, shards(): pl.pallas_call(functools.partial(noise_kernel, half), out_shape=(spectrum...  3.09 us
  transfers between devices with their start and end apart: 8, of which 7 were waited for; matrix products, arithmetic and copies ran while one was open for 0% of the time, Pallas kernels for 4%

profile of v1, /device:TPU:15, one launch (start us, length us, event | category | flops | bytes accessed | tf_op | source)
XLA Modules:
  0.0 82.6 jit_solution(3023239159092383268)
XLA Ops:
  0.0 0.0 copy-start
  0.0 1.2 %fusion.2 = (bf16[6,128,256]{2,1,0:T(8,128)(2,1)S(1)}, bf16[6,128,256]{2,1,0:T(8,128)(2,1)S(1)}) fusion(bf16[6,256,256]{2,1,0:T(8,128)(2,1)} %core_ref.1), kind=kLoop, calls=%fused_computation.7 | loop fusion | bytes 1572864 | tf_op jit(solution)/shard_map/slice | solution.py:260
  1.2 3.5 %collective-permute-start = (bf16[6,128,256]{2,1,0:T(8,128)(2,1)S(1)}, bf16[6,128,256]{2,1,0:T(8,128)(2,1)S(1)}, u32[]{:S(2)}, u32[]{:S(2)}) collective-permute-start(bf16[6,128,256]{2,1,0:T(8,128)(2,1)S(1)} %get-tuple-element.20), channel_id=1, source_target_pairs={{0,16},{16,32},{32,48},{48,64},{64,80},{80,96},{96,112},{112,128},... | collective-permute-start | bytes 1179656 | tf_op jit(solution)/shard_map/ppermute | solution.py:232
  4.8 6.7 %collective-permute-start.1 = (bf16[6,128,256]{2,1,0:T(8,128)(2,1)S(1)}, bf16[6,128,256]{2,1,0:T(8,128)(2,1)S(1)}, u32[]{:S(2)}, u32[]{:S(2)}) collective-permute-start(bf16[6,128,256]{2,1,0:T(8,128)(2,1)S(1)} %get-tuple-element.19), channel_id=1, source_target_pairs={{16,0},{32,16},{48,32},{64,48},{80,64},{96,80},{112,96},{128,112},... | collective-permute-start | bytes 1179656 | tf_op jit(solution)/shard_map/ppermute | solution.py:232
  11.5 6.9 %collective-permute-done.up_ref = bf16[6,128,256]{2,1,0:T(8,128)(2,1)S(1)} collective-permute-done((bf16[6,128,256]{2,1,0:T(8,128)(2,1)S(1)}, bf16[6,128,256]{2,1,0:T(8,128)(2,1)S(1)}, u32[]{:S(2)}, u32[]{:S(2)}) %collective-permute-start) | collective-permute-done | bytes 393248 | tf_op jit(solution)/shard_map/ppermute | solution.py:232
  18.4 0.0 copy-start.1
  18.4 0.0 copy-done
  18.4 0.1 constant_dynamic-update-slice_fusion.1
  18.5 0.8 collective-permute-done.1.down_ref
  19.3 0.0 copy-start.2
  19.3 0.4 fusion.1
  19.7 0.0 copy-done.1
  19.7 0.3 copy-done.2
  20.0 4.0 %collective-permute-start.2 = (bf16[6,512,128]{2,1,0:T(8,128)(2,1)S(1)}, bf16[6,512,128]{2,1,0:T(8,128)(2,1)S(1)}, u32[]{:S(2)}, u32[]{:S(2)}) collective-permute-start(bf16[6,512,128]{2,1,0:T(8,128)(2,1)S(1)} %get-tuple-element.18), channel_id=1, source_target_pairs={{0,1},{1,2},{2,3},{3,4},{4,5},{5,6},{6,7},{7,8},{8,9},{9,10},{10,1... | collective-permute-start | bytes 2359304 | tf_op jit(solution)/shard_map/ppermute | solution.py:232
  24.0 1.9 %collective-permute-start.3 = (bf16[6,512,128]{2,1,0:T(8,128)(2,1)S(1)}, bf16[6,512,128]{2,1,0:T(8,128)(2,1)S(1)}, u32[]{:S(2)}, u32[]{:S(2)}) collective-permute-start(bf16[6,512,128]{2,1,0:T(8,128)(2,1)S(1)} %get-tuple-element.17), channel_id=1, source_target_pairs={{1,0},{2,1},{3,2},{4,3},{5,4},{6,5},{7,6},{8,7},{9,8},{10,9},{11,1... | collective-permute-start | bytes 2359304 | tf_op jit(solution)/shard_map/ppermute | solution.py:232
  25.9 3.1 %noise_spectrum.1 = (f32[264,512]{1,0:T(8,128)}, f32[264,512]{1,0:T(8,128)}) custom-call(bf16[512,512]{1,0:T(8,128)(2,1)} %noise_ref.1, bf16[528,512]{1,0:T(8,128)(2,1)} %constant.14.clone.left_ref, bf16[512,512]{1,0:T(8,128)(2,1)} %constant.15.clone.right_ref), custom_call_target="tpu_custom_call" | custom-call | flops 536870912 | bytes 1572864 | tf_op jit(solution)/shard_map/noise_spectrum/pallas_call | solution.py:251
  29.0 9.0 %collective-permute-done.2.before_ref = bf16[6,512,128]{2,1,0:T(8,128)(2,1)S(1)} collective-permute-done((bf16[6,512,128]{2,1,0:T(8,128)(2,1)S(1)}, bf16[6,512,128]{2,1,0:T(8,128)(2,1)S(1)}, u32[]{:S(2)}, u32[]{:S(2)}) %collective-permute-start.2) | collective-permute-done | bytes 786464 | tf_op jit(solution)/shard_map/ppermute | solution.py:232
  38.0 0.0 copy-start.3
  38.0 5.6 %collective-permute-done.3.after_ref = bf16[6,512,128]{2,1,0:T(8,128)(2,1)S(1)} collective-permute-done((bf16[6,512,128]{2,1,0:T(8,128)(2,1)S(1)}, bf16[6,512,128]{2,1,0:T(8,128)(2,1)S(1)}, u32[]{:S(2)}, u32[]{:S(2)}) %collective-permute-start.3) | collective-permute-done | bytes 786464 | tf_op jit(solution)/shard_map/ppermute | solution.py:232
  43.6 0.0 copy-done.3
  43.6 0.9 %copy-done.4 = bf16[6,512,128]{2,1,0:T(8,128)(2,1)} copy-done((bf16[6,512,128]{2,1,0:T(8,128)(2,1)}, bf16[6,512,128]{2,1,0:T(8,128)(2,1)S(1)}, u32[]{:S(2)}) %copy-start.4) | copy-done | bytes 786456
  44.5 14.7 %tile_model.1 = (bf16[128,512]{1,0:T(8,128)(2,1)}, f32[256,512]{1,0:T(8,128)}, bf16[128,512]{1,0:T(8,128)(2,1)}) custom-call(bf16[6,256,256]{2,1,0:T(8,128)(2,1)} %core_ref.1, bf16[6,128,256]{2,1,0:T(8,128)(2,1)} %copy-done.1, bf16[6,128,256]{2,1,0:T(8,128)(2,1)} %copy-done.2, bf16[6,512,128]{2,1,0:T(8,128)(2,1)} %copy-done.3, ...), custom_call_target="tpu_custom_call" | custom-call | flops 4831838208 | bytes 5242880 | tf_op jit(solution)/shard_map/tile_model/pallas_call | solution.py:265
  59.2 1.9 %collective-permute-start.4 = (bf16[128,512]{1,0:T(8,128)(2,1)}, bf16[128,512]{1,0:T(8,128)(2,1)S(1)}, u32[]{:S(2)}, u32[]{:S(2)}) collective-permute-start(bf16[128,512]{1,0:T(8,128)(2,1)} %get-tuple-element.13), channel_id=1, source_target_pairs={{0,16},{16,32},{32,48},{48,64},{64,80},{80,96},{96,112},{112,128},... | collective-permute-start | bytes 393224 | tf_op jit(solution)/shard_map/ppermute | solution.py:232
  61.1 7.7 %collective-permute-start.5 = (bf16[128,512]{1,0:T(8,128)(2,1)}, bf16[128,512]{1,0:T(8,128)(2,1)S(1)}, u32[]{:S(2)}, u32[]{:S(2)}) collective-permute-start(bf16[128,512]{1,0:T(8,128)(2,1)} %get-tuple-element.14), channel_id=1, source_target_pairs={{16,0},{32,16},{48,32},{64,48},{80,64},{96,80},{112,96},{128,112},... | collective-permute-start | bytes 393224 | tf_op jit(solution)/shard_map/ppermute | solution.py:232
  68.8 0.9 %collective-permute-done.4 = bf16[128,512]{1,0:T(8,128)(2,1)S(1)} collective-permute-done((bf16[128,512]{1,0:T(8,128)(2,1)}, bf16[128,512]{1,0:T(8,128)(2,1)S(1)}, u32[]{:S(2)}, u32[]{:S(2)}) %collective-permute-start.4) | collective-permute-done | bytes 131104 | tf_op jit(solution)/shard_map/ppermute | solution.py:232
  69.8 1.9 %collective-permute-done.5 = bf16[128,512]{1,0:T(8,128)(2,1)S(1)} collective-permute-done((bf16[128,512]{1,0:T(8,128)(2,1)}, bf16[128,512]{1,0:T(8,128)(2,1)S(1)}, u32[]{:S(2)}, u32[]{:S(2)}) %collective-permute-start.5) | collective-permute-done | bytes 131104 | tf_op jit(solution)/shard_map/ppermute | solution.py:232
  71.6 1.1 %fusion = (bf16[256,512]{1,0:T(8,128)(2,1)S(1)}, f32[256,512]{1,0:T(8,128)S(1)}) fusion(f32[256,512]{1,0:T(8,128)} %get-tuple-element.12, bf16[128,512]{1,0:T(8,128)(2,1)S(1)} %collective-permute-done.5, bf16[128,512]{1,0:T(8,128)(2,1)S(1)} %collective-permute-done.4), kind=kLoop, calls=%fused_computation.5 | loop fusion | flops 786432 | bytes 1572864 | tf_op jit(solution)/shard_map/convert.1
  72.8 2.6 %collective-permute-start.6 = (bf16[256,128]{1,0:T(8,128)(2,1)S(1)}, bf16[256,128]{1,0:T(8,128)(2,1)S(1)}, u32[]{:S(2)}, u32[]{:S(2)}) collective-permute-start(bf16[256,128]{1,0:T(8,128)(2,1)S(1)} %get-tuple-element.21), channel_id=1, source_target_pairs={{0,1},{1,2},{2,3},{3,4},{4,5},{5,6},{6,7},{7,8},{8,9},{9,10},{10,1... | collective-permute-start | bytes 196616 | tf_op jit(solution)/shard_map/ppermute | solution.py:232
  75.4 1.9 %collective-permute-start.7 = (bf16[256,128]{1,0:T(8,128)(2,1)S(1)}, bf16[256,128]{1,0:T(8,128)(2,1)S(1)}, u32[]{:S(2)}, u32[]{:S(2)}) collective-permute-start(bf16[256,128]{1,0:T(8,128)(2,1)S(1)} %get-tuple-element.22), channel_id=1, source_target_pairs={{1,0},{2,1},{3,2},{4,3},{5,4},{6,5},{7,6},{8,7},{9,8},{10,9},{11,1... | collective-permute-start | bytes 196616 | tf_op jit(solution)/shard_map/ppermute | solution.py:232
  77.3 0.0 collective-permute-done.6
  77.3 4.5 %collective-permute-done.7 = bf16[256,128]{1,0:T(8,128)(2,1)S(1)} collective-permute-done((bf16[256,128]{1,0:T(8,128)(2,1)S(1)}, bf16[256,128]{1,0:T(8,128)(2,1)S(1)}, u32[]{:S(2)}, u32[]{:S(2)}) %collective-permute-start.7) | collective-permute-done | bytes 65568 | tf_op jit(solution)/shard_map/ppermute | solution.py:232
  81.9 0.7 slice_add_fusion
  (4 shorter events, 0.1 us)
Async XLA Ops:
  0.0 18.4 %copy-start = (bf16[6,256,256]{2,1,0:T(8,128)(2,1)S(1)}, bf16[6,256,256]{2,1,0:T(8,128)(2,1)}, u32[]{:S(2)}) copy-start(bf16[6,256,256]{2,1,0:T(8,128)(2,1)} %core_ref.1) | copy-start | bytes 2359300
  1.2 17.2 %collective-permute-start = (bf16[6,128,256]{2,1,0:T(8,128)(2,1)S(1)}, bf16[6,128,256]{2,1,0:T(8,128)(2,1)S(1)}, u32[]{:S(2)}, u32[]{:S(2)}) collective-permute-start(bf16[6,128,256]{2,1,0:T(8,128)(2,1)S(1)} %get-tuple-element.20), channel_id=1, source_target_pairs={{0,16},{16,32},{32,48},{48,64},{64,80},{80,96},{96,112},{112,128},... | collective-permute-start | bytes 1179656 | tf_op jit(solution)/shard_map/ppermute | solution.py:232
  4.8 14.5 %collective-permute-start.1 = (bf16[6,128,256]{2,1,0:T(8,128)(2,1)S(1)}, bf16[6,128,256]{2,1,0:T(8,128)(2,1)S(1)}, u32[]{:S(2)}, u32[]{:S(2)}) collective-permute-start(bf16[6,128,256]{2,1,0:T(8,128)(2,1)S(1)} %get-tuple-element.19), channel_id=1, source_target_pairs={{16,0},{32,16},{48,32},{64,48},{80,64},{96,80},{112,96},{128,112},... | collective-permute-start | bytes 1179656 | tf_op jit(solution)/shard_map/ppermute | solution.py:232
  18.4 1.3 %copy-start.1 = (bf16[6,128,256]{2,1,0:T(8,128)(2,1)}, bf16[6,128,256]{2,1,0:T(8,128)(2,1)S(1)}, u32[]{:S(2)}) copy-start(bf16[6,128,256]{2,1,0:T(8,128)(2,1)S(1)} %collective-permute-done.up_ref) | copy-start | bytes 1179652
  19.3 0.7 copy-start.2
  20.0 18.0 %collective-permute-start.2 = (bf16[6,512,128]{2,1,0:T(8,128)(2,1)S(1)}, bf16[6,512,128]{2,1,0:T(8,128)(2,1)S(1)}, u32[]{:S(2)}, u32[]{:S(2)}) collective-permute-start(bf16[6,512,128]{2,1,0:T(8,128)(2,1)S(1)} %get-tuple-element.18), channel_id=1, source_target_pairs={{0,1},{1,2},{2,3},{3,4},{4,5},{5,6},{6,7},{7,8},{8,9},{9,10},{10,1... | collective-permute-start | bytes 2359304 | tf_op jit(solution)/shard_map/ppermute | solution.py:232
  24.0 19.6 %collective-permute-start.3 = (bf16[6,512,128]{2,1,0:T(8,128)(2,1)S(1)}, bf16[6,512,128]{2,1,0:T(8,128)(2,1)S(1)}, u32[]{:S(2)}, u32[]{:S(2)}) collective-permute-start(bf16[6,512,128]{2,1,0:T(8,128)(2,1)S(1)} %get-tuple-element.17), channel_id=1, source_target_pairs={{1,0},{2,1},{3,2},{4,3},{5,4},{6,5},{7,6},{8,7},{9,8},{10,9},{11,1... | collective-permute-start | bytes 2359304 | tf_op jit(solution)/shard_map/ppermute | solution.py:232
  38.0 5.6 %copy-start.3 = (bf16[6,512,128]{2,1,0:T(8,128)(2,1)}, bf16[6,512,128]{2,1,0:T(8,128)(2,1)S(1)}, u32[]{:S(2)}) copy-start(bf16[6,512,128]{2,1,0:T(8,128)(2,1)S(1)} %collective-permute-done.2.before_ref) | copy-start | bytes 2359300
  43.6 0.9 %copy-start.4 = (bf16[6,512,128]{2,1,0:T(8,128)(2,1)}, bf16[6,512,128]{2,1,0:T(8,128)(2,1)S(1)}, u32[]{:S(2)}) copy-start(bf16[6,512,128]{2,1,0:T(8,128)(2,1)S(1)} %collective-permute-done.3.after_ref) | copy-start | bytes 2359300
  59.2 10.6 %collective-permute-start.4 = (bf16[128,512]{1,0:T(8,128)(2,1)}, bf16[128,512]{1,0:T(8,128)(2,1)S(1)}, u32[]{:S(2)}, u32[]{:S(2)}) collective-permute-start(bf16[128,512]{1,0:T(8,128)(2,1)} %get-tuple-element.13), channel_id=1, source_target_pairs={{0,16},{16,32},{32,48},{48,64},{64,80},{80,96},{96,112},{112,128},... | collective-permute-start | bytes 393224 | tf_op jit(solution)/shard_map/ppermute | solution.py:232
  61.1 10.5 %collective-permute-start.5 = (bf16[128,512]{1,0:T(8,128)(2,1)}, bf16[128,512]{1,0:T(8,128)(2,1)S(1)}, u32[]{:S(2)}, u32[]{:S(2)}) collective-permute-start(bf16[128,512]{1,0:T(8,128)(2,1)} %get-tuple-element.14), channel_id=1, source_target_pairs={{16,0},{32,16},{48,32},{64,48},{80,64},{96,80},{112,96},{128,112},... | collective-permute-start | bytes 393224 | tf_op jit(solution)/shard_map/ppermute | solution.py:232
  72.8 4.5 %collective-permute-start.6 = (bf16[256,128]{1,0:T(8,128)(2,1)S(1)}, bf16[256,128]{1,0:T(8,128)(2,1)S(1)}, u32[]{:S(2)}, u32[]{:S(2)}) collective-permute-start(bf16[256,128]{1,0:T(8,128)(2,1)S(1)} %get-tuple-element.21), channel_id=1, source_target_pairs={{0,1},{1,2},{2,3},{3,4},{4,5},{5,6},{6,7},{7,8},{8,9},{9,10},{10,1... | collective-permute-start | bytes 196616 | tf_op jit(solution)/shard_map/ppermute | solution.py:232
  75.4 6.5 %collective-permute-start.7 = (bf16[256,128]{1,0:T(8,128)(2,1)S(1)}, bf16[256,128]{1,0:T(8,128)(2,1)S(1)}, u32[]{:S(2)}, u32[]{:S(2)}) collective-permute-start(bf16[256,128]{1,0:T(8,128)(2,1)S(1)} %get-tuple-element.22), channel_id=1, source_target_pairs={{1,0},{2,1},{3,2},{4,3},{5,4},{6,5},{7,6},{8,7},{9,8},{10,9},{11,1... | collective-permute-start | bytes 196616 | tf_op jit(solution)/shard_map/ppermute | solution.py:232

commit v2 on v1

--- a/solution.py
+++ b/solution.py
@@ -34,6 +34,9 @@
     left[length] = cos[half]
     right = np.concatenate([cos[:, :half], sin[:, :half]], axis=1)
     right[:, half] = cos[:, half]
+    margin = half // 2
+    right = np.roll(right, -margin, axis=0)
+    right = np.concatenate([right[:half], np.roll(right[half:], margin, axis=0)], axis=0)
     inverse_right = np.concatenate([2 * cos[:half], -2 * sin[:half]], axis=0)
     inverse_right[0] = cos[0]
     inverse_right[half] = cos[half]
@@ -92,8 +95,13 @@
 
 
 def noise_kernel(half, noise_ref, left_ref, right_ref, re_ref, im_ref):
+    margin = half // 2
     halves = dot(left_ref[...], noise_ref[...]).astype(BF16)
-    spectra = dot(halves, right_ref[...])
+    spectra = (
+        dot(halves[:, margin : margin + half], right_ref[:half])
+        + dot(halves[:, :margin], right_ref[half : half + margin])
+        + dot(halves[:, margin + half :], right_ref[half + margin :])
+    )
     cc, cs, sc, ss, nc, ns = quarters(spectra, half)
     edge = first_column((half, half))
     re_ref[:half, :half] = jnp.where(edge, cc, cc - ss)
@@ -107,66 +115,102 @@
     im_ref[half : half + 8, half:] = jnp.where(edge, 0.0, ns)
 
 
+def aligned(offset, step):
+    return offset if isinstance(offset, int) else pl.multiple_of(offset, step)
+
+
+def fill(tile, source, rows_ref, cols_ref, source_row, height, row, col, tile_col):
+    splits, width = source.shape[0], source.shape[2]
+    step = 32
+    pc = cols_ref[:1, pl.ds(aligned(col, 128), width)]
+
+    def strip(number, carry):
+        start = pl.multiple_of(source_row + number * step, step)
+        target = pl.multiple_of(row + number * step, step)
+        members = [source[s, pl.ds(start, step), :].astype(F32) for s in range(splits)]
+        mean = functools.reduce(lambda a, b: a + b, members) * (1.0 / splits)
+        weights = rows_ref[pl.ds(target, step), :1] * pc
+        for s in range(splits):
+            tile[s, pl.ds(target, step), pl.ds(aligned(tile_col, 128), width)] = (
+                weights * (members[s] - mean)
+            ).astype(BF16)
+        return carry
+
+    lax.fori_loop(0, height // step, strip, 0)
+
+
+def sides(half):
+    far = half + half // 2
+    first = jnp.where(lax.axis_index("dec") % 2 == 0, far, 0)
+    outer = jnp.where(lax.axis_index("ra") % 2 == 0, 0, far)
+    return first, far - first, outer, far - outer
+
+
+def core_kernel(half, core_ref, first_ref, second_ref, rows_ref, cols_ref, left_ref, halves_ref, tile):
+    margin = half // 2
+    splits = core_ref.shape[0]
+    first, second, _, _ = sides(half)
+    fill(tile, core_ref, rows_ref, cols_ref, 0, half, margin, margin, 0)
+    fill(tile, first_ref, rows_ref, cols_ref, 0, margin, first, margin, 0)
+    fill(tile, second_ref, rows_ref, cols_ref, 0, margin, second, margin, 0)
+
+    def transform(s, carry):
+        halves_ref[s] = dot(left_ref[...], tile[s]).astype(BF16)
+        return carry
+
+    lax.fori_loop(0, splits, transform, 0)
+
+
 def main_kernel(
     half, scale,
-    core_ref, up_ref, down_ref, before_ref, after_ref, re_ref, im_ref,
+    core_ref, outer_ref, first_ref, second_ref, inner_ref, re_ref, im_ref,
     rows_ref, cols_ref, left_ref, right_ref, band_rows_ref, band_columns_ref,
     inverse_right_ref,
-    top_ref, inside_ref, bottom_ref,
-    tile, power, stacked,
+    first_out_ref, second_out_ref, inside_ref,
+    tile, power, stacked, strips,
 ):
     length = 2 * half
     margin = half // 2
     splits = core_ref.shape[0]
-
-    def fill(source, row, col):
-        height, width = source.shape[1:]
-        step = 32
-        pc = cols_ref[:1, col : col + width]
-
-        def strip(number, carry):
-            start = pl.multiple_of(number * step, step)
-            target = pl.multiple_of(row + start, step)
-            members = [source[s, pl.ds(start, step), :].astype(F32) for s in range(splits)]
-            mean = functools.reduce(lambda a, b: a + b, members) * (1.0 / splits)
-            weights = rows_ref[pl.ds(target, step), :1] * pc
-            for s in range(splits):
-                tile[s, pl.ds(target, step), col : col + width] = (
-                    weights * (members[s] - mean)
-                ).astype(BF16)
-            return carry
-
-        lax.fori_loop(0, height // step, strip, 0)
-
-    fill(up_ref, 0, margin)
-    fill(core_ref, margin, margin)
-    fill(down_ref, margin + half, margin)
-    fill(before_ref, 0, 0)
-    fill(after_ref, 0, margin + half)
-
-    power[...] = jnp.zeros_like(power)
+    first, second, outer, inner = sides(half)
+    outer_col = jnp.where(outer == 0, 0, margin)
+    inner_col = margin - outer_col
+    fill(tile, outer_ref, rows_ref, cols_ref, 0, half, margin, outer, outer_col)
+    fill(tile, first_ref, rows_ref, cols_ref, 0, margin, first, outer, outer_col)
+    fill(tile, second_ref, rows_ref, cols_ref, 0, margin, second, outer, outer_col)
+    fill(tile, inner_ref, rows_ref, cols_ref, 0, margin, first, inner, inner_col)
+    fill(tile, inner_ref, rows_ref, cols_ref, margin, half, margin, inner, inner_col)
+    fill(tile, inner_ref, rows_ref, cols_ref, margin + half, margin, second, inner, inner_col)
+
     edge = first_column((half, half))
     edge8 = first_column((8, half))
 
     def accumulate(s, carry):
-        halves = dot(left_ref[...], tile[s]).astype(BF16)
+        halves = jnp.concatenate(
+            [core_ref[s], dot(left_ref[...], tile[s]).astype(BF16)], axis=1
+        )
         spectra = dot(halves, right_ref[...])
         cc, cs, sc, ss, nc, ns = quarters(spectra, half)
         e = jnp.where(edge, cc, cc - ss)
         f = jnp.where(edge, sc, cs + sc)
         g = jnp.where(edge, cs, cc + ss)
         h = jnp.where(edge, ss, cs - sc)
-        power[:half, :half] += e * e + f * f
-        power[:half, half:] += g * g + h * h
         nc, ns = nc * nc, ns * ns
-        power[half : half + 8, :half] += jnp.where(edge8, nc, nc + ns)
-        power[half : half + 8, half:] += jnp.where(edge8, ns, nc + ns)
-        return carry
-
-    lax.fori_loop(0, splits, accumulate, 0)
-
-    stack_rows = half + 128
-    stacked[...] = jnp.zeros_like(stacked)
+        terms = (
+            e * e + f * f, g * g + h * h, jnp.where(edge8, nc, nc + ns), jnp.where(edge8, ns, nc + ns)
+        )
+        places = (
+            (slice(0, half), slice(0, half)), (slice(0, half), slice(half, length)),
+            (slice(half, half + 8), slice(0, half)), (slice(half, half + 8), slice(half, length)),
+        )
+        for term, place in zip(terms, places):
+            power[place] = term if carry else power[place] + term
+
+    accumulate(0, True)
+    for s in range(1, splits):
+        accumulate(s, False)
+
+    stacked[:, half + 24 :, :] = jnp.zeros((3, stacked.shape[1] - half - 24, length), BF16)
     for part, values in enumerate(three_parts(power[...])):
         stacked[part, : half + 8, :] = values
     for place, start in ((half + 8, 0), (half + 16, half - 8)):
@@ -213,27 +257,55 @@
     v = dot(right_ref[...], near_v) + dot(right_ref[...], far_v)
     joined = jnp.concatenate([u.astype(BF16), v.astype(BF16)], axis=1)
     real_part = dot(joined, inverse_right_ref[...])
-    window = rows_ref[:, :1] * cols_ref[:1, :]
-    values = window * real_part * (1.0 / (length * length))
-    top_ref[...] = values[:margin].astype(BF16)
-    bottom_ref[...] = values[margin + half :].astype(BF16)
-    inside_ref[...] = values[margin : margin + half]
-
-
-def steps(axis):
+    norm = 1.0 / (length * length)
+    pc = cols_ref[:1, :]
+    inside_ref[...] = rows_ref[margin : margin + half, :1] * pc * real_part[:half] * norm
+    strips[:margin] = (rows_ref[:margin, :1] * pc * real_part[half : half + margin] * norm).astype(BF16)
+    strips[margin:] = (rows_ref[margin + half :, :1] * pc * real_part[half + margin :] * norm).astype(BF16)
+    place = pl.multiple_of(jnp.where(first == 0, 0, margin), margin)
+    first_out_ref[...] = strips[pl.ds(place, margin), :]
+    second_out_ref[...] = strips[pl.ds(pl.multiple_of(margin - place, margin), margin), :]
+
+
+def fold_rows_kernel(half, inside_ref, first_ref, second_ref, center_ref, outer_ref, inner_ref, total):
+    margin = half // 2
+    first, second, outer, inner = sides(half)
+    for source, place in ((first_ref, first), (second_ref, second)):
+        rows = pl.ds(pl.multiple_of(jnp.where(place == 0, 0, margin), margin), margin)
+        total[rows, :] = inside_ref[rows, :] + source[...].astype(F32)
+    center_ref[...] = total[:, margin : margin + half]
+    outer_ref[...] = total[:, pl.ds(pl.multiple_of(outer, margin), margin)].astype(BF16)
+    inner_ref[...] = total[:, pl.ds(pl.multiple_of(inner, margin), margin)].astype(BF16)
+
+
+def fold_columns_kernel(half, center_ref, outer_ref, inner_ref, out_ref):
+    margin = half // 2
+    _, _, outer, inner = sides(half)
+    for source, place in ((outer_ref, outer), (inner_ref, inner)):
+        columns = pl.ds(pl.multiple_of(jnp.where(place == 0, 0, margin), margin), margin)
+        out_ref[:, columns] = center_ref[:, columns] + source[...].astype(F32)
+
+
+def swap(values, axis, offset):
     count = lax.axis_size(axis)
-    forward = [(i, i + 1) for i in range(count - 1)]
-    backward = [(target, source) for source, target in forward]
-    return forward, backward
-
-
-def exchange(last, first, axis):
-    forward, backward = steps(axis)
-    return lax.ppermute(last, axis, forward), lax.ppermute(first, axis, backward)
+    pairs = [(i, i + 1) for i in range(offset, count - 1, 2)]
+    return lax.ppermute(values, axis, pairs + [(b, a) for a, b in pairs])
 
 
 def whole(count):
     return [pl.BlockSpec(memory_space=pltpu.VMEM)] * count
+
+
+def kernel_call(body, name, outs, count, scratch=(), flops=0):
+    return pl.pallas_call(
+        body,
+        out_shape=outs,
+        in_specs=whole(count),
+        out_specs=jax.tree.map(lambda _: pl.BlockSpec(memory_space=pltpu.VMEM), outs),
+        scratch_shapes=list(scratch),
+        cost_estimate=pl.CostEstimate(flops=flops, bytes_accessed=1 << 20, transcendentals=0),
+        name=name,
+    )
 
 
 def shards(tables, split_maps, white_noise):
@@ -246,48 +318,76 @@
     rows = jnp.asarray(np.ascontiguousarray(np.broadcast_to(profile[:, None], (length, 128))))
     cols = jnp.asarray(np.ascontiguousarray(np.broadcast_to(profile[None, :], (8, length))))
     scale = 1.0 / ((2 * SMOOTH + 1) ** 2 * (splits - 1) * tables["energy"])
+    odd_row = lax.axis_index("dec") % 2
+    odd_col = lax.axis_index("ra") % 2
+    cube = length**3
+
+    outer_columns = lax.dynamic_slice_in_dim(split_maps, odd_col * margin, margin, axis=2)
+    first_rows = lax.dynamic_slice_in_dim(split_maps, (1 - odd_row) * margin, margin, axis=1)
+    second_rows = lax.dynamic_slice_in_dim(split_maps, odd_row * margin, margin, axis=1)
+    outer = swap(outer_columns, "ra", 1)
+    first = swap(first_rows, "dec", 0)
+    second = swap(second_rows, "dec", 1)
 
     spectrum = jax.ShapeDtypeStruct((half + 8, length), F32)
-    re, im = pl.pallas_call(
-        functools.partial(noise_kernel, half),
-        out_shape=(spectrum, spectrum),
-        in_specs=whole(3),
-        out_specs=tuple(whole(2)),
-        cost_estimate=pl.CostEstimate(flops=4 * length**3, bytes_accessed=6 * length**2, transcendentals=0),
-        name="noise_spectrum",
+    re, im = kernel_call(
+        functools.partial(noise_kernel, half), "noise_spectrum", (spectrum, spectrum), 3, flops=3 * cube
     )(white_noise, constant["left"], constant["right"])
 
-    up, down = exchange(split_maps[:, core_side - margin :], split_maps[:, :margin], "dec")
-    tall = jnp.concatenate([up, split_maps, down], axis=1)
-    before, after = exchange(tall[:, :, core_side - margin :], tall[:, :, :margin], "ra")
+    first_corner = swap(lax.dynamic_slice_in_dim(outer, (1 - odd_row) * margin, margin, axis=1), "dec", 0)
+    second_corner = swap(lax.dynamic_slice_in_dim(outer, odd_row * margin, margin, axis=1), "dec", 1)
+    inner = swap(
+        jnp.concatenate(
+            [
+                lax.dynamic_slice_in_dim(block, (1 - odd_col) * margin, margin, axis=2)
+                for block in (first, split_maps, second)
+            ],
+            axis=1,
+        ),
+        "ra",
+        0,
+    )
+    halves = kernel_call(
+        functools.partial(core_kernel, half),
+        "core_columns",
+        jax.ShapeDtypeStruct((splits, length + 16, half), BF16),
+        6,
+        [pltpu.VMEM((splits, length, half), BF16)],
+        flops=6 * cube,
+    )(split_maps, first, second, rows, cols, constant["left"])
 
     strip = jax.ShapeDtypeStruct((margin, length), BF16)
-    top, inside, bottom = pl.pallas_call(
+    first, second, inside = kernel_call(
         functools.partial(main_kernel, half, scale),
-        out_shape=(strip, jax.ShapeDtypeStruct((half, length), F32), strip),
-        in_specs=whole(14),
-        out_specs=tuple(whole(3)),
-        scratch_shapes=[
-            pltpu.VMEM((splits, length, length), BF16),
+        "tile_model",
+        (strip, strip, jax.ShapeDtypeStruct((half, length), F32)),
+        14,
+        [
+            pltpu.VMEM((splits, length, half), BF16),
             pltpu.VMEM((half + 8, length), F32),
             pltpu.VMEM((3, half + 128, length), BF16),
+            pltpu.VMEM((half, length), BF16),
         ],
-        cost_estimate=pl.CostEstimate(flops=36 * length**3, bytes_accessed=20 * length**2, transcendentals=0),
-        name="tile_model",
+        flops=20 * cube,
     )(
-        split_maps, up, down, before, after, re, im, rows, cols,
+        halves, outer, first_corner, second_corner, inner, re, im, rows, cols,
         constant["left"], constant["right"], constant["band_rows"], constant["band_columns"],
         constant["inverse_right"],
     )
 
-    from_up, from_down = exchange(bottom, top, "dec")
-    inside = inside + jnp.concatenate([from_up, from_down], axis=0).astype(F32)
-    from_before, from_after = exchange(
-        inside[:, length - margin :].astype(BF16), inside[:, :margin].astype(BF16), "ra"
-    )
-    return inside[:, margin : margin + core_side] + jnp.concatenate(
-        [from_before, from_after], axis=1
-    ).astype(F32)
+    first = swap(first, "dec", 0)
+    second = swap(second, "dec", 1)
+    column = jax.ShapeDtypeStruct((half, margin), BF16)
+    block = jax.ShapeDtypeStruct((half, half), F32)
+    center, outer, inner = kernel_call(
+        functools.partial(fold_rows_kernel, half), "fold_rows", (block, column, column), 3,
+        [pltpu.VMEM((half, length), F32)],
+    )(inside, first, second)
+    outer = swap(outer, "ra", 1)
+    inner = swap(inner, "ra", 0)
+    return kernel_call(functools.partial(fold_columns_kernel, half), "fold_columns", block, 3)(
+        center, outer, inner
+    )
 
 
 def solution(mesh):

time: 83 us -> 87.6 us (1.055)
  Pallas kernels: 17.8 us -> 24.6 us
  starting transfers between devices: 30.3 us -> 26.7 us
  waiting for transfers between devices: 29.6 us -> 32 us
  other arithmetic: 1.86 us -> 0.05 us
    pallas_call x2 -> x5, Pallas kernels: 17.8 us -> 24.6 us  [the longest x1 11.7 us: shards(): kernel_call(functools.partial(main_kernel, half, scale), 'tile_model', (s...]
    ppermute x8 -> x10, starting transfers between devices: 30.3 us -> 26.7 us  [swap(): return lax.ppermute(values, axis, pairs + [(b, a) for a, b in pairs])]
    ppermute x8 -> x10, waiting for transfers between devices: 29.6 us -> 32 us  [swap(): return lax.ppermute(values, axis, pairs + [(b, a) for a, b in pairs])]
    slice x3 -> x0, local copies, waits for them, and re-layouts: 1.62 us -> none  [the longest x1 1.24 us: shards(): split_maps[:, :margin]]
    dynamic_slice x0 -> x5, local copies, waits for them, and re-layouts: none -> 1.48 us  [the longest x1 1.24 us: shards(): lax.dynamic_slice_in_dim(split_maps, odd_row * margin, margin, axis=1)]
    another operation x1 -> x0, other arithmetic: 1.12 us -> none
    unnamed x12 -> x22, local copies, waits for them, and re-layouts: 1.33 us -> 2.28 us
  transfers between devices with their start and end apart: 8 -> 10, of which waited for: 7 -> 6; matrix products, arithmetic and copies ran while one was open for 0% -> 0% of each run, Pallas kernels for 4% -> 11%
where the time goes in v2:
time: 87.6 us; the launch traced here: 87.3 us
  waiting for transfers between devices  32 us (37%)
  starting transfers between devices  26.7 us (30%)
  Pallas kernels  24.6 us (28%)
  local copies, waits for them, and re-layouts  3.77 us (4%)
    ppermute x10, waiting for transfers between devices, swap(): return lax.ppermute(values, axis, pairs + [(b, a) for a, b in pairs])  32 us
    ppermute x10, starting transfers between devices, swap(): return lax.ppermute(values, axis, pairs + [(b, a) for a, b in pairs])  26.7 us
    pallas_call x1, Pallas kernels, shards(): kernel_call(functools.partial(main_kernel, half, scale), 'tile_model', (s...  11.7 us
    pallas_call x1, Pallas kernels, shards(): kernel_call(functools.partial(core_kernel, half), 'core_columns', jax.Sha...  5.99 us
    pallas_call x1, Pallas kernels, shards(): kernel_call(functools.partial(noise_kernel, half), 'noise_spectrum', (spe...  3.22 us
    unnamed x22, local copies, waits for them, and re-layouts  2.28 us
    pallas_call x1, Pallas kernels, shards(): kernel_call(functools.partial(fold_rows_kernel, half), 'fold_rows', (bloc...  2.01 us
  transfers between devices with their start and end apart: 10, of which 6 were waited for; matrix products, arithmetic and copies ran while one was open for 0% of the time, Pallas kernels for 11%

profile of v2, /device:TPU:15, one launch (start us, length us, event | category | flops | bytes accessed | tf_op | source)
XLA Modules:
  0.0 87.3 jit_solution(7917615927376566065)
XLA Ops:
  0.0 1.2 %constant_dynamic-slice_fusion.6 = (bf16[6,128,256]{2,1,0:T(8,128)(2,1)S(1)}, bf16[6,128,256]{2,1,0:T(8,128)(2,1)S(1)}) fusion(bf16[6,256,256]{2,1,0:T(8,128)(2,1)} %core_ref.1, s32[]{:T(128)S(6)} %select_n.29, s32[]{:T(128)S(6)} %select_n.28), kind=kLoop, calls=%fused_computation.7 | loop fusion | bytes 1572872 | tf_op jit(solution)/shard_map/dynamic_slice | solution.py:327
  1.2 8.3 %collective-permute-start.1 = (bf16[6,128,256]{2,1,0:T(8,128)(2,1)S(1)}, bf16[6,128,256]{2,1,0:T(8,128)(2,1)S(1)}, u32[]{:S(2)}, u32[]{:S(2)}) collective-permute-start(bf16[6,128,256]{2,1,0:T(8,128)(2,1)S(1)} %get-tuple-element.23), channel_id=1, source_target_pairs={{16,32},{48,64},{80,96},{112,128},{144,160},{176,192},{208,224},{3... | collective-permute-start | bytes 1179656 | tf_op jit(solution)/shard_map/ppermute | solution.py:292
  9.6 0.1 collective-permute-start
  9.7 0.1 constant_dynamic-slice_fusion.1
  9.9 8.5 %collective-permute-done.1.second_ref = bf16[6,128,256]{2,1,0:T(8,128)(2,1)S(1)} collective-permute-done((bf16[6,128,256]{2,1,0:T(8,128)(2,1)S(1)}, bf16[6,128,256]{2,1,0:T(8,128)(2,1)S(1)}, u32[]{:S(2)}, u32[]{:S(2)}) %collective-permute-start.1) | collective-permute-done | bytes 393248 | tf_op jit(solution)/shard_map/ppermute | solution.py:292
  18.4 0.9 %collective-permute-done.first_ref = bf16[6,128,256]{2,1,0:T(8,128)(2,1)S(1)} collective-permute-done((bf16[6,128,256]{2,1,0:T(8,128)(2,1)S(1)}, bf16[6,128,256]{2,1,0:T(8,128)(2,1)S(1)}, u32[]{:S(2)}, u32[]{:S(2)}) %collective-permute-start) | collective-permute-done | bytes 393248 | tf_op jit(solution)/shard_map/ppermute | solution.py:292
  19.4 0.1 pad_maximum_fusion
  19.4 2.0 %collective-permute-start.5 = (bf16[6,512,128]{2,1,0:T(8,128)(2,1)S(1)}, bf16[6,512,128]{2,1,0:T(8,128)(2,1)S(1)}, u32[]{:S(2)}, u32[]{:S(2)}) collective-permute-start(bf16[6,512,128]{2,1,0:T(8,128)(2,1)S(1)} %pad_maximum_fusion), channel_id=1, source_target_pairs={{0,1},{2,3},{4,5},{6,7},{8,9},{10,11},{12,13},{14,15},{1,0},{3,2},... | collective-permute-start | bytes 2359304 | tf_op jit(solution)/shard_map/ppermute | solution.py:292
  21.4 2.5 %collective-permute-start.2 = (bf16[6,256,128]{2,1,0:T(8,128)(2,1)S(1)}, bf16[6,256,128]{2,1,0:T(8,128)(2,1)S(1)}, u32[]{:S(2)}, u32[]{:S(2)}) collective-permute-start(bf16[6,256,128]{2,1,0:T(8,128)(2,1)S(1)} %get-tuple-element.22), channel_id=1, source_target_pairs={{1,2},{3,4},{5,6},{7,8},{9,10},{11,12},{13,14},{2,1},{4,3},{6,5},{... | collective-permute-start | bytes 1179656 | tf_op jit(solution)/shard_map/ppermute | solution.py:292
  23.9 11.2 %collective-permute-done.2.outer_ref = bf16[6,256,128]{2,1,0:T(8,128)(2,1)S(1)} collective-permute-done((bf16[6,256,128]{2,1,0:T(8,128)(2,1)S(1)}, bf16[6,256,128]{2,1,0:T(8,128)(2,1)S(1)}, u32[]{:S(2)}, u32[]{:S(2)}) %collective-permute-start.2) | collective-permute-done | bytes 393248 | tf_op jit(solution)/shard_map/ppermute | solution.py:292
  35.1 5.5 %collective-permute-start.4 = (bf16[6,128,128]{2,1,0:T(8,128)(2,1)S(1)}, bf16[6,128,128]{2,1,0:T(8,128)(2,1)S(1)}, u32[]{:S(2)}, u32[]{:S(2)}) collective-permute-start(bf16[6,128,128]{2,1,0:T(8,128)(2,1)S(1)} %get-tuple-element.25), channel_id=1, source_target_pairs={{16,32},{48,64},{80,96},{112,128},{144,160},{176,192},{208,224},{3... | collective-permute-start | bytes 589832 | tf_op jit(solution)/shard_map/ppermute | solution.py:292
  40.6 0.1 collective-permute-start.3
  40.7 3.2 %noise_spectrum.1 = (f32[264,512]{1,0:T(8,128)}, f32[264,512]{1,0:T(8,128)}) custom-call(bf16[512,512]{1,0:T(8,128)(2,1)} %noise_ref.1, bf16[528,512]{1,0:T(8,128)(2,1)} %constant.44.clone.left_ref, bf16[512,512]{1,0:T(8,128)(2,1)} %constant.45.clone.right_ref), custom_call_target="tpu_custom_call" | custom-call | flops 402653184 | bytes 1048576 | tf_op jit(solution)/shard_map/noise_spectrum/pallas_call | solution.py:333
  43.9 6.0 %core_columns.1.core_ref = bf16[6,528,256]{2,1,0:T(8,128)(2,1)} custom-call(bf16[6,256,256]{2,1,0:T(8,128)(2,1)} %core_ref.1, bf16[6,128,256]{2,1,0:T(8,128)(2,1)} %copy-done.2, bf16[6,128,256]{2,1,0:T(8,128)(2,1)} %copy-done.1, f32[512,128]{1,0:T(8,128)} %constant.49.clone.rows_ref, f32[8,512]{1,0:T(8,128)} %constant.50.clone.cols_ref, ...), custom_call_target="tpu_custom_call" | custom-call | flops 805306368 | bytes 1048576 | tf_op jit(solution)/shard_map/core_columns/pallas_call | solution.py:350
  49.9 0.0 collective-permute-done.4.second_ref
  49.9 0.0 copy-start.10
  49.9 0.6 copy-done.9
  50.6 0.1 copy-done.10
  50.6 0.3 copy-done.8
  50.9 11.7 %tile_model.1 = (bf16[128,512]{1,0:T(8,128)(2,1)}, bf16[128,512]{1,0:T(8,128)(2,1)}, f32[256,512]{1,0:T(8,128)}) custom-call(bf16[6,528,256]{2,1,0:T(8,128)(2,1)} %core_columns.1.core_ref, bf16[6,256,128]{2,1,0:T(8,128)(2,1)} %copy-done.3, bf16[6,128,128]{2,1,0:T(8,128)(2,1)} %copy-done.10, bf16[6,128,128]{2,1,0:T(8,128)(2,1)} %copy-done.9, ...), custom_call_target="tpu_custom_call" | custom-call | flops 2684354560 | bytes 1048576 | tf_op jit(solution)/shard_map/tile_model/pallas_call | solution.py:360
  62.6 1.4 %collective-permute-start.6 = (bf16[128,512]{1,0:T(8,128)(2,1)}, bf16[128,512]{1,0:T(8,128)(2,1)S(1)}, u32[]{:S(2)}, u32[]{:S(2)}) collective-permute-start(bf16[128,512]{1,0:T(8,128)(2,1)} %get-tuple-element.16), channel_id=1, source_target_pairs={{0,16},{32,48},{64,80},{96,112},{128,144},{160,176},{192,208},{224... | collective-permute-start | bytes 393224 | tf_op jit(solution)/shard_map/ppermute | solution.py:292
  64.1 3.4 %collective-permute-start.7 = (bf16[128,512]{1,0:T(8,128)(2,1)}, bf16[128,512]{1,0:T(8,128)(2,1)S(1)}, u32[]{:S(2)}, u32[]{:S(2)}) collective-permute-start(bf16[128,512]{1,0:T(8,128)(2,1)} %get-tuple-element.17), channel_id=1, source_target_pairs={{16,32},{48,64},{80,96},{112,128},{144,160},{176,192},{208,224},{3... | collective-permute-start | bytes 393224 | tf_op jit(solution)/shard_map/ppermute | solution.py:292
  67.5 0.7 collective-permute-done.6.first_ref
  68.2 6.7 %collective-permute-done.7.second_ref = bf16[128,512]{1,0:T(8,128)(2,1)S(1)} collective-permute-done((bf16[128,512]{1,0:T(8,128)(2,1)}, bf16[128,512]{1,0:T(8,128)(2,1)S(1)}, u32[]{:S(2)}, u32[]{:S(2)}) %collective-permute-start.7) | collective-permute-done | bytes 131104 | tf_op jit(solution)/shard_map/ppermute | solution.py:292
  74.9 0.6 copy-done.5
  75.6 2.0 %fold_rows.1 = (f32[256,256]{1,0:T(8,128)}, bf16[256,128]{1,0:T(8,128)(2,1)}, bf16[256,128]{1,0:T(8,128)(2,1)}) custom-call(f32[256,512]{1,0:T(8,128)} %get-tuple-element.15.inside_ref, bf16[128,512]{1,0:T(8,128)(2,1)} %copy-done.4, bf16[128,512]{1,0:T(8,128)(2,1)} %copy-done.5), custom_call_target="tpu_custom_call" | custom-call | bytes 1048576 | tf_op jit(solution)/shard_map/fold_rows/pallas_call | solution.py:382
  77.6 3.3 %collective-permute-start.8 = (bf16[256,128]{1,0:T(8,128)(2,1)}, bf16[256,128]{1,0:T(8,128)(2,1)S(1)}, u32[]{:S(2)}, u32[]{:S(2)}) collective-permute-start(bf16[256,128]{1,0:T(8,128)(2,1)} %get-tuple-element.19), channel_id=1, source_target_pairs={{1,2},{3,4},{5,6},{7,8},{9,10},{11,12},{13,14},{2,1},{4,3},{6,5},{... | collective-permute-start | bytes 196616 | tf_op jit(solution)/shard_map/ppermute | solution.py:292
  80.9 0.1 collective-permute-start.9
  81.0 3.9 %collective-permute-done.8.outer_ref = bf16[256,128]{1,0:T(8,128)(2,1)S(1)} collective-permute-done((bf16[256,128]{1,0:T(8,128)(2,1)}, bf16[256,128]{1,0:T(8,128)(2,1)S(1)}, u32[]{:S(2)}, u32[]{:S(2)}) %collective-permute-start.8) | collective-permute-done | bytes 65568 | tf_op jit(solution)/shard_map/ppermute | solution.py:292
  85.0 0.6 copy-done.6
  85.6 0.0 copy-done.7
  85.6 1.7 %fold_columns.1 = f32[256,256]{1,0:T(8,128)} custom-call(f32[256,256]{1,0:T(8,128)} %get-tuple-element.18.center_ref, bf16[256,128]{1,0:T(8,128)(2,1)} %copy-done.6, bf16[256,128]{1,0:T(8,128)(2,1)} %copy-done.7), custom_call_target="tpu_custom_call" | custom-call | bytes 1048576 | tf_op jit(solution)/shard_map/fold_columns/pallas_call | solution.py:388
  (21 shorter events, 0.1 us)
Async XLA Ops:
  0.0 9.7 %copy-start = (bf16[6,256,256]{2,1,0:T(8,128)(2,1)S(1)}, bf16[6,256,256]{2,1,0:T(8,128)(2,1)}, u32[]{:S(2)}) copy-start(bf16[6,256,256]{2,1,0:T(8,128)(2,1)} %core_ref.1) | copy-start | bytes 2359300
  1.2 17.2 %collective-permute-start.1 = (bf16[6,128,256]{2,1,0:T(8,128)(2,1)S(1)}, bf16[6,128,256]{2,1,0:T(8,128)(2,1)S(1)}, u32[]{:S(2)}, u32[]{:S(2)}) collective-permute-start(bf16[6,128,256]{2,1,0:T(8,128)(2,1)S(1)} %get-tuple-element.23), channel_id=1, source_target_pairs={{16,32},{48,64},{80,96},{112,128},{144,160},{176,192},{208,224},{3... | collective-permute-start | bytes 1179656 | tf_op jit(solution)/shard_map/ppermute | solution.py:292
  9.6 9.8 %collective-permute-start = (bf16[6,128,256]{2,1,0:T(8,128)(2,1)S(1)}, bf16[6,128,256]{2,1,0:T(8,128)(2,1)S(1)}, u32[]{:S(2)}, u32[]{:S(2)}) collective-permute-start(bf16[6,128,256]{2,1,0:T(8,128)(2,1)S(1)} %get-tuple-element.24), channel_id=1, source_target_pairs={{0,16},{32,48},{64,80},{96,112},{128,144},{160,176},{192,208},{224... | collective-permute-start | bytes 1179656 | tf_op jit(solution)/shard_map/ppermute | solution.py:292
  18.4 16.7 %copy-start.1 = (bf16[6,128,256]{2,1,0:T(8,128)(2,1)}, bf16[6,128,256]{2,1,0:T(8,128)(2,1)S(1)}, u32[]{:S(2)}) copy-start(bf16[6,128,256]{2,1,0:T(8,128)(2,1)S(1)} %collective-permute-done.1.second_ref) | copy-start | bytes 1179652
  19.3 24.6 %copy-start.2 = (bf16[6,128,256]{2,1,0:T(8,128)(2,1)}, bf16[6,128,256]{2,1,0:T(8,128)(2,1)S(1)}, u32[]{:S(2)}) copy-start(bf16[6,128,256]{2,1,0:T(8,128)(2,1)S(1)} %collective-permute-done.first_ref) | copy-start | bytes 1179652
  19.4 30.5 %collective-permute-start.5 = (bf16[6,512,128]{2,1,0:T(8,128)(2,1)S(1)}, bf16[6,512,128]{2,1,0:T(8,128)(2,1)S(1)}, u32[]{:S(2)}, u32[]{:S(2)}) collective-permute-start(bf16[6,512,128]{2,1,0:T(8,128)(2,1)S(1)} %pad_maximum_fusion), channel_id=1, source_target_pairs={{0,1},{2,3},{4,5},{6,7},{8,9},{10,11},{12,13},{14,15},{1,0},{3,2},... | collective-permute-start | bytes 2359304 | tf_op jit(solution)/shard_map/ppermute | solution.py:292
  21.4 13.6 %collective-permute-start.2 = (bf16[6,256,128]{2,1,0:T(8,128)(2,1)S(1)}, bf16[6,256,128]{2,1,0:T(8,128)(2,1)S(1)}, u32[]{:S(2)}, u32[]{:S(2)}) collective-permute-start(bf16[6,256,128]{2,1,0:T(8,128)(2,1)S(1)} %get-tuple-element.22), channel_id=1, source_target_pairs={{1,2},{3,4},{5,6},{7,8},{9,10},{11,12},{13,14},{2,1},{4,3},{6,5},{... | collective-permute-start | bytes 1179656 | tf_op jit(solution)/shard_map/ppermute | solution.py:292
  35.0 14.8 %copy-start.3 = (bf16[6,256,128]{2,1,0:T(8,128)(2,1)}, bf16[6,256,128]{2,1,0:T(8,128)(2,1)S(1)}, u32[]{:S(2)}) copy-start(bf16[6,256,128]{2,1,0:T(8,128)(2,1)S(1)} %collective-permute-done.2.outer_ref) | copy-start | bytes 1179652
  35.1 14.8 %collective-permute-start.4 = (bf16[6,128,128]{2,1,0:T(8,128)(2,1)S(1)}, bf16[6,128,128]{2,1,0:T(8,128)(2,1)S(1)}, u32[]{:S(2)}, u32[]{:S(2)}) collective-permute-start(bf16[6,128,128]{2,1,0:T(8,128)(2,1)S(1)} %get-tuple-element.25), channel_id=1, source_target_pairs={{16,32},{48,64},{80,96},{112,128},{144,160},{176,192},{208,224},{3... | collective-permute-start | bytes 589832 | tf_op jit(solution)/shard_map/ppermute | solution.py:292
  40.6 9.3 %collective-permute-start.3 = (bf16[6,128,128]{2,1,0:T(8,128)(2,1)S(1)}, bf16[6,128,128]{2,1,0:T(8,128)(2,1)S(1)}, u32[]{:S(2)}, u32[]{:S(2)}) collective-permute-start(bf16[6,128,128]{2,1,0:T(8,128)(2,1)S(1)} %get-tuple-element.26), channel_id=1, source_target_pairs={{0,16},{32,48},{64,80},{96,112},{128,144},{160,176},{192,208},{224... | collective-permute-start | bytes 589832 | tf_op jit(solution)/shard_map/ppermute | solution.py:292
  49.9 0.7 copy-start.9
  49.9 0.7 copy-start.10
  49.9 1.0 %copy-start.8 = (bf16[6,512,128]{2,1,0:T(8,128)(2,1)}, bf16[6,512,128]{2,1,0:T(8,128)(2,1)S(1)}, u32[]{:S(2)}) copy-start(bf16[6,512,128]{2,1,0:T(8,128)(2,1)S(1)} %collective-permute-done.5.inner_ref) | copy-start | bytes 2359300
  62.6 5.6 %collective-permute-start.6 = (bf16[128,512]{1,0:T(8,128)(2,1)}, bf16[128,512]{1,0:T(8,128)(2,1)S(1)}, u32[]{:S(2)}, u32[]{:S(2)}) collective-permute-start(bf16[128,512]{1,0:T(8,128)(2,1)} %get-tuple-element.16), channel_id=1, source_target_pairs={{0,16},{32,48},{64,80},{96,112},{128,144},{160,176},{192,208},{224... | collective-permute-start | bytes 393224 | tf_op jit(solution)/shard_map/ppermute | solution.py:292
  64.1 10.9 %collective-permute-start.7 = (bf16[128,512]{1,0:T(8,128)(2,1)}, bf16[128,512]{1,0:T(8,128)(2,1)S(1)}, u32[]{:S(2)}, u32[]{:S(2)}) collective-permute-start(bf16[128,512]{1,0:T(8,128)(2,1)} %get-tuple-element.17), channel_id=1, source_target_pairs={{16,32},{48,64},{80,96},{112,128},{144,160},{176,192},{208,224},{3... | collective-permute-start | bytes 393224 | tf_op jit(solution)/shard_map/ppermute | solution.py:292
  68.2 6.7 %copy-start.4 = (bf16[128,512]{1,0:T(8,128)(2,1)}, bf16[128,512]{1,0:T(8,128)(2,1)S(1)}, u32[]{:S(2)}) copy-start(bf16[128,512]{1,0:T(8,128)(2,1)S(1)} %collective-permute-done.6.first_ref) | copy-start | bytes 393220
  74.9 0.6 copy-start.5
  77.6 7.4 %collective-permute-start.8 = (bf16[256,128]{1,0:T(8,128)(2,1)}, bf16[256,128]{1,0:T(8,128)(2,1)S(1)}, u32[]{:S(2)}, u32[]{:S(2)}) collective-permute-start(bf16[256,128]{1,0:T(8,128)(2,1)} %get-tuple-element.19), channel_id=1, source_target_pairs={{1,2},{3,4},{5,6},{7,8},{9,10},{11,12},{13,14},{2,1},{4,3},{6,5},{... | collective-permute-start | bytes 196616 | tf_op jit(solution)/shard_map/ppermute | solution.py:292
  80.9 4.0 %collective-permute-start.9 = (bf16[256,128]{1,0:T(8,128)(2,1)}, bf16[256,128]{1,0:T(8,128)(2,1)S(1)}, u32[]{:S(2)}, u32[]{:S(2)}) collective-permute-start(bf16[256,128]{1,0:T(8,128)(2,1)} %get-tuple-element.20), channel_id=1, source_target_pairs={{0,1},{2,3},{4,5},{6,7},{8,9},{10,11},{12,13},{14,15},{1,0},{3,2},... | collective-permute-start | bytes 196616 | tf_op jit(solution)/shard_map/ppermute | solution.py:292
  85.0 0.6 copy-start.6
  85.0 0.6 copy-start.7

commit v3 on v2

--- a/solution.py
+++ b/solution.py
@@ -154,11 +154,8 @@
     fill(tile, first_ref, rows_ref, cols_ref, 0, margin, first, margin, 0)
     fill(tile, second_ref, rows_ref, cols_ref, 0, margin, second, margin, 0)
 
-    def transform(s, carry):
+    for s in range(splits):
         halves_ref[s] = dot(left_ref[...], tile[s]).astype(BF16)
-        return carry
-
-    lax.fori_loop(0, splits, transform, 0)
 
 
 def main_kernel(
@@ -296,7 +293,7 @@
     return [pl.BlockSpec(memory_space=pltpu.VMEM)] * count
 
 
-def kernel_call(body, name, outs, count, scratch=(), flops=0):
+def kernel_call(body, name, outs, count, scratch=(), flops=0, vmem=24):
     return pl.pallas_call(
         body,
         out_shape=outs,
@@ -304,6 +301,7 @@
         out_specs=jax.tree.map(lambda _: pl.BlockSpec(memory_space=pltpu.VMEM), outs),
         scratch_shapes=list(scratch),
         cost_estimate=pl.CostEstimate(flops=flops, bytes_accessed=1 << 20, transcendentals=0),
+        compiler_params=pltpu.CompilerParams(vmem_limit_bytes=vmem << 20),
         name=name,
     )
 
@@ -333,6 +331,8 @@
     re, im = kernel_call(
         functools.partial(noise_kernel, half), "noise_spectrum", (spectrum, spectrum), 3, flops=3 * cube
     )(white_noise, constant["left"], constant["right"])
+
+    outer, first, second, re, im = lax.optimization_barrier((outer, first, second, re, im))
 
     first_corner = swap(lax.dynamic_slice_in_dim(outer, (1 - odd_row) * margin, margin, axis=1), "dec", 0)
     second_corner = swap(lax.dynamic_slice_in_dim(outer, odd_row * margin, margin, axis=1), "dec", 1)

time: 87.6 us -> 63.1 us (0.72)
  Pallas kernels: 24.6 us -> 12 us
  waiting for transfers between devices: 32 us -> 20.6 us
  local copies, waits for them, and re-layouts: 3.77 us -> 1.52 us
  starting transfers between devices: 26.7 us -> 28 us
    ppermute x10, waiting for transfers between devices: 32 us -> 20.6 us  [swap(): return lax.ppermute(values, axis, pairs + [(b, a) for a, b in pairs])]
    pallas_call x1, Pallas kernels: 11.7 us -> 7.9 us  [shards(): kernel_call(functools.partial(main_kernel, half, scale), 'tile_model', (s...]
    pallas_call x1, Pallas kernels: 5.99 us -> 2.37 us  [shards(): kernel_call(functools.partial(core_kernel, half), 'core_columns', jax.Sha...]
    pallas_call x1, Pallas kernels: 3.22 us -> 0.87 us  [shards(): kernel_call(functools.partial(noise_kernel, half), 'noise_spectrum', (spe...]
    unnamed x22 -> x18, local copies, waits for them, and re-layouts: 2.28 us -> 0.05 us
    pallas_call x1, Pallas kernels: 2.01 us -> 0.11 us  [shards(): kernel_call(functools.partial(fold_rows_kernel, half), 'fold_rows', (bloc...]
    ppermute x10, starting transfers between devices: 26.7 us -> 28 us  [swap(): return lax.ppermute(values, axis, pairs + [(b, a) for a, b in pairs])]
    dynamic_slice x1, local copies, waits for them, and re-layouts: 1.24 us -> 0.06 us  [shards(): lax.dynamic_slice_in_dim(split_maps, odd_row * margin, margin, axis=1)]
  transfers between devices with their start and end apart: 10 -> 10, of which waited for: 6 -> 6; matrix products, arithmetic and copies ran while one was open for 0% -> 0% of each run, Pallas kernels for 11% -> 5%
where the time goes in v3:
time: 63.1 us; the launch traced here: 62.4 us
  starting transfers between devices  28 us (44%)
  waiting for transfers between devices  20.6 us (33%)
  Pallas kernels  12 us (19%)
  local copies, waits for them, and re-layouts  1.52 us (2%)
    ppermute x10, starting transfers between devices, swap(): return lax.ppermute(values, axis, pairs + [(b, a) for a, b in pairs])  28 us
    ppermute x10, waiting for transfers between devices, swap(): return lax.ppermute(values, axis, pairs + [(b, a) for a, b in pairs])  20.6 us
    pallas_call x1, Pallas kernels, shards(): kernel_call(functools.partial(main_kernel, half, scale), 'tile_model', (s...  7.9 us
    pallas_call x1, Pallas kernels, shards(): kernel_call(functools.partial(core_kernel, half), 'core_columns', jax.Sha...  2.37 us
    dynamic_slice x2, local copies, waits for them, and re-layouts, shards(): lax.dynamic_slice_in_dim(block, (1 - odd_col) * margin, margin, axis=2)  1.39 us
  transfers between devices with their start and end apart: 10, of which 6 were waited for; matrix products, arithmetic and copies ran while one was open for 0% of the time, Pallas kernels for 5%

profile of v3, /device:TPU:15, one launch (start us, length us, event | category | flops | bytes accessed | tf_op | source)
XLA Modules:
  0.0 62.4 jit_solution(10192923287216624098)
XLA Ops:
  0.0 0.0 copy-start.3
  0.0 1.3 %constant_dynamic-slice_fusion.1 = (bf16[6,256,128]{2,1,0:T(8,128)(2,1)S(1)}, bf16[6,256,128]{2,1,0:T(8,128)(2,1)S(1)}) fusion(bf16[6,256,256]{2,1,0:T(8,128)(2,1)} %core_ref.1, s32[]{:T(128)S(6)} %select_n.32, s32[]{:T(128)S(6)} %select_n.28), kind=kLoop, calls=%fused_computation.2 | loop fusion | bytes 1572872 | tf_op jit(solution)/shard_map/dynamic_slice | solution.py:342
  1.3 4.0 %collective-permute-start = (bf16[6,256,128]{2,1,0:T(8,128)(2,1)S(1)}, bf16[6,256,128]{2,1,0:T(8,128)(2,1)S(1)}, u32[]{:S(2)}, u32[]{:S(2)}) collective-permute-start(bf16[6,256,128]{2,1,0:T(8,128)(2,1)S(1)} %get-tuple-element.32), channel_id=1, source_target_pairs={{1,2},{3,4},{5,6},{7,8},{9,10},{11,12},{13,14},{2,1},{4,3},{6,5},{... | collective-permute-start | bytes 1179656 | tf_op jit(solution)/shard_map/ppermute | solution.py:289
  5.4 0.1 constant_dynamic-slice_fusion.5
  5.5 8.0 %collective-permute-start.2 = (bf16[6,128,256]{2,1,0:T(8,128)(2,1)S(1)}, bf16[6,128,256]{2,1,0:T(8,128)(2,1)S(1)}, u32[]{:S(2)}, u32[]{:S(2)}) collective-permute-start(bf16[6,128,256]{2,1,0:T(8,128)(2,1)S(1)} %get-tuple-element.33), channel_id=1, source_target_pairs={{16,32},{48,64},{80,96},{112,128},{144,160},{176,192},{208,224},{3... | collective-permute-start | bytes 1179656 | tf_op jit(solution)/shard_map/ppermute | solution.py:289
  13.5 0.1 collective-permute-start.1
  13.7 0.9 %noise_spectrum.1 = (f32[264,512]{1,0:T(8,128)S(1)}, f32[264,512]{1,0:T(8,128)S(1)}) custom-call(bf16[512,512]{1,0:T(8,128)(2,1)S(1)} %copy-done.2, bf16[528,512]{1,0:T(8,128)(2,1)S(1)} %copy-done.1, bf16[512,512]{1,0:T(8,128)(2,1)S(1)} %copy-done.3), custom_call_target="tpu_custom_call" | custom-call | flops 402653184 | bytes 1048576 | tf_op jit(solution)/shard_map/noise_spectrum/pallas_call | solution.py:331
  14.5 1.2 %collective-permute-done.outer_ref = bf16[6,256,128]{2,1,0:T(8,128)(2,1)S(1)} collective-permute-done((bf16[6,256,128]{2,1,0:T(8,128)(2,1)S(1)}, bf16[6,256,128]{2,1,0:T(8,128)(2,1)S(1)}, u32[]{:S(2)}, u32[]{:S(2)}) %collective-permute-start) | collective-permute-done | bytes 393248 | tf_op jit(solution)/shard_map/ppermute | solution.py:289
  15.7 6.3 %collective-permute-done.2.second_ref = bf16[6,128,256]{2,1,0:T(8,128)(2,1)S(1)} collective-permute-done((bf16[6,128,256]{2,1,0:T(8,128)(2,1)S(1)}, bf16[6,128,256]{2,1,0:T(8,128)(2,1)S(1)}, u32[]{:S(2)}, u32[]{:S(2)}) %collective-permute-start.2) | collective-permute-done | bytes 393248 | tf_op jit(solution)/shard_map/ppermute | solution.py:289
  22.0 2.0 %collective-permute-done.1.first_ref = bf16[6,128,256]{2,1,0:T(8,128)(2,1)S(1)} collective-permute-done((bf16[6,128,256]{2,1,0:T(8,128)(2,1)S(1)}, bf16[6,128,256]{2,1,0:T(8,128)(2,1)S(1)}, u32[]{:S(2)}, u32[]{:S(2)}) %collective-permute-start.1) | collective-permute-done | bytes 393248 | tf_op jit(solution)/shard_map/ppermute | solution.py:289
  24.1 0.1 constant_dynamic-slice_fusion
  24.1 0.1 pad_maximum_fusion
  24.2 0.5 collective-permute-start.5
  24.7 4.9 %collective-permute-start.4 = (bf16[6,128,128]{2,1,0:T(8,128)(2,1)S(1)}, bf16[6,128,128]{2,1,0:T(8,128)(2,1)S(1)}, u32[]{:S(2)}, u32[]{:S(2)}) collective-permute-start(bf16[6,128,128]{2,1,0:T(8,128)(2,1)S(1)} %get-tuple-element.35), channel_id=1, source_target_pairs={{16,32},{48,64},{80,96},{112,128},{144,160},{176,192},{208,224},{3... | collective-permute-start | bytes 589832 | tf_op jit(solution)/shard_map/ppermute | solution.py:289
  29.6 0.0 copy-start.6
  29.6 0.0 copy-start.7
  29.6 0.0 copy-start.8
  29.7 0.1 collective-permute-start.3
  29.8 2.4 %core_columns.1.core_ref = bf16[6,528,256]{2,1,0:T(8,128)(2,1)S(1)} custom-call(bf16[6,256,256]{2,1,0:T(8,128)(2,1)S(1)} %copy-done, bf16[6,128,256]{2,1,0:T(8,128)(2,1)S(1)} %collective-permute-done.1.first_ref, bf16[6,128,256]{2,1,0:T(8,128)(2,1)S(1)} %collective-permute-done.2.second_ref, f32[512,128]{1,0:T(8,128)S(1)} %copy-done.4, ...), custom_call_target="tpu_custom_call" | custom-call | flops 805306368 | bytes 1048576 | tf_op jit(solution)/shard_map/core_columns/pallas_call | solution.py:350
  32.2 4.4 %collective-permute-done.4.second_ref = bf16[6,128,128]{2,1,0:T(8,128)(2,1)S(1)} collective-permute-done((bf16[6,128,128]{2,1,0:T(8,128)(2,1)S(1)}, bf16[6,128,128]{2,1,0:T(8,128)(2,1)S(1)}, u32[]{:S(2)}, u32[]{:S(2)}) %collective-permute-start.4) | collective-permute-done | bytes 196640 | tf_op jit(solution)/shard_map/ppermute | solution.py:289
  36.6 0.0 collective-permute-done.3.first_ref
  36.6 0.0 collective-permute-done.5.inner_ref
  36.6 7.9 %tile_model.1 = (bf16[128,512]{1,0:T(8,128)(2,1)S(1)}, bf16[128,512]{1,0:T(8,128)(2,1)S(1)}, f32[256,512]{1,0:T(8,128)S(1)}) custom-call(bf16[6,528,256]{2,1,0:T(8,128)(2,1)S(1)} %core_columns.1.core_ref, bf16[6,256,128]{2,1,0:T(8,128)(2,1)S(1)} %collective-permute-done.outer_ref, bf16[6,128,128]{2,1,0:T(8,128)(2,1)S(1)} %collective-permute-done.3.first_ref, ...), custom_call_target="tpu_custom_call" | custom-call | flops 2684354560 | bytes 1048576 | tf_op jit(solution)/shard_map/tile_model/pallas_call | solution.py:360
  44.5 0.1 collective-permute-start.6
  44.6 4.6 %collective-permute-start.7 = (bf16[128,512]{1,0:T(8,128)(2,1)S(1)}, bf16[128,512]{1,0:T(8,128)(2,1)S(1)}, u32[]{:S(2)}, u32[]{:S(2)}) collective-permute-start(bf16[128,512]{1,0:T(8,128)(2,1)S(1)} %get-tuple-element.27), channel_id=1, source_target_pairs={{16,32},{48,64},{80,96},{112,128},{144,160},{176,192},{208,224},{3... | collective-permute-start | bytes 393224 | tf_op jit(solution)/shard_map/ppermute | solution.py:289
  49.2 4.7 %collective-permute-done.7.second_ref = bf16[128,512]{1,0:T(8,128)(2,1)S(1)} collective-permute-done((bf16[128,512]{1,0:T(8,128)(2,1)S(1)}, bf16[128,512]{1,0:T(8,128)(2,1)S(1)}, u32[]{:S(2)}, u32[]{:S(2)}) %collective-permute-start.7) | collective-permute-done | bytes 131104 | tf_op jit(solution)/shard_map/ppermute | solution.py:289
  53.9 0.1 fold_rows.1
  54.0 5.6 %collective-permute-start.8 = (bf16[256,128]{1,0:T(8,128)(2,1)S(1)}, bf16[256,128]{1,0:T(8,128)(2,1)S(1)}, u32[]{:S(2)}, u32[]{:S(2)}) collective-permute-start(bf16[256,128]{1,0:T(8,128)(2,1)S(1)} %get-tuple-element.29), channel_id=1, source_target_pairs={{1,2},{3,4},{5,6},{7,8},{9,10},{11,12},{13,14},{2,1},{4,3},{6,5},{... | collective-permute-start | bytes 196616 | tf_op jit(solution)/shard_map/ppermute | solution.py:289
  59.7 0.1 collective-permute-start.9
  59.8 1.9 %collective-permute-done.8.outer_ref = bf16[256,128]{1,0:T(8,128)(2,1)S(1)} collective-permute-done((bf16[256,128]{1,0:T(8,128)(2,1)S(1)}, bf16[256,128]{1,0:T(8,128)(2,1)S(1)}, u32[]{:S(2)}, u32[]{:S(2)}) %collective-permute-start.8) | collective-permute-done | bytes 65568 | tf_op jit(solution)/shard_map/ppermute | solution.py:289
  61.7 0.0 collective-permute-done.9.inner_ref
  61.7 0.7 %fold_columns.1 = f32[256,256]{1,0:T(8,128)} custom-call(f32[256,256]{1,0:T(8,128)S(1)} %get-tuple-element.28.center_ref, bf16[256,128]{1,0:T(8,128)(2,1)S(1)} %collective-permute-done.8.outer_ref, bf16[256,128]{1,0:T(8,128)(2,1)S(1)} %collective-permute-done.9.inner_ref), custom_call_target="tpu_custom_call" | custom-call | bytes 1048576 | tf_op jit(solution)/shard_map/fold_columns/pallas_call | solution.py:388
  (16 shorter events, 0.1 us)
Async XLA Ops:
  0.0 5.4 %copy-start = (bf16[6,256,256]{2,1,0:T(8,128)(2,1)S(1)}, bf16[6,256,256]{2,1,0:T(8,128)(2,1)}, u32[]{:S(2)}) copy-start(bf16[6,256,256]{2,1,0:T(8,128)(2,1)} %core_ref.1) | copy-start | bytes 2359300
  0.0 13.6 %copy-start.1 = (bf16[528,512]{1,0:T(8,128)(2,1)S(1)}, bf16[528,512]{1,0:T(8,128)(2,1)}, u32[]{:S(2)}) copy-start(bf16[528,512]{1,0:T(8,128)(2,1)} %constant.44.clone.left_ref) | copy-start | bytes 1622020
  0.0 13.6 %copy-start.2 = (bf16[512,512]{1,0:T(8,128)(2,1)S(1)}, bf16[512,512]{1,0:T(8,128)(2,1)}, u32[]{:S(2)}) copy-start(bf16[512,512]{1,0:T(8,128)(2,1)} %noise_ref.1) | copy-start | bytes 1572868
  0.0 13.6 %copy-start.3 = (bf16[512,512]{1,0:T(8,128)(2,1)S(1)}, bf16[512,512]{1,0:T(8,128)(2,1)}, u32[]{:S(2)}) copy-start(bf16[512,512]{1,0:T(8,128)(2,1)} %constant.45.clone.right_ref) | copy-start | bytes 1572868
  1.3 14.4 %collective-permute-start = (bf16[6,256,128]{2,1,0:T(8,128)(2,1)S(1)}, bf16[6,256,128]{2,1,0:T(8,128)(2,1)S(1)}, u32[]{:S(2)}, u32[]{:S(2)}) collective-permute-start(bf16[6,256,128]{2,1,0:T(8,128)(2,1)S(1)} %get-tuple-element.32), channel_id=1, source_target_pairs={{1,2},{3,4},{5,6},{7,8},{9,10},{11,12},{13,14},{2,1},{4,3},{6,5},{... | collective-permute-start | bytes 1179656 | tf_op jit(solution)/shard_map/ppermute | solution.py:289
  5.5 16.5 %collective-permute-start.2 = (bf16[6,128,256]{2,1,0:T(8,128)(2,1)S(1)}, bf16[6,128,256]{2,1,0:T(8,128)(2,1)S(1)}, u32[]{:S(2)}, u32[]{:S(2)}) collective-permute-start(bf16[6,128,256]{2,1,0:T(8,128)(2,1)S(1)} %get-tuple-element.33), channel_id=1, source_target_pairs={{16,32},{48,64},{80,96},{112,128},{144,160},{176,192},{208,224},{3... | collective-permute-start | bytes 1179656 | tf_op jit(solution)/shard_map/ppermute | solution.py:289
  13.5 10.5 %collective-permute-start.1 = (bf16[6,128,256]{2,1,0:T(8,128)(2,1)S(1)}, bf16[6,128,256]{2,1,0:T(8,128)(2,1)S(1)}, u32[]{:S(2)}, u32[]{:S(2)}) collective-permute-start(bf16[6,128,256]{2,1,0:T(8,128)(2,1)S(1)} %get-tuple-element.34), channel_id=1, source_target_pairs={{0,16},{32,48},{64,80},{96,112},{128,144},{160,176},{192,208},{224... | collective-permute-start | bytes 1179656 | tf_op jit(solution)/shard_map/ppermute | solution.py:289
  24.1 5.7 %copy-start.4 = (f32[512,128]{1,0:T(8,128)S(1)}, f32[512,128]{1,0:T(8,128)}, u32[]{:S(2)}) copy-start(f32[512,128]{1,0:T(8,128)} %constant.49.clone.rows_ref) | copy-start | bytes 786436
  24.1 5.7 %copy-start.5 = (f32[8,512]{1,0:T(8,128)S(1)}, f32[8,512]{1,0:T(8,128)}, u32[]{:S(2)}) copy-start(f32[8,512]{1,0:T(8,128)} %constant.50.clone.cols_ref) | copy-start | bytes 49156
  24.2 12.4 %collective-permute-start.5 = (bf16[6,512,128]{2,1,0:T(8,128)(2,1)S(1)}, bf16[6,512,128]{2,1,0:T(8,128)(2,1)S(1)}, u32[]{:S(2)}, u32[]{:S(2)}) collective-permute-start(bf16[6,512,128]{2,1,0:T(8,128)(2,1)S(1)} %pad_maximum_fusion), channel_id=1, source_target_pairs={{0,1},{2,3},{4,5},{6,7},{8,9},{10,11},{12,13},{14,15},{1,0},{3,2},... | collective-permute-start | bytes 2359304 | tf_op jit(solution)/shard_map/ppermute | solution.py:289
  24.7 11.9 %collective-permute-start.4 = (bf16[6,128,128]{2,1,0:T(8,128)(2,1)S(1)}, bf16[6,128,128]{2,1,0:T(8,128)(2,1)S(1)}, u32[]{:S(2)}, u32[]{:S(2)}) collective-permute-start(bf16[6,128,128]{2,1,0:T(8,128)(2,1)S(1)} %get-tuple-element.35), channel_id=1, source_target_pairs={{16,32},{48,64},{80,96},{112,128},{144,160},{176,192},{208,224},{3... | collective-permute-start | bytes 589832 | tf_op jit(solution)/shard_map/ppermute | solution.py:289
  29.6 6.9 %copy-start.6 = (bf16[512,512]{1,0:T(8,128)(2,1)S(1)}, bf16[512,512]{1,0:T(8,128)(2,1)}, u32[]{:S(2)}) copy-start(bf16[512,512]{1,0:T(8,128)(2,1)} %constant.47.clone.band_columns_ref) | copy-start | bytes 1572868
  29.6 6.9 %copy-start.7 = (bf16[512,512]{1,0:T(8,128)(2,1)S(1)}, bf16[512,512]{1,0:T(8,128)(2,1)}, u32[]{:S(2)}) copy-start(bf16[512,512]{1,0:T(8,128)(2,1)} %constant.46.clone.inverse_right_ref) | copy-start | bytes 1572868
  29.6 6.9 %copy-start.8 = (bf16[272,384]{1,0:T(8,128)(2,1)S(1)}, bf16[272,384]{1,0:T(8,128)(2,1)}, u32[]{:S(2)}) copy-start(bf16[272,384]{1,0:T(8,128)(2,1)} %constant.48.clone.band_rows_ref) | copy-start | bytes 626692
  29.7 6.9 %collective-permute-start.3 = (bf16[6,128,128]{2,1,0:T(8,128)(2,1)S(1)}, bf16[6,128,128]{2,1,0:T(8,128)(2,1)S(1)}, u32[]{:S(2)}, u32[]{:S(2)}) collective-permute-start(bf16[6,128,128]{2,1,0:T(8,128)(2,1)S(1)} %get-tuple-element.36), channel_id=1, source_target_pairs={{0,16},{32,48},{64,80},{96,112},{128,144},{160,176},{192,208},{224... | collective-permute-start | bytes 589832 | tf_op jit(solution)/shard_map/ppermute | solution.py:289
  44.5 4.7 %collective-permute-start.6 = (bf16[128,512]{1,0:T(8,128)(2,1)S(1)}, bf16[128,512]{1,0:T(8,128)(2,1)S(1)}, u32[]{:S(2)}, u32[]{:S(2)}) collective-permute-start(bf16[128,512]{1,0:T(8,128)(2,1)S(1)} %get-tuple-element.26), channel_id=1, source_target_pairs={{0,16},{32,48},{64,80},{96,112},{128,144},{160,176},{192,208},{224... | collective-permute-start | bytes 393224 | tf_op jit(solution)/shard_map/ppermute | solution.py:289
  44.6 9.3 %collective-permute-start.7 = (bf16[128,512]{1,0:T(8,128)(2,1)S(1)}, bf16[128,512]{1,0:T(8,128)(2,1)S(1)}, u32[]{:S(2)}, u32[]{:S(2)}) collective-permute-start(bf16[128,512]{1,0:T(8,128)(2,1)S(1)} %get-tuple-element.27), channel_id=1, source_target_pairs={{16,32},{48,64},{80,96},{112,128},{144,160},{176,192},{208,224},{3... | collective-permute-start | bytes 393224 | tf_op jit(solution)/shard_map/ppermute | solution.py:289
  54.0 7.6 %collective-permute-start.8 = (bf16[256,128]{1,0:T(8,128)(2,1)S(1)}, bf16[256,128]{1,0:T(8,128)(2,1)S(1)}, u32[]{:S(2)}, u32[]{:S(2)}) collective-permute-start(bf16[256,128]{1,0:T(8,128)(2,1)S(1)} %get-tuple-element.29), channel_id=1, source_target_pairs={{1,2},{3,4},{5,6},{7,8},{9,10},{11,12},{13,14},{2,1},{4,3},{6,5},{... | collective-permute-start | bytes 196616 | tf_op jit(solution)/shard_map/ppermute | solution.py:289
  59.7 2.0 %collective-permute-start.9 = (bf16[256,128]{1,0:T(8,128)(2,1)S(1)}, bf16[256,128]{1,0:T(8,128)(2,1)S(1)}, u32[]{:S(2)}, u32[]{:S(2)}) collective-permute-start(bf16[256,128]{1,0:T(8,128)(2,1)S(1)} %get-tuple-element.30), channel_id=1, source_target_pairs={{0,1},{2,3},{4,5},{6,7},{8,9},{10,11},{12,13},{14,15},{1,0},{3,2},... | collective-permute-start | bytes 196616 | tf_op jit(solution)/shard_map/ppermute | solution.py:289

commit v4 on v3

--- a/solution.py
+++ b/solution.py
@@ -158,35 +158,50 @@
         halves_ref[s] = dot(left_ref[...], tile[s]).astype(BF16)
 
 
+def inner_kernel(half, after_ref, inner_ref, rows_ref, cols_ref, left_ref, halves_ref, tile):
+    del after_ref
+    margin = half // 2
+    first, second, _, inner = sides(half)
+    fill(tile, inner_ref, rows_ref, cols_ref, 0, margin, first, inner, 0)
+    fill(tile, inner_ref, rows_ref, cols_ref, margin, half, margin, inner, 0)
+    fill(tile, inner_ref, rows_ref, cols_ref, margin + half, margin, second, inner, 0)
+    for s in range(inner_ref.shape[0]):
+        halves_ref[s] = dot(left_ref[...], tile[s]).astype(BF16)
+
+
+def outer_kernel(half, after_ref, outer_ref, first_ref, second_ref, rows_ref, cols_ref, left_ref, halves_ref, tile):
+    del after_ref
+    margin = half // 2
+    first, second, outer, _ = sides(half)
+    fill(tile, outer_ref, rows_ref, cols_ref, 0, half, margin, outer, 0)
+    fill(tile, first_ref, rows_ref, cols_ref, 0, margin, first, outer, 0)
+    fill(tile, second_ref, rows_ref, cols_ref, 0, margin, second, outer, 0)
+    for s in range(outer_ref.shape[0]):
+        halves_ref[s] = dot(left_ref[...], tile[s]).astype(BF16)
+
+
 def main_kernel(
     half, scale,
-    core_ref, outer_ref, first_ref, second_ref, inner_ref, re_ref, im_ref,
-    rows_ref, cols_ref, left_ref, right_ref, band_rows_ref, band_columns_ref,
+    core_ref, inner_ref, outer_ref, re_ref, im_ref,
+    rows_ref, cols_ref, right_ref, band_rows_ref, band_columns_ref,
     inverse_right_ref,
     first_out_ref, second_out_ref, inside_ref,
-    tile, power, stacked, strips,
+    table, power, stacked, strips,
 ):
     length = 2 * half
     margin = half // 2
     splits = core_ref.shape[0]
-    first, second, outer, inner = sides(half)
-    outer_col = jnp.where(outer == 0, 0, margin)
-    inner_col = margin - outer_col
-    fill(tile, outer_ref, rows_ref, cols_ref, 0, half, margin, outer, outer_col)
-    fill(tile, first_ref, rows_ref, cols_ref, 0, margin, first, outer, outer_col)
-    fill(tile, second_ref, rows_ref, cols_ref, 0, margin, second, outer, outer_col)
-    fill(tile, inner_ref, rows_ref, cols_ref, 0, margin, first, inner, inner_col)
-    fill(tile, inner_ref, rows_ref, cols_ref, margin, half, margin, inner, inner_col)
-    fill(tile, inner_ref, rows_ref, cols_ref, margin + half, margin, second, inner, inner_col)
+    first, _, _, inner = sides(half)
+    place = pl.multiple_of(half + jnp.where(inner == 0, 0, margin), margin)
+    table[:margin] = right_ref[pl.ds(place, margin), :]
+    table[margin:] = right_ref[pl.ds(pl.multiple_of(length + margin - place, margin), margin), :]
 
     edge = first_column((half, half))
     edge8 = first_column((8, half))
 
     def accumulate(s, carry):
-        halves = jnp.concatenate(
-            [core_ref[s], dot(left_ref[...], tile[s]).astype(BF16)], axis=1
-        )
-        spectra = dot(halves, right_ref[...])
+        halves = jnp.concatenate([inner_ref[s], outer_ref[s]], axis=1)
+        spectra = dot(core_ref[s], right_ref[:half]) + dot(halves, table[...])
         cc, cs, sc, ss, nc, ns = quarters(spectra, half)
         e = jnp.where(edge, cc, cc - ss)
         f = jnp.where(edge, sc, cs + sc)
@@ -332,10 +347,12 @@
         functools.partial(noise_kernel, half), "noise_spectrum", (spectrum, spectrum), 3, flops=3 * cube
     )(white_noise, constant["left"], constant["right"])
 
-    outer, first, second, re, im = lax.optimization_barrier((outer, first, second, re, im))
-
-    first_corner = swap(lax.dynamic_slice_in_dim(outer, (1 - odd_row) * margin, margin, axis=1), "dec", 0)
-    second_corner = swap(lax.dynamic_slice_in_dim(outer, odd_row * margin, margin, axis=1), "dec", 1)
+    outer, re, im = lax.optimization_barrier((outer, re, im))
+    first_corner = lax.dynamic_slice_in_dim(outer, (1 - odd_row) * margin, margin, axis=1)
+    second_corner = lax.dynamic_slice_in_dim(outer, odd_row * margin, margin, axis=1)
+    first, second, _, _ = lax.optimization_barrier((first, second, first_corner, second_corner))
+    first_corner = swap(first_corner, "dec", 0)
+    second_corner = swap(second_corner, "dec", 1)
     inner = swap(
         jnp.concatenate(
             [
@@ -347,31 +364,39 @@
         "ra",
         0,
     )
-    halves = kernel_call(
-        functools.partial(core_kernel, half),
-        "core_columns",
-        jax.ShapeDtypeStruct((splits, length + 16, half), BF16),
-        6,
-        [pltpu.VMEM((splits, length, half), BF16)],
-        flops=6 * cube,
-    )(split_maps, first, second, rows, cols, constant["left"])
+    def columns(body, name, width, count, flops):
+        return kernel_call(
+            functools.partial(body, half),
+            name,
+            jax.ShapeDtypeStruct((splits, length + 16, width), BF16),
+            count,
+            [pltpu.VMEM((splits, length, width), BF16)],
+            flops=flops,
+        )
+
+    left = constant["left"]
+    core = columns(core_kernel, "core_columns", half, 6, cube)(split_maps, first, second, rows, cols, left)
+    outer = columns(outer_kernel, "outer_columns", margin, 7, 400000 * cube // 1000)(
+        core, outer, first_corner, second_corner, rows, cols, left
+    )
+    inner = columns(inner_kernel, "inner_columns", margin, 5, cube)(outer, inner, rows, cols, left)
 
     strip = jax.ShapeDtypeStruct((margin, length), BF16)
     first, second, inside = kernel_call(
         functools.partial(main_kernel, half, scale),
         "tile_model",
         (strip, strip, jax.ShapeDtypeStruct((half, length), F32)),
-        14,
+        11,
         [
-            pltpu.VMEM((splits, length, half), BF16),
+            pltpu.VMEM((half, length), BF16),
             pltpu.VMEM((half + 8, length), F32),
             pltpu.VMEM((3, half + 128, length), BF16),
             pltpu.VMEM((half, length), BF16),
         ],
         flops=20 * cube,
     )(
-        halves, outer, first_corner, second_corner, inner, re, im, rows, cols,
-        constant["left"], constant["right"], constant["band_rows"], constant["band_columns"],
+        core, inner, outer, re, im, rows, cols,
+        constant["right"], constant["band_rows"], constant["band_columns"],
         constant["inverse_right"],
     )
 

time: 63.1 us -> 59.2 us (0.938)
  the two profiles are of different devices: /device:TPU:15 before, /device:TPU:206 now
where the time goes in v4:
time: 59.2 us; the launch traced here: 59 us
  starting transfers between devices  26.2 us (44%)
  waiting for transfers between devices  18.1 us (31%)
  Pallas kernels  12.9 us (22%)
  local copies, waits for them, and re-layouts  1.52 us (3%)
    ppermute x10, starting transfers between devices, swap(): return lax.ppermute(values, axis, pairs + [(b, a) for a, b in pairs])  26.2 us
    ppermute x10, waiting for transfers between devices, swap(): return lax.ppermute(values, axis, pairs + [(b, a) for a, b in pairs])  18.1 us
    pallas_call x1, Pallas kernels, shards(): kernel_call(functools.partial(main_kernel, half, scale), 'tile_model', (s...  4.35 us
    pallas_call x1, Pallas kernels, shards(): columns(core_kernel, 'core_columns', half, 6, cube)  2.36 us
    pallas_call x1, Pallas kernels, shards(): columns(inner_kernel, 'inner_columns', margin, 5, cube)  2.27 us
    pallas_call x1, Pallas kernels, shards(): columns(outer_kernel, 'outer_columns', margin, 7, 400000 * cube // 1000)  2.24 us
    dynamic_slice x2, local copies, waits for them, and re-layouts, shards(): lax.dynamic_slice_in_dim(block, (1 - odd_col) * margin, margin, axis=2)  1.39 us
  transfers between devices with their start and end apart: 10, of which 5 were waited for; matrix products, arithmetic and copies ran while one was open for 0% of the time, Pallas kernels for 9%

profile of v4, /device:TPU:206, one launch (start us, length us, event | category | flops | bytes accessed | tf_op | source)
XLA Modules:
  0.0 59.0 jit_solution(11907030549080788176)
XLA Ops:
  0.0 0.0 copy-start.4
  0.0 1.3 %constant_dynamic-slice_fusion.1 = (bf16[6,256,128]{2,1,0:T(8,128)(2,1)S(1)}, bf16[6,256,128]{2,1,0:T(8,128)(2,1)S(1)}) fusion(bf16[6,256,256]{2,1,0:T(8,128)(2,1)} %core_ref.1, s32[]{:T(128)S(6)} %select_n.32, s32[]{:T(128)S(6)} %select_n.31), kind=kLoop, calls=%fused_computation.2 | loop fusion | bytes 1572872 | tf_op jit(solution)/shard_map/dynamic_slice | solution.py:359
  1.3 2.2 %collective-permute-start.2 = (bf16[6,256,128]{2,1,0:T(8,128)(2,1)S(1)}, bf16[6,256,128]{2,1,0:T(8,128)(2,1)S(1)}, u32[]{:S(2)}, u32[]{:S(2)}) collective-permute-start(bf16[6,256,128]{2,1,0:T(8,128)(2,1)S(1)} %get-tuple-element.32), channel_id=1, source_target_pairs={{1,2},{3,4},{5,6},{7,8},{9,10},{11,12},{13,14},{2,1},{4,3},{6,5},{... | collective-permute-start | bytes 1179656 | tf_op jit(solution)/shard_map/ppermute | solution.py:304
  3.6 0.1 constant_dynamic-slice_fusion.6
  3.6 2.9 %collective-permute-start.1 = (bf16[6,128,256]{2,1,0:T(8,128)(2,1)S(1)}, bf16[6,128,256]{2,1,0:T(8,128)(2,1)S(1)}, u32[]{:S(2)}, u32[]{:S(2)}) collective-permute-start(bf16[6,128,256]{2,1,0:T(8,128)(2,1)S(1)} %get-tuple-element.33), channel_id=1, source_target_pairs={{16,32},{48,64},{80,96},{112,128},{144,160},{176,192},{208,224},{3... | collective-permute-start | bytes 1179656 | tf_op jit(solution)/shard_map/ppermute | solution.py:304
  6.6 0.1 collective-permute-start
  6.7 0.9 %noise_spectrum.1 = (f32[264,512]{1,0:T(8,128)S(1)}, f32[264,512]{1,0:T(8,128)S(1)}) custom-call(bf16[512,512]{1,0:T(8,128)(2,1)S(1)} %copy-done.3, bf16[528,512]{1,0:T(8,128)(2,1)S(1)} %copy-done.1, bf16[512,512]{1,0:T(8,128)(2,1)S(1)} %copy-done.4), custom_call_target="tpu_custom_call" | custom-call | flops 402653184 | bytes 1048576 | tf_op jit(solution)/shard_map/noise_spectrum/pallas_call | solution.py:346
  7.6 7.0 %collective-permute-done.2.outer_ref = bf16[6,256,128]{2,1,0:T(8,128)(2,1)S(1)} collective-permute-done((bf16[6,256,128]{2,1,0:T(8,128)(2,1)S(1)}, bf16[6,256,128]{2,1,0:T(8,128)(2,1)S(1)}, u32[]{:S(2)}, u32[]{:S(2)}) %collective-permute-start.2) | collective-permute-done | bytes 393248 | tf_op jit(solution)/shard_map/ppermute | solution.py:304
  14.6 3.0 %collective-permute-start.4 = (bf16[6,128,128]{2,1,0:T(8,128)(2,1)S(1)}, bf16[6,128,128]{2,1,0:T(8,128)(2,1)S(1)}, u32[]{:S(2)}, u32[]{:S(2)}) collective-permute-start(bf16[6,128,128]{2,1,0:T(8,128)(2,1)S(1)} %get-tuple-element.35), channel_id=1, source_target_pairs={{16,32},{48,64},{80,96},{112,128},{144,160},{176,192},{208,224},{3... | collective-permute-start | bytes 589832 | tf_op jit(solution)/shard_map/ppermute | solution.py:304
  17.6 11.5 %collective-permute-start.3 = (bf16[6,128,128]{2,1,0:T(8,128)(2,1)S(1)}, bf16[6,128,128]{2,1,0:T(8,128)(2,1)S(1)}, u32[]{:S(2)}, u32[]{:S(2)}) collective-permute-start(bf16[6,128,128]{2,1,0:T(8,128)(2,1)S(1)} %get-tuple-element.36), channel_id=1, source_target_pairs={{0,16},{32,48},{64,80},{96,112},{128,144},{160,176},{192,208},{224... | collective-permute-start | bytes 589832 | tf_op jit(solution)/shard_map/ppermute | solution.py:304
  29.2 0.0 collective-permute-done.1.second_ref
  29.2 0.0 collective-permute-done.first_ref
  29.2 0.1 constant_dynamic-slice_fusion
  29.2 0.1 pad_maximum_fusion
  29.3 0.5 collective-permute-start.5
  29.8 2.4 %core_columns.1.after_ref.core_ref = bf16[6,528,256]{2,1,0:T(8,128)(2,1)S(1)} custom-call(bf16[6,256,256]{2,1,0:T(8,128)(2,1)S(1)} %copy-done, bf16[6,128,256]{2,1,0:T(8,128)(2,1)S(1)} %collective-permute-done.first_ref, bf16[6,128,256]{2,1,0:T(8,128)(2,1)S(1)} %collective-permute-done.1.second_ref, f32[512,128]{1,0:T(8,128)S(1)} %copy-done.2, ...), custom_call_target="tpu_custom_call" | custom-call | flops 134217728 | bytes 1048576 | tf_op jit(solution)/shard_map/core_columns/pallas_call | solution.py:378
  32.2 2.6 %collective-permute-done.3.first_ref = bf16[6,128,128]{2,1,0:T(8,128)(2,1)S(1)} collective-permute-done((bf16[6,128,128]{2,1,0:T(8,128)(2,1)S(1)}, bf16[6,128,128]{2,1,0:T(8,128)(2,1)S(1)}, u32[]{:S(2)}, u32[]{:S(2)}) %collective-permute-start.3) | collective-permute-done | bytes 196640 | tf_op jit(solution)/shard_map/ppermute | solution.py:304
  34.9 2.2 %outer_columns.1.after_ref.outer_ref = bf16[6,528,128]{2,1,0:T(8,128)(2,1)S(1)} custom-call(bf16[6,528,256]{2,1,0:T(8,128)(2,1)S(1)} %core_columns.1.after_ref.core_ref, bf16[6,256,128]{2,1,0:T(8,128)(2,1)S(1)} %collective-permute-done.2.outer_ref, bf16[6,128,128]{2,1,0:T(8,128)(2,1)S(1)} %collective-permute-done.3.first_ref, ...), custom_call_target="tpu_custom_call" | custom-call | flops 53687091200 | bytes 1048576 | tf_op jit(solution)/shard_map/outer_columns/pallas_call | solution.py:379
  37.1 0.0 copy-start.6
  37.1 0.0 copy-start.7
  37.1 0.0 copy-start.8
  37.2 2.3 %inner_columns.1.inner_ref = bf16[6,528,128]{2,1,0:T(8,128)(2,1)S(1)} custom-call(bf16[6,528,128]{2,1,0:T(8,128)(2,1)S(1)} %outer_columns.1.after_ref.outer_ref, bf16[6,512,128]{2,1,0:T(8,128)(2,1)S(1)} %collective-permute-done.5.inner_ref, f32[512,128]{1,0:T(8,128)S(1)} %copy-done.2, f32[8,512]{1,0:T(8,128)S(1)} %copy-done.5, bf16[528,512]{1,0:T(8,128)(2,1)S(1)} %copy-done.1), custom_call_target="tpu_custom_call" | custom-call | flops 134217728 | bytes 1048576 | tf_op jit(solution)/shard_map/inner_columns/pallas_call | solution.py:382
  39.5 4.3 %tile_model.1 = (bf16[128,512]{1,0:T(8,128)(2,1)S(1)}, bf16[128,512]{1,0:T(8,128)(2,1)S(1)}, f32[256,512]{1,0:T(8,128)S(1)}) custom-call(bf16[6,528,256]{2,1,0:T(8,128)(2,1)S(1)} %core_columns.1.after_ref.core_ref, bf16[6,528,128]{2,1,0:T(8,128)(2,1)S(1)} %inner_columns.1.inner_ref, bf16[6,528,128]{2,1,0:T(8,128)(2,1)S(1)} %outer_columns.1.after_ref.outer_ref, ...), custom_call_target="tpu_custom_call" | custom-call | flops 2684354560 | bytes 1048576 | tf_op jit(solution)/shard_map/tile_model/pallas_call | solution.py:385
  43.8 1.9 %collective-permute-start.6 = (bf16[128,512]{1,0:T(8,128)(2,1)S(1)}, bf16[128,512]{1,0:T(8,128)(2,1)S(1)}, u32[]{:S(2)}, u32[]{:S(2)}) collective-permute-start(bf16[128,512]{1,0:T(8,128)(2,1)S(1)} %get-tuple-element.26), channel_id=1, source_target_pairs={{0,16},{32,48},{64,80},{96,112},{128,144},{160,176},{192,208},{224... | collective-permute-start | bytes 393224 | tf_op jit(solution)/shard_map/ppermute | solution.py:304
  45.7 1.9 %collective-permute-start.7 = (bf16[128,512]{1,0:T(8,128)(2,1)S(1)}, bf16[128,512]{1,0:T(8,128)(2,1)S(1)}, u32[]{:S(2)}, u32[]{:S(2)}) collective-permute-start(bf16[128,512]{1,0:T(8,128)(2,1)S(1)} %get-tuple-element.27), channel_id=1, source_target_pairs={{16,32},{48,64},{80,96},{112,128},{144,160},{176,192},{208,224},{3... | collective-permute-start | bytes 393224 | tf_op jit(solution)/shard_map/ppermute | solution.py:304
  47.6 1.8 %collective-permute-done.6.first_ref = bf16[128,512]{1,0:T(8,128)(2,1)S(1)} collective-permute-done((bf16[128,512]{1,0:T(8,128)(2,1)S(1)}, bf16[128,512]{1,0:T(8,128)(2,1)S(1)}, u32[]{:S(2)}, u32[]{:S(2)}) %collective-permute-start.6) | collective-permute-done | bytes 131104 | tf_op jit(solution)/shard_map/ppermute | solution.py:304
  49.4 3.2 %collective-permute-done.7.second_ref = bf16[128,512]{1,0:T(8,128)(2,1)S(1)} collective-permute-done((bf16[128,512]{1,0:T(8,128)(2,1)S(1)}, bf16[128,512]{1,0:T(8,128)(2,1)S(1)}, u32[]{:S(2)}, u32[]{:S(2)}) %collective-permute-start.7) | collective-permute-done | bytes 131104 | tf_op jit(solution)/shard_map/ppermute | solution.py:304
  52.6 0.1 fold_rows.1
  52.7 1.9 %collective-permute-start.8 = (bf16[256,128]{1,0:T(8,128)(2,1)S(1)}, bf16[256,128]{1,0:T(8,128)(2,1)S(1)}, u32[]{:S(2)}, u32[]{:S(2)}) collective-permute-start(bf16[256,128]{1,0:T(8,128)(2,1)S(1)} %get-tuple-element.29), channel_id=1, source_target_pairs={{1,2},{3,4},{5,6},{7,8},{9,10},{11,12},{13,14},{2,1},{4,3},{6,5},{... | collective-permute-start | bytes 196616 | tf_op jit(solution)/shard_map/ppermute | solution.py:304
  54.6 0.2 collective-permute-start.9
  54.9 3.4 %collective-permute-done.8.outer_ref = bf16[256,128]{1,0:T(8,128)(2,1)S(1)} collective-permute-done((bf16[256,128]{1,0:T(8,128)(2,1)S(1)}, bf16[256,128]{1,0:T(8,128)(2,1)S(1)}, u32[]{:S(2)}, u32[]{:S(2)}) %collective-permute-start.8) | collective-permute-done | bytes 65568 | tf_op jit(solution)/shard_map/ppermute | solution.py:304
  58.3 0.7 %fold_columns.1 = f32[256,256]{1,0:T(8,128)} custom-call(f32[256,256]{1,0:T(8,128)S(1)} %get-tuple-element.28.center_ref, bf16[256,128]{1,0:T(8,128)(2,1)S(1)} %collective-permute-done.8.outer_ref, bf16[256,128]{1,0:T(8,128)(2,1)S(1)} %collective-permute-done.9.inner_ref), custom_call_target="tpu_custom_call" | custom-call | bytes 1048576 | tf_op jit(solution)/shard_map/fold_columns/pallas_call | solution.py:413
  (18 shorter events, 0.1 us)
Async XLA Ops:
  0.0 3.6 %copy-start = (bf16[6,256,256]{2,1,0:T(8,128)(2,1)S(1)}, bf16[6,256,256]{2,1,0:T(8,128)(2,1)}, u32[]{:S(2)}) copy-start(bf16[6,256,256]{2,1,0:T(8,128)(2,1)} %core_ref.1) | copy-start | bytes 2359300
  0.0 6.7 %copy-start.1 = (bf16[528,512]{1,0:T(8,128)(2,1)S(1)}, bf16[528,512]{1,0:T(8,128)(2,1)}, u32[]{:S(2)}) copy-start(bf16[528,512]{1,0:T(8,128)(2,1)} %constant.44.clone.left_ref) | copy-start | bytes 1622020
  0.0 6.7 %copy-start.3 = (bf16[512,512]{1,0:T(8,128)(2,1)S(1)}, bf16[512,512]{1,0:T(8,128)(2,1)}, u32[]{:S(2)}) copy-start(bf16[512,512]{1,0:T(8,128)(2,1)} %noise_ref.1) | copy-start | bytes 1572868
  0.0 6.7 %copy-start.4 = (bf16[512,512]{1,0:T(8,128)(2,1)S(1)}, bf16[512,512]{1,0:T(8,128)(2,1)}, u32[]{:S(2)}) copy-start(bf16[512,512]{1,0:T(8,128)(2,1)} %constant.45.clone.right_ref) | copy-start | bytes 1572868
  1.3 13.2 %collective-permute-start.2 = (bf16[6,256,128]{2,1,0:T(8,128)(2,1)S(1)}, bf16[6,256,128]{2,1,0:T(8,128)(2,1)S(1)}, u32[]{:S(2)}, u32[]{:S(2)}) collective-permute-start(bf16[6,256,128]{2,1,0:T(8,128)(2,1)S(1)} %get-tuple-element.32), channel_id=1, source_target_pairs={{1,2},{3,4},{5,6},{7,8},{9,10},{11,12},{13,14},{2,1},{4,3},{6,5},{... | collective-permute-start | bytes 1179656 | tf_op jit(solution)/shard_map/ppermute | solution.py:304
  3.6 25.5 %collective-permute-start.1 = (bf16[6,128,256]{2,1,0:T(8,128)(2,1)S(1)}, bf16[6,128,256]{2,1,0:T(8,128)(2,1)S(1)}, u32[]{:S(2)}, u32[]{:S(2)}) collective-permute-start(bf16[6,128,256]{2,1,0:T(8,128)(2,1)S(1)} %get-tuple-element.33), channel_id=1, source_target_pairs={{16,32},{48,64},{80,96},{112,128},{144,160},{176,192},{208,224},{3... | collective-permute-start | bytes 1179656 | tf_op jit(solution)/shard_map/ppermute | solution.py:304
  6.6 22.6 %collective-permute-start = (bf16[6,128,256]{2,1,0:T(8,128)(2,1)S(1)}, bf16[6,128,256]{2,1,0:T(8,128)(2,1)S(1)}, u32[]{:S(2)}, u32[]{:S(2)}) collective-permute-start(bf16[6,128,256]{2,1,0:T(8,128)(2,1)S(1)} %get-tuple-element.34), channel_id=1, source_target_pairs={{0,16},{32,48},{64,80},{96,112},{128,144},{160,176},{192,208},{224... | collective-permute-start | bytes 1179656 | tf_op jit(solution)/shard_map/ppermute | solution.py:304
  14.6 15.3 %copy-start.2 = (f32[512,128]{1,0:T(8,128)S(1)}, f32[512,128]{1,0:T(8,128)}, u32[]{:S(2)}) copy-start(f32[512,128]{1,0:T(8,128)} %constant.49.clone.rows_ref) | copy-start | bytes 786436
  14.6 15.3 %copy-start.5 = (f32[8,512]{1,0:T(8,128)S(1)}, f32[8,512]{1,0:T(8,128)}, u32[]{:S(2)}) copy-start(f32[8,512]{1,0:T(8,128)} %constant.50.clone.cols_ref) | copy-start | bytes 49156
  14.6 17.6 %collective-permute-start.4 = (bf16[6,128,128]{2,1,0:T(8,128)(2,1)S(1)}, bf16[6,128,128]{2,1,0:T(8,128)(2,1)S(1)}, u32[]{:S(2)}, u32[]{:S(2)}) collective-permute-start(bf16[6,128,128]{2,1,0:T(8,128)(2,1)S(1)} %get-tuple-element.35), channel_id=1, source_target_pairs={{16,32},{48,64},{80,96},{112,128},{144,160},{176,192},{208,224},{3... | collective-permute-start | bytes 589832 | tf_op jit(solution)/shard_map/ppermute | solution.py:304
  17.6 17.2 %collective-permute-start.3 = (bf16[6,128,128]{2,1,0:T(8,128)(2,1)S(1)}, bf16[6,128,128]{2,1,0:T(8,128)(2,1)S(1)}, u32[]{:S(2)}, u32[]{:S(2)}) collective-permute-start(bf16[6,128,128]{2,1,0:T(8,128)(2,1)S(1)} %get-tuple-element.36), channel_id=1, source_target_pairs={{0,16},{32,48},{64,80},{96,112},{128,144},{160,176},{192,208},{224... | collective-permute-start | bytes 589832 | tf_op jit(solution)/shard_map/ppermute | solution.py:304
  29.3 7.9 %collective-permute-start.5 = (bf16[6,512,128]{2,1,0:T(8,128)(2,1)S(1)}, bf16[6,512,128]{2,1,0:T(8,128)(2,1)S(1)}, u32[]{:S(2)}, u32[]{:S(2)}) collective-permute-start(bf16[6,512,128]{2,1,0:T(8,128)(2,1)S(1)} %pad_maximum_fusion), channel_id=1, source_target_pairs={{0,1},{2,3},{4,5},{6,7},{8,9},{10,11},{12,13},{14,15},{1,0},{3,2},... | collective-permute-start | bytes 2359304 | tf_op jit(solution)/shard_map/ppermute | solution.py:304
  37.1 2.3 %copy-start.6 = (bf16[512,512]{1,0:T(8,128)(2,1)S(1)}, bf16[512,512]{1,0:T(8,128)(2,1)}, u32[]{:S(2)}) copy-start(bf16[512,512]{1,0:T(8,128)(2,1)} %constant.47.clone.band_columns_ref) | copy-start | bytes 1572868
  37.1 2.3 %copy-start.7 = (bf16[512,512]{1,0:T(8,128)(2,1)S(1)}, bf16[512,512]{1,0:T(8,128)(2,1)}, u32[]{:S(2)}) copy-start(bf16[512,512]{1,0:T(8,128)(2,1)} %constant.46.clone.inverse_right_ref) | copy-start | bytes 1572868
  37.1 2.3 %copy-start.8 = (bf16[272,384]{1,0:T(8,128)(2,1)S(1)}, bf16[272,384]{1,0:T(8,128)(2,1)}, u32[]{:S(2)}) copy-start(bf16[272,384]{1,0:T(8,128)(2,1)} %constant.48.clone.band_rows_ref) | copy-start | bytes 626692
  43.8 5.6 %collective-permute-start.6 = (bf16[128,512]{1,0:T(8,128)(2,1)S(1)}, bf16[128,512]{1,0:T(8,128)(2,1)S(1)}, u32[]{:S(2)}, u32[]{:S(2)}) collective-permute-start(bf16[128,512]{1,0:T(8,128)(2,1)S(1)} %get-tuple-element.26), channel_id=1, source_target_pairs={{0,16},{32,48},{64,80},{96,112},{128,144},{160,176},{192,208},{224... | collective-permute-start | bytes 393224 | tf_op jit(solution)/shard_map/ppermute | solution.py:304
  45.7 6.9 %collective-permute-start.7 = (bf16[128,512]{1,0:T(8,128)(2,1)S(1)}, bf16[128,512]{1,0:T(8,128)(2,1)S(1)}, u32[]{:S(2)}, u32[]{:S(2)}) collective-permute-start(bf16[128,512]{1,0:T(8,128)(2,1)S(1)} %get-tuple-element.27), channel_id=1, source_target_pairs={{16,32},{48,64},{80,96},{112,128},{144,160},{176,192},{208,224},{3... | collective-permute-start | bytes 393224 | tf_op jit(solution)/shard_map/ppermute | solution.py:304
  52.7 5.6 %collective-permute-start.8 = (bf16[256,128]{1,0:T(8,128)(2,1)S(1)}, bf16[256,128]{1,0:T(8,128)(2,1)S(1)}, u32[]{:S(2)}, u32[]{:S(2)}) collective-permute-start(bf16[256,128]{1,0:T(8,128)(2,1)S(1)} %get-tuple-element.29), channel_id=1, source_target_pairs={{1,2},{3,4},{5,6},{7,8},{9,10},{11,12},{13,14},{2,1},{4,3},{6,5},{... | collective-permute-start | bytes 196616 | tf_op jit(solution)/shard_map/ppermute | solution.py:304
  54.6 3.7 %collective-permute-start.9 = (bf16[256,128]{1,0:T(8,128)(2,1)S(1)}, bf16[256,128]{1,0:T(8,128)(2,1)S(1)}, u32[]{:S(2)}, u32[]{:S(2)}) collective-permute-start(bf16[256,128]{1,0:T(8,128)(2,1)S(1)} %get-tuple-element.30), channel_id=1, source_target_pairs={{0,1},{2,3},{4,5},{6,7},{8,9},{10,11},{12,13},{14,15},{1,0},{3,2},... | collective-permute-start | bytes 196616 | tf_op jit(solution)/shard_map/ppermute | solution.py:304

commit v5 on v4

--- a/solution.py
+++ b/solution.py
@@ -74,12 +74,9 @@
     return lax.broadcasted_iota(jnp.int32, shape, 1) == 0
 
 
-def three_parts(values):
+def two_parts(values):
     high = values.astype(BF16)
-    rest = values - high.astype(F32)
-    middle = rest.astype(BF16)
-    low = (rest - middle.astype(F32)).astype(BF16)
-    return high, middle, low
+    return high, (values - high.astype(F32)).astype(BF16)
 
 
 def quarters(spectra, half):
@@ -129,7 +126,7 @@
         target = pl.multiple_of(row + number * step, step)
         members = [source[s, pl.ds(start, step), :].astype(F32) for s in range(splits)]
         mean = functools.reduce(lambda a, b: a + b, members) * (1.0 / splits)
-        weights = rows_ref[pl.ds(target, step), :1] * pc
+        weights = jnp.concatenate([rows_ref[pl.ds(target, step), :]] * (width // 128), axis=1) * pc
         for s in range(splits):
             tile[s, pl.ds(target, step), pl.ds(aligned(tile_col, 128), width)] = (
                 weights * (members[s] - mean)
@@ -146,7 +143,7 @@
     return first, far - first, outer, far - outer
 
 
-def core_kernel(half, core_ref, first_ref, second_ref, rows_ref, cols_ref, left_ref, halves_ref, tile):
+def core_kernel(half, core_ref, first_ref, second_ref, rows_ref, cols_ref, left_ref, right_ref, spectra_ref, tile):
     margin = half // 2
     splits = core_ref.shape[0]
     first, second, _, _ = sides(half)
@@ -155,7 +152,16 @@
     fill(tile, second_ref, rows_ref, cols_ref, 0, margin, second, margin, 0)
 
     for s in range(splits):
-        halves_ref[s] = dot(left_ref[...], tile[s]).astype(BF16)
+        halves = dot(left_ref[...], tile[s]).astype(BF16)
+        spectra_ref[s] = dot(halves, right_ref[:half])
+
+
+def transform_pairs(tile, left_ref, halves_ref):
+    splits, _, width = tile.shape
+    for s in range(0, splits, 2):
+        halves = dot(left_ref[...], jnp.concatenate([tile[s], tile[s + 1]], axis=1)).astype(BF16)
+        halves_ref[s] = halves[:, :width]
+        halves_ref[s + 1] = halves[:, width:]
 
 
 def inner_kernel(half, after_ref, inner_ref, rows_ref, cols_ref, left_ref, halves_ref, tile):
@@ -165,8 +171,7 @@
     fill(tile, inner_ref, rows_ref, cols_ref, 0, margin, first, inner, 0)
     fill(tile, inner_ref, rows_ref, cols_ref, margin, half, margin, inner, 0)
     fill(tile, inner_ref, rows_ref, cols_ref, margin + half, margin, second, inner, 0)
-    for s in range(inner_ref.shape[0]):
-        halves_ref[s] = dot(left_ref[...], tile[s]).astype(BF16)
+    transform_pairs(tile, left_ref, halves_ref)
 
 
 def outer_kernel(half, after_ref, outer_ref, first_ref, second_ref, rows_ref, cols_ref, left_ref, halves_ref, tile):
@@ -176,8 +181,7 @@
     fill(tile, outer_ref, rows_ref, cols_ref, 0, half, margin, outer, 0)
     fill(tile, first_ref, rows_ref, cols_ref, 0, margin, first, outer, 0)
     fill(tile, second_ref, rows_ref, cols_ref, 0, margin, second, outer, 0)
-    for s in range(outer_ref.shape[0]):
-        halves_ref[s] = dot(left_ref[...], tile[s]).astype(BF16)
+    transform_pairs(tile, left_ref, halves_ref)
 
 
 def main_kernel(
@@ -201,7 +205,7 @@
 
     def accumulate(s, carry):
         halves = jnp.concatenate([inner_ref[s], outer_ref[s]], axis=1)
-        spectra = dot(core_ref[s], right_ref[:half]) + dot(halves, table[...])
+        spectra = core_ref[s] + dot(halves, table[...])
         cc, cs, sc, ss, nc, ns = quarters(spectra, half)
         e = jnp.where(edge, cc, cc - ss)
         f = jnp.where(edge, sc, cs + sc)
@@ -222,8 +226,8 @@
     for s in range(1, splits):
         accumulate(s, False)
 
-    stacked[:, half + 24 :, :] = jnp.zeros((3, stacked.shape[1] - half - 24, length), BF16)
-    for part, values in enumerate(three_parts(power[...])):
+    stacked[:, half + 24 :, :] = jnp.zeros((2, stacked.shape[1] - half - 24, length), BF16)
+    for part, values in enumerate(two_parts(power[...])):
         stacked[part, : half + 8, :] = values
     for place, start in ((half + 8, 0), (half + 16, half - 8)):
         a = power[start : start + 8, :half]
@@ -231,19 +235,13 @@
         mirrored = jnp.concatenate(
             [jnp.where(edge8, a, b), jnp.where(edge8, b, a)], axis=1
         )
-        for part, values in enumerate(three_parts(mirrored)):
+        for part, values in enumerate(two_parts(mirrored)):
             stacked[part, place : place + 8, :] = values
     smooth = (
-        dot(band_rows_ref[...], stacked[2])
-        + dot(band_rows_ref[...], stacked[1])
-        + dot(band_rows_ref[...], stacked[0])
-    )
-    high, middle, low = three_parts(smooth)
-    smooth = (
-        dot(low, band_columns_ref[...])
-        + dot(middle, band_columns_ref[...])
-        + dot(high, band_columns_ref[...])
-    )
+        dot(band_rows_ref[...], stacked[1]) + dot(band_rows_ref[...], stacked[0])
+    )
+    high, low = two_parts(smooth)
+    smooth = dot(low, band_columns_ref[...]) + dot(high, band_columns_ref[...])
     gain = jnp.sqrt(jnp.maximum(smooth[: half + 8], 0.0) * scale)
     gr = (gain * re_ref[...]).astype(BF16)
     gi = (gain * im_ref[...]).astype(BF16)
@@ -269,11 +267,15 @@
     v = dot(right_ref[...], near_v) + dot(right_ref[...], far_v)
     joined = jnp.concatenate([u.astype(BF16), v.astype(BF16)], axis=1)
     real_part = dot(joined, inverse_right_ref[...])
-    norm = 1.0 / (length * length)
-    pc = cols_ref[:1, :]
-    inside_ref[...] = rows_ref[margin : margin + half, :1] * pc * real_part[:half] * norm
-    strips[:margin] = (rows_ref[:margin, :1] * pc * real_part[half : half + margin] * norm).astype(BF16)
-    strips[margin:] = (rows_ref[margin + half :, :1] * pc * real_part[half + margin :] * norm).astype(BF16)
+    pc = cols_ref[:1, :] * (1.0 / (length * length))
+
+    def windowed(row, place, count):
+        profile = jnp.concatenate([rows_ref[row : row + count, :]] * (length // 128), axis=1)
+        return profile * pc * real_part[place : place + count]
+
+    inside_ref[...] = windowed(margin, 0, half)
+    strips[:margin] = windowed(0, half, margin).astype(BF16)
+    strips[margin:] = windowed(margin + half, half + margin, margin).astype(BF16)
     place = pl.multiple_of(jnp.where(first == 0, 0, margin), margin)
     first_out_ref[...] = strips[pl.ds(place, margin), :]
     second_out_ref[...] = strips[pl.ds(pl.multiple_of(margin - place, margin), margin), :]
@@ -364,22 +366,29 @@
         "ra",
         0,
     )
-    def columns(body, name, width, count, flops):
+    def columns(body, name, count, flops):
         return kernel_call(
             functools.partial(body, half),
             name,
-            jax.ShapeDtypeStruct((splits, length + 16, width), BF16),
+            jax.ShapeDtypeStruct((splits, length + 16, margin), BF16),
             count,
-            [pltpu.VMEM((splits, length, width), BF16)],
+            [pltpu.VMEM((splits, length, margin), BF16)],
             flops=flops,
         )
 
-    left = constant["left"]
-    core = columns(core_kernel, "core_columns", half, 6, cube)(split_maps, first, second, rows, cols, left)
-    outer = columns(outer_kernel, "outer_columns", margin, 7, 400000 * cube // 1000)(
+    left, right = constant["left"], constant["right"]
+    core = kernel_call(
+        functools.partial(core_kernel, half),
+        "core_columns",
+        jax.ShapeDtypeStruct((splits, length + 16, length), F32),
+        7,
+        [pltpu.VMEM((splits, length, half), BF16)],
+        flops=cube,
+    )(split_maps, first, second, rows, cols, left, right)
+    outer = columns(outer_kernel, "outer_columns", 7, 400000 * cube // 1000)(
         core, outer, first_corner, second_corner, rows, cols, left
     )
-    inner = columns(inner_kernel, "inner_columns", margin, 5, cube)(outer, inner, rows, cols, left)
+    inner = columns(inner_kernel, "inner_columns", 5, cube)(outer, inner, rows, cols, left)
 
     strip = jax.ShapeDtypeStruct((margin, length), BF16)
     first, second, inside = kernel_call(
@@ -390,7 +399,7 @@
         [
             pltpu.VMEM((half, length), BF16),
             pltpu.VMEM((half + 8, length), F32),
-            pltpu.VMEM((3, half + 128, length), BF16),
+            pltpu.VMEM((2, half + 128, length), BF16),
             pltpu.VMEM((half, length), BF16),
         ],
         flops=20 * cube,
@@ -400,8 +409,8 @@
         constant["inverse_right"],
     )
 
+    second = swap(second, "dec", 1)
     first = swap(first, "dec", 0)
-    second = swap(second, "dec", 1)
     column = jax.ShapeDtypeStruct((half, margin), BF16)
     block = jax.ShapeDtypeStruct((half, half), F32)
     center, outer, inner = kernel_call(

time: 59.2 us -> 56.1 us (0.948)
  Pallas kernels: 12.9 us -> 9.87 us
    pallas_call x3, Pallas kernels: 6.87 us -> 4.59 us  [the longest x1 2.71 us: shards(): kernel_call(functools.partial(core_kernel, half), 'core_columns', jax.Sha...]
    pallas_call x1, Pallas kernels: 4.35 us -> 3.57 us  [shards(): kernel_call(functools.partial(main_kernel, half, scale), 'tile_model', (s...]
  transfers between devices with their start and end apart: 10 -> 10, of which waited for: 5 -> 5; matrix products, arithmetic and copies ran while one was open for 0% -> 0% of each run, Pallas kernels for 9% -> 8%
where the time goes in v5:
time: 56.1 us; the launch traced here: 55.8 us
  starting transfers between devices  26.2 us (47%)
  waiting for transfers between devices  17.7 us (32%)
  Pallas kernels  9.87 us (18%)
  local copies, waits for them, and re-layouts  1.76 us (3%)
    ppermute x10, starting transfers between devices, swap(): return lax.ppermute(values, axis, pairs + [(b, a) for a, b in pairs])  26.2 us
    ppermute x10, waiting for transfers between devices, swap(): return lax.ppermute(values, axis, pairs + [(b, a) for a, b in pairs])  17.7 us
    pallas_call x1, Pallas kernels, shards(): kernel_call(functools.partial(main_kernel, half, scale), 'tile_model', (s...  3.57 us
    pallas_call x1, Pallas kernels, shards(): kernel_call(functools.partial(core_kernel, half), 'core_columns', jax.Sha...  2.71 us
    dynamic_slice x2, local copies, waits for them, and re-layouts, shards(): lax.dynamic_slice_in_dim(block, (1 - odd_col) * margin, margin, axis=2)  1.39 us
  transfers between devices with their start and end apart: 10, of which 5 were waited for; matrix products, arithmetic and copies ran while one was open for 0% of the time, Pallas kernels for 8%

profile of v5, /device:TPU:206, one launch (start us, length us, event | category | flops | bytes accessed | tf_op | source)
XLA Modules:
  0.0 55.8 jit_solution(18437461464629060075)
XLA Ops:
  0.0 1.3 %constant_dynamic-slice_fusion.1 = (bf16[6,256,128]{2,1,0:T(8,128)(2,1)S(1)}, bf16[6,256,128]{2,1,0:T(8,128)(2,1)S(1)}) fusion(bf16[6,256,256]{2,1,0:T(8,128)(2,1)} %core_ref.1, s32[]{:T(128)S(6)} %select_n.32, s32[]{:T(128)S(6)} %select_n.31), kind=kLoop, calls=%fused_computation.2 | loop fusion | bytes 1572872 | tf_op jit(solution)/shard_map/dynamic_slice | solution.py:361
  1.3 2.2 %collective-permute-start.2 = (bf16[6,256,128]{2,1,0:T(8,128)(2,1)S(1)}, bf16[6,256,128]{2,1,0:T(8,128)(2,1)S(1)}, u32[]{:S(2)}, u32[]{:S(2)}) collective-permute-start(bf16[6,256,128]{2,1,0:T(8,128)(2,1)S(1)} %get-tuple-element.32), channel_id=1, source_target_pairs={{1,2},{3,4},{5,6},{7,8},{9,10},{11,12},{13,14},{2,1},{4,3},{6,5},{... | collective-permute-start | bytes 1179656 | tf_op jit(solution)/shard_map/ppermute | solution.py:306
  3.6 0.1 constant_dynamic-slice_fusion.6
  3.6 2.9 %collective-permute-start.1 = (bf16[6,128,256]{2,1,0:T(8,128)(2,1)S(1)}, bf16[6,128,256]{2,1,0:T(8,128)(2,1)S(1)}, u32[]{:S(2)}, u32[]{:S(2)}) collective-permute-start(bf16[6,128,256]{2,1,0:T(8,128)(2,1)S(1)} %get-tuple-element.33), channel_id=1, source_target_pairs={{16,32},{48,64},{80,96},{112,128},{144,160},{176,192},{208,224},{3... | collective-permute-start | bytes 1179656 | tf_op jit(solution)/shard_map/ppermute | solution.py:306
  6.6 0.1 collective-permute-start
  6.7 0.9 %noise_spectrum.1 = (f32[264,512]{1,0:T(8,128)S(1)}, f32[264,512]{1,0:T(8,128)S(1)}) custom-call(bf16[512,512]{1,0:T(8,128)(2,1)S(1)} %copy-done.4, bf16[528,512]{1,0:T(8,128)(2,1)S(1)} %copy-done.1, bf16[512,512]{1,0:T(8,128)(2,1)S(1)} %copy-done.2), custom_call_target="tpu_custom_call" | custom-call | flops 402653184 | bytes 1048576 | tf_op jit(solution)/shard_map/noise_spectrum/pallas_call | solution.py:348
  7.6 7.0 %collective-permute-done.2.outer_ref = bf16[6,256,128]{2,1,0:T(8,128)(2,1)S(1)} collective-permute-done((bf16[6,256,128]{2,1,0:T(8,128)(2,1)S(1)}, bf16[6,256,128]{2,1,0:T(8,128)(2,1)S(1)}, u32[]{:S(2)}, u32[]{:S(2)}) %collective-permute-start.2) | collective-permute-done | bytes 393248 | tf_op jit(solution)/shard_map/ppermute | solution.py:306
  14.6 3.0 %collective-permute-start.4 = (bf16[6,128,128]{2,1,0:T(8,128)(2,1)S(1)}, bf16[6,128,128]{2,1,0:T(8,128)(2,1)S(1)}, u32[]{:S(2)}, u32[]{:S(2)}) collective-permute-start(bf16[6,128,128]{2,1,0:T(8,128)(2,1)S(1)} %get-tuple-element.35), channel_id=1, source_target_pairs={{16,32},{48,64},{80,96},{112,128},{144,160},{176,192},{208,224},{3... | collective-permute-start | bytes 589832 | tf_op jit(solution)/shard_map/ppermute | solution.py:306
  17.6 11.5 %collective-permute-start.3 = (bf16[6,128,128]{2,1,0:T(8,128)(2,1)S(1)}, bf16[6,128,128]{2,1,0:T(8,128)(2,1)S(1)}, u32[]{:S(2)}, u32[]{:S(2)}) collective-permute-start(bf16[6,128,128]{2,1,0:T(8,128)(2,1)S(1)} %get-tuple-element.36), channel_id=1, source_target_pairs={{0,16},{32,48},{64,80},{96,112},{128,144},{160,176},{192,208},{224... | collective-permute-start | bytes 589832 | tf_op jit(solution)/shard_map/ppermute | solution.py:306
  29.2 0.1 constant_dynamic-slice_fusion
  29.2 0.1 pad_maximum_fusion
  29.3 0.5 collective-permute-start.5
  29.8 2.7 %core_columns.1.after_ref.core_ref = f32[6,528,512]{2,1,0:T(8,128)S(1)} custom-call(bf16[6,256,256]{2,1,0:T(8,128)(2,1)S(1)} %copy-done, bf16[6,128,256]{2,1,0:T(8,128)(2,1)S(1)} %collective-permute-done.first_ref, bf16[6,128,256]{2,1,0:T(8,128)(2,1)S(1)} %collective-permute-done.1.second_ref, f32[512,128]{1,0:T(8,128)S(1)} %copy-done.3, ...), custom_call_target="tpu_custom_call" | custom-call | flops 134217728 | bytes 1048576 | tf_op jit(solution)/shard_map/core_columns/pallas_call | solution.py:380
  32.6 2.3 %collective-permute-done.3.first_ref = bf16[6,128,128]{2,1,0:T(8,128)(2,1)S(1)} collective-permute-done((bf16[6,128,128]{2,1,0:T(8,128)(2,1)S(1)}, bf16[6,128,128]{2,1,0:T(8,128)(2,1)S(1)}, u32[]{:S(2)}, u32[]{:S(2)}) %collective-permute-start.3) | collective-permute-done | bytes 196640 | tf_op jit(solution)/shard_map/ppermute | solution.py:306
  34.9 0.9 %outer_columns.1.after_ref.outer_ref = bf16[6,528,128]{2,1,0:T(8,128)(2,1)S(1)} custom-call(f32[6,528,512]{2,1,0:T(8,128)S(1)} %core_columns.1.after_ref.core_ref, bf16[6,256,128]{2,1,0:T(8,128)(2,1)S(1)} %collective-permute-done.2.outer_ref, bf16[6,128,128]{2,1,0:T(8,128)(2,1)S(1)} %collective-permute-done.3.first_ref, ...), custom_call_target="tpu_custom_call" | custom-call | flops 53687091200 | bytes 1048576 | tf_op jit(solution)/shard_map/outer_columns/pallas_call | solution.py:388
  35.8 0.0 copy-start.5
  35.8 0.0 copy-start.6
  35.8 0.0 copy-start.7
  35.8 1.0 %inner_columns.1.inner_ref = bf16[6,528,128]{2,1,0:T(8,128)(2,1)S(1)} custom-call(bf16[6,528,128]{2,1,0:T(8,128)(2,1)S(1)} %outer_columns.1.after_ref.outer_ref, bf16[6,512,128]{2,1,0:T(8,128)(2,1)S(1)} %collective-permute-done.5.inner_ref, f32[512,128]{1,0:T(8,128)S(1)} %copy-done.3, f32[8,512]{1,0:T(8,128)S(1)} %copy-done.8, bf16[528,512]{1,0:T(8,128)(2,1)S(1)} %copy-done.1), custom_call_target="tpu_custom_call" | custom-call | flops 134217728 | bytes 1048576 | tf_op jit(solution)/shard_map/inner_columns/pallas_call | solution.py:391
  36.8 0.0 copy-done.5
  36.8 0.2 copy-done.6
  37.0 0.0 copy-done.7
  37.0 3.6 %tile_model.1 = (bf16[128,512]{1,0:T(8,128)(2,1)S(1)}, bf16[128,512]{1,0:T(8,128)(2,1)S(1)}, f32[256,512]{1,0:T(8,128)S(1)}) custom-call(f32[6,528,512]{2,1,0:T(8,128)S(1)} %core_columns.1.after_ref.core_ref, bf16[6,528,128]{2,1,0:T(8,128)(2,1)S(1)} %inner_columns.1.inner_ref, bf16[6,528,128]{2,1,0:T(8,128)(2,1)S(1)} %outer_columns.1.after_ref.outer_ref, ...), custom_call_target="tpu_custom_call" | custom-call | flops 2684354560 | bytes 1048576 | tf_op jit(solution)/shard_map/tile_model/pallas_call | solution.py:394
  40.6 1.9 %collective-permute-start.6 = (bf16[128,512]{1,0:T(8,128)(2,1)S(1)}, bf16[128,512]{1,0:T(8,128)(2,1)S(1)}, u32[]{:S(2)}, u32[]{:S(2)}) collective-permute-start(bf16[128,512]{1,0:T(8,128)(2,1)S(1)} %get-tuple-element.26), channel_id=1, source_target_pairs={{0,16},{32,48},{64,80},{96,112},{128,144},{160,176},{192,208},{224... | collective-permute-start | bytes 393224 | tf_op jit(solution)/shard_map/ppermute | solution.py:306
  42.5 1.9 %collective-permute-start.7 = (bf16[128,512]{1,0:T(8,128)(2,1)S(1)}, bf16[128,512]{1,0:T(8,128)(2,1)S(1)}, u32[]{:S(2)}, u32[]{:S(2)}) collective-permute-start(bf16[128,512]{1,0:T(8,128)(2,1)S(1)} %get-tuple-element.27), channel_id=1, source_target_pairs={{16,32},{48,64},{80,96},{112,128},{144,160},{176,192},{208,224},{3... | collective-permute-start | bytes 393224 | tf_op jit(solution)/shard_map/ppermute | solution.py:306
  44.4 1.8 %collective-permute-done.6.first_ref = bf16[128,512]{1,0:T(8,128)(2,1)S(1)} collective-permute-done((bf16[128,512]{1,0:T(8,128)(2,1)S(1)}, bf16[128,512]{1,0:T(8,128)(2,1)S(1)}, u32[]{:S(2)}, u32[]{:S(2)}) %collective-permute-start.6) | collective-permute-done | bytes 131104 | tf_op jit(solution)/shard_map/ppermute | solution.py:306
  46.2 3.2 %collective-permute-done.7.second_ref = bf16[128,512]{1,0:T(8,128)(2,1)S(1)} collective-permute-done((bf16[128,512]{1,0:T(8,128)(2,1)S(1)}, bf16[128,512]{1,0:T(8,128)(2,1)S(1)}, u32[]{:S(2)}, u32[]{:S(2)}) %collective-permute-start.7) | collective-permute-done | bytes 131104 | tf_op jit(solution)/shard_map/ppermute | solution.py:306
  49.4 0.1 fold_rows.1
  49.5 1.9 %collective-permute-start.8 = (bf16[256,128]{1,0:T(8,128)(2,1)S(1)}, bf16[256,128]{1,0:T(8,128)(2,1)S(1)}, u32[]{:S(2)}, u32[]{:S(2)}) collective-permute-start(bf16[256,128]{1,0:T(8,128)(2,1)S(1)} %get-tuple-element.29), channel_id=1, source_target_pairs={{1,2},{3,4},{5,6},{7,8},{9,10},{11,12},{13,14},{2,1},{4,3},{6,5},{... | collective-permute-start | bytes 196616 | tf_op jit(solution)/shard_map/ppermute | solution.py:306
  51.4 0.2 collective-permute-start.9
  51.7 3.4 %collective-permute-done.8.outer_ref = bf16[256,128]{1,0:T(8,128)(2,1)S(1)} collective-permute-done((bf16[256,128]{1,0:T(8,128)(2,1)S(1)}, bf16[256,128]{1,0:T(8,128)(2,1)S(1)}, u32[]{:S(2)}, u32[]{:S(2)}) %collective-permute-start.8) | collective-permute-done | bytes 65568 | tf_op jit(solution)/shard_map/ppermute | solution.py:306
  55.1 0.7 %fold_columns.1 = f32[256,256]{1,0:T(8,128)} custom-call(f32[256,256]{1,0:T(8,128)S(1)} %get-tuple-element.28.center_ref, bf16[256,128]{1,0:T(8,128)(2,1)S(1)} %collective-permute-done.8.outer_ref, bf16[256,128]{1,0:T(8,128)(2,1)S(1)} %collective-permute-done.9.inner_ref), custom_call_target="tpu_custom_call" | custom-call | bytes 1048576 | tf_op jit(solution)/shard_map/fold_columns/pallas_call | solution.py:422
  (18 shorter events, 0.1 us)
Async XLA Ops:
  0.0 3.6 %copy-start = (bf16[6,256,256]{2,1,0:T(8,128)(2,1)S(1)}, bf16[6,256,256]{2,1,0:T(8,128)(2,1)}, u32[]{:S(2)}) copy-start(bf16[6,256,256]{2,1,0:T(8,128)(2,1)} %core_ref.1) | copy-start | bytes 2359300
  0.0 6.7 %copy-start.1 = (bf16[528,512]{1,0:T(8,128)(2,1)S(1)}, bf16[528,512]{1,0:T(8,128)(2,1)}, u32[]{:S(2)}) copy-start(bf16[528,512]{1,0:T(8,128)(2,1)} %constant.44.clone.left_ref) | copy-start | bytes 1622020
  0.0 6.7 %copy-start.2 = (bf16[512,512]{1,0:T(8,128)(2,1)S(1)}, bf16[512,512]{1,0:T(8,128)(2,1)}, u32[]{:S(2)}) copy-start(bf16[512,512]{1,0:T(8,128)(2,1)} %constant.45.clone.right_ref) | copy-start | bytes 1572868
  0.0 6.7 %copy-start.4 = (bf16[512,512]{1,0:T(8,128)(2,1)S(1)}, bf16[512,512]{1,0:T(8,128)(2,1)}, u32[]{:S(2)}) copy-start(bf16[512,512]{1,0:T(8,128)(2,1)} %noise_ref.1) | copy-start | bytes 1572868
  1.3 13.2 %collective-permute-start.2 = (bf16[6,256,128]{2,1,0:T(8,128)(2,1)S(1)}, bf16[6,256,128]{2,1,0:T(8,128)(2,1)S(1)}, u32[]{:S(2)}, u32[]{:S(2)}) collective-permute-start(bf16[6,256,128]{2,1,0:T(8,128)(2,1)S(1)} %get-tuple-element.32), channel_id=1, source_target_pairs={{1,2},{3,4},{5,6},{7,8},{9,10},{11,12},{13,14},{2,1},{4,3},{6,5},{... | collective-permute-start | bytes 1179656 | tf_op jit(solution)/shard_map/ppermute | solution.py:306
  3.6 25.5 %collective-permute-start.1 = (bf16[6,128,256]{2,1,0:T(8,128)(2,1)S(1)}, bf16[6,128,256]{2,1,0:T(8,128)(2,1)S(1)}, u32[]{:S(2)}, u32[]{:S(2)}) collective-permute-start(bf16[6,128,256]{2,1,0:T(8,128)(2,1)S(1)} %get-tuple-element.33), channel_id=1, source_target_pairs={{16,32},{48,64},{80,96},{112,128},{144,160},{176,192},{208,224},{3... | collective-permute-start | bytes 1179656 | tf_op jit(solution)/shard_map/ppermute | solution.py:306
  6.6 22.6 %collective-permute-start = (bf16[6,128,256]{2,1,0:T(8,128)(2,1)S(1)}, bf16[6,128,256]{2,1,0:T(8,128)(2,1)S(1)}, u32[]{:S(2)}, u32[]{:S(2)}) collective-permute-start(bf16[6,128,256]{2,1,0:T(8,128)(2,1)S(1)} %get-tuple-element.34), channel_id=1, source_target_pairs={{0,16},{32,48},{64,80},{96,112},{128,144},{160,176},{192,208},{224... | collective-permute-start | bytes 1179656 | tf_op jit(solution)/shard_map/ppermute | solution.py:306
  14.6 15.3 %copy-start.3 = (f32[512,128]{1,0:T(8,128)S(1)}, f32[512,128]{1,0:T(8,128)}, u32[]{:S(2)}) copy-start(f32[512,128]{1,0:T(8,128)} %constant.49.clone.rows_ref) | copy-start | bytes 786436
  14.6 15.3 %copy-start.8 = (f32[8,512]{1,0:T(8,128)S(1)}, f32[8,512]{1,0:T(8,128)}, u32[]{:S(2)}) copy-start(f32[8,512]{1,0:T(8,128)} %constant.50.clone.cols_ref) | copy-start | bytes 49156
  14.6 18.0 %collective-permute-start.4 = (bf16[6,128,128]{2,1,0:T(8,128)(2,1)S(1)}, bf16[6,128,128]{2,1,0:T(8,128)(2,1)S(1)}, u32[]{:S(2)}, u32[]{:S(2)}) collective-permute-start(bf16[6,128,128]{2,1,0:T(8,128)(2,1)S(1)} %get-tuple-element.35), channel_id=1, source_target_pairs={{16,32},{48,64},{80,96},{112,128},{144,160},{176,192},{208,224},{3... | collective-permute-start | bytes 589832 | tf_op jit(solution)/shard_map/ppermute | solution.py:306
  17.6 17.2 %collective-permute-start.3 = (bf16[6,128,128]{2,1,0:T(8,128)(2,1)S(1)}, bf16[6,128,128]{2,1,0:T(8,128)(2,1)S(1)}, u32[]{:S(2)}, u32[]{:S(2)}) collective-permute-start(bf16[6,128,128]{2,1,0:T(8,128)(2,1)S(1)} %get-tuple-element.36), channel_id=1, source_target_pairs={{0,16},{32,48},{64,80},{96,112},{128,144},{160,176},{192,208},{224... | collective-permute-start | bytes 589832 | tf_op jit(solution)/shard_map/ppermute | solution.py:306
  29.3 6.5 %collective-permute-start.5 = (bf16[6,512,128]{2,1,0:T(8,128)(2,1)S(1)}, bf16[6,512,128]{2,1,0:T(8,128)(2,1)S(1)}, u32[]{:S(2)}, u32[]{:S(2)}) collective-permute-start(bf16[6,512,128]{2,1,0:T(8,128)(2,1)S(1)} %pad_maximum_fusion), channel_id=1, source_target_pairs={{0,1},{2,3},{4,5},{6,7},{8,9},{10,11},{12,13},{14,15},{1,0},{3,2},... | collective-permute-start | bytes 2359304 | tf_op jit(solution)/shard_map/ppermute | solution.py:306
  35.8 1.0 %copy-start.5 = (bf16[512,512]{1,0:T(8,128)(2,1)S(1)}, bf16[512,512]{1,0:T(8,128)(2,1)}, u32[]{:S(2)}) copy-start(bf16[512,512]{1,0:T(8,128)(2,1)} %constant.47.clone.band_columns_ref) | copy-start | bytes 1572868
  35.8 1.2 %copy-start.6 = (bf16[512,512]{1,0:T(8,128)(2,1)S(1)}, bf16[512,512]{1,0:T(8,128)(2,1)}, u32[]{:S(2)}) copy-start(bf16[512,512]{1,0:T(8,128)(2,1)} %constant.46.clone.inverse_right_ref) | copy-start | bytes 1572868
  35.8 1.2 %copy-start.7 = (bf16[272,384]{1,0:T(8,128)(2,1)S(1)}, bf16[272,384]{1,0:T(8,128)(2,1)}, u32[]{:S(2)}) copy-start(bf16[272,384]{1,0:T(8,128)(2,1)} %constant.48.clone.band_rows_ref) | copy-start | bytes 626692
  40.6 5.6 %collective-permute-start.6 = (bf16[128,512]{1,0:T(8,128)(2,1)S(1)}, bf16[128,512]{1,0:T(8,128)(2,1)S(1)}, u32[]{:S(2)}, u32[]{:S(2)}) collective-permute-start(bf16[128,512]{1,0:T(8,128)(2,1)S(1)} %get-tuple-element.26), channel_id=1, source_target_pairs={{0,16},{32,48},{64,80},{96,112},{128,144},{160,176},{192,208},{224... | collective-permute-start | bytes 393224 | tf_op jit(solution)/shard_map/ppermute | solution.py:306
  42.5 6.9 %collective-permute-start.7 = (bf16[128,512]{1,0:T(8,128)(2,1)S(1)}, bf16[128,512]{1,0:T(8,128)(2,1)S(1)}, u32[]{:S(2)}, u32[]{:S(2)}) collective-permute-start(bf16[128,512]{1,0:T(8,128)(2,1)S(1)} %get-tuple-element.27), channel_id=1, source_target_pairs={{16,32},{48,64},{80,96},{112,128},{144,160},{176,192},{208,224},{3... | collective-permute-start | bytes 393224 | tf_op jit(solution)/shard_map/ppermute | solution.py:306
  49.5 5.6 %collective-permute-start.8 = (bf16[256,128]{1,0:T(8,128)(2,1)S(1)}, bf16[256,128]{1,0:T(8,128)(2,1)S(1)}, u32[]{:S(2)}, u32[]{:S(2)}) collective-permute-start(bf16[256,128]{1,0:T(8,128)(2,1)S(1)} %get-tuple-element.29), channel_id=1, source_target_pairs={{1,2},{3,4},{5,6},{7,8},{9,10},{11,12},{13,14},{2,1},{4,3},{6,5},{... | collective-permute-start | bytes 196616 | tf_op jit(solution)/shard_map/ppermute | solution.py:306
  51.4 3.7 %collective-permute-start.9 = (bf16[256,128]{1,0:T(8,128)(2,1)S(1)}, bf16[256,128]{1,0:T(8,128)(2,1)S(1)}, u32[]{:S(2)}, u32[]{:S(2)}) collective-permute-start(bf16[256,128]{1,0:T(8,128)(2,1)S(1)} %get-tuple-element.30), channel_id=1, source_target_pairs={{0,1},{2,3},{4,5},{6,7},{8,9},{10,11},{12,13},{14,15},{1,0},{3,2},... | collective-permute-start | bytes 196616 | tf_op jit(solution)/shard_map/ppermute | solution.py:306

commit v6 on v5

--- a/solution.py
+++ b/solution.py
@@ -143,6 +143,23 @@
     return first, far - first, outer, far - outer
 
 
+def cut_kernel(half, maps_ref, first_ref, second_ref, semaphores):
+    margin = half // 2
+    first, second, outer, _ = sides(half)
+    columns = pl.ds(pl.multiple_of(jnp.where(outer == 0, 0, margin), margin), margin)
+    copies = []
+    for number, (target, place) in enumerate(((first_ref, first), (second_ref, second))):
+        rows = pl.ds(pl.multiple_of(jnp.where(place == 0, 0, margin), margin), margin)
+        for s in range(target.shape[0]):
+            copies.append(
+                pltpu.make_async_copy(maps_ref.at[s, rows, columns], target.at[s], semaphores.at[number, s])
+            )
+    for copy in copies:
+        copy.start()
+    for copy in copies:
+        copy.wait()
+
+
 def core_kernel(half, core_ref, first_ref, second_ref, rows_ref, cols_ref, left_ref, right_ref, spectra_ref, tile):
     margin = half // 2
     splits = core_ref.shape[0]
@@ -174,11 +191,16 @@
     transform_pairs(tile, left_ref, halves_ref)
 
 
-def outer_kernel(half, after_ref, outer_ref, first_ref, second_ref, rows_ref, cols_ref, left_ref, halves_ref, tile):
+def outer_kernel(
+    half, after_ref, outer_first_ref, outer_second_ref, first_ref, second_ref, rows_ref, cols_ref, left_ref,
+    halves_ref, tile,
+):
     del after_ref
     margin = half // 2
     first, second, outer, _ = sides(half)
-    fill(tile, outer_ref, rows_ref, cols_ref, 0, half, margin, outer, 0)
+    for source, place in ((outer_first_ref, first), (outer_second_ref, second)):
+        row = jnp.where(place == 0, margin, half)
+        fill(tile, source, rows_ref, cols_ref, 0, margin, row, outer, 0)
     fill(tile, first_ref, rows_ref, cols_ref, 0, margin, first, outer, 0)
     fill(tile, second_ref, rows_ref, cols_ref, 0, margin, second, outer, 0)
     transform_pairs(tile, left_ref, halves_ref)
@@ -337,24 +359,32 @@
     odd_col = lax.axis_index("ra") % 2
     cube = length**3
 
-    outer_columns = lax.dynamic_slice_in_dim(split_maps, odd_col * margin, margin, axis=2)
-    first_rows = lax.dynamic_slice_in_dim(split_maps, (1 - odd_row) * margin, margin, axis=1)
-    second_rows = lax.dynamic_slice_in_dim(split_maps, odd_row * margin, margin, axis=1)
-    outer = swap(outer_columns, "ra", 1)
+    piece = jax.ShapeDtypeStruct((splits, margin, margin), BF16)
+    outer_first, outer_second = pl.pallas_call(
+        functools.partial(cut_kernel, half),
+        out_shape=(piece, piece),
+        in_specs=[pl.BlockSpec(memory_space=pl.ANY)],
+        out_specs=tuple(whole(2)),
+        scratch_shapes=[pltpu.SemaphoreType.DMA((2, splits))],
+        compiler_params=pltpu.CompilerParams(vmem_limit_bytes=4 << 20),
+        name="cut_outer",
+    )(split_maps)
+    outer_first, outer_second, whole_core = lax.optimization_barrier((outer_first, outer_second, split_maps))
+    first_rows = lax.dynamic_slice_in_dim(whole_core, (1 - odd_row) * margin, margin, axis=1)
+    second_rows = lax.dynamic_slice_in_dim(whole_core, odd_row * margin, margin, axis=1)
+    outer_first = swap(outer_first, "ra", 1)
+    second = swap(second_rows, "dec", 1)
     first = swap(first_rows, "dec", 0)
-    second = swap(second_rows, "dec", 1)
+    outer_second = swap(outer_second, "ra", 1)
 
     spectrum = jax.ShapeDtypeStruct((half + 8, length), F32)
     re, im = kernel_call(
-        functools.partial(noise_kernel, half), "noise_spectrum", (spectrum, spectrum), 3, flops=3 * cube
+        functools.partial(noise_kernel, half), "noise_spectrum", (spectrum, spectrum), 3, flops=50 * cube
     )(white_noise, constant["left"], constant["right"])
 
-    outer, re, im = lax.optimization_barrier((outer, re, im))
-    first_corner = lax.dynamic_slice_in_dim(outer, (1 - odd_row) * margin, margin, axis=1)
-    second_corner = lax.dynamic_slice_in_dim(outer, odd_row * margin, margin, axis=1)
-    first, second, _, _ = lax.optimization_barrier((first, second, first_corner, second_corner))
-    first_corner = swap(first_corner, "dec", 0)
-    second_corner = swap(second_corner, "dec", 1)
+    first, second, _, _, re, im = lax.optimization_barrier((first, second, outer_first, outer_second, re, im))
+    first_corner = swap(outer_first, "dec", 0)
+    second_corner = swap(outer_second, "dec", 1)
     inner = swap(
         jnp.concatenate(
             [
@@ -385,8 +415,8 @@
         [pltpu.VMEM((splits, length, half), BF16)],
         flops=cube,
     )(split_maps, first, second, rows, cols, left, right)
-    outer = columns(outer_kernel, "outer_columns", 7, 400000 * cube // 1000)(
-        core, outer, first_corner, second_corner, rows, cols, left
+    outer = columns(outer_kernel, "outer_columns", 8, 400000 * cube // 1000)(
+        core, outer_first, outer_second, first_corner, second_corner, rows, cols, left
     )
     inner = columns(inner_kernel, "inner_columns", 5, cube)(outer, inner, rows, cols, left)
 

time: 56.1 us -> 59.6 us (1.062)
  the two profiles are of different devices: /device:TPU:206 before, /device:TPU:15 now
where the time goes in v6:
time: 59.6 us; the launch traced here: 58.6 us
  starting transfers between devices  31 us (52%)
  Pallas kernels  11.6 us (19%)
  waiting for transfers between devices  11 us (18%)
  local copies, waits for them, and re-layouts  4.68 us (8%)
    ppermute x11, starting transfers between devices, swap(): return lax.ppermute(values, axis, pairs + [(b, a) for a, b in pairs])  31 us
    ppermute x11, waiting for transfers between devices, swap(): return lax.ppermute(values, axis, pairs + [(b, a) for a, b in pairs])  11 us
    pallas_call x1, Pallas kernels, shards(): kernel_call(functools.partial(main_kernel, half, scale), 'tile_model', (s...  3.42 us
    pallas_call x1, Pallas kernels, shards(): kernel_call(functools.partial(core_kernel, half), 'core_columns', jax.Sha...  2.72 us
    unnamed x24, local copies, waits for them, and re-layouts  2.39 us
    dynamic_slice x1, local copies, waits for them, and re-layouts, shards(): lax.dynamic_slice_in_dim(whole_core, odd_row * margin, margin, axis=1)  2.15 us
    pallas_call x1, Pallas kernels, shards(): columns(outer_kernel, 'outer_columns', 8, 400000 * cube // 1000)  1.85 us
  transfers between devices with their start and end apart: 11, of which 4 were waited for; matrix products, arithmetic and copies ran while one was open for 4% of the time, Pallas kernels for 9%

profile of v6, /device:TPU:15, one launch (start us, length us, event | category | flops | bytes accessed | tf_op | source)
XLA Modules:
  0.0 58.6 jit_solution(13562893898062770847)
XLA Ops:
  0.0 1.1 %copy-done = bf16[6,256,256]{2,1,0:T(8,128)(2,1)S(1)} copy-done((bf16[6,256,256]{2,1,0:T(8,128)(2,1)S(1)}, bf16[6,256,256]{2,1,0:T(8,128)(2,1)}, u32[]{:S(2)}) %copy-start) | copy-done | bytes 786456
  1.1 0.9 %cut_outer.1 = (bf16[6,128,128]{2,1,0:T(8,128)(2,1)}, bf16[6,128,128]{2,1,0:T(8,128)(2,1)}) custom-call(bf16[6,256,256]{2,1,0:T(8,128)(2,1)S(1)} %copy-done), custom_call_target="tpu_custom_call" | custom-call | tf_op jit(solution)/shard_map/cut_outer/pallas_call | solution.py:363
  2.1 4.0 %collective-permute-start.2 = (bf16[6,128,128]{2,1,0:T(8,128)(2,1)}, bf16[6,128,128]{2,1,0:T(8,128)(2,1)S(1)}, u32[]{:S(2)}, u32[]{:S(2)}) collective-permute-start(bf16[6,128,128]{2,1,0:T(8,128)(2,1)} %get-tuple-element.25), channel_id=1, source_target_pairs={{1,2},{3,4},{5,6},{7,8},{9,10},{11,12},{13,14},{2,1},{4,3},{6,5},{... | collective-permute-start | bytes 589832 | tf_op jit(solution)/shard_map/ppermute | solution.py:328
  6.1 2.4 %collective-permute-start.3 = (bf16[6,128,128]{2,1,0:T(8,128)(2,1)}, bf16[6,128,128]{2,1,0:T(8,128)(2,1)}, u32[]{:S(2)}, u32[]{:S(2)}) collective-permute-start(bf16[6,128,128]{2,1,0:T(8,128)(2,1)} %get-tuple-element.26), channel_id=1, source_target_pairs={{1,2},{3,4},{5,6},{7,8},{9,10},{11,12},{13,14},{2,1},{4,3},{6,5},{... | collective-permute-start | bytes 589832 | tf_op jit(solution)/shard_map/ppermute | solution.py:328
  8.6 2.1 %constant_dynamic-slice_fusion.3 = (bf16[6,128,256]{2,1,0:T(8,128)(2,1)}, bf16[6,128,256]{2,1,0:T(8,128)(2,1)}) fusion(bf16[6,256,256]{2,1,0:T(8,128)(2,1)} %core_ref.1, s32[]{:T(128)S(6)} %select_n.24, s32[]{:T(128)S(6)} %select_n.23), kind=kLoop, calls=%fused_computation.4 | loop fusion | bytes 1572872 | tf_op jit(solution)/shard_map/dynamic_slice | solution.py:374
  10.7 8.3 %collective-permute-start.1 = (bf16[6,128,256]{2,1,0:T(8,128)(2,1)}, bf16[6,128,256]{2,1,0:T(8,128)(2,1)S(1)}, u32[]{:S(2)}, u32[]{:S(2)}) collective-permute-start(bf16[6,128,256]{2,1,0:T(8,128)(2,1)} %get-tuple-element.39), channel_id=1, source_target_pairs={{16,32},{48,64},{80,96},{112,128},{144,160},{176,192},{208,224},{3... | collective-permute-start | bytes 1179656 | tf_op jit(solution)/shard_map/ppermute | solution.py:328
  19.1 0.1 collective-permute-start
  19.2 0.9 %noise_spectrum.1 = (f32[264,512]{1,0:T(8,128)S(1)}, f32[264,512]{1,0:T(8,128)S(1)}) custom-call(bf16[512,512]{1,0:T(8,128)(2,1)S(1)} %copy-done.11, bf16[528,512]{1,0:T(8,128)(2,1)S(1)} %copy-done.3, bf16[512,512]{1,0:T(8,128)(2,1)S(1)} %copy-done.4), custom_call_target="tpu_custom_call" | custom-call | flops 6710886400 | bytes 1048576 | tf_op jit(solution)/shard_map/noise_spectrum/pallas_call | solution.py:381
  20.1 0.8 %copy-done.5 = f32[264,512]{1,0:T(8,128)} copy-done((f32[264,512]{1,0:T(8,128)}, f32[264,512]{1,0:T(8,128)S(1)}, u32[]{:S(2)}) %copy-start.5) | copy-done | bytes 540696
  20.9 0.1 constant_dynamic-slice_fusion.1
  21.0 1.5 %collective-permute-start.4 = (bf16[6,128,128]{2,1,0:T(8,128)(2,1)S(1)}, bf16[6,128,128]{2,1,0:T(8,128)(2,1)S(1)}, u32[]{:S(2)}, u32[]{:S(2)}) collective-permute-start(bf16[6,128,128]{2,1,0:T(8,128)(2,1)S(1)} %collective-permute-done.2.outer_first_ref), channel_id=1, source_target_pairs={{0,16},{32,48},{64,80},{96,112},{128,144},{160,176},{192,208},{224... | collective-permute-start | bytes 589832 | tf_op jit(solution)/shard_map/ppermute | solution.py:328
  22.5 2.3 %collective-permute-start.5 = (bf16[6,128,128]{2,1,0:T(8,128)(2,1)}, bf16[6,128,128]{2,1,0:T(8,128)(2,1)S(1)}, u32[]{:S(2)}, u32[]{:S(2)}) collective-permute-start(bf16[6,128,128]{2,1,0:T(8,128)(2,1)} %collective-permute-done.3.outer_second_ref), channel_id=1, source_target_pairs={{16,32},{48,64},{80,96},{112,128},{144,160},{176,192},{208,224},{3... | collective-permute-start | bytes 589832 | tf_op jit(solution)/shard_map/ppermute | solution.py:328
  24.8 4.0 %collective-permute-done.1.second_ref = bf16[6,128,256]{2,1,0:T(8,128)(2,1)S(1)} collective-permute-done((bf16[6,128,256]{2,1,0:T(8,128)(2,1)}, bf16[6,128,256]{2,1,0:T(8,128)(2,1)S(1)}, u32[]{:S(2)}, u32[]{:S(2)}) %collective-permute-start.1) | collective-permute-done | bytes 393248 | tf_op jit(solution)/shard_map/ppermute | solution.py:328
  28.9 1.2 %collective-permute-done.first_ref = bf16[6,128,256]{2,1,0:T(8,128)(2,1)S(1)} collective-permute-done((bf16[6,128,256]{2,1,0:T(8,128)(2,1)}, bf16[6,128,256]{2,1,0:T(8,128)(2,1)S(1)}, u32[]{:S(2)}, u32[]{:S(2)}) %collective-permute-start) | collective-permute-done | bytes 393248 | tf_op jit(solution)/shard_map/ppermute | solution.py:328
  30.1 0.1 constant_dynamic-slice_fusion
  30.1 0.1 pad_maximum_fusion
  30.2 1.4 %collective-permute-start.6 = (bf16[6,512,128]{2,1,0:T(8,128)(2,1)S(1)}, bf16[6,512,128]{2,1,0:T(8,128)(2,1)S(1)}, u32[]{:S(2)}, u32[]{:S(2)}) collective-permute-start(bf16[6,512,128]{2,1,0:T(8,128)(2,1)S(1)} %pad_maximum_fusion), channel_id=1, source_target_pairs={{0,1},{2,3},{4,5},{6,7},{8,9},{10,11},{12,13},{14,15},{1,0},{3,2},... | collective-permute-start | bytes 2359304 | tf_op jit(solution)/shard_map/ppermute | solution.py:328
  31.6 2.7 %core_columns.1.after_ref.core_ref = f32[6,528,512]{2,1,0:T(8,128)S(1)} custom-call(bf16[6,256,256]{2,1,0:T(8,128)(2,1)S(1)} %copy-done.1, bf16[6,128,256]{2,1,0:T(8,128)(2,1)S(1)} %collective-permute-done.first_ref, bf16[6,128,256]{2,1,0:T(8,128)(2,1)S(1)} %collective-permute-done.1.second_ref, f32[512,128]{1,0:T(8,128)S(1)} %copy-done.2, ...), custom_call_target="tpu_custom_call" | custom-call | flops 134217728 | bytes 1048576 | tf_op jit(solution)/shard_map/core_columns/pallas_call | solution.py:410
  34.3 1.9 %outer_columns.1.after_ref.outer_ref = bf16[6,528,128]{2,1,0:T(8,128)(2,1)S(1)} custom-call(f32[6,528,512]{2,1,0:T(8,128)S(1)} %core_columns.1.after_ref.core_ref, bf16[6,128,128]{2,1,0:T(8,128)(2,1)S(1)} %collective-permute-done.2.outer_first_ref, bf16[6,128,128]{2,1,0:T(8,128)(2,1)} %collective-permute-done.3.outer_second_ref, ...), custom_call_target="tpu_custom_call" | custom-call | flops 53687091200 | bytes 1048576 | tf_op jit(solution)/shard_map/outer_columns/pallas_call | solution.py:418
  36.2 1.0 %inner_columns.1.inner_ref = bf16[6,528,128]{2,1,0:T(8,128)(2,1)S(1)} custom-call(bf16[6,528,128]{2,1,0:T(8,128)(2,1)S(1)} %outer_columns.1.after_ref.outer_ref, bf16[6,512,128]{2,1,0:T(8,128)(2,1)S(1)} %collective-permute-done.6.inner_ref, f32[512,128]{1,0:T(8,128)S(1)} %copy-done.2, f32[8,512]{1,0:T(8,128)S(1)} %copy-done.10, bf16[528,512]{1,0:T(8,128)(2,1)S(1)} %copy-done.3), custom_call_target="tpu_custom_call" | custom-call | flops 134217728 | bytes 1048576 | tf_op jit(solution)/shard_map/inner_columns/pallas_call | solution.py:421
  37.2 0.2 copy-done.7
  37.4 0.2 copy-done.8
  37.6 0.0 copy-done.9
  37.6 3.4 %tile_model.1 = (bf16[128,512]{1,0:T(8,128)(2,1)S(1)}, bf16[128,512]{1,0:T(8,128)(2,1)S(1)}, f32[256,512]{1,0:T(8,128)S(1)}) custom-call(f32[6,528,512]{2,1,0:T(8,128)S(1)} %core_columns.1.after_ref.core_ref, bf16[6,528,128]{2,1,0:T(8,128)(2,1)S(1)} %inner_columns.1.inner_ref, bf16[6,528,128]{2,1,0:T(8,128)(2,1)S(1)} %outer_columns.1.after_ref.outer_ref, ...), custom_call_target="tpu_custom_call" | custom-call | flops 2684354560 | bytes 1048576 | tf_op jit(solution)/shard_map/tile_model/pallas_call | solution.py:424
  41.0 0.3 collective-permute-start.7
  41.3 5.4 %collective-permute-start.8 = (bf16[128,512]{1,0:T(8,128)(2,1)S(1)}, bf16[128,512]{1,0:T(8,128)(2,1)S(1)}, u32[]{:S(2)}, u32[]{:S(2)}) collective-permute-start(bf16[128,512]{1,0:T(8,128)(2,1)S(1)} %get-tuple-element.35), channel_id=1, source_target_pairs={{16,32},{48,64},{80,96},{112,128},{144,160},{176,192},{208,224},{3... | collective-permute-start | bytes 393224 | tf_op jit(solution)/shard_map/ppermute | solution.py:328
  46.7 3.9 %collective-permute-done.8.second_ref = bf16[128,512]{1,0:T(8,128)(2,1)S(1)} collective-permute-done((bf16[128,512]{1,0:T(8,128)(2,1)S(1)}, bf16[128,512]{1,0:T(8,128)(2,1)S(1)}, u32[]{:S(2)}, u32[]{:S(2)}) %collective-permute-start.8) | collective-permute-done | bytes 131104 | tf_op jit(solution)/shard_map/ppermute | solution.py:328
  50.6 0.1 fold_rows.1
  50.7 5.2 %collective-permute-start.9 = (bf16[256,128]{1,0:T(8,128)(2,1)S(1)}, bf16[256,128]{1,0:T(8,128)(2,1)S(1)}, u32[]{:S(2)}, u32[]{:S(2)}) collective-permute-start(bf16[256,128]{1,0:T(8,128)(2,1)S(1)} %get-tuple-element.37), channel_id=1, source_target_pairs={{1,2},{3,4},{5,6},{7,8},{9,10},{11,12},{13,14},{2,1},{4,3},{6,5},{... | collective-permute-start | bytes 196616 | tf_op jit(solution)/shard_map/ppermute | solution.py:328
  55.9 0.1 collective-permute-start.10
  56.0 1.8 %collective-permute-done.9.outer_ref = bf16[256,128]{1,0:T(8,128)(2,1)S(1)} collective-permute-done((bf16[256,128]{1,0:T(8,128)(2,1)S(1)}, bf16[256,128]{1,0:T(8,128)(2,1)S(1)}, u32[]{:S(2)}, u32[]{:S(2)}) %collective-permute-start.9) | collective-permute-done | bytes 65568 | tf_op jit(solution)/shard_map/ppermute | solution.py:328
  57.9 0.7 %fold_columns.1 = f32[256,256]{1,0:T(8,128)} custom-call(f32[256,256]{1,0:T(8,128)S(1)} %get-tuple-element.36.center_ref, bf16[256,128]{1,0:T(8,128)(2,1)S(1)} %collective-permute-done.9.outer_ref, bf16[256,128]{1,0:T(8,128)(2,1)S(1)} %collective-permute-done.10.inner_ref), custom_call_target="tpu_custom_call" | custom-call | bytes 1048576 | tf_op jit(solution)/shard_map/fold_columns/pallas_call | solution.py:452
  (26 shorter events, 0.1 us)
Async XLA Ops:
  0.0 1.1 %copy-start = (bf16[6,256,256]{2,1,0:T(8,128)(2,1)S(1)}, bf16[6,256,256]{2,1,0:T(8,128)(2,1)}, u32[]{:S(2)}) copy-start(bf16[6,256,256]{2,1,0:T(8,128)(2,1)} %core_ref.1) | copy-start | bytes 2359300
  1.1 18.0 %copy-start.3 = (bf16[528,512]{1,0:T(8,128)(2,1)S(1)}, bf16[528,512]{1,0:T(8,128)(2,1)}, u32[]{:S(2)}) copy-start(bf16[528,512]{1,0:T(8,128)(2,1)} %constant.44.clone.left_ref) | copy-start | bytes 1622020
  1.1 18.1 %copy-start.4 = (bf16[512,512]{1,0:T(8,128)(2,1)S(1)}, bf16[512,512]{1,0:T(8,128)(2,1)}, u32[]{:S(2)}) copy-start(bf16[512,512]{1,0:T(8,128)(2,1)} %constant.45.clone.right_ref) | copy-start | bytes 1572868
  2.1 18.9 %collective-permute-start.2 = (bf16[6,128,128]{2,1,0:T(8,128)(2,1)}, bf16[6,128,128]{2,1,0:T(8,128)(2,1)S(1)}, u32[]{:S(2)}, u32[]{:S(2)}) collective-permute-start(bf16[6,128,128]{2,1,0:T(8,128)(2,1)} %get-tuple-element.25), channel_id=1, source_target_pairs={{1,2},{3,4},{5,6},{7,8},{9,10},{11,12},{13,14},{2,1},{4,3},{6,5},{... | collective-permute-start | bytes 589832 | tf_op jit(solution)/shard_map/ppermute | solution.py:328
  6.1 16.4 %collective-permute-start.3 = (bf16[6,128,128]{2,1,0:T(8,128)(2,1)}, bf16[6,128,128]{2,1,0:T(8,128)(2,1)}, u32[]{:S(2)}, u32[]{:S(2)}) collective-permute-start(bf16[6,128,128]{2,1,0:T(8,128)(2,1)} %get-tuple-element.26), channel_id=1, source_target_pairs={{1,2},{3,4},{5,6},{7,8},{9,10},{11,12},{13,14},{2,1},{4,3},{6,5},{... | collective-permute-start | bytes 589832 | tf_op jit(solution)/shard_map/ppermute | solution.py:328
  8.6 10.6 %copy-start.11 = (bf16[512,512]{1,0:T(8,128)(2,1)S(1)}, bf16[512,512]{1,0:T(8,128)(2,1)}, u32[]{:S(2)}) copy-start(bf16[512,512]{1,0:T(8,128)(2,1)} %noise_ref.1) | copy-start | bytes 1572868
  10.7 18.1 %collective-permute-start.1 = (bf16[6,128,256]{2,1,0:T(8,128)(2,1)}, bf16[6,128,256]{2,1,0:T(8,128)(2,1)S(1)}, u32[]{:S(2)}, u32[]{:S(2)}) collective-permute-start(bf16[6,128,256]{2,1,0:T(8,128)(2,1)} %get-tuple-element.39), channel_id=1, source_target_pairs={{16,32},{48,64},{80,96},{112,128},{144,160},{176,192},{208,224},{3... | collective-permute-start | bytes 1179656 | tf_op jit(solution)/shard_map/ppermute | solution.py:328
  19.1 1.9 %copy-start.1 = (bf16[6,256,256]{2,1,0:T(8,128)(2,1)S(1)}, bf16[6,256,256]{2,1,0:T(8,128)(2,1)}, u32[]{:S(2)}) copy-start(bf16[6,256,256]{2,1,0:T(8,128)(2,1)} %core_ref.1) | copy-start | bytes 2359300
  19.1 11.0 %collective-permute-start = (bf16[6,128,256]{2,1,0:T(8,128)(2,1)}, bf16[6,128,256]{2,1,0:T(8,128)(2,1)S(1)}, u32[]{:S(2)}, u32[]{:S(2)}) collective-permute-start(bf16[6,128,256]{2,1,0:T(8,128)(2,1)} %get-tuple-element.40), channel_id=1, source_target_pairs={{0,16},{32,48},{64,80},{96,112},{128,144},{160,176},{192,208},{224... | collective-permute-start | bytes 1179656 | tf_op jit(solution)/shard_map/ppermute | solution.py:328
  20.1 0.8 %copy-start.5 = (f32[264,512]{1,0:T(8,128)}, f32[264,512]{1,0:T(8,128)S(1)}, u32[]{:S(2)}) copy-start(f32[264,512]{1,0:T(8,128)S(1)} %get-tuple-element.32.im_ref) | copy-start | bytes 1622020
  20.9 10.7 %copy-start.2 = (f32[512,128]{1,0:T(8,128)S(1)}, f32[512,128]{1,0:T(8,128)}, u32[]{:S(2)}) copy-start(f32[512,128]{1,0:T(8,128)} %constant.49.clone.rows_ref) | copy-start | bytes 786436
  20.9 10.7 %copy-start.10 = (f32[8,512]{1,0:T(8,128)S(1)}, f32[8,512]{1,0:T(8,128)}, u32[]{:S(2)}) copy-start(f32[8,512]{1,0:T(8,128)} %constant.50.clone.cols_ref) | copy-start | bytes 49156
  21.0 13.3 %collective-permute-start.4 = (bf16[6,128,128]{2,1,0:T(8,128)(2,1)S(1)}, bf16[6,128,128]{2,1,0:T(8,128)(2,1)S(1)}, u32[]{:S(2)}, u32[]{:S(2)}) collective-permute-start(bf16[6,128,128]{2,1,0:T(8,128)(2,1)S(1)} %collective-permute-done.2.outer_first_ref), channel_id=1, source_target_pairs={{0,16},{32,48},{64,80},{96,112},{128,144},{160,176},{192,208},{224... | collective-permute-start | bytes 589832 | tf_op jit(solution)/shard_map/ppermute | solution.py:328
  22.5 11.8 %collective-permute-start.5 = (bf16[6,128,128]{2,1,0:T(8,128)(2,1)}, bf16[6,128,128]{2,1,0:T(8,128)(2,1)S(1)}, u32[]{:S(2)}, u32[]{:S(2)}) collective-permute-start(bf16[6,128,128]{2,1,0:T(8,128)(2,1)} %collective-permute-done.3.outer_second_ref), channel_id=1, source_target_pairs={{16,32},{48,64},{80,96},{112,128},{144,160},{176,192},{208,224},{3... | collective-permute-start | bytes 589832 | tf_op jit(solution)/shard_map/ppermute | solution.py:328
  30.2 6.0 %collective-permute-start.6 = (bf16[6,512,128]{2,1,0:T(8,128)(2,1)S(1)}, bf16[6,512,128]{2,1,0:T(8,128)(2,1)S(1)}, u32[]{:S(2)}, u32[]{:S(2)}) collective-permute-start(bf16[6,512,128]{2,1,0:T(8,128)(2,1)S(1)} %pad_maximum_fusion), channel_id=1, source_target_pairs={{0,1},{2,3},{4,5},{6,7},{8,9},{10,11},{12,13},{14,15},{1,0},{3,2},... | collective-permute-start | bytes 2359304 | tf_op jit(solution)/shard_map/ppermute | solution.py:328
  36.2 1.0 %copy-start.6 = (f32[264,512]{1,0:T(8,128)S(1)}, f32[264,512]{1,0:T(8,128)}, u32[]{:S(2)}) copy-start(f32[264,512]{1,0:T(8,128)} %copy-done.5) | copy-start | bytes 1622020
  36.2 1.2 %copy-start.7 = (bf16[512,512]{1,0:T(8,128)(2,1)S(1)}, bf16[512,512]{1,0:T(8,128)(2,1)}, u32[]{:S(2)}) copy-start(bf16[512,512]{1,0:T(8,128)(2,1)} %constant.47.clone.band_columns_ref) | copy-start | bytes 1572868
  36.2 1.3 %copy-start.8 = (bf16[512,512]{1,0:T(8,128)(2,1)S(1)}, bf16[512,512]{1,0:T(8,128)(2,1)}, u32[]{:S(2)}) copy-start(bf16[512,512]{1,0:T(8,128)(2,1)} %constant.46.clone.inverse_right_ref) | copy-start | bytes 1572868
  36.2 1.4 %copy-start.9 = (bf16[272,384]{1,0:T(8,128)(2,1)S(1)}, bf16[272,384]{1,0:T(8,128)(2,1)}, u32[]{:S(2)}) copy-start(bf16[272,384]{1,0:T(8,128)(2,1)} %constant.48.clone.band_rows_ref) | copy-start | bytes 626692
  41.0 5.7 %collective-permute-start.7 = (bf16[128,512]{1,0:T(8,128)(2,1)S(1)}, bf16[128,512]{1,0:T(8,128)(2,1)S(1)}, u32[]{:S(2)}, u32[]{:S(2)}) collective-permute-start(bf16[128,512]{1,0:T(8,128)(2,1)S(1)} %get-tuple-element.34), channel_id=1, source_target_pairs={{0,16},{32,48},{64,80},{96,112},{128,144},{160,176},{192,208},{224... | collective-permute-start | bytes 393224 | tf_op jit(solution)/shard_map/ppermute | solution.py:328
  41.3 9.3 %collective-permute-start.8 = (bf16[128,512]{1,0:T(8,128)(2,1)S(1)}, bf16[128,512]{1,0:T(8,128)(2,1)S(1)}, u32[]{:S(2)}, u32[]{:S(2)}) collective-permute-start(bf16[128,512]{1,0:T(8,128)(2,1)S(1)} %get-tuple-element.35), channel_id=1, source_target_pairs={{16,32},{48,64},{80,96},{112,128},{144,160},{176,192},{208,224},{3... | collective-permute-start | bytes 393224 | tf_op jit(solution)/shard_map/ppermute | solution.py:328
  50.7 7.1 %collective-permute-start.9 = (bf16[256,128]{1,0:T(8,128)(2,1)S(1)}, bf16[256,128]{1,0:T(8,128)(2,1)S(1)}, u32[]{:S(2)}, u32[]{:S(2)}) collective-permute-start(bf16[256,128]{1,0:T(8,128)(2,1)S(1)} %get-tuple-element.37), channel_id=1, source_target_pairs={{1,2},{3,4},{5,6},{7,8},{9,10},{11,12},{13,14},{2,1},{4,3},{6,5},{... | collective-permute-start | bytes 196616 | tf_op jit(solution)/shard_map/ppermute | solution.py:328
  55.9 1.9 %collective-permute-start.10 = (bf16[256,128]{1,0:T(8,128)(2,1)S(1)}, bf16[256,128]{1,0:T(8,128)(2,1)S(1)}, u32[]{:S(2)}, u32[]{:S(2)}) collective-permute-start(bf16[256,128]{1,0:T(8,128)(2,1)S(1)} %get-tuple-element.38), channel_id=1, source_target_pairs={{0,1},{2,3},{4,5},{6,7},{8,9},{10,11},{12,13},{14,15},{1,0},{3,2},... | collective-permute-start | bytes 196616 | tf_op jit(solution)/shard_map/ppermute | solution.py:328

commit v7 on v6

--- a/solution.py
+++ b/solution.py
@@ -116,10 +116,12 @@
     return offset if isinstance(offset, int) else pl.multiple_of(offset, step)
 
 
-def fill(tile, source, rows_ref, cols_ref, source_row, height, row, col, tile_col):
+def fill(tile, source, rows_ref, cols_ref, source_row, height, row, col, tile_col, exists=None):
     splits, width = source.shape[0], source.shape[2]
     step = 32
     pc = cols_ref[:1, pl.ds(aligned(col, 128), width)]
+    if exists is not None:
+        pc = pc * exists
 
     def strip(number, carry):
         start = pl.multiple_of(source_row + number * step, step)
@@ -143,30 +145,36 @@
     return first, far - first, outer, far - outer
 
 
-def cut_kernel(half, maps_ref, first_ref, second_ref, semaphores):
+def inside_sky():
+    flags = []
+    for axis in ("dec", "ra"):
+        index = lax.axis_index(axis)
+        edge = jnp.logical_or(index == 0, index == lax.axis_size(axis) - 1)
+        flags.append(jnp.where(edge, 0.0, 1.0).astype(F32))
+    return flags
+
+
+def cut_kernel(half, maps_ref, outer_first_ref, outer_second_ref, first_ref, second_ref):
     margin = half // 2
     first, second, outer, _ = sides(half)
     columns = pl.ds(pl.multiple_of(jnp.where(outer == 0, 0, margin), margin), margin)
-    copies = []
-    for number, (target, place) in enumerate(((first_ref, first), (second_ref, second))):
+    for piece, strip, place in (
+        (outer_first_ref, first_ref, first), (outer_second_ref, second_ref, second)
+    ):
         rows = pl.ds(pl.multiple_of(jnp.where(place == 0, 0, margin), margin), margin)
-        for s in range(target.shape[0]):
-            copies.append(
-                pltpu.make_async_copy(maps_ref.at[s, rows, columns], target.at[s], semaphores.at[number, s])
-            )
-    for copy in copies:
-        copy.start()
-    for copy in copies:
-        copy.wait()
+        for s in range(maps_ref.shape[0]):
+            piece[s] = maps_ref[s, rows, columns]
+            strip[s] = maps_ref[s, rows, :]
 
 
 def core_kernel(half, core_ref, first_ref, second_ref, rows_ref, cols_ref, left_ref, right_ref, spectra_ref, tile):
     margin = half // 2
     splits = core_ref.shape[0]
     first, second, _, _ = sides(half)
+    has_second, _ = inside_sky()
     fill(tile, core_ref, rows_ref, cols_ref, 0, half, margin, margin, 0)
     fill(tile, first_ref, rows_ref, cols_ref, 0, margin, first, margin, 0)
-    fill(tile, second_ref, rows_ref, cols_ref, 0, margin, second, margin, 0)
+    fill(tile, second_ref, rows_ref, cols_ref, 0, margin, second, margin, 0, has_second)
 
     for s in range(splits):
         halves = dot(left_ref[...], tile[s]).astype(BF16)
@@ -185,9 +193,10 @@
     del after_ref
     margin = half // 2
     first, second, _, inner = sides(half)
+    has_second, _ = inside_sky()
     fill(tile, inner_ref, rows_ref, cols_ref, 0, margin, first, inner, 0)
     fill(tile, inner_ref, rows_ref, cols_ref, margin, half, margin, inner, 0)
-    fill(tile, inner_ref, rows_ref, cols_ref, margin + half, margin, second, inner, 0)
+    fill(tile, inner_ref, rows_ref, cols_ref, margin + half, margin, second, inner, 0, has_second)
     transform_pairs(tile, left_ref, halves_ref)
 
 
@@ -198,11 +207,12 @@
     del after_ref
     margin = half // 2
     first, second, outer, _ = sides(half)
+    has_second, has_outer = inside_sky()
     for source, place in ((outer_first_ref, first), (outer_second_ref, second)):
         row = jnp.where(place == 0, margin, half)
-        fill(tile, source, rows_ref, cols_ref, 0, margin, row, outer, 0)
-    fill(tile, first_ref, rows_ref, cols_ref, 0, margin, first, outer, 0)
-    fill(tile, second_ref, rows_ref, cols_ref, 0, margin, second, outer, 0)
+        fill(tile, source, rows_ref, cols_ref, 0, margin, row, outer, 0, has_outer)
+    fill(tile, first_ref, rows_ref, cols_ref, 0, margin, first, outer, 0, has_outer)
+    fill(tile, second_ref, rows_ref, cols_ref, 0, margin, second, outer, 0, has_outer * has_second)
     transform_pairs(tile, left_ref, halves_ref)
 
 
@@ -306,9 +316,10 @@
 def fold_rows_kernel(half, inside_ref, first_ref, second_ref, center_ref, outer_ref, inner_ref, total):
     margin = half // 2
     first, second, outer, inner = sides(half)
-    for source, place in ((first_ref, first), (second_ref, second)):
+    has_second, _ = inside_sky()
+    for source, place, exists in ((first_ref, first, 1.0), (second_ref, second, has_second)):
         rows = pl.ds(pl.multiple_of(jnp.where(place == 0, 0, margin), margin), margin)
-        total[rows, :] = inside_ref[rows, :] + source[...].astype(F32)
+        total[rows, :] = inside_ref[rows, :] + source[...].astype(F32) * exists
     center_ref[...] = total[:, margin : margin + half]
     outer_ref[...] = total[:, pl.ds(pl.multiple_of(outer, margin), margin)].astype(BF16)
     inner_ref[...] = total[:, pl.ds(pl.multiple_of(inner, margin), margin)].astype(BF16)
@@ -317,22 +328,34 @@
 def fold_columns_kernel(half, center_ref, outer_ref, inner_ref, out_ref):
     margin = half // 2
     _, _, outer, inner = sides(half)
-    for source, place in ((outer_ref, outer), (inner_ref, inner)):
+    _, has_outer = inside_sky()
+    for source, place, exists in ((outer_ref, outer, has_outer), (inner_ref, inner, 1.0)):
         columns = pl.ds(pl.multiple_of(jnp.where(place == 0, 0, margin), margin), margin)
-        out_ref[:, columns] = center_ref[:, columns] + source[...].astype(F32)
-
-
-def swap(values, axis, offset):
-    count = lax.axis_size(axis)
-    pairs = [(i, i + 1) for i in range(offset, count - 1, 2)]
-    return lax.ppermute(values, axis, pairs + [(b, a) for a, b in pairs])
+        out_ref[:, columns] = center_ref[:, columns] + source[...].astype(F32) * exists
+
+
+def swap_rows(values, offset):
+    rows, columns = lax.axis_size("dec"), lax.axis_size("ra")
+    pairs = []
+    for i in range(rows):
+        partner = i + 1 if i % 2 == offset else i - 1
+        for j in range(columns):
+            target = partner * columns + j if 0 <= partner < rows else i * columns + (j ^ 1)
+            pairs.append((i * columns + j, target))
+    return lax.ppermute(values, ("dec", "ra"), pairs)
+
+
+def swap_columns(values, offset):
+    count = lax.axis_size("ra")
+    pairs = [(i, (i + 1 if i % 2 == offset else i - 1) % count) for i in range(count)]
+    return lax.ppermute(values, "ra", pairs)
 
 
 def whole(count):
     return [pl.BlockSpec(memory_space=pltpu.VMEM)] * count
 
 
-def kernel_call(body, name, outs, count, scratch=(), flops=0, vmem=24):
+def kernel_call(body, name, outs, count, scratch=(), flops=0, vmem=16):
     return pl.pallas_call(
         body,
         out_shape=outs,
@@ -355,27 +378,18 @@
     rows = jnp.asarray(np.ascontiguousarray(np.broadcast_to(profile[:, None], (length, 128))))
     cols = jnp.asarray(np.ascontiguousarray(np.broadcast_to(profile[None, :], (8, length))))
     scale = 1.0 / ((2 * SMOOTH + 1) ** 2 * (splits - 1) * tables["energy"])
-    odd_row = lax.axis_index("dec") % 2
     odd_col = lax.axis_index("ra") % 2
     cube = length**3
 
     piece = jax.ShapeDtypeStruct((splits, margin, margin), BF16)
-    outer_first, outer_second = pl.pallas_call(
-        functools.partial(cut_kernel, half),
-        out_shape=(piece, piece),
-        in_specs=[pl.BlockSpec(memory_space=pl.ANY)],
-        out_specs=tuple(whole(2)),
-        scratch_shapes=[pltpu.SemaphoreType.DMA((2, splits))],
-        compiler_params=pltpu.CompilerParams(vmem_limit_bytes=4 << 20),
-        name="cut_outer",
+    strip = jax.ShapeDtypeStruct((splits, margin, half), BF16)
+    outer_first, outer_second, first, second = kernel_call(
+        functools.partial(cut_kernel, half), "cut", (piece, piece, strip, strip), 1, vmem=8
     )(split_maps)
-    outer_first, outer_second, whole_core = lax.optimization_barrier((outer_first, outer_second, split_maps))
-    first_rows = lax.dynamic_slice_in_dim(whole_core, (1 - odd_row) * margin, margin, axis=1)
-    second_rows = lax.dynamic_slice_in_dim(whole_core, odd_row * margin, margin, axis=1)
-    outer_first = swap(outer_first, "ra", 1)
-    second = swap(second_rows, "dec", 1)
-    first = swap(first_rows, "dec", 0)
-    outer_second = swap(outer_second, "ra", 1)
+    outer_first = swap_columns(outer_first, 1)
+    second = swap_rows(second, 1)
+    first = swap_rows(first, 0)
+    outer_second = swap_columns(outer_second, 1)
 
     spectrum = jax.ShapeDtypeStruct((half + 8, length), F32)
     re, im = kernel_call(
@@ -383,9 +397,9 @@
     )(white_noise, constant["left"], constant["right"])
 
     first, second, _, _, re, im = lax.optimization_barrier((first, second, outer_first, outer_second, re, im))
-    first_corner = swap(outer_first, "dec", 0)
-    second_corner = swap(outer_second, "dec", 1)
-    inner = swap(
+    first_corner = swap_rows(outer_first, 0)
+    second_corner = swap_rows(outer_second, 1)
+    inner = swap_columns(
         jnp.concatenate(
             [
                 lax.dynamic_slice_in_dim(block, (1 - odd_col) * margin, margin, axis=2)
@@ -393,7 +407,6 @@
             ],
             axis=1,
         ),
-        "ra",
         0,
     )
     def columns(body, name, count, flops):
@@ -439,16 +452,16 @@
         constant["inverse_right"],
     )
 
-    second = swap(second, "dec", 1)
-    first = swap(first, "dec", 0)
+    second = swap_rows(second, 1)
+    first = swap_rows(first, 0)
     column = jax.ShapeDtypeStruct((half, margin), BF16)
     block = jax.ShapeDtypeStruct((half, half), F32)
     center, outer, inner = kernel_call(
         functools.partial(fold_rows_kernel, half), "fold_rows", (block, column, column), 3,
         [pltpu.VMEM((half, length), F32)],
     )(inside, first, second)
-    outer = swap(outer, "ra", 1)
-    inner = swap(inner, "ra", 0)
+    outer = swap_columns(outer, 1)
+    inner = swap_columns(inner, 0)
     return kernel_call(functools.partial(fold_columns_kernel, half), "fold_columns", block, 3)(
         center, outer, inner
     )

time: 59.6 us -> 51.8 us (0.87)
  the two profiles are of different devices: /device:TPU:15 before, /device:TPU:196 now
where the time goes in v7:
time: 51.8 us; the launch traced here: 51.5 us
  starting transfers between devices  21.1 us (41%)
  waiting for transfers between devices  13.7 us (26%)
  Pallas kernels  11.8 us (23%)
  local copies, waits for them, and re-layouts  4.7 us (9%)
    ppermute x6, starting transfers between devices, swap_rows(): return lax.ppermute(values, ('dec', 'ra'), pairs)  16.9 us
    ppermute x6, waiting for transfers between devices, swap_rows(): return lax.ppermute(values, ('dec', 'ra'), pairs)  8 us
    ppermute x5, waiting for transfers between devices, swap_columns(): return lax.ppermute(values, 'ra', pairs)  5.7 us
    unnamed x24, local copies, waits for them, and re-layouts  4.54 us
    ppermute x5, starting transfers between devices, swap_columns(): return lax.ppermute(values, 'ra', pairs)  4.14 us
    pallas_call x1, Pallas kernels, shards(): kernel_call(functools.partial(main_kernel, half, scale), 'tile_model', (s...  3.57 us
    pallas_call x1, Pallas kernels, shards(): kernel_call(functools.partial(core_kernel, half), 'core_columns', jax.Sha...  2.74 us
    pallas_call x1, Pallas kernels, shards(): columns(outer_kernel, 'outer_columns', 8, 400000 * cube // 1000)  1.95 us
  transfers between devices with their start and end apart: 11, of which 5 were waited for; matrix products, arithmetic and copies ran while one was open for 0% of the time, Pallas kernels for 11%

profile of v7, /device:TPU:196, one launch (start us, length us, event | category | flops | bytes accessed | tf_op | source)
XLA Modules:
  0.0 51.5 jit_solution(4908812408292079889)
XLA Ops:
  0.0 1.1 %copy-done = bf16[6,256,256]{2,1,0:T(8,128)(2,1)S(1)} copy-done((bf16[6,256,256]{2,1,0:T(8,128)(2,1)S(1)}, bf16[6,256,256]{2,1,0:T(8,128)(2,1)}, u32[]{:S(2)}) %copy-start) | copy-done | bytes 786456
  1.1 0.9 %cut.1 = (bf16[6,128,128]{2,1,0:T(8,128)(2,1)}, bf16[6,128,128]{2,1,0:T(8,128)(2,1)}, bf16[6,128,256]{2,1,0:T(8,128)(2,1)S(1)}, bf16[6,128,256]{2,1,0:T(8,128)(2,1)S(1)}) custom-call(bf16[6,256,256]{2,1,0:T(8,128)(2,1)S(1)} %copy-done), custom_call_target="tpu_custom_call" | custom-call | bytes 1048576 | tf_op jit(solution)/shard_map/cut/pallas_call | solution.py:386
  2.0 3.1 %collective-permute-start.2 = (bf16[6,128,128]{2,1,0:T(8,128)(2,1)}, bf16[6,128,128]{2,1,0:T(8,128)(2,1)}, u32[]{:S(2)}, u32[]{:S(2)}) collective-permute-start(bf16[6,128,128]{2,1,0:T(8,128)(2,1)} %get-tuple-element.23), channel_id=1, source_target_pairs={{0,15},{1,2},{2,1},{3,4},{4,3},{5,6},{6,5},{7,8},{8,7},{9,10},{10,... | collective-permute-start | bytes 589832 | tf_op jit(solution)/shard_map/ppermute | solution.py:351
  5.1 0.8 %collective-permute-start.3 = (bf16[6,128,128]{2,1,0:T(8,128)(2,1)}, bf16[6,128,128]{2,1,0:T(8,128)(2,1)}, u32[]{:S(2)}, u32[]{:S(2)}) collective-permute-start(bf16[6,128,128]{2,1,0:T(8,128)(2,1)} %get-tuple-element.24), channel_id=1, source_target_pairs={{0,15},{1,2},{2,1},{3,4},{4,3},{5,6},{6,5},{7,8},{8,7},{9,10},{10,... | collective-permute-start | bytes 589832 | tf_op jit(solution)/shard_map/ppermute | solution.py:351
  5.8 1.0 %collective-permute-start = (bf16[6,128,256]{2,1,0:T(8,128)(2,1)S(1)}, bf16[6,128,256]{2,1,0:T(8,128)(2,1)S(1)}, u32[]{:S(2)}, u32[]{:S(2)}) collective-permute-start(bf16[6,128,256]{2,1,0:T(8,128)(2,1)S(1)} %get-tuple-element.21), channel_id=1, source_target_pairs={{0,16},{1,17},{2,18},{3,19},{4,20},{5,21},{6,22},{7,23},{8,24},{9,... | collective-permute-start | bytes 1179656 | tf_op jit(solution)/shard_map/ppermute | solution.py:345
  6.9 1.0 %collective-permute-start.1 = (bf16[6,128,256]{2,1,0:T(8,128)(2,1)S(1)}, bf16[6,128,256]{2,1,0:T(8,128)(2,1)S(1)}, u32[]{:S(2)}, u32[]{:S(2)}) collective-permute-start(bf16[6,128,256]{2,1,0:T(8,128)(2,1)S(1)} %get-tuple-element.22), channel_id=1, source_target_pairs={{0,1},{1,0},{2,3},{3,2},{4,5},{5,4},{6,7},{7,6},{8,9},{9,8},{10,11... | collective-permute-start | bytes 1179656 | tf_op jit(solution)/shard_map/ppermute | solution.py:345
  7.9 1.0 %copy-done.3 = bf16[528,512]{1,0:T(8,128)(2,1)S(1)} copy-done((bf16[528,512]{1,0:T(8,128)(2,1)S(1)}, bf16[528,512]{1,0:T(8,128)(2,1)}, u32[]{:S(2)}) %copy-start.3) | copy-done | bytes 540696
  8.9 1.0 %copy-done.5 = bf16[512,512]{1,0:T(8,128)(2,1)S(1)} copy-done((bf16[512,512]{1,0:T(8,128)(2,1)S(1)}, bf16[512,512]{1,0:T(8,128)(2,1)}, u32[]{:S(2)}) %copy-start.5) | copy-done | bytes 524312
  10.0 1.0 %copy-done.11 = bf16[512,512]{1,0:T(8,128)(2,1)S(1)} copy-done((bf16[512,512]{1,0:T(8,128)(2,1)S(1)}, bf16[512,512]{1,0:T(8,128)(2,1)}, u32[]{:S(2)}) %copy-start.11) | copy-done | bytes 524312
  11.0 0.9 %noise_spectrum.1 = (f32[264,512]{1,0:T(8,128)S(1)}, f32[264,512]{1,0:T(8,128)S(1)}) custom-call(bf16[512,512]{1,0:T(8,128)(2,1)S(1)} %copy-done.11, bf16[528,512]{1,0:T(8,128)(2,1)S(1)} %copy-done.3, bf16[512,512]{1,0:T(8,128)(2,1)S(1)} %copy-done.5), custom_call_target="tpu_custom_call" | custom-call | flops 6710886400 | bytes 1048576 | tf_op jit(solution)/shard_map/noise_spectrum/pallas_call | solution.py:395
  11.9 0.1 constant_dynamic-slice_fusion.1
  12.0 11.9 %collective-permute-start.4 = (bf16[6,128,128]{2,1,0:T(8,128)(2,1)}, bf16[6,128,128]{2,1,0:T(8,128)(2,1)S(1)}, u32[]{:S(2)}, u32[]{:S(2)}) collective-permute-start(bf16[6,128,128]{2,1,0:T(8,128)(2,1)} %collective-permute-done.2.outer_first_ref), channel_id=1, source_target_pairs={{0,16},{1,17},{2,18},{3,19},{4,20},{5,21},{6,22},{7,23},{8,24},{9,... | collective-permute-start | bytes 589832 | tf_op jit(solution)/shard_map/ppermute | solution.py:345
  24.0 0.1 constant_dynamic-slice_fusion
  24.1 0.1 pad_maximum_fusion
  24.2 0.1 collective-permute-start.6
  24.3 2.7 %core_columns.1.after_ref.core_ref = f32[6,528,512]{2,1,0:T(8,128)S(1)} custom-call(bf16[6,256,256]{2,1,0:T(8,128)(2,1)S(1)} %copy-done.1, bf16[6,128,256]{2,1,0:T(8,128)(2,1)S(1)} %collective-permute-done.first_ref, bf16[6,128,256]{2,1,0:T(8,128)(2,1)S(1)} %collective-permute-done.1.second_ref, f32[512,128]{1,0:T(8,128)S(1)} %copy-done.2, ...), custom_call_target="tpu_custom_call" | custom-call | flops 134217728 | bytes 1048576 | tf_op jit(solution)/shard_map/core_columns/pallas_call | solution.py:423
  27.0 0.8 %collective-permute-done.4.first_ref = bf16[6,128,128]{2,1,0:T(8,128)(2,1)S(1)} collective-permute-done((bf16[6,128,128]{2,1,0:T(8,128)(2,1)}, bf16[6,128,128]{2,1,0:T(8,128)(2,1)S(1)}, u32[]{:S(2)}, u32[]{:S(2)}) %collective-permute-start.4) | collective-permute-done | bytes 196640 | tf_op jit(solution)/shard_map/ppermute | solution.py:345
  27.8 2.0 %collective-permute-done.5.second_ref = bf16[6,128,128]{2,1,0:T(8,128)(2,1)S(1)} collective-permute-done((bf16[6,128,128]{2,1,0:T(8,128)(2,1)}, bf16[6,128,128]{2,1,0:T(8,128)(2,1)S(1)}, u32[]{:S(2)}, u32[]{:S(2)}) %collective-permute-start.5) | collective-permute-done | bytes 196640 | tf_op jit(solution)/shard_map/ppermute | solution.py:345
  29.9 1.9 %outer_columns.1.after_ref.outer_ref = bf16[6,528,128]{2,1,0:T(8,128)(2,1)S(1)} custom-call(f32[6,528,512]{2,1,0:T(8,128)S(1)} %core_columns.1.after_ref.core_ref, bf16[6,128,128]{2,1,0:T(8,128)(2,1)} %collective-permute-done.2.outer_first_ref, bf16[6,128,128]{2,1,0:T(8,128)(2,1)} %collective-permute-done.3.outer_second_ref, ...), custom_call_target="tpu_custom_call" | custom-call | flops 53687091200 | bytes 1048576 | tf_op jit(solution)/shard_map/outer_columns/pallas_call | solution.py:431
  31.9 1.0 %inner_columns.1.inner_ref = bf16[6,528,128]{2,1,0:T(8,128)(2,1)S(1)} custom-call(bf16[6,528,128]{2,1,0:T(8,128)(2,1)S(1)} %outer_columns.1.after_ref.outer_ref, bf16[6,512,128]{2,1,0:T(8,128)(2,1)S(1)} %collective-permute-done.6.inner_ref, f32[512,128]{1,0:T(8,128)S(1)} %copy-done.2, f32[8,512]{1,0:T(8,128)S(1)} %copy-done.10, bf16[528,512]{1,0:T(8,128)(2,1)S(1)} %copy-done.4), custom_call_target="tpu_custom_call" | custom-call | flops 134217728 | bytes 1048576 | tf_op jit(solution)/shard_map/inner_columns/pallas_call | solution.py:434
  32.8 0.0 copy-done.7
  32.9 0.2 copy-done.8
  33.0 0.0 copy-done.9
  33.1 3.6 %tile_model.1 = (bf16[128,512]{1,0:T(8,128)(2,1)S(1)}, bf16[128,512]{1,0:T(8,128)(2,1)S(1)}, f32[256,512]{1,0:T(8,128)S(1)}) custom-call(f32[6,528,512]{2,1,0:T(8,128)S(1)} %core_columns.1.after_ref.core_ref, bf16[6,528,128]{2,1,0:T(8,128)(2,1)S(1)} %inner_columns.1.inner_ref, bf16[6,528,128]{2,1,0:T(8,128)(2,1)S(1)} %outer_columns.1.after_ref.outer_ref, ...), custom_call_target="tpu_custom_call" | custom-call | flops 2684354560 | bytes 1048576 | tf_op jit(solution)/shard_map/tile_model/pallas_call | solution.py:437
  36.7 3.0 %collective-permute-start.7 = (bf16[128,512]{1,0:T(8,128)(2,1)S(1)}, bf16[128,512]{1,0:T(8,128)(2,1)S(1)}, u32[]{:S(2)}, u32[]{:S(2)}) collective-permute-start(bf16[128,512]{1,0:T(8,128)(2,1)S(1)} %get-tuple-element.32), channel_id=1, source_target_pairs={{0,16},{1,17},{2,18},{3,19},{4,20},{5,21},{6,22},{7,23},{8,24},{9,... | collective-permute-start | bytes 393224 | tf_op jit(solution)/shard_map/ppermute | solution.py:345
  39.6 3.7 %collective-permute-done.7.first_ref = bf16[128,512]{1,0:T(8,128)(2,1)S(1)} collective-permute-done((bf16[128,512]{1,0:T(8,128)(2,1)S(1)}, bf16[128,512]{1,0:T(8,128)(2,1)S(1)}, u32[]{:S(2)}, u32[]{:S(2)}) %collective-permute-start.7) | collective-permute-done | bytes 131104 | tf_op jit(solution)/shard_map/ppermute | solution.py:345
  43.3 1.5 %collective-permute-done.8.second_ref = bf16[128,512]{1,0:T(8,128)(2,1)S(1)} collective-permute-done((bf16[128,512]{1,0:T(8,128)(2,1)S(1)}, bf16[128,512]{1,0:T(8,128)(2,1)S(1)}, u32[]{:S(2)}, u32[]{:S(2)}) %collective-permute-start.8) | collective-permute-done | bytes 131104 | tf_op jit(solution)/shard_map/ppermute | solution.py:345
  44.8 0.1 fold_rows.1
  44.9 0.2 collective-permute-start.9
  45.1 0.0 collective-permute-start.10
  45.1 5.7 %collective-permute-done.9.outer_ref = bf16[256,128]{1,0:T(8,128)(2,1)S(1)} collective-permute-done((bf16[256,128]{1,0:T(8,128)(2,1)S(1)}, bf16[256,128]{1,0:T(8,128)(2,1)S(1)}, u32[]{:S(2)}, u32[]{:S(2)}) %collective-permute-start.9) | collective-permute-done | bytes 65568 | tf_op jit(solution)/shard_map/ppermute | solution.py:351
  50.8 0.7 %fold_columns.1 = f32[256,256]{1,0:T(8,128)} custom-call(f32[256,256]{1,0:T(8,128)S(1)} %get-tuple-element.34.center_ref, bf16[256,128]{1,0:T(8,128)(2,1)S(1)} %collective-permute-done.9.outer_ref, bf16[256,128]{1,0:T(8,128)(2,1)S(1)} %collective-permute-done.10.inner_ref), custom_call_target="tpu_custom_call" | custom-call | bytes 1048576 | tf_op jit(solution)/shard_map/fold_columns/pallas_call | solution.py:465
  (25 shorter events, 0.1 us)
Async XLA Ops:
  0.0 1.1 %copy-start = (bf16[6,256,256]{2,1,0:T(8,128)(2,1)S(1)}, bf16[6,256,256]{2,1,0:T(8,128)(2,1)}, u32[]{:S(2)}) copy-start(bf16[6,256,256]{2,1,0:T(8,128)(2,1)} %core_ref.1) | copy-start | bytes 2359300
  2.0 10.0 %collective-permute-start.2 = (bf16[6,128,128]{2,1,0:T(8,128)(2,1)}, bf16[6,128,128]{2,1,0:T(8,128)(2,1)}, u32[]{:S(2)}, u32[]{:S(2)}) collective-permute-start(bf16[6,128,128]{2,1,0:T(8,128)(2,1)} %get-tuple-element.23), channel_id=1, source_target_pairs={{0,15},{1,2},{2,1},{3,4},{4,3},{5,6},{6,5},{7,8},{8,7},{9,10},{10,... | collective-permute-start | bytes 589832 | tf_op jit(solution)/shard_map/ppermute | solution.py:351
  5.1 18.9 %collective-permute-start.3 = (bf16[6,128,128]{2,1,0:T(8,128)(2,1)}, bf16[6,128,128]{2,1,0:T(8,128)(2,1)}, u32[]{:S(2)}, u32[]{:S(2)}) collective-permute-start(bf16[6,128,128]{2,1,0:T(8,128)(2,1)} %get-tuple-element.24), channel_id=1, source_target_pairs={{0,15},{1,2},{2,1},{3,4},{4,3},{5,6},{6,5},{7,8},{8,7},{9,10},{10,... | collective-permute-start | bytes 589832 | tf_op jit(solution)/shard_map/ppermute | solution.py:351
  5.8 18.2 %collective-permute-start = (bf16[6,128,256]{2,1,0:T(8,128)(2,1)S(1)}, bf16[6,128,256]{2,1,0:T(8,128)(2,1)S(1)}, u32[]{:S(2)}, u32[]{:S(2)}) collective-permute-start(bf16[6,128,256]{2,1,0:T(8,128)(2,1)S(1)} %get-tuple-element.21), channel_id=1, source_target_pairs={{0,16},{1,17},{2,18},{3,19},{4,20},{5,21},{6,22},{7,23},{8,24},{9,... | collective-permute-start | bytes 1179656 | tf_op jit(solution)/shard_map/ppermute | solution.py:345
  6.9 5.0 %copy-start.1 = (bf16[6,256,256]{2,1,0:T(8,128)(2,1)S(1)}, bf16[6,256,256]{2,1,0:T(8,128)(2,1)}, u32[]{:S(2)}) copy-start(bf16[6,256,256]{2,1,0:T(8,128)(2,1)} %core_ref.1) | copy-start | bytes 2359300
  6.9 17.1 %collective-permute-start.1 = (bf16[6,128,256]{2,1,0:T(8,128)(2,1)S(1)}, bf16[6,128,256]{2,1,0:T(8,128)(2,1)S(1)}, u32[]{:S(2)}, u32[]{:S(2)}) collective-permute-start(bf16[6,128,256]{2,1,0:T(8,128)(2,1)S(1)} %get-tuple-element.22), channel_id=1, source_target_pairs={{0,1},{1,0},{2,3},{3,2},{4,5},{5,4},{6,7},{7,6},{8,9},{9,8},{10,11... | collective-permute-start | bytes 1179656 | tf_op jit(solution)/shard_map/ppermute | solution.py:345
  7.9 1.0 %copy-start.3 = (bf16[528,512]{1,0:T(8,128)(2,1)S(1)}, bf16[528,512]{1,0:T(8,128)(2,1)}, u32[]{:S(2)}) copy-start(bf16[528,512]{1,0:T(8,128)(2,1)} %constant.37.clone.left_ref) | copy-start | bytes 1622020
  8.9 1.0 %copy-start.5 = (bf16[512,512]{1,0:T(8,128)(2,1)S(1)}, bf16[512,512]{1,0:T(8,128)(2,1)}, u32[]{:S(2)}) copy-start(bf16[512,512]{1,0:T(8,128)(2,1)} %constant.38.clone.right_ref) | copy-start | bytes 1572868
  10.0 1.0 %copy-start.11 = (bf16[512,512]{1,0:T(8,128)(2,1)S(1)}, bf16[512,512]{1,0:T(8,128)(2,1)}, u32[]{:S(2)}) copy-start(bf16[512,512]{1,0:T(8,128)(2,1)} %noise_ref.1) | copy-start | bytes 1572868
  11.9 12.4 %copy-start.2 = (f32[512,128]{1,0:T(8,128)S(1)}, f32[512,128]{1,0:T(8,128)}, u32[]{:S(2)}) copy-start(f32[512,128]{1,0:T(8,128)} %constant.42.clone.rows_ref) | copy-start | bytes 786436
  11.9 12.4 %copy-start.4 = (bf16[528,512]{1,0:T(8,128)(2,1)S(1)}, bf16[528,512]{1,0:T(8,128)(2,1)}, u32[]{:S(2)}) copy-start(bf16[528,512]{1,0:T(8,128)(2,1)} %constant.37.clone.left_ref) | copy-start | bytes 1622020
  11.9 12.4 %copy-start.6 = (bf16[512,512]{1,0:T(8,128)(2,1)S(1)}, bf16[512,512]{1,0:T(8,128)(2,1)}, u32[]{:S(2)}) copy-start(bf16[512,512]{1,0:T(8,128)(2,1)} %constant.38.clone.right_ref) | copy-start | bytes 1572868
  11.9 12.4 %copy-start.10 = (f32[8,512]{1,0:T(8,128)S(1)}, f32[8,512]{1,0:T(8,128)}, u32[]{:S(2)}) copy-start(f32[8,512]{1,0:T(8,128)} %constant.43.clone.cols_ref) | copy-start | bytes 49156
  12.0 15.8 %collective-permute-start.4 = (bf16[6,128,128]{2,1,0:T(8,128)(2,1)}, bf16[6,128,128]{2,1,0:T(8,128)(2,1)S(1)}, u32[]{:S(2)}, u32[]{:S(2)}) collective-permute-start(bf16[6,128,128]{2,1,0:T(8,128)(2,1)} %collective-permute-done.2.outer_first_ref), channel_id=1, source_target_pairs={{0,16},{1,17},{2,18},{3,19},{4,20},{5,21},{6,22},{7,23},{8,24},{9,... | collective-permute-start | bytes 589832 | tf_op jit(solution)/shard_map/ppermute | solution.py:345
  24.0 5.9 %collective-permute-start.5 = (bf16[6,128,128]{2,1,0:T(8,128)(2,1)}, bf16[6,128,128]{2,1,0:T(8,128)(2,1)S(1)}, u32[]{:S(2)}, u32[]{:S(2)}) collective-permute-start(bf16[6,128,128]{2,1,0:T(8,128)(2,1)} %collective-permute-done.3.outer_second_ref), channel_id=1, source_target_pairs={{0,1},{1,0},{2,3},{3,2},{4,5},{5,4},{6,7},{7,6},{8,9},{9,8},{10,11... | collective-permute-start | bytes 589832 | tf_op jit(solution)/shard_map/ppermute | solution.py:345
  24.2 7.7 %collective-permute-start.6 = (bf16[6,512,128]{2,1,0:T(8,128)(2,1)S(1)}, bf16[6,512,128]{2,1,0:T(8,128)(2,1)S(1)}, u32[]{:S(2)}, u32[]{:S(2)}) collective-permute-start(bf16[6,512,128]{2,1,0:T(8,128)(2,1)S(1)} %pad_maximum_fusion), channel_id=1, source_target_pairs={{0,1},{1,0},{2,3},{3,2},{4,5},{5,4},{6,7},{7,6},{8,9},{9,8},{10,11... | collective-permute-start | bytes 2359304 | tf_op jit(solution)/shard_map/ppermute | solution.py:351
  31.8 1.0 %copy-start.7 = (bf16[512,512]{1,0:T(8,128)(2,1)S(1)}, bf16[512,512]{1,0:T(8,128)(2,1)}, u32[]{:S(2)}) copy-start(bf16[512,512]{1,0:T(8,128)(2,1)} %constant.40.clone.band_columns_ref) | copy-start | bytes 1572868
  31.8 1.2 %copy-start.8 = (bf16[512,512]{1,0:T(8,128)(2,1)S(1)}, bf16[512,512]{1,0:T(8,128)(2,1)}, u32[]{:S(2)}) copy-start(bf16[512,512]{1,0:T(8,128)(2,1)} %constant.39.clone.inverse_right_ref) | copy-start | bytes 1572868
  31.9 1.2 %copy-start.9 = (bf16[272,384]{1,0:T(8,128)(2,1)S(1)}, bf16[272,384]{1,0:T(8,128)(2,1)}, u32[]{:S(2)}) copy-start(bf16[272,384]{1,0:T(8,128)(2,1)} %constant.41.clone.band_rows_ref) | copy-start | bytes 626692
  36.7 6.7 %collective-permute-start.7 = (bf16[128,512]{1,0:T(8,128)(2,1)S(1)}, bf16[128,512]{1,0:T(8,128)(2,1)S(1)}, u32[]{:S(2)}, u32[]{:S(2)}) collective-permute-start(bf16[128,512]{1,0:T(8,128)(2,1)S(1)} %get-tuple-element.32), channel_id=1, source_target_pairs={{0,16},{1,17},{2,18},{3,19},{4,20},{5,21},{6,22},{7,23},{8,24},{9,... | collective-permute-start | bytes 393224 | tf_op jit(solution)/shard_map/ppermute | solution.py:345
  39.6 5.2 %collective-permute-start.8 = (bf16[128,512]{1,0:T(8,128)(2,1)S(1)}, bf16[128,512]{1,0:T(8,128)(2,1)S(1)}, u32[]{:S(2)}, u32[]{:S(2)}) collective-permute-start(bf16[128,512]{1,0:T(8,128)(2,1)S(1)} %get-tuple-element.33), channel_id=1, source_target_pairs={{0,1},{1,0},{2,3},{3,2},{4,5},{5,4},{6,7},{7,6},{8,9},{9,8},{10,11... | collective-permute-start | bytes 393224 | tf_op jit(solution)/shard_map/ppermute | solution.py:345
  44.9 5.9 %collective-permute-start.9 = (bf16[256,128]{1,0:T(8,128)(2,1)S(1)}, bf16[256,128]{1,0:T(8,128)(2,1)S(1)}, u32[]{:S(2)}, u32[]{:S(2)}) collective-permute-start(bf16[256,128]{1,0:T(8,128)(2,1)S(1)} %get-tuple-element.35), channel_id=1, source_target_pairs={{0,15},{1,2},{2,1},{3,4},{4,3},{5,6},{6,5},{7,8},{8,7},{9,10},{10,... | collective-permute-start | bytes 196616 | tf_op jit(solution)/shard_map/ppermute | solution.py:351
  45.1 5.7 %collective-permute-start.10 = (bf16[256,128]{1,0:T(8,128)(2,1)S(1)}, bf16[256,128]{1,0:T(8,128)(2,1)S(1)}, u32[]{:S(2)}, u32[]{:S(2)}) collective-permute-start(bf16[256,128]{1,0:T(8,128)(2,1)S(1)} %get-tuple-element.36), channel_id=1, source_target_pairs={{0,1},{1,0},{2,3},{3,2},{4,5},{5,4},{6,7},{7,6},{8,9},{9,8},{10,11... | collective-permute-start | bytes 196616 | tf_op jit(solution)/shard_map/ppermute | solution.py:351

commit v8 on v7

--- a/solution.py
+++ b/solution.py
@@ -167,18 +167,23 @@
             strip[s] = maps_ref[s, rows, :]
 
 
-def core_kernel(half, core_ref, first_ref, second_ref, rows_ref, cols_ref, left_ref, right_ref, spectra_ref, tile):
+def core_kernel(
+    half, core_ref, first_ref, second_ref, outer_first_ref, outer_second_ref, rows_ref, cols_ref, left_ref, right_ref,
+    spectra_ref, outer_ref, tile,
+):
     margin = half // 2
     splits = core_ref.shape[0]
-    first, second, _, _ = sides(half)
-    has_second, _ = inside_sky()
+    first, second, outer, _ = sides(half)
+    has_second, has_outer = inside_sky()
     fill(tile, core_ref, rows_ref, cols_ref, 0, half, margin, margin, 0)
     fill(tile, first_ref, rows_ref, cols_ref, 0, margin, first, margin, 0)
     fill(tile, second_ref, rows_ref, cols_ref, 0, margin, second, margin, 0, has_second)
-
     for s in range(splits):
         halves = dot(left_ref[...], tile[s]).astype(BF16)
         spectra_ref[s] = dot(halves, right_ref[:half])
+    for source, place in ((outer_first_ref, first), (outer_second_ref, second)):
+        row = jnp.where(place == 0, margin, half)
+        fill(outer_ref, source, rows_ref, cols_ref, 0, margin, row, outer, 0, has_outer)
 
 
 def transform_pairs(tile, left_ref, halves_ref):
@@ -201,19 +206,16 @@
 
 
 def outer_kernel(
-    half, after_ref, outer_first_ref, outer_second_ref, first_ref, second_ref, rows_ref, cols_ref, left_ref,
-    halves_ref, tile,
+    half, after_ref, tile, first_ref, second_ref, rows_ref, cols_ref, left_ref, halves_ref, full
 ):
     del after_ref
     margin = half // 2
     first, second, outer, _ = sides(half)
     has_second, has_outer = inside_sky()
-    for source, place in ((outer_first_ref, first), (outer_second_ref, second)):
-        row = jnp.where(place == 0, margin, half)
-        fill(tile, source, rows_ref, cols_ref, 0, margin, row, outer, 0, has_outer)
-    fill(tile, first_ref, rows_ref, cols_ref, 0, margin, first, outer, 0, has_outer)
-    fill(tile, second_ref, rows_ref, cols_ref, 0, margin, second, outer, 0, has_outer * has_second)
-    transform_pairs(tile, left_ref, halves_ref)
+    full[:, margin : margin + half, :] = tile[:, margin : margin + half, :]
+    fill(full, first_ref, rows_ref, cols_ref, 0, margin, first, outer, 0, has_outer)
+    fill(full, second_ref, rows_ref, cols_ref, 0, margin, second, outer, 0, has_outer * has_second)
+    transform_pairs(full, left_ref, halves_ref)
 
 
 def main_kernel(
@@ -389,12 +391,13 @@
     outer_first = swap_columns(outer_first, 1)
     second = swap_rows(second, 1)
     first = swap_rows(first, 0)
-    outer_second = swap_columns(outer_second, 1)
-
     spectrum = jax.ShapeDtypeStruct((half + 8, length), F32)
     re, im = kernel_call(
         functools.partial(noise_kernel, half), "noise_spectrum", (spectrum, spectrum), 3, flops=50 * cube
     )(white_noise, constant["left"], constant["right"])
+
+    outer_second, outer_first = lax.optimization_barrier((outer_second, outer_first))
+    outer_second = swap_columns(outer_second, 1)
 
     first, second, _, _, re, im = lax.optimization_barrier((first, second, outer_first, outer_second, re, im))
     first_corner = swap_rows(outer_first, 0)
@@ -420,16 +423,19 @@
         )
 
     left, right = constant["left"], constant["right"]
-    core = kernel_call(
+    core, outer = kernel_call(
         functools.partial(core_kernel, half),
         "core_columns",
-        jax.ShapeDtypeStruct((splits, length + 16, length), F32),
-        7,
+        (
+            jax.ShapeDtypeStruct((splits, length + 16, length), F32),
+            jax.ShapeDtypeStruct((splits, length, margin), BF16),
+        ),
+        9,
         [pltpu.VMEM((splits, length, half), BF16)],
         flops=cube,
-    )(split_maps, first, second, rows, cols, left, right)
-    outer = columns(outer_kernel, "outer_columns", 8, 400000 * cube // 1000)(
-        core, outer_first, outer_second, first_corner, second_corner, rows, cols, left
+    )(split_maps, first, second, outer_first, outer_second, rows, cols, left, right)
+    outer = columns(outer_kernel, "outer_columns", 7, 400000 * cube // 1000)(
+        core, outer, first_corner, second_corner, rows, cols, left
     )
     inner = columns(inner_kernel, "inner_columns", 5, cube)(outer, inner, rows, cols, left)
 

time: 51.8 us -> 54.1 us (1.044)
  waiting for transfers between devices: 13.7 us -> 17.1 us
  Pallas kernels: 11.8 us -> 10.9 us
    ppermute x5, waiting for transfers between devices: 5.7 us -> 9.5 us  [swap_columns(): return lax.ppermute(values, 'ra', pairs)]
    pallas_call x2, Pallas kernels: 4.68 us -> 3.69 us  [the longest x1 2.91 us: shards(): kernel_call(functools.partial(core_kernel, half), 'core_columns', (jax.Sh...]
    ppermute x6, starting transfers between devices: 16.9 us -> 16 us  [swap_rows(): return lax.ppermute(values, ('dec', 'ra'), pairs)]
    ppermute x5, starting transfers between devices: 4.14 us -> 4.85 us  [swap_columns(): return lax.ppermute(values, 'ra', pairs)]
  transfers between devices with their start and end apart: 11 -> 11, of which waited for: 5 -> 7; matrix products, arithmetic and copies ran while one was open for 0% -> 0% of each run, Pallas kernels for 11% -> 8%
where the time goes in v8:
time: 54.1 us; the launch traced here: 53.9 us
  starting transfers between devices  20.9 us (39%)
  waiting for transfers between devices  17.1 us (32%)
  Pallas kernels  10.9 us (20%)
  local copies, waits for them, and re-layouts  4.7 us (9%)
    ppermute x6, starting transfers between devices, swap_rows(): return lax.ppermute(values, ('dec', 'ra'), pairs)  16 us
    ppermute x5, waiting for transfers between devices, swap_columns(): return lax.ppermute(values, 'ra', pairs)  9.5 us
    ppermute x6, waiting for transfers between devices, swap_rows(): return lax.ppermute(values, ('dec', 'ra'), pairs)  7.61 us
    ppermute x5, starting transfers between devices, swap_columns(): return lax.ppermute(values, 'ra', pairs)  4.85 us
    unnamed x24, local copies, waits for them, and re-layouts  4.55 us
    pallas_call x1, Pallas kernels, shards(): kernel_call(functools.partial(main_kernel, half, scale), 'tile_model', (s...  3.56 us
    pallas_call x1, Pallas kernels, shards(): kernel_call(functools.partial(core_kernel, half), 'core_columns', (jax.Sh...  2.91 us
  transfers between devices with their start and end apart: 11, of which 7 were waited for; matrix products, arithmetic and copies ran while one was open for 0% of the time, Pallas kernels for 8%

profile of v8, /device:TPU:196, one launch (start us, length us, event | category | flops | bytes accessed | tf_op | source)
XLA Modules:
  0.0 53.9 jit_solution(18222757202568105328)
XLA Ops:
  0.0 1.1 %copy-done = bf16[6,256,256]{2,1,0:T(8,128)(2,1)S(1)} copy-done((bf16[6,256,256]{2,1,0:T(8,128)(2,1)S(1)}, bf16[6,256,256]{2,1,0:T(8,128)(2,1)}, u32[]{:S(2)}) %copy-start) | copy-done | bytes 786456
  1.1 0.9 %cut.1 = (bf16[6,128,128]{2,1,0:T(8,128)(2,1)S(1)}, bf16[6,128,128]{2,1,0:T(8,128)(2,1)}, bf16[6,128,256]{2,1,0:T(8,128)(2,1)}, bf16[6,128,256]{2,1,0:T(8,128)(2,1)S(1)}) custom-call(bf16[6,256,256]{2,1,0:T(8,128)(2,1)S(1)} %copy-done), custom_call_target="tpu_custom_call" | custom-call | bytes 1048576 | tf_op jit(solution)/shard_map/cut/pallas_call | solution.py:388
  2.1 3.1 %collective-permute-start.2 = (bf16[6,128,128]{2,1,0:T(8,128)(2,1)S(1)}, bf16[6,128,128]{2,1,0:T(8,128)(2,1)S(1)}, u32[]{:S(2)}, u32[]{:S(2)}) collective-permute-start(bf16[6,128,128]{2,1,0:T(8,128)(2,1)S(1)} %get-tuple-element.28), channel_id=1, source_target_pairs={{0,15},{1,2},{2,1},{3,4},{4,3},{5,6},{6,5},{7,8},{8,7},{9,10},{10,... | collective-permute-start | bytes 589832 | tf_op jit(solution)/shard_map/ppermute | solution.py:353
  5.2 1.0 %collective-permute-start = (bf16[6,128,256]{2,1,0:T(8,128)(2,1)}, bf16[6,128,256]{2,1,0:T(8,128)(2,1)S(1)}, u32[]{:S(2)}, u32[]{:S(2)}) collective-permute-start(bf16[6,128,256]{2,1,0:T(8,128)(2,1)} %get-tuple-element.25), channel_id=1, source_target_pairs={{0,16},{1,17},{2,18},{3,19},{4,20},{5,21},{6,22},{7,23},{8,24},{9,... | collective-permute-start | bytes 1179656 | tf_op jit(solution)/shard_map/ppermute | solution.py:347
  6.2 1.0 %collective-permute-start.1 = (bf16[6,128,256]{2,1,0:T(8,128)(2,1)S(1)}, bf16[6,128,256]{2,1,0:T(8,128)(2,1)S(1)}, u32[]{:S(2)}, u32[]{:S(2)}) collective-permute-start(bf16[6,128,256]{2,1,0:T(8,128)(2,1)S(1)} %get-tuple-element.26), channel_id=1, source_target_pairs={{0,1},{1,0},{2,3},{3,2},{4,5},{5,4},{6,7},{7,6},{8,9},{9,8},{10,11... | collective-permute-start | bytes 1179656 | tf_op jit(solution)/shard_map/ppermute | solution.py:347
  7.2 3.9 %collective-permute-done.2.outer_first_ref = bf16[6,128,128]{2,1,0:T(8,128)(2,1)S(1)} collective-permute-done((bf16[6,128,128]{2,1,0:T(8,128)(2,1)S(1)}, bf16[6,128,128]{2,1,0:T(8,128)(2,1)S(1)}, u32[]{:S(2)}, u32[]{:S(2)}) %collective-permute-start.2) | collective-permute-done | bytes 196640 | tf_op jit(solution)/shard_map/ppermute | solution.py:353
  11.1 1.2 %collective-permute-start.3 = (bf16[6,128,128]{2,1,0:T(8,128)(2,1)}, bf16[6,128,128]{2,1,0:T(8,128)(2,1)S(1)}, u32[]{:S(2)}, u32[]{:S(2)}) collective-permute-start(bf16[6,128,128]{2,1,0:T(8,128)(2,1)} %get-tuple-element.30), channel_id=1, source_target_pairs={{0,15},{1,2},{2,1},{3,4},{4,3},{5,6},{6,5},{7,8},{8,7},{9,10},{10,... | collective-permute-start | bytes 589832 | tf_op jit(solution)/shard_map/ppermute | solution.py:353
  12.4 1.0 %copy-done.3 = bf16[528,512]{1,0:T(8,128)(2,1)S(1)} copy-done((bf16[528,512]{1,0:T(8,128)(2,1)S(1)}, bf16[528,512]{1,0:T(8,128)(2,1)}, u32[]{:S(2)}) %copy-start.3) | copy-done | bytes 540696
  13.4 1.0 %copy-done.5 = bf16[512,512]{1,0:T(8,128)(2,1)S(1)} copy-done((bf16[512,512]{1,0:T(8,128)(2,1)S(1)}, bf16[512,512]{1,0:T(8,128)(2,1)}, u32[]{:S(2)}) %copy-start.5) | copy-done | bytes 524312
  14.5 1.0 %copy-done.11 = bf16[512,512]{1,0:T(8,128)(2,1)S(1)} copy-done((bf16[512,512]{1,0:T(8,128)(2,1)S(1)}, bf16[512,512]{1,0:T(8,128)(2,1)}, u32[]{:S(2)}) %copy-start.11) | copy-done | bytes 524312
  15.5 0.9 %noise_spectrum.1 = (f32[264,512]{1,0:T(8,128)S(1)}, f32[264,512]{1,0:T(8,128)S(1)}) custom-call(bf16[512,512]{1,0:T(8,128)(2,1)S(1)} %copy-done.11, bf16[528,512]{1,0:T(8,128)(2,1)S(1)} %copy-done.3, bf16[512,512]{1,0:T(8,128)(2,1)S(1)} %copy-done.5), custom_call_target="tpu_custom_call" | custom-call | flops 6710886400 | bytes 1048576 | tf_op jit(solution)/shard_map/noise_spectrum/pallas_call | solution.py:395
  16.4 0.1 constant_dynamic-slice_fusion.1
  16.5 10.6 %collective-permute-start.4 = (bf16[6,128,128]{2,1,0:T(8,128)(2,1)S(1)}, bf16[6,128,128]{2,1,0:T(8,128)(2,1)S(1)}, u32[]{:S(2)}, u32[]{:S(2)}) collective-permute-start(bf16[6,128,128]{2,1,0:T(8,128)(2,1)S(1)} %collective-permute-done.2.outer_first_ref), channel_id=1, source_target_pairs={{0,16},{1,17},{2,18},{3,19},{4,20},{5,21},{6,22},{7,23},{8,24},{9,... | collective-permute-start | bytes 589832 | tf_op jit(solution)/shard_map/ppermute | solution.py:347
  27.1 0.1 collective-permute-start.5
  27.2 0.1 constant_dynamic-slice_fusion
  27.4 0.1 collective-permute-start.6
  27.5 2.9 %core_columns.1 = (f32[6,528,512]{2,1,0:T(8,128)S(1)}, bf16[6,512,128]{2,1,0:T(8,128)(2,1)S(1)}) custom-call(bf16[6,256,256]{2,1,0:T(8,128)(2,1)S(1)} %copy-done.1, bf16[6,128,256]{2,1,0:T(8,128)(2,1)S(1)} %collective-permute-done.first_ref, bf16[6,128,256]{2,1,0:T(8,128)(2,1)S(1)} %collective-permute-done.1.second_ref, ...), custom_call_target="tpu_custom_call" | custom-call | flops 134217728 | bytes 1048576 | tf_op jit(solution)/shard_map/core_columns/pallas_call | solution.py:426
  30.4 0.3 collective-permute-done.4.first_ref
  30.8 2.1 %collective-permute-done.5.second_ref = bf16[6,128,128]{2,1,0:T(8,128)(2,1)S(1)} collective-permute-done((bf16[6,128,128]{2,1,0:T(8,128)(2,1)S(1)}, bf16[6,128,128]{2,1,0:T(8,128)(2,1)S(1)}, u32[]{:S(2)}, u32[]{:S(2)}) %collective-permute-start.5) | collective-permute-done | bytes 196640 | tf_op jit(solution)/shard_map/ppermute | solution.py:347
  32.9 0.8 %outer_columns.1.after_ref.outer_ref = bf16[6,528,128]{2,1,0:T(8,128)(2,1)S(1)} custom-call(f32[6,528,512]{2,1,0:T(8,128)S(1)} %get-tuple-element.35.after_ref.core_ref, bf16[6,512,128]{2,1,0:T(8,128)(2,1)S(1)} %get-tuple-element.36.tile, bf16[6,128,128]{2,1,0:T(8,128)(2,1)S(1)} %collective-permute-done.4.first_ref, ...), custom_call_target="tpu_custom_call" | custom-call | flops 53687091200 | bytes 1048576 | tf_op jit(solution)/shard_map/outer_columns/pallas_call | solution.py:437
  33.7 1.0 %inner_columns.1.inner_ref = bf16[6,528,128]{2,1,0:T(8,128)(2,1)S(1)} custom-call(bf16[6,528,128]{2,1,0:T(8,128)(2,1)S(1)} %outer_columns.1.after_ref.outer_ref, bf16[6,512,128]{2,1,0:T(8,128)(2,1)S(1)} %collective-permute-done.6.inner_ref, f32[512,128]{1,0:T(8,128)S(1)} %copy-done.2, f32[8,512]{1,0:T(8,128)S(1)} %copy-done.10, bf16[528,512]{1,0:T(8,128)(2,1)S(1)} %copy-done.4), custom_call_target="tpu_custom_call" | custom-call | flops 134217728 | bytes 1048576 | tf_op jit(solution)/shard_map/inner_columns/pallas_call | solution.py:440
  34.7 0.2 copy-done.8
  34.9 3.6 %tile_model.1 = (bf16[128,512]{1,0:T(8,128)(2,1)S(1)}, bf16[128,512]{1,0:T(8,128)(2,1)S(1)}, f32[256,512]{1,0:T(8,128)S(1)}) custom-call(f32[6,528,512]{2,1,0:T(8,128)S(1)} %get-tuple-element.35.after_ref.core_ref, bf16[6,528,128]{2,1,0:T(8,128)(2,1)S(1)} %inner_columns.1.inner_ref, bf16[6,528,128]{2,1,0:T(8,128)(2,1)S(1)} %outer_columns.1.after_ref.outer_ref, ...), custom_call_target="tpu_custom_call" | custom-call | flops 2684354560 | bytes 1048576 | tf_op jit(solution)/shard_map/tile_model/pallas_call | solution.py:443
  38.5 3.4 %collective-permute-start.7 = (bf16[128,512]{1,0:T(8,128)(2,1)S(1)}, bf16[128,512]{1,0:T(8,128)(2,1)S(1)}, u32[]{:S(2)}, u32[]{:S(2)}) collective-permute-start(bf16[128,512]{1,0:T(8,128)(2,1)S(1)} %get-tuple-element.40), channel_id=1, source_target_pairs={{0,16},{1,17},{2,18},{3,19},{4,20},{5,21},{6,22},{7,23},{8,24},{9,... | collective-permute-start | bytes 393224 | tf_op jit(solution)/shard_map/ppermute | solution.py:347
  41.9 3.7 %collective-permute-done.7.first_ref = bf16[128,512]{1,0:T(8,128)(2,1)S(1)} collective-permute-done((bf16[128,512]{1,0:T(8,128)(2,1)S(1)}, bf16[128,512]{1,0:T(8,128)(2,1)S(1)}, u32[]{:S(2)}, u32[]{:S(2)}) %collective-permute-start.7) | collective-permute-done | bytes 131104 | tf_op jit(solution)/shard_map/ppermute | solution.py:347
  45.5 1.5 %collective-permute-done.8.second_ref = bf16[128,512]{1,0:T(8,128)(2,1)S(1)} collective-permute-done((bf16[128,512]{1,0:T(8,128)(2,1)S(1)}, bf16[128,512]{1,0:T(8,128)(2,1)S(1)}, u32[]{:S(2)}, u32[]{:S(2)}) %collective-permute-start.8) | collective-permute-done | bytes 131104 | tf_op jit(solution)/shard_map/ppermute | solution.py:347
  47.0 0.1 fold_rows.1
  47.1 0.1 collective-permute-start.10
  47.2 0.3 collective-permute-start.9
  47.6 0.9 %collective-permute-done.10.inner_ref = bf16[256,128]{1,0:T(8,128)(2,1)S(1)} collective-permute-done((bf16[256,128]{1,0:T(8,128)(2,1)S(1)}, bf16[256,128]{1,0:T(8,128)(2,1)S(1)}, u32[]{:S(2)}, u32[]{:S(2)}) %collective-permute-start.10) | collective-permute-done | bytes 65568 | tf_op jit(solution)/shard_map/ppermute | solution.py:353
  48.5 4.6 %collective-permute-done.9.outer_ref = bf16[256,128]{1,0:T(8,128)(2,1)S(1)} collective-permute-done((bf16[256,128]{1,0:T(8,128)(2,1)S(1)}, bf16[256,128]{1,0:T(8,128)(2,1)S(1)}, u32[]{:S(2)}, u32[]{:S(2)}) %collective-permute-start.9) | collective-permute-done | bytes 65568 | tf_op jit(solution)/shard_map/ppermute | solution.py:353
  53.1 0.7 %fold_columns.1 = f32[256,256]{1,0:T(8,128)} custom-call(f32[256,256]{1,0:T(8,128)S(1)} %get-tuple-element.42.center_ref, bf16[256,128]{1,0:T(8,128)(2,1)S(1)} %collective-permute-done.9.outer_ref, bf16[256,128]{1,0:T(8,128)(2,1)S(1)} %collective-permute-done.10.inner_ref), custom_call_target="tpu_custom_call" | custom-call | bytes 1048576 | tf_op jit(solution)/shard_map/fold_columns/pallas_call | solution.py:471
  (25 shorter events, 0.2 us)
Async XLA Ops:
  0.0 1.1 %copy-start = (bf16[6,256,256]{2,1,0:T(8,128)(2,1)S(1)}, bf16[6,256,256]{2,1,0:T(8,128)(2,1)}, u32[]{:S(2)}) copy-start(bf16[6,256,256]{2,1,0:T(8,128)(2,1)} %core_ref.1) | copy-start | bytes 2359300
  2.1 9.0 %collective-permute-start.2 = (bf16[6,128,128]{2,1,0:T(8,128)(2,1)S(1)}, bf16[6,128,128]{2,1,0:T(8,128)(2,1)S(1)}, u32[]{:S(2)}, u32[]{:S(2)}) collective-permute-start(bf16[6,128,128]{2,1,0:T(8,128)(2,1)S(1)} %get-tuple-element.28), channel_id=1, source_target_pairs={{0,15},{1,2},{2,1},{3,4},{4,3},{5,6},{6,5},{7,8},{8,7},{9,10},{10,... | collective-permute-start | bytes 589832 | tf_op jit(solution)/shard_map/ppermute | solution.py:353
  5.2 22.0 %collective-permute-start = (bf16[6,128,256]{2,1,0:T(8,128)(2,1)}, bf16[6,128,256]{2,1,0:T(8,128)(2,1)S(1)}, u32[]{:S(2)}, u32[]{:S(2)}) collective-permute-start(bf16[6,128,256]{2,1,0:T(8,128)(2,1)} %get-tuple-element.25), channel_id=1, source_target_pairs={{0,16},{1,17},{2,18},{3,19},{4,20},{5,21},{6,22},{7,23},{8,24},{9,... | collective-permute-start | bytes 1179656 | tf_op jit(solution)/shard_map/ppermute | solution.py:347
  6.2 20.9 %collective-permute-start.1 = (bf16[6,128,256]{2,1,0:T(8,128)(2,1)S(1)}, bf16[6,128,256]{2,1,0:T(8,128)(2,1)S(1)}, u32[]{:S(2)}, u32[]{:S(2)}) collective-permute-start(bf16[6,128,256]{2,1,0:T(8,128)(2,1)S(1)} %get-tuple-element.26), channel_id=1, source_target_pairs={{0,1},{1,0},{2,3},{3,2},{4,5},{5,4},{6,7},{7,6},{8,9},{9,8},{10,11... | collective-permute-start | bytes 1179656 | tf_op jit(solution)/shard_map/ppermute | solution.py:347
  11.1 5.3 %copy-start.1 = (bf16[6,256,256]{2,1,0:T(8,128)(2,1)S(1)}, bf16[6,256,256]{2,1,0:T(8,128)(2,1)}, u32[]{:S(2)}) copy-start(bf16[6,256,256]{2,1,0:T(8,128)(2,1)} %core_ref.1) | copy-start | bytes 2359300
  11.1 16.0 %collective-permute-start.3 = (bf16[6,128,128]{2,1,0:T(8,128)(2,1)}, bf16[6,128,128]{2,1,0:T(8,128)(2,1)S(1)}, u32[]{:S(2)}, u32[]{:S(2)}) collective-permute-start(bf16[6,128,128]{2,1,0:T(8,128)(2,1)} %get-tuple-element.30), channel_id=1, source_target_pairs={{0,15},{1,2},{2,1},{3,4},{4,3},{5,6},{6,5},{7,8},{8,7},{9,10},{10,... | collective-permute-start | bytes 589832 | tf_op jit(solution)/shard_map/ppermute | solution.py:353
  12.4 1.0 %copy-start.3 = (bf16[528,512]{1,0:T(8,128)(2,1)S(1)}, bf16[528,512]{1,0:T(8,128)(2,1)}, u32[]{:S(2)}) copy-start(bf16[528,512]{1,0:T(8,128)(2,1)} %constant.37.clone.left_ref) | copy-start | bytes 1622020
  13.4 1.0 %copy-start.5 = (bf16[512,512]{1,0:T(8,128)(2,1)S(1)}, bf16[512,512]{1,0:T(8,128)(2,1)}, u32[]{:S(2)}) copy-start(bf16[512,512]{1,0:T(8,128)(2,1)} %constant.38.clone.right_ref) | copy-start | bytes 1572868
  14.5 1.0 %copy-start.11 = (bf16[512,512]{1,0:T(8,128)(2,1)S(1)}, bf16[512,512]{1,0:T(8,128)(2,1)}, u32[]{:S(2)}) copy-start(bf16[512,512]{1,0:T(8,128)(2,1)} %noise_ref.1) | copy-start | bytes 1572868
  16.4 11.1 %copy-start.2 = (f32[512,128]{1,0:T(8,128)S(1)}, f32[512,128]{1,0:T(8,128)}, u32[]{:S(2)}) copy-start(f32[512,128]{1,0:T(8,128)} %constant.42.clone.rows_ref) | copy-start | bytes 786436
  16.4 11.1 %copy-start.4 = (bf16[528,512]{1,0:T(8,128)(2,1)S(1)}, bf16[528,512]{1,0:T(8,128)(2,1)}, u32[]{:S(2)}) copy-start(bf16[528,512]{1,0:T(8,128)(2,1)} %constant.37.clone.left_ref) | copy-start | bytes 1622020
  16.4 11.1 %copy-start.6 = (bf16[512,512]{1,0:T(8,128)(2,1)S(1)}, bf16[512,512]{1,0:T(8,128)(2,1)}, u32[]{:S(2)}) copy-start(bf16[512,512]{1,0:T(8,128)(2,1)} %constant.38.clone.right_ref) | copy-start | bytes 1572868
  16.4 11.1 %copy-start.10 = (f32[8,512]{1,0:T(8,128)S(1)}, f32[8,512]{1,0:T(8,128)}, u32[]{:S(2)}) copy-start(f32[8,512]{1,0:T(8,128)} %constant.43.clone.cols_ref) | copy-start | bytes 49156
  16.5 14.2 %collective-permute-start.4 = (bf16[6,128,128]{2,1,0:T(8,128)(2,1)S(1)}, bf16[6,128,128]{2,1,0:T(8,128)(2,1)S(1)}, u32[]{:S(2)}, u32[]{:S(2)}) collective-permute-start(bf16[6,128,128]{2,1,0:T(8,128)(2,1)S(1)} %collective-permute-done.2.outer_first_ref), channel_id=1, source_target_pairs={{0,16},{1,17},{2,18},{3,19},{4,20},{5,21},{6,22},{7,23},{8,24},{9,... | collective-permute-start | bytes 589832 | tf_op jit(solution)/shard_map/ppermute | solution.py:347
  27.1 5.8 %collective-permute-start.5 = (bf16[6,128,128]{2,1,0:T(8,128)(2,1)S(1)}, bf16[6,128,128]{2,1,0:T(8,128)(2,1)S(1)}, u32[]{:S(2)}, u32[]{:S(2)}) collective-permute-start(bf16[6,128,128]{2,1,0:T(8,128)(2,1)S(1)} %collective-permute-done.3.outer_second_ref), channel_id=1, source_target_pairs={{0,1},{1,0},{2,3},{3,2},{4,5},{5,4},{6,7},{7,6},{8,9},{9,8},{10,11... | collective-permute-start | bytes 589832 | tf_op jit(solution)/shard_map/ppermute | solution.py:347
  27.4 6.3 %collective-permute-start.6 = (bf16[6,512,128]{2,1,0:T(8,128)(2,1)S(1)}, bf16[6,512,128]{2,1,0:T(8,128)(2,1)S(1)}, u32[]{:S(2)}, u32[]{:S(2)}) collective-permute-start(bf16[6,512,128]{2,1,0:T(8,128)(2,1)S(1)} %pad_maximum_fusion), channel_id=1, source_target_pairs={{0,1},{1,0},{2,3},{3,2},{4,5},{5,4},{6,7},{7,6},{8,9},{9,8},{10,11... | collective-permute-start | bytes 2359304 | tf_op jit(solution)/shard_map/ppermute | solution.py:353
  33.7 1.0 %copy-start.7 = (bf16[512,512]{1,0:T(8,128)(2,1)S(1)}, bf16[512,512]{1,0:T(8,128)(2,1)}, u32[]{:S(2)}) copy-start(bf16[512,512]{1,0:T(8,128)(2,1)} %constant.39.clone.inverse_right_ref) | copy-start | bytes 1572868
  33.7 1.2 %copy-start.8 = (bf16[512,512]{1,0:T(8,128)(2,1)S(1)}, bf16[512,512]{1,0:T(8,128)(2,1)}, u32[]{:S(2)}) copy-start(bf16[512,512]{1,0:T(8,128)(2,1)} %constant.40.clone.band_columns_ref) | copy-start | bytes 1572868
  33.7 1.2 %copy-start.9 = (bf16[272,384]{1,0:T(8,128)(2,1)S(1)}, bf16[272,384]{1,0:T(8,128)(2,1)}, u32[]{:S(2)}) copy-start(bf16[272,384]{1,0:T(8,128)(2,1)} %constant.41.clone.band_rows_ref) | copy-start | bytes 626692
  38.5 7.1 %collective-permute-start.7 = (bf16[128,512]{1,0:T(8,128)(2,1)S(1)}, bf16[128,512]{1,0:T(8,128)(2,1)S(1)}, u32[]{:S(2)}, u32[]{:S(2)}) collective-permute-start(bf16[128,512]{1,0:T(8,128)(2,1)S(1)} %get-tuple-element.40), channel_id=1, source_target_pairs={{0,16},{1,17},{2,18},{3,19},{4,20},{5,21},{6,22},{7,23},{8,24},{9,... | collective-permute-start | bytes 393224 | tf_op jit(solution)/shard_map/ppermute | solution.py:347
  41.8 5.2 %collective-permute-start.8 = (bf16[128,512]{1,0:T(8,128)(2,1)S(1)}, bf16[128,512]{1,0:T(8,128)(2,1)S(1)}, u32[]{:S(2)}, u32[]{:S(2)}) collective-permute-start(bf16[128,512]{1,0:T(8,128)(2,1)S(1)} %get-tuple-element.41), channel_id=1, source_target_pairs={{0,1},{1,0},{2,3},{3,2},{4,5},{5,4},{6,7},{7,6},{8,9},{9,8},{10,11... | collective-permute-start | bytes 393224 | tf_op jit(solution)/shard_map/ppermute | solution.py:347
  47.1 1.3 %collective-permute-start.10 = (bf16[256,128]{1,0:T(8,128)(2,1)S(1)}, bf16[256,128]{1,0:T(8,128)(2,1)S(1)}, u32[]{:S(2)}, u32[]{:S(2)}) collective-permute-start(bf16[256,128]{1,0:T(8,128)(2,1)S(1)} %get-tuple-element.44), channel_id=1, source_target_pairs={{0,1},{1,0},{2,3},{3,2},{4,5},{5,4},{6,7},{7,6},{8,9},{9,8},{10,11... | collective-permute-start | bytes 196616 | tf_op jit(solution)/shard_map/ppermute | solution.py:353
  47.2 5.9 %collective-permute-start.9 = (bf16[256,128]{1,0:T(8,128)(2,1)S(1)}, bf16[256,128]{1,0:T(8,128)(2,1)S(1)}, u32[]{:S(2)}, u32[]{:S(2)}) collective-permute-start(bf16[256,128]{1,0:T(8,128)(2,1)S(1)} %get-tuple-element.43), channel_id=1, source_target_pairs={{0,15},{1,2},{2,1},{3,4},{4,3},{5,6},{6,5},{7,8},{8,7},{9,10},{10,... | collective-permute-start | bytes 196616 | tf_op jit(solution)/shard_map/ppermute | solution.py:353

commit v9 on v8

--- a/solution.py
+++ b/solution.py
@@ -140,7 +140,7 @@
 
 def sides(half):
     far = half + half // 2
-    first = jnp.where(lax.axis_index("dec") % 2 == 0, far, 0)
+    first = jnp.where(lax.axis_index("dec") % 2 == 0, 0, far)
     outer = jnp.where(lax.axis_index("ra") % 2 == 0, 0, far)
     return first, far - first, outer, far - outer
 
@@ -174,10 +174,10 @@
     margin = half // 2
     splits = core_ref.shape[0]
     first, second, outer, _ = sides(half)
-    has_second, has_outer = inside_sky()
+    has_first, has_outer = inside_sky()
     fill(tile, core_ref, rows_ref, cols_ref, 0, half, margin, margin, 0)
-    fill(tile, first_ref, rows_ref, cols_ref, 0, margin, first, margin, 0)
-    fill(tile, second_ref, rows_ref, cols_ref, 0, margin, second, margin, 0, has_second)
+    fill(tile, first_ref, rows_ref, cols_ref, 0, margin, first, margin, 0, has_first)
+    fill(tile, second_ref, rows_ref, cols_ref, 0, margin, second, margin, 0)
     for s in range(splits):
         halves = dot(left_ref[...], tile[s]).astype(BF16)
         spectra_ref[s] = dot(halves, right_ref[:half])
@@ -198,10 +198,10 @@
     del after_ref
     margin = half // 2
     first, second, _, inner = sides(half)
-    has_second, _ = inside_sky()
-    fill(tile, inner_ref, rows_ref, cols_ref, 0, margin, first, inner, 0)
+    has_first, _ = inside_sky()
+    fill(tile, inner_ref, rows_ref, cols_ref, 0, margin, first, inner, 0, has_first)
     fill(tile, inner_ref, rows_ref, cols_ref, margin, half, margin, inner, 0)
-    fill(tile, inner_ref, rows_ref, cols_ref, margin + half, margin, second, inner, 0, has_second)
+    fill(tile, inner_ref, rows_ref, cols_ref, margin + half, margin, second, inner, 0)
     transform_pairs(tile, left_ref, halves_ref)
 
 
@@ -211,10 +211,10 @@
     del after_ref
     margin = half // 2
     first, second, outer, _ = sides(half)
-    has_second, has_outer = inside_sky()
+    has_first, has_outer = inside_sky()
     full[:, margin : margin + half, :] = tile[:, margin : margin + half, :]
-    fill(full, first_ref, rows_ref, cols_ref, 0, margin, first, outer, 0, has_outer)
-    fill(full, second_ref, rows_ref, cols_ref, 0, margin, second, outer, 0, has_outer * has_second)
+    fill(full, first_ref, rows_ref, cols_ref, 0, margin, first, outer, 0, has_outer * has_first)
+    fill(full, second_ref, rows_ref, cols_ref, 0, margin, second, outer, 0, has_outer)
     transform_pairs(full, left_ref, halves_ref)
 
 
@@ -318,8 +318,8 @@
 def fold_rows_kernel(half, inside_ref, first_ref, second_ref, center_ref, outer_ref, inner_ref, total):
     margin = half // 2
     first, second, outer, inner = sides(half)
-    has_second, _ = inside_sky()
-    for source, place, exists in ((first_ref, first, 1.0), (second_ref, second, has_second)):
+    has_first, _ = inside_sky()
+    for source, place, exists in ((first_ref, first, has_first), (second_ref, second, 1.0)):
         rows = pl.ds(pl.multiple_of(jnp.where(place == 0, 0, margin), margin), margin)
         total[rows, :] = inside_ref[rows, :] + source[...].astype(F32) * exists
     center_ref[...] = total[:, margin : margin + half]
@@ -389,19 +389,17 @@
         functools.partial(cut_kernel, half), "cut", (piece, piece, strip, strip), 1, vmem=8
     )(split_maps)
     outer_first = swap_columns(outer_first, 1)
-    second = swap_rows(second, 1)
-    first = swap_rows(first, 0)
+    second = swap_rows(second, 0)
+    first = swap_rows(first, 1)
+    outer_second = swap_columns(outer_second, 1)
     spectrum = jax.ShapeDtypeStruct((half + 8, length), F32)
     re, im = kernel_call(
         functools.partial(noise_kernel, half), "noise_spectrum", (spectrum, spectrum), 3, flops=50 * cube
     )(white_noise, constant["left"], constant["right"])
 
-    outer_second, outer_first = lax.optimization_barrier((outer_second, outer_first))
-    outer_second = swap_columns(outer_second, 1)
-
     first, second, _, _, re, im = lax.optimization_barrier((first, second, outer_first, outer_second, re, im))
-    first_corner = swap_rows(outer_first, 0)
-    second_corner = swap_rows(outer_second, 1)
+    first_corner = swap_rows(outer_first, 1)
+    second_corner = swap_rows(outer_second, 0)
     inner = swap_columns(
         jnp.concatenate(
             [
@@ -458,8 +456,8 @@
         constant["inverse_right"],
     )
 
-    second = swap_rows(second, 1)
-    first = swap_rows(first, 0)
+    second = swap_rows(second, 0)
+    first = swap_rows(first, 1)
     column = jax.ShapeDtypeStruct((half, margin), BF16)
     block = jax.ShapeDtypeStruct((half, half), F32)
     center, outer, inner = kernel_call(

time: 54.1 us -> 53.4 us (0.987)
  the two profiles are of different devices: /device:TPU:196 before, /device:TPU:228 now
where the time goes in v9:
time: 53.4 us; the launch traced here: 53.1 us
  waiting for transfers between devices  28.4 us (53%)
  Pallas kernels  10.9 us (20%)
  starting transfers between devices  8.76 us (16%)
  local copies, waits for them, and re-layouts  4.7 us (9%)
    ppermute x5, waiting for transfers between devices, swap_columns(): return lax.ppermute(values, 'ra', pairs)  20.1 us
    ppermute x6, waiting for transfers between devices, swap_rows(): return lax.ppermute(values, ('dec', 'ra'), pairs)  8.27 us
    ppermute x5, starting transfers between devices, swap_columns(): return lax.ppermute(values, 'ra', pairs)  6.56 us
    unnamed x24, local copies, waits for them, and re-layouts  4.54 us
    pallas_call x1, Pallas kernels, shards(): kernel_call(functools.partial(main_kernel, half, scale), 'tile_model', (s...  3.56 us
    pallas_call x1, Pallas kernels, shards(): kernel_call(functools.partial(core_kernel, half), 'core_columns', (jax.Sh...  2.91 us
    ppermute x6, starting transfers between devices, swap_rows(): return lax.ppermute(values, ('dec', 'ra'), pairs)  2.2 us
  transfers between devices with their start and end apart: 11, of which 6 were waited for; matrix products, arithmetic and copies ran while one was open for 0% of the time, Pallas kernels for 9%

profile of v9, /device:TPU:228, one launch (start us, length us, event | category | flops | bytes accessed | tf_op | source)
XLA Modules:
  0.0 53.1 jit_solution(5497624369526023918)
XLA Ops:
  0.0 1.1 %copy-done = bf16[6,256,256]{2,1,0:T(8,128)(2,1)S(1)} copy-done((bf16[6,256,256]{2,1,0:T(8,128)(2,1)S(1)}, bf16[6,256,256]{2,1,0:T(8,128)(2,1)}, u32[]{:S(2)}) %copy-start) | copy-done | bytes 786456
  1.1 1.0 %cut.1 = (bf16[6,128,128]{2,1,0:T(8,128)(2,1)}, bf16[6,128,128]{2,1,0:T(8,128)(2,1)}, bf16[6,128,256]{2,1,0:T(8,128)(2,1)}, bf16[6,128,256]{2,1,0:T(8,128)(2,1)S(1)}) custom-call(bf16[6,256,256]{2,1,0:T(8,128)(2,1)S(1)} %copy-done), custom_call_target="tpu_custom_call" | custom-call | bytes 1048576 | tf_op jit(solution)/shard_map/cut/pallas_call | solution.py:388
  2.1 3.1 %collective-permute-start.2 = (bf16[6,128,128]{2,1,0:T(8,128)(2,1)}, bf16[6,128,128]{2,1,0:T(8,128)(2,1)S(1)}, u32[]{:S(2)}, u32[]{:S(2)}) collective-permute-start(bf16[6,128,128]{2,1,0:T(8,128)(2,1)} %get-tuple-element.25), channel_id=1, source_target_pairs={{0,15},{1,2},{2,1},{3,4},{4,3},{5,6},{6,5},{7,8},{8,7},{9,10},{10,... | collective-permute-start | bytes 589832 | tf_op jit(solution)/shard_map/ppermute | solution.py:353
  5.2 0.8 %collective-permute-start.3 = (bf16[6,128,128]{2,1,0:T(8,128)(2,1)}, bf16[6,128,128]{2,1,0:T(8,128)(2,1)S(1)}, u32[]{:S(2)}, u32[]{:S(2)}) collective-permute-start(bf16[6,128,128]{2,1,0:T(8,128)(2,1)} %get-tuple-element.26), channel_id=1, source_target_pairs={{0,15},{1,2},{2,1},{3,4},{4,3},{5,6},{6,5},{7,8},{8,7},{9,10},{10,... | collective-permute-start | bytes 589832 | tf_op jit(solution)/shard_map/ppermute | solution.py:353
  6.0 2.0 %collective-permute-start.1 = (bf16[6,128,256]{2,1,0:T(8,128)(2,1)S(1)}, bf16[6,128,256]{2,1,0:T(8,128)(2,1)S(1)}, u32[]{:S(2)}, u32[]{:S(2)}) collective-permute-start(bf16[6,128,256]{2,1,0:T(8,128)(2,1)S(1)} %get-tuple-element.24), channel_id=1, source_target_pairs={{0,16},{1,17},{2,18},{3,19},{4,20},{5,21},{6,22},{7,23},{8,24},{9,... | collective-permute-start | bytes 1179656 | tf_op jit(solution)/shard_map/ppermute | solution.py:347
  8.0 1.0 %copy-done.3 = bf16[528,512]{1,0:T(8,128)(2,1)S(1)} copy-done((bf16[528,512]{1,0:T(8,128)(2,1)S(1)}, bf16[528,512]{1,0:T(8,128)(2,1)}, u32[]{:S(2)}) %copy-start.3) | copy-done | bytes 540696
  9.0 1.0 %copy-done.5 = bf16[512,512]{1,0:T(8,128)(2,1)S(1)} copy-done((bf16[512,512]{1,0:T(8,128)(2,1)S(1)}, bf16[512,512]{1,0:T(8,128)(2,1)}, u32[]{:S(2)}) %copy-start.5) | copy-done | bytes 524312
  10.1 1.0 %copy-done.11 = bf16[512,512]{1,0:T(8,128)(2,1)S(1)} copy-done((bf16[512,512]{1,0:T(8,128)(2,1)S(1)}, bf16[512,512]{1,0:T(8,128)(2,1)}, u32[]{:S(2)}) %copy-start.11) | copy-done | bytes 524312
  11.1 0.9 %noise_spectrum.1 = (f32[264,512]{1,0:T(8,128)S(1)}, f32[264,512]{1,0:T(8,128)S(1)}) custom-call(bf16[512,512]{1,0:T(8,128)(2,1)S(1)} %copy-done.11, bf16[528,512]{1,0:T(8,128)(2,1)S(1)} %copy-done.3, bf16[512,512]{1,0:T(8,128)(2,1)S(1)} %copy-done.5), custom_call_target="tpu_custom_call" | custom-call | flops 6710886400 | bytes 1048576 | tf_op jit(solution)/shard_map/noise_spectrum/pallas_call | solution.py:396
  12.1 0.1 constant_dynamic-slice_fusion.1
  12.2 10.9 %collective-permute-done.2.outer_first_ref = bf16[6,128,128]{2,1,0:T(8,128)(2,1)S(1)} collective-permute-done((bf16[6,128,128]{2,1,0:T(8,128)(2,1)}, bf16[6,128,128]{2,1,0:T(8,128)(2,1)S(1)}, u32[]{:S(2)}, u32[]{:S(2)}) %collective-permute-start.2) | collective-permute-done | bytes 196640 | tf_op jit(solution)/shard_map/ppermute | solution.py:353
  23.1 5.1 %collective-permute-done.3.outer_second_ref = bf16[6,128,128]{2,1,0:T(8,128)(2,1)S(1)} collective-permute-done((bf16[6,128,128]{2,1,0:T(8,128)(2,1)}, bf16[6,128,128]{2,1,0:T(8,128)(2,1)S(1)}, u32[]{:S(2)}, u32[]{:S(2)}) %collective-permute-start.3) | collective-permute-done | bytes 196640 | tf_op jit(solution)/shard_map/ppermute | solution.py:353
  28.2 0.1 constant_dynamic-slice_fusion
  28.3 0.1 pad_maximum_fusion
  28.4 0.1 collective-permute-start.6
  28.5 2.9 %core_columns.1 = (f32[6,528,512]{2,1,0:T(8,128)S(1)}, bf16[6,512,128]{2,1,0:T(8,128)(2,1)S(1)}) custom-call(bf16[6,256,256]{2,1,0:T(8,128)(2,1)S(1)} %copy-done.1, bf16[6,128,256]{2,1,0:T(8,128)(2,1)S(1)} %collective-permute-done.first_ref, bf16[6,128,256]{2,1,0:T(8,128)(2,1)S(1)} %collective-permute-done.1.second_ref, ...), custom_call_target="tpu_custom_call" | custom-call | flops 134217728 | bytes 1048576 | tf_op jit(solution)/shard_map/core_columns/pallas_call | solution.py:424
  31.5 2.4 %collective-permute-done.5.second_ref = bf16[6,128,128]{2,1,0:T(8,128)(2,1)S(1)} collective-permute-done((bf16[6,128,128]{2,1,0:T(8,128)(2,1)S(1)}, bf16[6,128,128]{2,1,0:T(8,128)(2,1)S(1)}, u32[]{:S(2)}, u32[]{:S(2)}) %collective-permute-start.5) | collective-permute-done | bytes 196640 | tf_op jit(solution)/shard_map/ppermute | solution.py:347
  33.9 0.8 %outer_columns.1.after_ref.outer_ref = bf16[6,528,128]{2,1,0:T(8,128)(2,1)S(1)} custom-call(f32[6,528,512]{2,1,0:T(8,128)S(1)} %get-tuple-element.31.after_ref.core_ref, bf16[6,512,128]{2,1,0:T(8,128)(2,1)S(1)} %get-tuple-element.32.tile, bf16[6,128,128]{2,1,0:T(8,128)(2,1)S(1)} %collective-permute-done.4.first_ref, ...), custom_call_target="tpu_custom_call" | custom-call | flops 53687091200 | bytes 1048576 | tf_op jit(solution)/shard_map/outer_columns/pallas_call | solution.py:435
  34.7 1.0 %inner_columns.1.inner_ref = bf16[6,528,128]{2,1,0:T(8,128)(2,1)S(1)} custom-call(bf16[6,528,128]{2,1,0:T(8,128)(2,1)S(1)} %outer_columns.1.after_ref.outer_ref, bf16[6,512,128]{2,1,0:T(8,128)(2,1)S(1)} %collective-permute-done.6.inner_ref, f32[512,128]{1,0:T(8,128)S(1)} %copy-done.2, f32[8,512]{1,0:T(8,128)S(1)} %copy-done.10, bf16[528,512]{1,0:T(8,128)(2,1)S(1)} %copy-done.4), custom_call_target="tpu_custom_call" | custom-call | flops 134217728 | bytes 1048576 | tf_op jit(solution)/shard_map/inner_columns/pallas_call | solution.py:438
  35.7 0.0 copy-done.7
  35.7 0.2 copy-done.8
  35.9 0.0 copy-done.9
  35.9 3.6 %tile_model.1 = (bf16[128,512]{1,0:T(8,128)(2,1)S(1)}, bf16[128,512]{1,0:T(8,128)(2,1)S(1)}, f32[256,512]{1,0:T(8,128)S(1)}) custom-call(f32[6,528,512]{2,1,0:T(8,128)S(1)} %get-tuple-element.31.after_ref.core_ref, bf16[6,528,128]{2,1,0:T(8,128)(2,1)S(1)} %inner_columns.1.inner_ref, bf16[6,528,128]{2,1,0:T(8,128)(2,1)S(1)} %outer_columns.1.after_ref.outer_ref, ...), custom_call_target="tpu_custom_call" | custom-call | flops 2684354560 | bytes 1048576 | tf_op jit(solution)/shard_map/tile_model/pallas_call | solution.py:441
  39.5 0.1 collective-permute-start.7
  39.6 0.1 collective-permute-start.8
  39.7 1.2 %collective-permute-done.7.first_ref = bf16[128,512]{1,0:T(8,128)(2,1)S(1)} collective-permute-done((bf16[128,512]{1,0:T(8,128)(2,1)S(1)}, bf16[128,512]{1,0:T(8,128)(2,1)S(1)}, u32[]{:S(2)}, u32[]{:S(2)}) %collective-permute-start.7) | collective-permute-done | bytes 131104 | tf_op jit(solution)/shard_map/ppermute | solution.py:347
  40.9 4.6 %collective-permute-done.8.second_ref = bf16[128,512]{1,0:T(8,128)(2,1)S(1)} collective-permute-done((bf16[128,512]{1,0:T(8,128)(2,1)S(1)}, bf16[128,512]{1,0:T(8,128)(2,1)S(1)}, u32[]{:S(2)}, u32[]{:S(2)}) %collective-permute-start.8) | collective-permute-done | bytes 131104 | tf_op jit(solution)/shard_map/ppermute | solution.py:347
  45.5 0.1 fold_rows.1
  45.7 0.1 collective-permute-start.10
  45.8 2.5 %collective-permute-start.9 = (bf16[256,128]{1,0:T(8,128)(2,1)S(1)}, bf16[256,128]{1,0:T(8,128)(2,1)S(1)}, u32[]{:S(2)}, u32[]{:S(2)}) collective-permute-start(bf16[256,128]{1,0:T(8,128)(2,1)S(1)} %get-tuple-element.39), channel_id=1, source_target_pairs={{0,15},{1,2},{2,1},{3,4},{4,3},{5,6},{6,5},{7,8},{8,7},{9,10},{10,... | collective-permute-start | bytes 196616 | tf_op jit(solution)/shard_map/ppermute | solution.py:353
  48.3 4.1 %collective-permute-done.9.outer_ref = bf16[256,128]{1,0:T(8,128)(2,1)S(1)} collective-permute-done((bf16[256,128]{1,0:T(8,128)(2,1)S(1)}, bf16[256,128]{1,0:T(8,128)(2,1)S(1)}, u32[]{:S(2)}, u32[]{:S(2)}) %collective-permute-start.9) | collective-permute-done | bytes 65568 | tf_op jit(solution)/shard_map/ppermute | solution.py:353
  52.3 0.7 %fold_columns.1 = f32[256,256]{1,0:T(8,128)} custom-call(f32[256,256]{1,0:T(8,128)S(1)} %get-tuple-element.38.center_ref, bf16[256,128]{1,0:T(8,128)(2,1)S(1)} %collective-permute-done.9.outer_ref, bf16[256,128]{1,0:T(8,128)(2,1)S(1)} %collective-permute-done.10.inner_ref), custom_call_target="tpu_custom_call" | custom-call | bytes 1048576 | tf_op jit(solution)/shard_map/fold_columns/pallas_call | solution.py:469
  (25 shorter events, 0.1 us)
Async XLA Ops:
  0.0 1.1 %copy-start = (bf16[6,256,256]{2,1,0:T(8,128)(2,1)S(1)}, bf16[6,256,256]{2,1,0:T(8,128)(2,1)}, u32[]{:S(2)}) copy-start(bf16[6,256,256]{2,1,0:T(8,128)(2,1)} %core_ref.1) | copy-start | bytes 2359300
  2.1 21.0 %collective-permute-start.2 = (bf16[6,128,128]{2,1,0:T(8,128)(2,1)}, bf16[6,128,128]{2,1,0:T(8,128)(2,1)S(1)}, u32[]{:S(2)}, u32[]{:S(2)}) collective-permute-start(bf16[6,128,128]{2,1,0:T(8,128)(2,1)} %get-tuple-element.25), channel_id=1, source_target_pairs={{0,15},{1,2},{2,1},{3,4},{4,3},{5,6},{6,5},{7,8},{8,7},{9,10},{10,... | collective-permute-start | bytes 589832 | tf_op jit(solution)/shard_map/ppermute | solution.py:353
  5.2 23.0 %collective-permute-start.3 = (bf16[6,128,128]{2,1,0:T(8,128)(2,1)}, bf16[6,128,128]{2,1,0:T(8,128)(2,1)S(1)}, u32[]{:S(2)}, u32[]{:S(2)}) collective-permute-start(bf16[6,128,128]{2,1,0:T(8,128)(2,1)} %get-tuple-element.26), channel_id=1, source_target_pairs={{0,15},{1,2},{2,1},{3,4},{4,3},{5,6},{6,5},{7,8},{8,7},{9,10},{10,... | collective-permute-start | bytes 589832 | tf_op jit(solution)/shard_map/ppermute | solution.py:353
  6.0 22.3 %collective-permute-start = (bf16[6,128,256]{2,1,0:T(8,128)(2,1)}, bf16[6,128,256]{2,1,0:T(8,128)(2,1)S(1)}, u32[]{:S(2)}, u32[]{:S(2)}) collective-permute-start(bf16[6,128,256]{2,1,0:T(8,128)(2,1)} %get-tuple-element.23), channel_id=1, source_target_pairs={{0,1},{1,0},{2,3},{3,2},{4,5},{5,4},{6,7},{7,6},{8,9},{9,8},{10,11... | collective-permute-start | bytes 1179656 | tf_op jit(solution)/shard_map/ppermute | solution.py:347
  6.0 6.0 %copy-start.1 = (bf16[6,256,256]{2,1,0:T(8,128)(2,1)S(1)}, bf16[6,256,256]{2,1,0:T(8,128)(2,1)}, u32[]{:S(2)}) copy-start(bf16[6,256,256]{2,1,0:T(8,128)(2,1)} %core_ref.1) | copy-start | bytes 2359300
  6.0 22.3 %collective-permute-start.1 = (bf16[6,128,256]{2,1,0:T(8,128)(2,1)S(1)}, bf16[6,128,256]{2,1,0:T(8,128)(2,1)S(1)}, u32[]{:S(2)}, u32[]{:S(2)}) collective-permute-start(bf16[6,128,256]{2,1,0:T(8,128)(2,1)S(1)} %get-tuple-element.24), channel_id=1, source_target_pairs={{0,16},{1,17},{2,18},{3,19},{4,20},{5,21},{6,22},{7,23},{8,24},{9,... | collective-permute-start | bytes 1179656 | tf_op jit(solution)/shard_map/ppermute | solution.py:347
  8.0 1.0 %copy-start.3 = (bf16[528,512]{1,0:T(8,128)(2,1)S(1)}, bf16[528,512]{1,0:T(8,128)(2,1)}, u32[]{:S(2)}) copy-start(bf16[528,512]{1,0:T(8,128)(2,1)} %constant.37.clone.left_ref) | copy-start | bytes 1622020
  9.0 1.0 %copy-start.5 = (bf16[512,512]{1,0:T(8,128)(2,1)S(1)}, bf16[512,512]{1,0:T(8,128)(2,1)}, u32[]{:S(2)}) copy-start(bf16[512,512]{1,0:T(8,128)(2,1)} %constant.38.clone.right_ref) | copy-start | bytes 1572868
  10.1 1.0 %copy-start.11 = (bf16[512,512]{1,0:T(8,128)(2,1)S(1)}, bf16[512,512]{1,0:T(8,128)(2,1)}, u32[]{:S(2)}) copy-start(bf16[512,512]{1,0:T(8,128)(2,1)} %noise_ref.1) | copy-start | bytes 1572868
  12.0 16.5 %copy-start.2 = (f32[512,128]{1,0:T(8,128)S(1)}, f32[512,128]{1,0:T(8,128)}, u32[]{:S(2)}) copy-start(f32[512,128]{1,0:T(8,128)} %constant.42.clone.rows_ref) | copy-start | bytes 786436
  12.0 16.5 %copy-start.4 = (bf16[528,512]{1,0:T(8,128)(2,1)S(1)}, bf16[528,512]{1,0:T(8,128)(2,1)}, u32[]{:S(2)}) copy-start(bf16[528,512]{1,0:T(8,128)(2,1)} %constant.37.clone.left_ref) | copy-start | bytes 1622020
  12.0 16.5 %copy-start.6 = (bf16[512,512]{1,0:T(8,128)(2,1)S(1)}, bf16[512,512]{1,0:T(8,128)(2,1)}, u32[]{:S(2)}) copy-start(bf16[512,512]{1,0:T(8,128)(2,1)} %constant.38.clone.right_ref) | copy-start | bytes 1572868
  12.1 16.5 %copy-start.10 = (f32[8,512]{1,0:T(8,128)S(1)}, f32[8,512]{1,0:T(8,128)}, u32[]{:S(2)}) copy-start(f32[8,512]{1,0:T(8,128)} %constant.43.clone.cols_ref) | copy-start | bytes 49156
  23.1 8.4 %collective-permute-start.4 = (bf16[6,128,128]{2,1,0:T(8,128)(2,1)S(1)}, bf16[6,128,128]{2,1,0:T(8,128)(2,1)S(1)}, u32[]{:S(2)}, u32[]{:S(2)}) collective-permute-start(bf16[6,128,128]{2,1,0:T(8,128)(2,1)S(1)} %collective-permute-done.2.outer_first_ref), channel_id=1, source_target_pairs={{0,1},{1,0},{2,3},{3,2},{4,5},{5,4},{6,7},{7,6},{8,9},{9,8},{10,11... | collective-permute-start | bytes 589832 | tf_op jit(solution)/shard_map/ppermute | solution.py:347
  28.2 5.7 %collective-permute-start.5 = (bf16[6,128,128]{2,1,0:T(8,128)(2,1)S(1)}, bf16[6,128,128]{2,1,0:T(8,128)(2,1)S(1)}, u32[]{:S(2)}, u32[]{:S(2)}) collective-permute-start(bf16[6,128,128]{2,1,0:T(8,128)(2,1)S(1)} %collective-permute-done.3.outer_second_ref), channel_id=1, source_target_pairs={{0,16},{1,17},{2,18},{3,19},{4,20},{5,21},{6,22},{7,23},{8,24},{9,... | collective-permute-start | bytes 589832 | tf_op jit(solution)/shard_map/ppermute | solution.py:347
  28.4 6.3 %collective-permute-start.6 = (bf16[6,512,128]{2,1,0:T(8,128)(2,1)S(1)}, bf16[6,512,128]{2,1,0:T(8,128)(2,1)S(1)}, u32[]{:S(2)}, u32[]{:S(2)}) collective-permute-start(bf16[6,512,128]{2,1,0:T(8,128)(2,1)S(1)} %pad_maximum_fusion), channel_id=1, source_target_pairs={{0,1},{1,0},{2,3},{3,2},{4,5},{5,4},{6,7},{7,6},{8,9},{9,8},{10,11... | collective-permute-start | bytes 2359304 | tf_op jit(solution)/shard_map/ppermute | solution.py:353
  34.7 1.0 %copy-start.7 = (bf16[512,512]{1,0:T(8,128)(2,1)S(1)}, bf16[512,512]{1,0:T(8,128)(2,1)}, u32[]{:S(2)}) copy-start(bf16[512,512]{1,0:T(8,128)(2,1)} %constant.39.clone.inverse_right_ref) | copy-start | bytes 1572868
  34.7 1.2 %copy-start.8 = (bf16[512,512]{1,0:T(8,128)(2,1)S(1)}, bf16[512,512]{1,0:T(8,128)(2,1)}, u32[]{:S(2)}) copy-start(bf16[512,512]{1,0:T(8,128)(2,1)} %constant.40.clone.band_columns_ref) | copy-start | bytes 1572868
  34.7 1.2 %copy-start.9 = (bf16[272,384]{1,0:T(8,128)(2,1)S(1)}, bf16[272,384]{1,0:T(8,128)(2,1)}, u32[]{:S(2)}) copy-start(bf16[272,384]{1,0:T(8,128)(2,1)} %constant.41.clone.band_rows_ref) | copy-start | bytes 626692
  39.5 1.4 %collective-permute-start.7 = (bf16[128,512]{1,0:T(8,128)(2,1)S(1)}, bf16[128,512]{1,0:T(8,128)(2,1)S(1)}, u32[]{:S(2)}, u32[]{:S(2)}) collective-permute-start(bf16[128,512]{1,0:T(8,128)(2,1)S(1)} %get-tuple-element.36), channel_id=1, source_target_pairs={{0,1},{1,0},{2,3},{3,2},{4,5},{5,4},{6,7},{7,6},{8,9},{9,8},{10,11... | collective-permute-start | bytes 393224 | tf_op jit(solution)/shard_map/ppermute | solution.py:347
  39.6 5.9 %collective-permute-start.8 = (bf16[128,512]{1,0:T(8,128)(2,1)S(1)}, bf16[128,512]{1,0:T(8,128)(2,1)S(1)}, u32[]{:S(2)}, u32[]{:S(2)}) collective-permute-start(bf16[128,512]{1,0:T(8,128)(2,1)S(1)} %get-tuple-element.37), channel_id=1, source_target_pairs={{0,16},{1,17},{2,18},{3,19},{4,20},{5,21},{6,22},{7,23},{8,24},{9,... | collective-permute-start | bytes 393224 | tf_op jit(solution)/shard_map/ppermute | solution.py:347
  45.7 2.6 %collective-permute-start.10 = (bf16[256,128]{1,0:T(8,128)(2,1)S(1)}, bf16[256,128]{1,0:T(8,128)(2,1)S(1)}, u32[]{:S(2)}, u32[]{:S(2)}) collective-permute-start(bf16[256,128]{1,0:T(8,128)(2,1)S(1)} %get-tuple-element.40), channel_id=1, source_target_pairs={{0,1},{1,0},{2,3},{3,2},{4,5},{5,4},{6,7},{7,6},{8,9},{9,8},{10,11... | collective-permute-start | bytes 196616 | tf_op jit(solution)/shard_map/ppermute | solution.py:353
  45.8 6.6 %collective-permute-start.9 = (bf16[256,128]{1,0:T(8,128)(2,1)S(1)}, bf16[256,128]{1,0:T(8,128)(2,1)S(1)}, u32[]{:S(2)}, u32[]{:S(2)}) collective-permute-start(bf16[256,128]{1,0:T(8,128)(2,1)S(1)} %get-tuple-element.39), channel_id=1, source_target_pairs={{0,15},{1,2},{2,1},{3,4},{4,3},{5,6},{6,5},{7,8},{8,7},{9,10},{10,... | collective-permute-start | bytes 196616 | tf_op jit(solution)/shard_map/ppermute | solution.py:353

commit v10 on v9

--- a/solution.py
+++ b/solution.py
@@ -117,7 +117,9 @@
 
 
 def fill(tile, source, rows_ref, cols_ref, source_row, height, row, col, tile_col, exists=None):
-    splits, width = source.shape[0], source.shape[2]
+    sources = source if isinstance(source, tuple) else (source,)
+    planes = [(ref, s) for ref in sources for s in range(ref.shape[0])]
+    splits, width = len(planes), sources[0].shape[2]
     step = 32
     pc = cols_ref[:1, pl.ds(aligned(col, 128), width)]
     if exists is not None:
@@ -126,7 +128,7 @@
     def strip(number, carry):
         start = pl.multiple_of(source_row + number * step, step)
         target = pl.multiple_of(row + number * step, step)
-        members = [source[s, pl.ds(start, step), :].astype(F32) for s in range(splits)]
+        members = [ref[s, pl.ds(start, step), :].astype(F32) for ref, s in planes]
         mean = functools.reduce(lambda a, b: a + b, members) * (1.0 / splits)
         weights = jnp.concatenate([rows_ref[pl.ds(target, step), :]] * (width // 128), axis=1) * pc
         for s in range(splits):
@@ -154,21 +156,26 @@
     return flags
 
 
-def cut_kernel(half, maps_ref, outer_first_ref, outer_second_ref, first_ref, second_ref):
+def cut_kernel(half, maps_ref, outer_first_ref, outer_second_ref, near_ref, far_ref, second_ref):
     margin = half // 2
     first, second, outer, _ = sides(half)
     columns = pl.ds(pl.multiple_of(jnp.where(outer == 0, 0, margin), margin), margin)
-    for piece, strip, place in (
-        (outer_first_ref, first_ref, first), (outer_second_ref, second_ref, second)
-    ):
+    splits, direct = maps_ref.shape[0], near_ref.shape[0]
+    for piece, place in ((outer_first_ref, first), (outer_second_ref, second)):
         rows = pl.ds(pl.multiple_of(jnp.where(place == 0, 0, margin), margin), margin)
-        for s in range(maps_ref.shape[0]):
+        for s in range(splits):
             piece[s] = maps_ref[s, rows, columns]
-            strip[s] = maps_ref[s, rows, :]
+            if piece is outer_second_ref:
+                second_ref[s] = maps_ref[s, rows, :]
+            elif s < direct:
+                near_ref[s] = maps_ref[s, rows, :]
+            else:
+                far_ref[s - direct] = maps_ref[s, rows, :]
 
 
 def core_kernel(
-    half, core_ref, first_ref, second_ref, outer_first_ref, outer_second_ref, rows_ref, cols_ref, left_ref, right_ref,
+    half, core_ref, near_ref, far_ref, second_ref, outer_first_ref, outer_second_ref,
+    rows_ref, cols_ref, left_ref, right_ref,
     spectra_ref, outer_ref, tile,
 ):
     margin = half // 2
@@ -176,11 +183,16 @@
     first, second, outer, _ = sides(half)
     has_first, has_outer = inside_sky()
     fill(tile, core_ref, rows_ref, cols_ref, 0, half, margin, margin, 0)
-    fill(tile, first_ref, rows_ref, cols_ref, 0, margin, first, margin, 0, has_first)
+    fill(tile, (near_ref, far_ref), rows_ref, cols_ref, 0, margin, first, margin, 0, has_first)
     fill(tile, second_ref, rows_ref, cols_ref, 0, margin, second, margin, 0)
-    for s in range(splits):
-        halves = dot(left_ref[...], tile[s]).astype(BF16)
-        spectra_ref[s] = dot(halves, right_ref[:half])
+
+    def transform(number, carry):
+        for s in (2 * number, 2 * number + 1):
+            halves = dot(left_ref[...], tile[s]).astype(BF16)
+            spectra_ref[s] = dot(halves, right_ref[:half])
+        return carry
+
+    lax.fori_loop(0, splits // 2, transform, 0)
     for source, place in ((outer_first_ref, first), (outer_second_ref, second)):
         row = jnp.where(place == 0, margin, half)
         fill(outer_ref, source, rows_ref, cols_ref, 0, margin, row, outer, 0, has_outer)
@@ -336,14 +348,29 @@
         out_ref[:, columns] = center_ref[:, columns] + source[...].astype(F32) * exists
 
 
-def swap_rows(values, offset):
+def partners(offset, side=False):
     rows, columns = lax.axis_size("dec"), lax.axis_size("ra")
     pairs = []
     for i in range(rows):
         partner = i + 1 if i % 2 == offset else i - 1
         for j in range(columns):
-            target = partner * columns + j if 0 <= partner < rows else i * columns + (j ^ 1)
-            pairs.append((i * columns + j, target))
+            target = (partner, j) if 0 <= partner < rows else (i, j ^ 1)
+            if side and i in (rows // 2 - 1, rows // 2):
+                target = (partner, j ^ 2)
+            pairs.append((i * columns + j, target[0] * columns + target[1]))
+    return pairs
+
+
+def swap_rows(values, offset, side=False):
+    return lax.ppermute(values, ("dec", "ra"), partners(offset, side))
+
+
+def swap_beside(values):
+    rows, columns = lax.axis_size("dec"), lax.axis_size("ra")
+    pairs = []
+    for i in range(rows):
+        flip = 2 if i in (rows // 2 - 1, rows // 2) else 1
+        pairs += [(i * columns + j, i * columns + (j ^ flip)) for j in range(columns)]
     return lax.ppermute(values, ("dec", "ra"), pairs)
 
 
@@ -385,26 +412,34 @@
 
     piece = jax.ShapeDtypeStruct((splits, margin, margin), BF16)
     strip = jax.ShapeDtypeStruct((splits, margin, half), BF16)
-    outer_first, outer_second, first, second = kernel_call(
-        functools.partial(cut_kernel, half), "cut", (piece, piece, strip, strip), 1, vmem=8
+    share = jax.ShapeDtypeStruct((splits // 2, margin, half), BF16)
+    outer_first, outer_second, near, far, second = kernel_call(
+        functools.partial(cut_kernel, half), "cut", (piece, piece, share, share, strip), 1, vmem=8
     )(split_maps)
     outer_first = swap_columns(outer_first, 1)
     second = swap_rows(second, 0)
-    first = swap_rows(first, 1)
+    row = lax.axis_index("dec")
+    middle = lax.axis_size("dec") // 2
+    beside = swap_beside(far)
+    near = swap_rows(near, 1)
+    far = swap_rows(jnp.where(jnp.logical_or(row == middle - 1, row == middle), beside, far), 1, side=True)
     outer_second = swap_columns(outer_second, 1)
+
     spectrum = jax.ShapeDtypeStruct((half + 8, length), F32)
     re, im = kernel_call(
         functools.partial(noise_kernel, half), "noise_spectrum", (spectrum, spectrum), 3, flops=50 * cube
     )(white_noise, constant["left"], constant["right"])
 
-    first, second, _, _, re, im = lax.optimization_barrier((first, second, outer_first, outer_second, re, im))
+    near, far, second, _, _, re, im = lax.optimization_barrier(
+        (near, far, second, outer_first, outer_second, re, im)
+    )
     first_corner = swap_rows(outer_first, 1)
     second_corner = swap_rows(outer_second, 0)
     inner = swap_columns(
         jnp.concatenate(
             [
                 lax.dynamic_slice_in_dim(block, (1 - odd_col) * margin, margin, axis=2)
-                for block in (first, split_maps, second)
+                for block in (jnp.concatenate([near, far], axis=0), split_maps, second)
             ],
             axis=1,
         ),
@@ -428,10 +463,10 @@
             jax.ShapeDtypeStruct((splits, length + 16, length), F32),
             jax.ShapeDtypeStruct((splits, length, margin), BF16),
         ),
-        9,
+        10,
         [pltpu.VMEM((splits, length, half), BF16)],
         flops=cube,
-    )(split_maps, first, second, outer_first, outer_second, rows, cols, left, right)
+    )(split_maps, near, far, second, outer_first, outer_second, rows, cols, left, right)
     outer = columns(outer_kernel, "outer_columns", 7, 400000 * cube // 1000)(
         core, outer, first_corner, second_corner, rows, cols, left
     )

time: 53.4 us -> 52 us (0.974)
  the two profiles are of different devices: /device:TPU:228 before, /device:TPU:4 now
where the time goes in v10:
time: 52 us; the launch traced here: 51.7 us
  starting transfers between devices  19.5 us (38%)
  waiting for transfers between devices  14.9 us (29%)
  Pallas kernels  11.6 us (22%)
  local copies, waits for them, and re-layouts  4.62 us (9%)
  other arithmetic  0.83 us (2%)
    ppermute x7, starting transfers between devices, swap_rows(): return lax.ppermute(values, ('dec', 'ra'), partners(offset, side))  13 us
    ppermute x7, waiting for transfers between devices, swap_rows(): return lax.ppermute(values, ('dec', 'ra'), partners(offset, side))  9.57 us
    ppermute x5, starting transfers between devices, swap_columns(): return lax.ppermute(values, 'ra', pairs)  5.39 us
    ppermute x5, waiting for transfers between devices, swap_columns(): return lax.ppermute(values, 'ra', pairs)  5.29 us
    unnamed x24, local copies, waits for them, and re-layouts  4.54 us
    pallas_call x1, Pallas kernels, shards(): kernel_call(functools.partial(core_kernel, half), 'core_columns', (jax.Sh...  3.73 us
    pallas_call x1, Pallas kernels, shards(): kernel_call(functools.partial(main_kernel, half, scale), 'tile_model', (s...  3.56 us
    ppermute x1, starting transfers between devices, swap_beside(): return lax.ppermute(values, ('dec', 'ra'), pairs)  1.2 us
  transfers between devices with their start and end apart: 13, of which 5 were waited for; matrix products, arithmetic and copies ran while one was open for 2% of the time, Pallas kernels for 10%

profile of v10, /device:TPU:4, one launch (start us, length us, event | category | flops | bytes accessed | tf_op | source)
XLA Modules:
  0.0 51.7 jit_solution(12444423300062608525)
XLA Ops:
  0.0 1.1 %copy-done = bf16[6,256,256]{2,1,0:T(8,128)(2,1)S(1)} copy-done((bf16[6,256,256]{2,1,0:T(8,128)(2,1)S(1)}, bf16[6,256,256]{2,1,0:T(8,128)(2,1)}, u32[]{:S(2)}) %copy-start) | copy-done | bytes 786456
  1.1 0.9 %cut.1 = (bf16[6,128,128]{2,1,0:T(8,128)(2,1)}, bf16[6,128,128]{2,1,0:T(8,128)(2,1)}, bf16[3,128,256]{2,1,0:T(8,128)(2,1)}, bf16[3,128,256]{2,1,0:T(8,128)(2,1)S(1)}, bf16[6,128,256]{2,1,0:T(8,128)(2,1)S(1)}) custom-call(bf16[6,256,256]{2,1,0:T(8,128)(2,1)S(1)} %copy-done), custom_call_target="tpu_custom_call" | custom-call | bytes 1048576 | tf_op jit(solution)/shard_map/cut/pallas_call | solution.py:416
  2.0 1.2 %collective-permute-start.1 = (bf16[3,128,256]{2,1,0:T(8,128)(2,1)S(1)}, bf16[3,128,256]{2,1,0:T(8,128)(2,1)S(1)}, u32[]{:S(2)}, u32[]{:S(2)}) collective-permute-start(bf16[3,128,256]{2,1,0:T(8,128)(2,1)S(1)} %get-tuple-element.26), channel_id=1, source_target_pairs={{0,1},{1,0},{2,3},{3,2},{4,5},{5,4},{6,7},{7,6},{8,9},{9,8},{10,11... | collective-permute-start | bytes 589832 | tf_op jit(solution)/shard_map/ppermute | solution.py:374
  3.2 2.4 %collective-permute-start.4 = (bf16[6,128,128]{2,1,0:T(8,128)(2,1)}, bf16[6,128,128]{2,1,0:T(8,128)(2,1)S(1)}, u32[]{:S(2)}, u32[]{:S(2)}) collective-permute-start(bf16[6,128,128]{2,1,0:T(8,128)(2,1)} %get-tuple-element.28), channel_id=1, source_target_pairs={{0,15},{1,2},{2,1},{3,4},{4,3},{5,6},{6,5},{7,8},{8,7},{9,10},{10,... | collective-permute-start | bytes 589832 | tf_op jit(solution)/shard_map/ppermute | solution.py:380
  5.7 1.4 %collective-permute-start.5 = (bf16[6,128,128]{2,1,0:T(8,128)(2,1)}, bf16[6,128,128]{2,1,0:T(8,128)(2,1)S(1)}, u32[]{:S(2)}, u32[]{:S(2)}) collective-permute-start(bf16[6,128,128]{2,1,0:T(8,128)(2,1)} %get-tuple-element.29), channel_id=1, source_target_pairs={{0,15},{1,2},{2,1},{3,4},{4,3},{5,6},{6,5},{7,8},{8,7},{9,10},{10,... | collective-permute-start | bytes 589832 | tf_op jit(solution)/shard_map/ppermute | solution.py:380
  7.1 0.7 %collective-permute-start.3 = (bf16[6,128,256]{2,1,0:T(8,128)(2,1)S(1)}, bf16[6,128,256]{2,1,0:T(8,128)(2,1)S(1)}, u32[]{:S(2)}, u32[]{:S(2)}) collective-permute-start(bf16[6,128,256]{2,1,0:T(8,128)(2,1)S(1)} %get-tuple-element.27), channel_id=1, source_target_pairs={{0,16},{1,17},{2,18},{3,19},{4,20},{5,21},{6,22},{7,23},{8,24},{9,... | collective-permute-start | bytes 1179656 | tf_op jit(solution)/shard_map/ppermute | solution.py:365
  7.8 5.4 %collective-permute-start = (bf16[3,128,256]{2,1,0:T(8,128)(2,1)}, bf16[3,128,256]{2,1,0:T(8,128)(2,1)S(1)}, u32[]{:S(2)}, u32[]{:S(2)}) collective-permute-start(bf16[3,128,256]{2,1,0:T(8,128)(2,1)} %get-tuple-element.25), channel_id=1, source_target_pairs={{0,1},{1,0},{2,3},{3,2},{4,5},{5,4},{6,7},{7,6},{8,9},{9,8},{10,11... | collective-permute-start | bytes 589832 | tf_op jit(solution)/shard_map/ppermute | solution.py:365
  13.2 0.7 %broadcast_select_fusion = bf16[3,128,256]{2,1,0:T(8,128)(2,1)} fusion(bf16[3,128,256]{2,1,0:T(8,128)(2,1)S(1)} %collective-permute-done.1, bf16[3,128,256]{2,1,0:T(8,128)(2,1)S(1)} %get-tuple-element.26, pred[]{:T(512)S(6)} %or.3), kind=kLoop, calls=%fused_computation.4 | loop fusion | flops 98304 | bytes 589825 | tf_op jit(solution)/shard_map/jit(_where)/select_n | solution.py:425
  13.9 2.5 %collective-permute-start.2 = (bf16[3,128,256]{2,1,0:T(8,128)(2,1)}, bf16[3,128,256]{2,1,0:T(8,128)(2,1)S(1)}, u32[]{:S(2)}, u32[]{:S(2)}) collective-permute-start(bf16[3,128,256]{2,1,0:T(8,128)(2,1)} %broadcast_select_fusion), channel_id=1, source_target_pairs={{0,1},{1,0},{2,3},{3,2},{4,5},{5,4},{6,7},{7,6},{8,9},{9,8},{10,11... | collective-permute-start | bytes 589832 | tf_op jit(solution)/shard_map/ppermute | solution.py:365
  16.3 1.0 %copy-done.3 = bf16[528,512]{1,0:T(8,128)(2,1)S(1)} copy-done((bf16[528,512]{1,0:T(8,128)(2,1)S(1)}, bf16[528,512]{1,0:T(8,128)(2,1)}, u32[]{:S(2)}) %copy-start.3) | copy-done | bytes 540696
  17.4 1.0 %copy-done.5 = bf16[512,512]{1,0:T(8,128)(2,1)S(1)} copy-done((bf16[512,512]{1,0:T(8,128)(2,1)S(1)}, bf16[512,512]{1,0:T(8,128)(2,1)}, u32[]{:S(2)}) %copy-start.5) | copy-done | bytes 524312
  18.4 1.0 %copy-done.11 = bf16[512,512]{1,0:T(8,128)(2,1)S(1)} copy-done((bf16[512,512]{1,0:T(8,128)(2,1)S(1)}, bf16[512,512]{1,0:T(8,128)(2,1)}, u32[]{:S(2)}) %copy-start.11) | copy-done | bytes 524312
  19.5 0.9 %noise_spectrum.1 = (f32[264,512]{1,0:T(8,128)S(1)}, f32[264,512]{1,0:T(8,128)S(1)}) custom-call(bf16[512,512]{1,0:T(8,128)(2,1)S(1)} %copy-done.11, bf16[528,512]{1,0:T(8,128)(2,1)S(1)} %copy-done.3, bf16[512,512]{1,0:T(8,128)(2,1)S(1)} %copy-done.5), custom_call_target="tpu_custom_call" | custom-call | flops 6710886400 | bytes 1048576 | tf_op jit(solution)/shard_map/noise_spectrum/pallas_call | solution.py:429
  20.4 0.1 constant_dynamic-slice_fusion.1
  20.5 1.3 %collective-permute-start.6 = (bf16[6,128,128]{2,1,0:T(8,128)(2,1)S(1)}, bf16[6,128,128]{2,1,0:T(8,128)(2,1)S(1)}, u32[]{:S(2)}, u32[]{:S(2)}) collective-permute-start(bf16[6,128,128]{2,1,0:T(8,128)(2,1)S(1)} %collective-permute-done.4.outer_first_ref), channel_id=1, source_target_pairs={{0,1},{1,0},{2,3},{3,2},{4,5},{5,4},{6,7},{7,6},{8,9},{9,8},{10,11... | collective-permute-start | bytes 589832 | tf_op jit(solution)/shard_map/ppermute | solution.py:365
  21.8 0.1 collective-permute-done.2.far_ref
  22.1 0.3 collective-permute-start.8
  22.4 3.7 %core_columns.1 = (f32[6,528,512]{2,1,0:T(8,128)S(1)}, bf16[6,512,128]{2,1,0:T(8,128)(2,1)S(1)}) custom-call(bf16[6,256,256]{2,1,0:T(8,128)(2,1)S(1)} %copy-done.1, bf16[3,128,256]{2,1,0:T(8,128)(2,1)S(1)} %collective-permute-done.near_ref, bf16[3,128,256]{2,1,0:T(8,128)(2,1)S(1)} %collective-permute-done.2.far_ref, ...), custom_call_target="tpu_custom_call" | custom-call | flops 134217728 | bytes 1048576 | tf_op jit(solution)/shard_map/core_columns/pallas_call | solution.py:459
  26.1 3.8 %collective-permute-done.6.first_ref = bf16[6,128,128]{2,1,0:T(8,128)(2,1)S(1)} collective-permute-done((bf16[6,128,128]{2,1,0:T(8,128)(2,1)S(1)}, bf16[6,128,128]{2,1,0:T(8,128)(2,1)S(1)}, u32[]{:S(2)}, u32[]{:S(2)}) %collective-permute-start.6) | collective-permute-done | bytes 196640 | tf_op jit(solution)/shard_map/ppermute | solution.py:365
  29.9 0.8 %outer_columns.1.after_ref.outer_ref = bf16[6,528,128]{2,1,0:T(8,128)(2,1)S(1)} custom-call(f32[6,528,512]{2,1,0:T(8,128)S(1)} %get-tuple-element.35.after_ref.core_ref, bf16[6,512,128]{2,1,0:T(8,128)(2,1)S(1)} %get-tuple-element.36.tile, bf16[6,128,128]{2,1,0:T(8,128)(2,1)S(1)} %collective-permute-done.6.first_ref, ...), custom_call_target="tpu_custom_call" | custom-call | flops 53687091200 | bytes 1048576 | tf_op jit(solution)/shard_map/outer_columns/pallas_call | solution.py:470
  30.7 1.0 %inner_columns.1.inner_ref = bf16[6,528,128]{2,1,0:T(8,128)(2,1)S(1)} custom-call(bf16[6,528,128]{2,1,0:T(8,128)(2,1)S(1)} %outer_columns.1.after_ref.outer_ref, bf16[6,512,128]{2,1,0:T(8,128)(2,1)S(1)} %collective-permute-done.8.inner_ref, f32[512,128]{1,0:T(8,128)S(1)} %copy-done.2, f32[8,512]{1,0:T(8,128)S(1)} %copy-done.10, bf16[528,512]{1,0:T(8,128)(2,1)S(1)} %copy-done.4), custom_call_target="tpu_custom_call" | custom-call | flops 134217728 | bytes 1048576 | tf_op jit(solution)/shard_map/inner_columns/pallas_call | solution.py:473
  31.7 0.2 copy-done.8
  31.9 3.6 %tile_model.1 = (bf16[128,512]{1,0:T(8,128)(2,1)S(1)}, bf16[128,512]{1,0:T(8,128)(2,1)S(1)}, f32[256,512]{1,0:T(8,128)S(1)}) custom-call(f32[6,528,512]{2,1,0:T(8,128)S(1)} %get-tuple-element.35.after_ref.core_ref, bf16[6,528,128]{2,1,0:T(8,128)(2,1)S(1)} %inner_columns.1.inner_ref, bf16[6,528,128]{2,1,0:T(8,128)(2,1)S(1)} %outer_columns.1.after_ref.outer_ref, ...), custom_call_target="tpu_custom_call" | custom-call | flops 2684354560 | bytes 1048576 | tf_op jit(solution)/shard_map/tile_model/pallas_call | solution.py:476
  35.5 0.1 collective-permute-start.10
  35.6 3.0 %collective-permute-start.9 = (bf16[128,512]{1,0:T(8,128)(2,1)S(1)}, bf16[128,512]{1,0:T(8,128)(2,1)S(1)}, u32[]{:S(2)}, u32[]{:S(2)}) collective-permute-start(bf16[128,512]{1,0:T(8,128)(2,1)S(1)} %get-tuple-element.40), channel_id=1, source_target_pairs={{0,1},{1,0},{2,3},{3,2},{4,5},{5,4},{6,7},{7,6},{8,9},{9,8},{10,11... | collective-permute-start | bytes 393224 | tf_op jit(solution)/shard_map/ppermute | solution.py:365
  38.6 1.9 %collective-permute-done.10.second_ref = bf16[128,512]{1,0:T(8,128)(2,1)S(1)} collective-permute-done((bf16[128,512]{1,0:T(8,128)(2,1)S(1)}, bf16[128,512]{1,0:T(8,128)(2,1)S(1)}, u32[]{:S(2)}, u32[]{:S(2)}) %collective-permute-start.10) | collective-permute-done | bytes 131104 | tf_op jit(solution)/shard_map/ppermute | solution.py:365
  40.6 3.7 %collective-permute-done.9.first_ref = bf16[128,512]{1,0:T(8,128)(2,1)S(1)} collective-permute-done((bf16[128,512]{1,0:T(8,128)(2,1)S(1)}, bf16[128,512]{1,0:T(8,128)(2,1)S(1)}, u32[]{:S(2)}, u32[]{:S(2)}) %collective-permute-start.9) | collective-permute-done | bytes 131104 | tf_op jit(solution)/shard_map/ppermute | solution.py:365
  44.3 0.1 fold_rows.1
  44.4 0.5 %collective-permute-start.11 = (bf16[256,128]{1,0:T(8,128)(2,1)S(1)}, bf16[256,128]{1,0:T(8,128)(2,1)S(1)}, u32[]{:S(2)}, u32[]{:S(2)}) collective-permute-start(bf16[256,128]{1,0:T(8,128)(2,1)S(1)} %get-tuple-element.43), channel_id=1, source_target_pairs={{0,15},{1,2},{2,1},{3,4},{4,3},{5,6},{6,5},{7,8},{8,7},{9,10},{10,... | collective-permute-start | bytes 196616 | tf_op jit(solution)/shard_map/ppermute | solution.py:380
  44.9 0.8 %collective-permute-start.12 = (bf16[256,128]{1,0:T(8,128)(2,1)S(1)}, bf16[256,128]{1,0:T(8,128)(2,1)S(1)}, u32[]{:S(2)}, u32[]{:S(2)}) collective-permute-start(bf16[256,128]{1,0:T(8,128)(2,1)S(1)} %get-tuple-element.44), channel_id=1, source_target_pairs={{0,1},{1,0},{2,3},{3,2},{4,5},{5,4},{6,7},{7,6},{8,9},{9,8},{10,11... | collective-permute-start | bytes 196616 | tf_op jit(solution)/shard_map/ppermute | solution.py:380
  45.7 5.3 %collective-permute-done.11.outer_ref = bf16[256,128]{1,0:T(8,128)(2,1)S(1)} collective-permute-done((bf16[256,128]{1,0:T(8,128)(2,1)S(1)}, bf16[256,128]{1,0:T(8,128)(2,1)S(1)}, u32[]{:S(2)}, u32[]{:S(2)}) %collective-permute-start.11) | collective-permute-done | bytes 65568 | tf_op jit(solution)/shard_map/ppermute | solution.py:380
  51.0 0.7 %fold_columns.1 = f32[256,256]{1,0:T(8,128)} custom-call(f32[256,256]{1,0:T(8,128)S(1)} %get-tuple-element.42.center_ref, bf16[256,128]{1,0:T(8,128)(2,1)S(1)} %collective-permute-done.11.outer_ref, bf16[256,128]{1,0:T(8,128)(2,1)S(1)} %collective-permute-done.12.inner_ref), custom_call_target="tpu_custom_call" | custom-call | bytes 1048576 | tf_op jit(solution)/shard_map/fold_columns/pallas_call | solution.py:504
  (30 shorter events, 0.3 us)
Async XLA Ops:
  0.0 1.1 %copy-start = (bf16[6,256,256]{2,1,0:T(8,128)(2,1)S(1)}, bf16[6,256,256]{2,1,0:T(8,128)(2,1)}, u32[]{:S(2)}) copy-start(bf16[6,256,256]{2,1,0:T(8,128)(2,1)} %core_ref.1) | copy-start | bytes 2359300
  2.0 11.2 %collective-permute-start.1 = (bf16[3,128,256]{2,1,0:T(8,128)(2,1)S(1)}, bf16[3,128,256]{2,1,0:T(8,128)(2,1)S(1)}, u32[]{:S(2)}, u32[]{:S(2)}) collective-permute-start(bf16[3,128,256]{2,1,0:T(8,128)(2,1)S(1)} %get-tuple-element.26), channel_id=1, source_target_pairs={{0,1},{1,0},{2,3},{3,2},{4,5},{5,4},{6,7},{7,6},{8,9},{9,8},{10,11... | collective-permute-start | bytes 589832 | tf_op jit(solution)/shard_map/ppermute | solution.py:374
  3.2 17.3 %collective-permute-start.4 = (bf16[6,128,128]{2,1,0:T(8,128)(2,1)}, bf16[6,128,128]{2,1,0:T(8,128)(2,1)S(1)}, u32[]{:S(2)}, u32[]{:S(2)}) collective-permute-start(bf16[6,128,128]{2,1,0:T(8,128)(2,1)} %get-tuple-element.28), channel_id=1, source_target_pairs={{0,15},{1,2},{2,1},{3,4},{4,3},{5,6},{6,5},{7,8},{8,7},{9,10},{10,... | collective-permute-start | bytes 589832 | tf_op jit(solution)/shard_map/ppermute | solution.py:380
  5.7 16.2 %collective-permute-start.5 = (bf16[6,128,128]{2,1,0:T(8,128)(2,1)}, bf16[6,128,128]{2,1,0:T(8,128)(2,1)S(1)}, u32[]{:S(2)}, u32[]{:S(2)}) collective-permute-start(bf16[6,128,128]{2,1,0:T(8,128)(2,1)} %get-tuple-element.29), channel_id=1, source_target_pairs={{0,15},{1,2},{2,1},{3,4},{4,3},{5,6},{6,5},{7,8},{8,7},{9,10},{10,... | collective-permute-start | bytes 589832 | tf_op jit(solution)/shard_map/ppermute | solution.py:380
  7.1 14.9 %collective-permute-start.3 = (bf16[6,128,256]{2,1,0:T(8,128)(2,1)S(1)}, bf16[6,128,256]{2,1,0:T(8,128)(2,1)S(1)}, u32[]{:S(2)}, u32[]{:S(2)}) collective-permute-start(bf16[6,128,256]{2,1,0:T(8,128)(2,1)S(1)} %get-tuple-element.27), channel_id=1, source_target_pairs={{0,16},{1,17},{2,18},{3,19},{4,20},{5,21},{6,22},{7,23},{8,24},{9,... | collective-permute-start | bytes 1179656 | tf_op jit(solution)/shard_map/ppermute | solution.py:365
  7.8 14.0 %collective-permute-start = (bf16[3,128,256]{2,1,0:T(8,128)(2,1)}, bf16[3,128,256]{2,1,0:T(8,128)(2,1)S(1)}, u32[]{:S(2)}, u32[]{:S(2)}) collective-permute-start(bf16[3,128,256]{2,1,0:T(8,128)(2,1)} %get-tuple-element.25), channel_id=1, source_target_pairs={{0,1},{1,0},{2,3},{3,2},{4,5},{5,4},{6,7},{7,6},{8,9},{9,8},{10,11... | collective-permute-start | bytes 589832 | tf_op jit(solution)/shard_map/ppermute | solution.py:365
  13.9 6.5 %copy-start.1 = (bf16[6,256,256]{2,1,0:T(8,128)(2,1)S(1)}, bf16[6,256,256]{2,1,0:T(8,128)(2,1)}, u32[]{:S(2)}) copy-start(bf16[6,256,256]{2,1,0:T(8,128)(2,1)} %core_ref.1) | copy-start | bytes 2359300
  13.9 8.1 %collective-permute-start.2 = (bf16[3,128,256]{2,1,0:T(8,128)(2,1)}, bf16[3,128,256]{2,1,0:T(8,128)(2,1)S(1)}, u32[]{:S(2)}, u32[]{:S(2)}) collective-permute-start(bf16[3,128,256]{2,1,0:T(8,128)(2,1)} %broadcast_select_fusion), channel_id=1, source_target_pairs={{0,1},{1,0},{2,3},{3,2},{4,5},{5,4},{6,7},{7,6},{8,9},{9,8},{10,11... | collective-permute-start | bytes 589832 | tf_op jit(solution)/shard_map/ppermute | solution.py:365
  16.3 1.0 %copy-start.3 = (bf16[528,512]{1,0:T(8,128)(2,1)S(1)}, bf16[528,512]{1,0:T(8,128)(2,1)}, u32[]{:S(2)}) copy-start(bf16[528,512]{1,0:T(8,128)(2,1)} %constant.44.clone.left_ref) | copy-start | bytes 1622020
  17.4 1.0 %copy-start.5 = (bf16[512,512]{1,0:T(8,128)(2,1)S(1)}, bf16[512,512]{1,0:T(8,128)(2,1)}, u32[]{:S(2)}) copy-start(bf16[512,512]{1,0:T(8,128)(2,1)} %constant.45.clone.right_ref) | copy-start | bytes 1572868
  18.4 1.0 %copy-start.11 = (bf16[512,512]{1,0:T(8,128)(2,1)S(1)}, bf16[512,512]{1,0:T(8,128)(2,1)}, u32[]{:S(2)}) copy-start(bf16[512,512]{1,0:T(8,128)(2,1)} %noise_ref.1) | copy-start | bytes 1572868
  20.4 2.0 %copy-start.2 = (f32[512,128]{1,0:T(8,128)S(1)}, f32[512,128]{1,0:T(8,128)}, u32[]{:S(2)}) copy-start(f32[512,128]{1,0:T(8,128)} %constant.49.clone.rows_ref) | copy-start | bytes 786436
  20.4 2.0 %copy-start.4 = (bf16[528,512]{1,0:T(8,128)(2,1)S(1)}, bf16[528,512]{1,0:T(8,128)(2,1)}, u32[]{:S(2)}) copy-start(bf16[528,512]{1,0:T(8,128)(2,1)} %constant.44.clone.left_ref) | copy-start | bytes 1622020
  20.4 2.0 %copy-start.6 = (bf16[512,512]{1,0:T(8,128)(2,1)S(1)}, bf16[512,512]{1,0:T(8,128)(2,1)}, u32[]{:S(2)}) copy-start(bf16[512,512]{1,0:T(8,128)(2,1)} %constant.45.clone.right_ref) | copy-start | bytes 1572868
  20.4 2.0 %copy-start.10 = (f32[8,512]{1,0:T(8,128)S(1)}, f32[8,512]{1,0:T(8,128)}, u32[]{:S(2)}) copy-start(f32[8,512]{1,0:T(8,128)} %constant.50.clone.cols_ref) | copy-start | bytes 49156
  20.5 9.4 %collective-permute-start.6 = (bf16[6,128,128]{2,1,0:T(8,128)(2,1)S(1)}, bf16[6,128,128]{2,1,0:T(8,128)(2,1)S(1)}, u32[]{:S(2)}, u32[]{:S(2)}) collective-permute-start(bf16[6,128,128]{2,1,0:T(8,128)(2,1)S(1)} %collective-permute-done.4.outer_first_ref), channel_id=1, source_target_pairs={{0,1},{1,0},{2,3},{3,2},{4,5},{5,4},{6,7},{7,6},{8,9},{9,8},{10,11... | collective-permute-start | bytes 589832 | tf_op jit(solution)/shard_map/ppermute | solution.py:365
  21.8 8.1 %collective-permute-start.7 = (bf16[6,128,128]{2,1,0:T(8,128)(2,1)S(1)}, bf16[6,128,128]{2,1,0:T(8,128)(2,1)S(1)}, u32[]{:S(2)}, u32[]{:S(2)}) collective-permute-start(bf16[6,128,128]{2,1,0:T(8,128)(2,1)S(1)} %collective-permute-done.5.outer_second_ref), channel_id=1, source_target_pairs={{0,16},{1,17},{2,18},{3,19},{4,20},{5,21},{6,22},{7,23},{8,24},{9,... | collective-permute-start | bytes 589832 | tf_op jit(solution)/shard_map/ppermute | solution.py:365
  22.1 8.6 %collective-permute-start.8 = (bf16[6,512,128]{2,1,0:T(8,128)(2,1)S(1)}, bf16[6,512,128]{2,1,0:T(8,128)(2,1)S(1)}, u32[]{:S(2)}, u32[]{:S(2)}) collective-permute-start(bf16[6,512,128]{2,1,0:T(8,128)(2,1)S(1)} %pad_maximum_fusion), channel_id=1, source_target_pairs={{0,1},{1,0},{2,3},{3,2},{4,5},{5,4},{6,7},{7,6},{8,9},{9,8},{10,11... | collective-permute-start | bytes 2359304 | tf_op jit(solution)/shard_map/ppermute | solution.py:380
  30.7 1.0 %copy-start.7 = (bf16[512,512]{1,0:T(8,128)(2,1)S(1)}, bf16[512,512]{1,0:T(8,128)(2,1)}, u32[]{:S(2)}) copy-start(bf16[512,512]{1,0:T(8,128)(2,1)} %constant.46.clone.inverse_right_ref) | copy-start | bytes 1572868
  30.7 1.2 %copy-start.8 = (bf16[512,512]{1,0:T(8,128)(2,1)S(1)}, bf16[512,512]{1,0:T(8,128)(2,1)}, u32[]{:S(2)}) copy-start(bf16[512,512]{1,0:T(8,128)(2,1)} %constant.47.clone.band_columns_ref) | copy-start | bytes 1572868
  30.7 1.2 %copy-start.9 = (bf16[272,384]{1,0:T(8,128)(2,1)S(1)}, bf16[272,384]{1,0:T(8,128)(2,1)}, u32[]{:S(2)}) copy-start(bf16[272,384]{1,0:T(8,128)(2,1)} %constant.48.clone.band_rows_ref) | copy-start | bytes 626692
  35.5 5.1 %collective-permute-start.10 = (bf16[128,512]{1,0:T(8,128)(2,1)S(1)}, bf16[128,512]{1,0:T(8,128)(2,1)S(1)}, u32[]{:S(2)}, u32[]{:S(2)}) collective-permute-start(bf16[128,512]{1,0:T(8,128)(2,1)S(1)} %get-tuple-element.41), channel_id=1, source_target_pairs={{0,16},{1,17},{2,18},{3,19},{4,20},{5,21},{6,22},{7,23},{8,24},{9,... | collective-permute-start | bytes 393224 | tf_op jit(solution)/shard_map/ppermute | solution.py:365
  35.6 8.7 %collective-permute-start.9 = (bf16[128,512]{1,0:T(8,128)(2,1)S(1)}, bf16[128,512]{1,0:T(8,128)(2,1)S(1)}, u32[]{:S(2)}, u32[]{:S(2)}) collective-permute-start(bf16[128,512]{1,0:T(8,128)(2,1)S(1)} %get-tuple-element.40), channel_id=1, source_target_pairs={{0,1},{1,0},{2,3},{3,2},{4,5},{5,4},{6,7},{7,6},{8,9},{9,8},{10,11... | collective-permute-start | bytes 393224 | tf_op jit(solution)/shard_map/ppermute | solution.py:365
  44.4 6.6 %collective-permute-start.11 = (bf16[256,128]{1,0:T(8,128)(2,1)S(1)}, bf16[256,128]{1,0:T(8,128)(2,1)S(1)}, u32[]{:S(2)}, u32[]{:S(2)}) collective-permute-start(bf16[256,128]{1,0:T(8,128)(2,1)S(1)} %get-tuple-element.43), channel_id=1, source_target_pairs={{0,15},{1,2},{2,1},{3,4},{4,3},{5,6},{6,5},{7,8},{8,7},{9,10},{10,... | collective-permute-start | bytes 196616 | tf_op jit(solution)/shard_map/ppermute | solution.py:380
  44.9 6.0 %collective-permute-start.12 = (bf16[256,128]{1,0:T(8,128)(2,1)S(1)}, bf16[256,128]{1,0:T(8,128)(2,1)S(1)}, u32[]{:S(2)}, u32[]{:S(2)}) collective-permute-start(bf16[256,128]{1,0:T(8,128)(2,1)S(1)} %get-tuple-element.44), channel_id=1, source_target_pairs={{0,1},{1,0},{2,3},{3,2},{4,5},{5,4},{6,7},{7,6},{8,9},{9,8},{10,11... | collective-permute-start | bytes 196616 | tf_op jit(solution)/shard_map/ppermute | solution.py:380

commit v11 on v10

--- a/solution.py
+++ b/solution.py
@@ -422,13 +422,14 @@
     middle = lax.axis_size("dec") // 2
     beside = swap_beside(far)
     near = swap_rows(near, 1)
-    far = swap_rows(jnp.where(jnp.logical_or(row == middle - 1, row == middle), beside, far), 1, side=True)
     outer_second = swap_columns(outer_second, 1)
 
     spectrum = jax.ShapeDtypeStruct((half + 8, length), F32)
     re, im = kernel_call(
         functools.partial(noise_kernel, half), "noise_spectrum", (spectrum, spectrum), 3, flops=50 * cube
     )(white_noise, constant["left"], constant["right"])
+    beside, re, im = lax.optimization_barrier((beside, re, im))
+    far = swap_rows(jnp.where(jnp.logical_or(row == middle - 1, row == middle), beside, far), 1, side=True)
 
     near, far, second, _, _, re, im = lax.optimization_barrier(
         (near, far, second, outer_first, outer_second, re, im)

time: 52 us -> 56.7 us (1.090)
  the two profiles are of different devices: /device:TPU:4 before, /device:TPU:15 now
where the time goes in v11:
time: 56.7 us; the launch traced here: 55.9 us
  waiting for transfers between devices  21.5 us (38%)
  starting transfers between devices  16.2 us (29%)
  Pallas kernels  11.7 us (21%)
  local copies, waits for them, and re-layouts  4.62 us (8%)
  other arithmetic  1.76 us (3%)
    ppermute x7, waiting for transfers between devices, swap_rows(): return lax.ppermute(values, ('dec', 'ra'), partners(offset, side))  17.4 us
    ppermute x7, starting transfers between devices, swap_rows(): return lax.ppermute(values, ('dec', 'ra'), partners(offset, side))  10.7 us
    ppermute x5, starting transfers between devices, swap_columns(): return lax.ppermute(values, 'ra', pairs)  4.87 us
    unnamed x24, local copies, waits for them, and re-layouts  4.54 us
    ppermute x5, waiting for transfers between devices, swap_columns(): return lax.ppermute(values, 'ra', pairs)  4.13 us
    pallas_call x1, Pallas kernels, shards(): kernel_call(functools.partial(core_kernel, half), 'core_columns', (jax.Sh...  3.73 us
    pallas_call x1, Pallas kernels, shards(): kernel_call(functools.partial(main_kernel, half, scale), 'tile_model', (s...  3.56 us
    select_n x1, other arithmetic, shards(): jnp.where(jnp.logical_or(row == middle - 1, row == middle), beside, far)  1.64 us
  transfers between devices with their start and end apart: 13, of which 4 were waited for; matrix products, arithmetic and copies ran while one was open for 3% of the time, Pallas kernels for 10%

profile of v11, /device:TPU:15, one launch (start us, length us, event | category | flops | bytes accessed | tf_op | source)
XLA Modules:
  0.0 55.9 jit_solution(7739713786654755334)
XLA Ops:
  0.0 1.1 %copy-done = bf16[6,256,256]{2,1,0:T(8,128)(2,1)S(1)} copy-done((bf16[6,256,256]{2,1,0:T(8,128)(2,1)S(1)}, bf16[6,256,256]{2,1,0:T(8,128)(2,1)}, u32[]{:S(2)}) %copy-start) | copy-done | bytes 786456
  1.1 0.9 %cut.1 = (bf16[6,128,128]{2,1,0:T(8,128)(2,1)}, bf16[6,128,128]{2,1,0:T(8,128)(2,1)}, bf16[3,128,256]{2,1,0:T(8,128)(2,1)}, bf16[3,128,256]{2,1,0:T(8,128)(2,1)S(1)}, bf16[6,128,256]{2,1,0:T(8,128)(2,1)S(1)}) custom-call(bf16[6,256,256]{2,1,0:T(8,128)(2,1)S(1)} %copy-done), custom_call_target="tpu_custom_call" | custom-call | bytes 1048576 | tf_op jit(solution)/shard_map/cut/pallas_call | solution.py:416
  2.0 0.5 collective-permute-start.1
  2.6 2.8 %collective-permute-start.4 = (bf16[6,128,128]{2,1,0:T(8,128)(2,1)}, bf16[6,128,128]{2,1,0:T(8,128)(2,1)S(1)}, u32[]{:S(2)}, u32[]{:S(2)}) collective-permute-start(bf16[6,128,128]{2,1,0:T(8,128)(2,1)} %get-tuple-element.34), channel_id=1, source_target_pairs={{0,15},{1,2},{2,1},{3,4},{4,3},{5,6},{6,5},{7,8},{8,7},{9,10},{10,... | collective-permute-start | bytes 589832 | tf_op jit(solution)/shard_map/ppermute | solution.py:380
  5.4 1.6 %collective-permute-start.3 = (bf16[6,128,256]{2,1,0:T(8,128)(2,1)S(1)}, bf16[6,128,256]{2,1,0:T(8,128)(2,1)S(1)}, u32[]{:S(2)}, u32[]{:S(2)}) collective-permute-start(bf16[6,128,256]{2,1,0:T(8,128)(2,1)S(1)} %get-tuple-element.33), channel_id=1, source_target_pairs={{0,16},{1,17},{2,18},{3,19},{4,20},{5,21},{6,22},{7,23},{8,24},{9,... | collective-permute-start | bytes 1179656 | tf_op jit(solution)/shard_map/ppermute | solution.py:365
  7.0 5.5 %collective-permute-start = (bf16[3,128,256]{2,1,0:T(8,128)(2,1)}, bf16[3,128,256]{2,1,0:T(8,128)(2,1)S(1)}, u32[]{:S(2)}, u32[]{:S(2)}) collective-permute-start(bf16[3,128,256]{2,1,0:T(8,128)(2,1)} %get-tuple-element.28), channel_id=1, source_target_pairs={{0,1},{1,0},{2,3},{3,2},{4,5},{5,4},{6,7},{7,6},{8,9},{9,8},{10,11... | collective-permute-start | bytes 589832 | tf_op jit(solution)/shard_map/ppermute | solution.py:365
  12.5 1.0 %copy-done.3 = bf16[528,512]{1,0:T(8,128)(2,1)S(1)} copy-done((bf16[528,512]{1,0:T(8,128)(2,1)S(1)}, bf16[528,512]{1,0:T(8,128)(2,1)}, u32[]{:S(2)}) %copy-start.3) | copy-done | bytes 540696
  13.5 1.0 %copy-done.5 = bf16[512,512]{1,0:T(8,128)(2,1)S(1)} copy-done((bf16[512,512]{1,0:T(8,128)(2,1)S(1)}, bf16[512,512]{1,0:T(8,128)(2,1)}, u32[]{:S(2)}) %copy-start.5) | copy-done | bytes 524312
  14.6 1.0 %copy-done.11 = bf16[512,512]{1,0:T(8,128)(2,1)S(1)} copy-done((bf16[512,512]{1,0:T(8,128)(2,1)S(1)}, bf16[512,512]{1,0:T(8,128)(2,1)}, u32[]{:S(2)}) %copy-start.11) | copy-done | bytes 524312
  15.6 0.9 %noise_spectrum.1 = (f32[264,512]{1,0:T(8,128)S(1)}, f32[264,512]{1,0:T(8,128)S(1)}) custom-call(bf16[512,512]{1,0:T(8,128)(2,1)S(1)} %copy-done.11, bf16[528,512]{1,0:T(8,128)(2,1)S(1)} %copy-done.3, bf16[512,512]{1,0:T(8,128)(2,1)S(1)} %copy-done.5), custom_call_target="tpu_custom_call" | custom-call | flops 6710886400 | bytes 1048576 | tf_op jit(solution)/shard_map/noise_spectrum/pallas_call | solution.py:428
  16.5 1.6 %broadcast_select_fusion = bf16[3,128,256]{2,1,0:T(8,128)(2,1)} fusion(bf16[3,128,256]{2,1,0:T(8,128)(2,1)} %collective-permute-done.1, bf16[3,128,256]{2,1,0:T(8,128)(2,1)S(1)} %get-tuple-element.29, pred[]{:T(512)S(6)} %or.3), kind=kLoop, calls=%fused_computation.4 | loop fusion | flops 98304 | bytes 589825 | tf_op jit(solution)/shard_map/jit(_where)/select_n | solution.py:432
  18.2 0.1 constant_dynamic-slice_fusion.1
  18.3 3.4 %collective-permute-start.6 = (bf16[6,128,128]{2,1,0:T(8,128)(2,1)S(1)}, bf16[6,128,128]{2,1,0:T(8,128)(2,1)S(1)}, u32[]{:S(2)}, u32[]{:S(2)}) collective-permute-start(bf16[6,128,128]{2,1,0:T(8,128)(2,1)S(1)} %collective-permute-done.4.outer_first_ref), channel_id=1, source_target_pairs={{0,1},{1,0},{2,3},{3,2},{4,5},{5,4},{6,7},{7,6},{8,9},{9,8},{10,11... | collective-permute-start | bytes 589832 | tf_op jit(solution)/shard_map/ppermute | solution.py:365
  21.7 8.7 %collective-permute-done.2.far_ref = bf16[3,128,256]{2,1,0:T(8,128)(2,1)S(1)} collective-permute-done((bf16[3,128,256]{2,1,0:T(8,128)(2,1)}, bf16[3,128,256]{2,1,0:T(8,128)(2,1)S(1)}, u32[]{:S(2)}, u32[]{:S(2)}) %collective-permute-start.2) | collective-permute-done | bytes 196640 | tf_op jit(solution)/shard_map/ppermute | solution.py:365
  30.4 0.1 fusion
  30.5 0.1 pad_maximum_fusion
  30.6 1.1 %collective-permute-start.8 = (bf16[6,512,128]{2,1,0:T(8,128)(2,1)S(1)}, bf16[6,512,128]{2,1,0:T(8,128)(2,1)S(1)}, u32[]{:S(2)}, u32[]{:S(2)}) collective-permute-start(bf16[6,512,128]{2,1,0:T(8,128)(2,1)S(1)} %pad_maximum_fusion), channel_id=1, source_target_pairs={{0,1},{1,0},{2,3},{3,2},{4,5},{5,4},{6,7},{7,6},{8,9},{9,8},{10,11... | collective-permute-start | bytes 2359304 | tf_op jit(solution)/shard_map/ppermute | solution.py:380
  31.7 3.7 %core_columns.1 = (f32[6,528,512]{2,1,0:T(8,128)S(1)}, bf16[6,512,128]{2,1,0:T(8,128)(2,1)S(1)}) custom-call(bf16[6,256,256]{2,1,0:T(8,128)(2,1)S(1)} %copy-done.1, bf16[3,128,256]{2,1,0:T(8,128)(2,1)S(1)} %collective-permute-done.near_ref, bf16[3,128,256]{2,1,0:T(8,128)(2,1)S(1)} %collective-permute-done.2.far_ref, ...), custom_call_target="tpu_custom_call" | custom-call | flops 134217728 | bytes 1048576 | tf_op jit(solution)/shard_map/core_columns/pallas_call | solution.py:460
  35.4 0.8 %outer_columns.1.after_ref.outer_ref = bf16[6,528,128]{2,1,0:T(8,128)(2,1)S(1)} custom-call(f32[6,528,512]{2,1,0:T(8,128)S(1)} %get-tuple-element.41.after_ref.core_ref, bf16[6,512,128]{2,1,0:T(8,128)(2,1)S(1)} %get-tuple-element.42.tile, bf16[6,128,128]{2,1,0:T(8,128)(2,1)S(1)} %collective-permute-done.6.first_ref, ...), custom_call_target="tpu_custom_call" | custom-call | flops 53687091200 | bytes 1048576 | tf_op jit(solution)/shard_map/outer_columns/pallas_call | solution.py:471
  36.3 1.0 %inner_columns.1.inner_ref = bf16[6,528,128]{2,1,0:T(8,128)(2,1)S(1)} custom-call(bf16[6,528,128]{2,1,0:T(8,128)(2,1)S(1)} %outer_columns.1.after_ref.outer_ref, bf16[6,512,128]{2,1,0:T(8,128)(2,1)S(1)} %collective-permute-done.8.inner_ref, f32[512,128]{1,0:T(8,128)S(1)} %copy-done.2, f32[8,512]{1,0:T(8,128)S(1)} %copy-done.10, bf16[528,512]{1,0:T(8,128)(2,1)S(1)} %copy-done.4), custom_call_target="tpu_custom_call" | custom-call | flops 134217728 | bytes 1048576 | tf_op jit(solution)/shard_map/inner_columns/pallas_call | solution.py:474
  37.3 0.2 copy-done.8
  37.4 0.0 copy-done.9
  37.5 3.6 %tile_model.1 = (bf16[128,512]{1,0:T(8,128)(2,1)S(1)}, bf16[128,512]{1,0:T(8,128)(2,1)S(1)}, f32[256,512]{1,0:T(8,128)S(1)}) custom-call(f32[6,528,512]{2,1,0:T(8,128)S(1)} %get-tuple-element.41.after_ref.core_ref, bf16[6,528,128]{2,1,0:T(8,128)(2,1)S(1)} %inner_columns.1.inner_ref, bf16[6,528,128]{2,1,0:T(8,128)(2,1)S(1)} %outer_columns.1.after_ref.outer_ref, ...), custom_call_target="tpu_custom_call" | custom-call | flops 2684354560 | bytes 1048576 | tf_op jit(solution)/shard_map/tile_model/pallas_call | solution.py:477
  41.0 0.1 collective-permute-start.10
  41.1 0.1 collective-permute-start.9
  41.2 5.0 %collective-permute-done.10.second_ref = bf16[128,512]{1,0:T(8,128)(2,1)S(1)} collective-permute-done((bf16[128,512]{1,0:T(8,128)(2,1)S(1)}, bf16[128,512]{1,0:T(8,128)(2,1)S(1)}, u32[]{:S(2)}, u32[]{:S(2)}) %collective-permute-start.10) | collective-permute-done | bytes 131104 | tf_op jit(solution)/shard_map/ppermute | solution.py:365
  46.2 3.7 %collective-permute-done.9.first_ref = bf16[128,512]{1,0:T(8,128)(2,1)S(1)} collective-permute-done((bf16[128,512]{1,0:T(8,128)(2,1)S(1)}, bf16[128,512]{1,0:T(8,128)(2,1)S(1)}, u32[]{:S(2)}, u32[]{:S(2)}) %collective-permute-start.9) | collective-permute-done | bytes 131104 | tf_op jit(solution)/shard_map/ppermute | solution.py:365
  49.9 0.1 fold_rows.1
  50.1 0.4 collective-permute-start.11
  50.5 0.6 %collective-permute-start.12 = (bf16[256,128]{1,0:T(8,128)(2,1)S(1)}, bf16[256,128]{1,0:T(8,128)(2,1)S(1)}, u32[]{:S(2)}, u32[]{:S(2)}) collective-permute-start(bf16[256,128]{1,0:T(8,128)(2,1)S(1)} %get-tuple-element.50), channel_id=1, source_target_pairs={{0,1},{1,0},{2,3},{3,2},{4,5},{5,4},{6,7},{7,6},{8,9},{9,8},{10,11... | collective-permute-start | bytes 196616 | tf_op jit(solution)/shard_map/ppermute | solution.py:380
  51.1 4.1 %collective-permute-done.11.outer_ref = bf16[256,128]{1,0:T(8,128)(2,1)S(1)} collective-permute-done((bf16[256,128]{1,0:T(8,128)(2,1)S(1)}, bf16[256,128]{1,0:T(8,128)(2,1)S(1)}, u32[]{:S(2)}, u32[]{:S(2)}) %collective-permute-start.11) | collective-permute-done | bytes 65568 | tf_op jit(solution)/shard_map/ppermute | solution.py:380
  55.2 0.7 %fold_columns.1 = f32[256,256]{1,0:T(8,128)} custom-call(f32[256,256]{1,0:T(8,128)S(1)} %get-tuple-element.48.center_ref, bf16[256,128]{1,0:T(8,128)(2,1)S(1)} %collective-permute-done.11.outer_ref, bf16[256,128]{1,0:T(8,128)(2,1)S(1)} %collective-permute-done.12.inner_ref), custom_call_target="tpu_custom_call" | custom-call | bytes 1048576 | tf_op jit(solution)/shard_map/fold_columns/pallas_call | solution.py:505
  (30 shorter events, 0.1 us)
Async XLA Ops:
  0.0 1.1 %copy-start = (bf16[6,256,256]{2,1,0:T(8,128)(2,1)S(1)}, bf16[6,256,256]{2,1,0:T(8,128)(2,1)}, u32[]{:S(2)}) copy-start(bf16[6,256,256]{2,1,0:T(8,128)(2,1)} %core_ref.1) | copy-start | bytes 2359300
  2.0 14.5 %collective-permute-start.1 = (bf16[3,128,256]{2,1,0:T(8,128)(2,1)S(1)}, bf16[3,128,256]{2,1,0:T(8,128)(2,1)}, u32[]{:S(2)}, u32[]{:S(2)}) collective-permute-start(bf16[3,128,256]{2,1,0:T(8,128)(2,1)S(1)} %get-tuple-element.29), channel_id=1, source_target_pairs={{0,1},{1,0},{2,3},{3,2},{4,5},{5,4},{6,7},{7,6},{8,9},{9,8},{10,11... | collective-permute-start | bytes 589832 | tf_op jit(solution)/shard_map/ppermute | solution.py:374
  2.6 15.7 %collective-permute-start.4 = (bf16[6,128,128]{2,1,0:T(8,128)(2,1)}, bf16[6,128,128]{2,1,0:T(8,128)(2,1)S(1)}, u32[]{:S(2)}, u32[]{:S(2)}) collective-permute-start(bf16[6,128,128]{2,1,0:T(8,128)(2,1)} %get-tuple-element.34), channel_id=1, source_target_pairs={{0,15},{1,2},{2,1},{3,4},{4,3},{5,6},{6,5},{7,8},{8,7},{9,10},{10,... | collective-permute-start | bytes 589832 | tf_op jit(solution)/shard_map/ppermute | solution.py:380
  5.3 16.4 %collective-permute-start.5 = (bf16[6,128,128]{2,1,0:T(8,128)(2,1)}, bf16[6,128,128]{2,1,0:T(8,128)(2,1)S(1)}, u32[]{:S(2)}, u32[]{:S(2)}) collective-permute-start(bf16[6,128,128]{2,1,0:T(8,128)(2,1)} %get-tuple-element.35), channel_id=1, source_target_pairs={{0,15},{1,2},{2,1},{3,4},{4,3},{5,6},{6,5},{7,8},{8,7},{9,10},{10,... | collective-permute-start | bytes 589832 | tf_op jit(solution)/shard_map/ppermute | solution.py:380
  5.4 25.1 %collective-permute-start.3 = (bf16[6,128,256]{2,1,0:T(8,128)(2,1)S(1)}, bf16[6,128,256]{2,1,0:T(8,128)(2,1)S(1)}, u32[]{:S(2)}, u32[]{:S(2)}) collective-permute-start(bf16[6,128,256]{2,1,0:T(8,128)(2,1)S(1)} %get-tuple-element.33), channel_id=1, source_target_pairs={{0,16},{1,17},{2,18},{3,19},{4,20},{5,21},{6,22},{7,23},{8,24},{9,... | collective-permute-start | bytes 1179656 | tf_op jit(solution)/shard_map/ppermute | solution.py:365
  7.0 11.2 %copy-start.1 = (bf16[6,256,256]{2,1,0:T(8,128)(2,1)S(1)}, bf16[6,256,256]{2,1,0:T(8,128)(2,1)}, u32[]{:S(2)}) copy-start(bf16[6,256,256]{2,1,0:T(8,128)(2,1)} %core_ref.1) | copy-start | bytes 2359300
  7.0 14.8 %collective-permute-start = (bf16[3,128,256]{2,1,0:T(8,128)(2,1)}, bf16[3,128,256]{2,1,0:T(8,128)(2,1)S(1)}, u32[]{:S(2)}, u32[]{:S(2)}) collective-permute-start(bf16[3,128,256]{2,1,0:T(8,128)(2,1)} %get-tuple-element.28), channel_id=1, source_target_pairs={{0,1},{1,0},{2,3},{3,2},{4,5},{5,4},{6,7},{7,6},{8,9},{9,8},{10,11... | collective-permute-start | bytes 589832 | tf_op jit(solution)/shard_map/ppermute | solution.py:365
  12.5 1.0 %copy-start.3 = (bf16[528,512]{1,0:T(8,128)(2,1)S(1)}, bf16[528,512]{1,0:T(8,128)(2,1)}, u32[]{:S(2)}) copy-start(bf16[528,512]{1,0:T(8,128)(2,1)} %constant.44.clone.left_ref) | copy-start | bytes 1622020
  13.5 1.0 %copy-start.5 = (bf16[512,512]{1,0:T(8,128)(2,1)S(1)}, bf16[512,512]{1,0:T(8,128)(2,1)}, u32[]{:S(2)}) copy-start(bf16[512,512]{1,0:T(8,128)(2,1)} %constant.45.clone.right_ref) | copy-start | bytes 1572868
  14.6 1.0 %copy-start.11 = (bf16[512,512]{1,0:T(8,128)(2,1)S(1)}, bf16[512,512]{1,0:T(8,128)(2,1)}, u32[]{:S(2)}) copy-start(bf16[512,512]{1,0:T(8,128)(2,1)} %noise_ref.1) | copy-start | bytes 1572868
  18.2 12.3 %collective-permute-start.2 = (bf16[3,128,256]{2,1,0:T(8,128)(2,1)}, bf16[3,128,256]{2,1,0:T(8,128)(2,1)S(1)}, u32[]{:S(2)}, u32[]{:S(2)}) collective-permute-start(bf16[3,128,256]{2,1,0:T(8,128)(2,1)} %broadcast_select_fusion), channel_id=1, source_target_pairs={{0,1},{1,0},{2,3},{3,2},{4,5},{5,4},{6,7},{7,6},{8,9},{9,8},{10,11... | collective-permute-start | bytes 589832 | tf_op jit(solution)/shard_map/ppermute | solution.py:365
  18.2 13.5 %copy-start.2 = (f32[512,128]{1,0:T(8,128)S(1)}, f32[512,128]{1,0:T(8,128)}, u32[]{:S(2)}) copy-start(f32[512,128]{1,0:T(8,128)} %constant.49.clone.rows_ref) | copy-start | bytes 786436
  18.2 13.5 %copy-start.4 = (bf16[528,512]{1,0:T(8,128)(2,1)S(1)}, bf16[528,512]{1,0:T(8,128)(2,1)}, u32[]{:S(2)}) copy-start(bf16[528,512]{1,0:T(8,128)(2,1)} %constant.44.clone.left_ref) | copy-start | bytes 1622020
  18.2 13.5 %copy-start.6 = (bf16[512,512]{1,0:T(8,128)(2,1)S(1)}, bf16[512,512]{1,0:T(8,128)(2,1)}, u32[]{:S(2)}) copy-start(bf16[512,512]{1,0:T(8,128)(2,1)} %constant.45.clone.right_ref) | copy-start | bytes 1572868
  18.2 13.5 %copy-start.10 = (f32[8,512]{1,0:T(8,128)S(1)}, f32[8,512]{1,0:T(8,128)}, u32[]{:S(2)}) copy-start(f32[8,512]{1,0:T(8,128)} %constant.50.clone.cols_ref) | copy-start | bytes 49156
  18.3 17.1 %collective-permute-start.6 = (bf16[6,128,128]{2,1,0:T(8,128)(2,1)S(1)}, bf16[6,128,128]{2,1,0:T(8,128)(2,1)S(1)}, u32[]{:S(2)}, u32[]{:S(2)}) collective-permute-start(bf16[6,128,128]{2,1,0:T(8,128)(2,1)S(1)} %collective-permute-done.4.outer_first_ref), channel_id=1, source_target_pairs={{0,1},{1,0},{2,3},{3,2},{4,5},{5,4},{6,7},{7,6},{8,9},{9,8},{10,11... | collective-permute-start | bytes 589832 | tf_op jit(solution)/shard_map/ppermute | solution.py:365
  21.7 13.7 %collective-permute-start.7 = (bf16[6,128,128]{2,1,0:T(8,128)(2,1)S(1)}, bf16[6,128,128]{2,1,0:T(8,128)(2,1)S(1)}, u32[]{:S(2)}, u32[]{:S(2)}) collective-permute-start(bf16[6,128,128]{2,1,0:T(8,128)(2,1)S(1)} %collective-permute-done.5.outer_second_ref), channel_id=1, source_target_pairs={{0,16},{1,17},{2,18},{3,19},{4,20},{5,21},{6,22},{7,23},{8,24},{9,... | collective-permute-start | bytes 589832 | tf_op jit(solution)/shard_map/ppermute | solution.py:365
  30.6 5.7 %collective-permute-start.8 = (bf16[6,512,128]{2,1,0:T(8,128)(2,1)S(1)}, bf16[6,512,128]{2,1,0:T(8,128)(2,1)S(1)}, u32[]{:S(2)}, u32[]{:S(2)}) collective-permute-start(bf16[6,512,128]{2,1,0:T(8,128)(2,1)S(1)} %pad_maximum_fusion), channel_id=1, source_target_pairs={{0,1},{1,0},{2,3},{3,2},{4,5},{5,4},{6,7},{7,6},{8,9},{9,8},{10,11... | collective-permute-start | bytes 2359304 | tf_op jit(solution)/shard_map/ppermute | solution.py:380
  36.2 1.0 %copy-start.7 = (bf16[512,512]{1,0:T(8,128)(2,1)S(1)}, bf16[512,512]{1,0:T(8,128)(2,1)}, u32[]{:S(2)}) copy-start(bf16[512,512]{1,0:T(8,128)(2,1)} %constant.46.clone.inverse_right_ref) | copy-start | bytes 1572868
  36.2 1.2 %copy-start.8 = (bf16[512,512]{1,0:T(8,128)(2,1)S(1)}, bf16[512,512]{1,0:T(8,128)(2,1)}, u32[]{:S(2)}) copy-start(bf16[512,512]{1,0:T(8,128)(2,1)} %constant.47.clone.band_columns_ref) | copy-start | bytes 1572868
  36.2 1.2 %copy-start.9 = (bf16[272,384]{1,0:T(8,128)(2,1)S(1)}, bf16[272,384]{1,0:T(8,128)(2,1)}, u32[]{:S(2)}) copy-start(bf16[272,384]{1,0:T(8,128)(2,1)} %constant.48.clone.band_rows_ref) | copy-start | bytes 626692
  41.0 5.2 %collective-permute-start.10 = (bf16[128,512]{1,0:T(8,128)(2,1)S(1)}, bf16[128,512]{1,0:T(8,128)(2,1)S(1)}, u32[]{:S(2)}, u32[]{:S(2)}) collective-permute-start(bf16[128,512]{1,0:T(8,128)(2,1)S(1)} %get-tuple-element.47), channel_id=1, source_target_pairs={{0,16},{1,17},{2,18},{3,19},{4,20},{5,21},{6,22},{7,23},{8,24},{9,... | collective-permute-start | bytes 393224 | tf_op jit(solution)/shard_map/ppermute | solution.py:365
  41.1 8.8 %collective-permute-start.9 = (bf16[128,512]{1,0:T(8,128)(2,1)S(1)}, bf16[128,512]{1,0:T(8,128)(2,1)S(1)}, u32[]{:S(2)}, u32[]{:S(2)}) collective-permute-start(bf16[128,512]{1,0:T(8,128)(2,1)S(1)} %get-tuple-element.46), channel_id=1, source_target_pairs={{0,1},{1,0},{2,3},{3,2},{4,5},{5,4},{6,7},{7,6},{8,9},{9,8},{10,11... | collective-permute-start | bytes 393224 | tf_op jit(solution)/shard_map/ppermute | solution.py:365
  50.1 5.1 %collective-permute-start.11 = (bf16[256,128]{1,0:T(8,128)(2,1)S(1)}, bf16[256,128]{1,0:T(8,128)(2,1)S(1)}, u32[]{:S(2)}, u32[]{:S(2)}) collective-permute-start(bf16[256,128]{1,0:T(8,128)(2,1)S(1)} %get-tuple-element.49), channel_id=1, source_target_pairs={{0,15},{1,2},{2,1},{3,4},{4,3},{5,6},{6,5},{7,8},{8,7},{9,10},{10,... | collective-permute-start | bytes 196616 | tf_op jit(solution)/shard_map/ppermute | solution.py:380
  50.5 4.7 %collective-permute-start.12 = (bf16[256,128]{1,0:T(8,128)(2,1)S(1)}, bf16[256,128]{1,0:T(8,128)(2,1)S(1)}, u32[]{:S(2)}, u32[]{:S(2)}) collective-permute-start(bf16[256,128]{1,0:T(8,128)(2,1)S(1)} %get-tuple-element.50), channel_id=1, source_target_pairs={{0,1},{1,0},{2,3},{3,2},{4,5},{5,4},{6,7},{7,6},{8,9},{9,8},{10,11... | collective-permute-start | bytes 196616 | tf_op jit(solution)/shard_map/ppermute | solution.py:380

commit v12 on v10

--- a/solution.py
+++ b/solution.py
@@ -412,9 +412,11 @@
 
     piece = jax.ShapeDtypeStruct((splits, margin, margin), BF16)
     strip = jax.ShapeDtypeStruct((splits, margin, half), BF16)
-    share = jax.ShapeDtypeStruct((splits // 2, margin, half), BF16)
+    aside = splits // 3
+    direct = jax.ShapeDtypeStruct((splits - aside, margin, half), BF16)
+    aside = jax.ShapeDtypeStruct((aside, margin, half), BF16)
     outer_first, outer_second, near, far, second = kernel_call(
-        functools.partial(cut_kernel, half), "cut", (piece, piece, share, share, strip), 1, vmem=8
+        functools.partial(cut_kernel, half), "cut", (piece, piece, direct, aside, strip), 1, vmem=8
     )(split_maps)
     outer_first = swap_columns(outer_first, 1)
     second = swap_rows(second, 0)

time: 52 us -> 50.6 us (0.973)
  waiting for transfers between devices: 14.9 us -> 11.6 us
  starting transfers between devices: 19.5 us -> 21.5 us
    ppermute x7, waiting for transfers between devices: 9.57 us -> 7.72 us  [swap_rows(): return lax.ppermute(values, ('dec', 'ra'), partners(offset, side))]
    ppermute x5, waiting for transfers between devices: 5.29 us -> 3.85 us  [swap_columns(): return lax.ppermute(values, 'ra', pairs)]
    ppermute x7, starting transfers between devices: 13 us -> 13.9 us  [swap_rows(): return lax.ppermute(values, ('dec', 'ra'), partners(offset, side))]
    ppermute x5, starting transfers between devices: 5.39 us -> 6.34 us  [swap_columns(): return lax.ppermute(values, 'ra', pairs)]
  transfers between devices with their start and end apart: 13 -> 13, of which waited for: 5 -> 5; matrix products, arithmetic and copies ran while one was open for 2% -> 2% of each run, Pallas kernels for 10% -> 11%
where the time goes in v12:
time: 50.6 us; the launch traced here: 50.4 us
  starting transfers between devices  21.5 us (42%)
  Pallas kernels  11.7 us (23%)
  waiting for transfers between devices  11.6 us (23%)
  local copies, waits for them, and re-layouts  4.62 us (9%)
  other arithmetic  0.8 us (2%)
    ppermute x7, starting transfers between devices, swap_rows(): return lax.ppermute(values, ('dec', 'ra'), partners(offset, side))  13.9 us
    ppermute x7, waiting for transfers between devices, swap_rows(): return lax.ppermute(values, ('dec', 'ra'), partners(offset, side))  7.72 us
    ppermute x5, starting transfers between devices, swap_columns(): return lax.ppermute(values, 'ra', pairs)  6.34 us
    unnamed x24, local copies, waits for them, and re-layouts  4.54 us
    ppermute x5, waiting for transfers between devices, swap_columns(): return lax.ppermute(values, 'ra', pairs)  3.85 us
    pallas_call x1, Pallas kernels, shards(): kernel_call(functools.partial(core_kernel, half), 'core_columns', (jax.Sh...  3.73 us
    pallas_call x1, Pallas kernels, shards(): kernel_call(functools.partial(main_kernel, half, scale), 'tile_model', (s...  3.56 us
    ppermute x1, starting transfers between devices, swap_beside(): return lax.ppermute(values, ('dec', 'ra'), pairs)  1.2 us
  transfers between devices with their start and end apart: 13, of which 5 were waited for; matrix products, arithmetic and copies ran while one was open for 2% of the time, Pallas kernels for 11%

profile of v12, /device:TPU:4, one launch (start us, length us, event | category | flops | bytes accessed | tf_op | source)
XLA Modules:
  0.0 50.4 jit_solution(11297721723114123548)
XLA Ops:
  0.0 1.1 %copy-done = bf16[6,256,256]{2,1,0:T(8,128)(2,1)S(1)} copy-done((bf16[6,256,256]{2,1,0:T(8,128)(2,1)S(1)}, bf16[6,256,256]{2,1,0:T(8,128)(2,1)}, u32[]{:S(2)}) %copy-start) | copy-done | bytes 786456
  1.1 0.9 %cut.1 = (bf16[6,128,128]{2,1,0:T(8,128)(2,1)}, bf16[6,128,128]{2,1,0:T(8,128)(2,1)}, bf16[4,128,256]{2,1,0:T(8,128)(2,1)}, bf16[2,128,256]{2,1,0:T(8,128)(2,1)S(1)}, bf16[6,128,256]{2,1,0:T(8,128)(2,1)S(1)}) custom-call(bf16[6,256,256]{2,1,0:T(8,128)(2,1)S(1)} %copy-done), custom_call_target="tpu_custom_call" | custom-call | bytes 1048576 | tf_op jit(solution)/shard_map/cut/pallas_call | solution.py:418
  2.0 1.2 %collective-permute-start.1 = (bf16[2,128,256]{2,1,0:T(8,128)(2,1)S(1)}, bf16[2,128,256]{2,1,0:T(8,128)(2,1)S(1)}, u32[]{:S(2)}, u32[]{:S(2)}) collective-permute-start(bf16[2,128,256]{2,1,0:T(8,128)(2,1)S(1)} %get-tuple-element.26), channel_id=1, source_target_pairs={{0,1},{1,0},{2,3},{3,2},{4,5},{5,4},{6,7},{7,6},{8,9},{9,8},{10,11... | collective-permute-start | bytes 393224 | tf_op jit(solution)/shard_map/ppermute | solution.py:374
  3.2 2.4 %collective-permute-start.4 = (bf16[6,128,128]{2,1,0:T(8,128)(2,1)}, bf16[6,128,128]{2,1,0:T(8,128)(2,1)S(1)}, u32[]{:S(2)}, u32[]{:S(2)}) collective-permute-start(bf16[6,128,128]{2,1,0:T(8,128)(2,1)} %get-tuple-element.28), channel_id=1, source_target_pairs={{0,15},{1,2},{2,1},{3,4},{4,3},{5,6},{6,5},{7,8},{8,7},{9,10},{10,... | collective-permute-start | bytes 589832 | tf_op jit(solution)/shard_map/ppermute | solution.py:380
  5.7 1.4 %collective-permute-start.5 = (bf16[6,128,128]{2,1,0:T(8,128)(2,1)}, bf16[6,128,128]{2,1,0:T(8,128)(2,1)S(1)}, u32[]{:S(2)}, u32[]{:S(2)}) collective-permute-start(bf16[6,128,128]{2,1,0:T(8,128)(2,1)} %get-tuple-element.29), channel_id=1, source_target_pairs={{0,15},{1,2},{2,1},{3,4},{4,3},{5,6},{6,5},{7,8},{8,7},{9,10},{10,... | collective-permute-start | bytes 589832 | tf_op jit(solution)/shard_map/ppermute | solution.py:380
  7.1 0.7 %collective-permute-start.3 = (bf16[6,128,256]{2,1,0:T(8,128)(2,1)S(1)}, bf16[6,128,256]{2,1,0:T(8,128)(2,1)S(1)}, u32[]{:S(2)}, u32[]{:S(2)}) collective-permute-start(bf16[6,128,256]{2,1,0:T(8,128)(2,1)S(1)} %get-tuple-element.27), channel_id=1, source_target_pairs={{0,16},{1,17},{2,18},{3,19},{4,20},{5,21},{6,22},{7,23},{8,24},{9,... | collective-permute-start | bytes 1179656 | tf_op jit(solution)/shard_map/ppermute | solution.py:365
  7.8 5.4 %collective-permute-start = (bf16[4,128,256]{2,1,0:T(8,128)(2,1)}, bf16[4,128,256]{2,1,0:T(8,128)(2,1)S(1)}, u32[]{:S(2)}, u32[]{:S(2)}) collective-permute-start(bf16[4,128,256]{2,1,0:T(8,128)(2,1)} %get-tuple-element.25), channel_id=1, source_target_pairs={{0,1},{1,0},{2,3},{3,2},{4,5},{5,4},{6,7},{7,6},{8,9},{9,8},{10,11... | collective-permute-start | bytes 786440 | tf_op jit(solution)/shard_map/ppermute | solution.py:365
  13.2 0.7 %broadcast_select_fusion = bf16[2,128,256]{2,1,0:T(8,128)(2,1)} fusion(bf16[2,128,256]{2,1,0:T(8,128)(2,1)S(1)} %collective-permute-done.1, bf16[2,128,256]{2,1,0:T(8,128)(2,1)S(1)} %get-tuple-element.26, pred[]{:T(512)S(6)} %or.3), kind=kLoop, calls=%fused_computation.4 | loop fusion | flops 65536 | bytes 393217 | tf_op jit(solution)/shard_map/jit(_where)/select_n | solution.py:427
  13.9 1.1 %collective-permute-start.2 = (bf16[2,128,256]{2,1,0:T(8,128)(2,1)}, bf16[2,128,256]{2,1,0:T(8,128)(2,1)S(1)}, u32[]{:S(2)}, u32[]{:S(2)}) collective-permute-start(bf16[2,128,256]{2,1,0:T(8,128)(2,1)} %broadcast_select_fusion), channel_id=1, source_target_pairs={{0,1},{1,0},{2,3},{3,2},{4,5},{5,4},{6,7},{7,6},{8,9},{9,8},{10,11... | collective-permute-start | bytes 393224 | tf_op jit(solution)/shard_map/ppermute | solution.py:365
  14.9 1.0 %copy-done.3 = bf16[528,512]{1,0:T(8,128)(2,1)S(1)} copy-done((bf16[528,512]{1,0:T(8,128)(2,1)S(1)}, bf16[528,512]{1,0:T(8,128)(2,1)}, u32[]{:S(2)}) %copy-start.3) | copy-done | bytes 540696
  16.0 1.0 %copy-done.5 = bf16[512,512]{1,0:T(8,128)(2,1)S(1)} copy-done((bf16[512,512]{1,0:T(8,128)(2,1)S(1)}, bf16[512,512]{1,0:T(8,128)(2,1)}, u32[]{:S(2)}) %copy-start.5) | copy-done | bytes 524312
  17.0 1.0 %copy-done.11 = bf16[512,512]{1,0:T(8,128)(2,1)S(1)} copy-done((bf16[512,512]{1,0:T(8,128)(2,1)S(1)}, bf16[512,512]{1,0:T(8,128)(2,1)}, u32[]{:S(2)}) %copy-start.11) | copy-done | bytes 524312
  18.1 0.9 %noise_spectrum.1 = (f32[264,512]{1,0:T(8,128)S(1)}, f32[264,512]{1,0:T(8,128)S(1)}) custom-call(bf16[512,512]{1,0:T(8,128)(2,1)S(1)} %copy-done.11, bf16[528,512]{1,0:T(8,128)(2,1)S(1)} %copy-done.3, bf16[512,512]{1,0:T(8,128)(2,1)S(1)} %copy-done.5), custom_call_target="tpu_custom_call" | custom-call | flops 6710886400 | bytes 1048576 | tf_op jit(solution)/shard_map/noise_spectrum/pallas_call | solution.py:431
  19.1 2.7 %collective-permute-start.6 = (bf16[6,128,128]{2,1,0:T(8,128)(2,1)S(1)}, bf16[6,128,128]{2,1,0:T(8,128)(2,1)S(1)}, u32[]{:S(2)}, u32[]{:S(2)}) collective-permute-start(bf16[6,128,128]{2,1,0:T(8,128)(2,1)S(1)} %collective-permute-done.4.outer_first_ref), channel_id=1, source_target_pairs={{0,1},{1,0},{2,3},{3,2},{4,5},{5,4},{6,7},{7,6},{8,9},{9,8},{10,11... | collective-permute-start | bytes 589832 | tf_op jit(solution)/shard_map/ppermute | solution.py:365
  21.9 0.1 fusion
  22.0 0.4 collective-permute-start.8
  22.4 3.7 %core_columns.1 = (f32[6,528,512]{2,1,0:T(8,128)S(1)}, bf16[6,512,128]{2,1,0:T(8,128)(2,1)S(1)}) custom-call(bf16[6,256,256]{2,1,0:T(8,128)(2,1)S(1)} %copy-done.1, bf16[4,128,256]{2,1,0:T(8,128)(2,1)S(1)} %collective-permute-done.near_ref, bf16[2,128,256]{2,1,0:T(8,128)(2,1)S(1)} %collective-permute-done.2.far_ref, ...), custom_call_target="tpu_custom_call" | custom-call | flops 134217728 | bytes 1048576 | tf_op jit(solution)/shard_map/core_columns/pallas_call | solution.py:461
  26.1 2.4 %collective-permute-done.6.first_ref = bf16[6,128,128]{2,1,0:T(8,128)(2,1)S(1)} collective-permute-done((bf16[6,128,128]{2,1,0:T(8,128)(2,1)S(1)}, bf16[6,128,128]{2,1,0:T(8,128)(2,1)S(1)}, u32[]{:S(2)}, u32[]{:S(2)}) %collective-permute-start.6) | collective-permute-done | bytes 196640 | tf_op jit(solution)/shard_map/ppermute | solution.py:365
  28.5 0.4 collective-permute-done.7.second_ref
  28.9 0.8 %outer_columns.1.after_ref.outer_ref = bf16[6,528,128]{2,1,0:T(8,128)(2,1)S(1)} custom-call(f32[6,528,512]{2,1,0:T(8,128)S(1)} %get-tuple-element.35.after_ref.core_ref, bf16[6,512,128]{2,1,0:T(8,128)(2,1)S(1)} %get-tuple-element.36.tile, bf16[6,128,128]{2,1,0:T(8,128)(2,1)S(1)} %collective-permute-done.6.first_ref, ...), custom_call_target="tpu_custom_call" | custom-call | flops 53687091200 | bytes 1048576 | tf_op jit(solution)/shard_map/outer_columns/pallas_call | solution.py:472
  29.8 1.0 %inner_columns.1.inner_ref = bf16[6,528,128]{2,1,0:T(8,128)(2,1)S(1)} custom-call(bf16[6,528,128]{2,1,0:T(8,128)(2,1)S(1)} %outer_columns.1.after_ref.outer_ref, bf16[6,512,128]{2,1,0:T(8,128)(2,1)S(1)} %collective-permute-done.8.inner_ref, f32[512,128]{1,0:T(8,128)S(1)} %copy-done.2, f32[8,512]{1,0:T(8,128)S(1)} %copy-done.10, bf16[528,512]{1,0:T(8,128)(2,1)S(1)} %copy-done.4), custom_call_target="tpu_custom_call" | custom-call | flops 134217728 | bytes 1048576 | tf_op jit(solution)/shard_map/inner_columns/pallas_call | solution.py:475
  30.8 0.2 copy-done.8
  31.0 3.6 %tile_model.1 = (bf16[128,512]{1,0:T(8,128)(2,1)S(1)}, bf16[128,512]{1,0:T(8,128)(2,1)S(1)}, f32[256,512]{1,0:T(8,128)S(1)}) custom-call(f32[6,528,512]{2,1,0:T(8,128)S(1)} %get-tuple-element.35.after_ref.core_ref, bf16[6,528,128]{2,1,0:T(8,128)(2,1)S(1)} %inner_columns.1.inner_ref, bf16[6,528,128]{2,1,0:T(8,128)(2,1)S(1)} %outer_columns.1.after_ref.outer_ref, ...), custom_call_target="tpu_custom_call" | custom-call | flops 2684354560 | bytes 1048576 | tf_op jit(solution)/shard_map/tile_model/pallas_call | solution.py:478
  34.5 0.4 collective-permute-start.10
  34.9 3.7 %collective-permute-start.9 = (bf16[128,512]{1,0:T(8,128)(2,1)S(1)}, bf16[128,512]{1,0:T(8,128)(2,1)S(1)}, u32[]{:S(2)}, u32[]{:S(2)}) collective-permute-start(bf16[128,512]{1,0:T(8,128)(2,1)S(1)} %get-tuple-element.40), channel_id=1, source_target_pairs={{0,1},{1,0},{2,3},{3,2},{4,5},{5,4},{6,7},{7,6},{8,9},{9,8},{10,11... | collective-permute-start | bytes 393224 | tf_op jit(solution)/shard_map/ppermute | solution.py:365
  38.6 1.0 %collective-permute-done.10.second_ref = bf16[128,512]{1,0:T(8,128)(2,1)S(1)} collective-permute-done((bf16[128,512]{1,0:T(8,128)(2,1)S(1)}, bf16[128,512]{1,0:T(8,128)(2,1)S(1)}, u32[]{:S(2)}, u32[]{:S(2)}) %collective-permute-start.10) | collective-permute-done | bytes 131104 | tf_op jit(solution)/shard_map/ppermute | solution.py:365
  39.6 4.0 %collective-permute-done.9.first_ref = bf16[128,512]{1,0:T(8,128)(2,1)S(1)} collective-permute-done((bf16[128,512]{1,0:T(8,128)(2,1)S(1)}, bf16[128,512]{1,0:T(8,128)(2,1)S(1)}, u32[]{:S(2)}, u32[]{:S(2)}) %collective-permute-start.9) | collective-permute-done | bytes 131104 | tf_op jit(solution)/shard_map/ppermute | solution.py:365
  43.5 0.1 fold_rows.1
  43.7 1.3 %collective-permute-start.11 = (bf16[256,128]{1,0:T(8,128)(2,1)S(1)}, bf16[256,128]{1,0:T(8,128)(2,1)S(1)}, u32[]{:S(2)}, u32[]{:S(2)}) collective-permute-start(bf16[256,128]{1,0:T(8,128)(2,1)S(1)} %get-tuple-element.43), channel_id=1, source_target_pairs={{0,15},{1,2},{2,1},{3,4},{4,3},{5,6},{6,5},{7,8},{8,7},{9,10},{10,... | collective-permute-start | bytes 196616 | tf_op jit(solution)/shard_map/ppermute | solution.py:380
  44.9 0.9 %collective-permute-start.12 = (bf16[256,128]{1,0:T(8,128)(2,1)S(1)}, bf16[256,128]{1,0:T(8,128)(2,1)S(1)}, u32[]{:S(2)}, u32[]{:S(2)}) collective-permute-start(bf16[256,128]{1,0:T(8,128)(2,1)S(1)} %get-tuple-element.44), channel_id=1, source_target_pairs={{0,1},{1,0},{2,3},{3,2},{4,5},{5,4},{6,7},{7,6},{8,9},{9,8},{10,11... | collective-permute-start | bytes 196616 | tf_op jit(solution)/shard_map/ppermute | solution.py:380
  45.8 3.8 %collective-permute-done.11.outer_ref = bf16[256,128]{1,0:T(8,128)(2,1)S(1)} collective-permute-done((bf16[256,128]{1,0:T(8,128)(2,1)S(1)}, bf16[256,128]{1,0:T(8,128)(2,1)S(1)}, u32[]{:S(2)}, u32[]{:S(2)}) %collective-permute-start.11) | collective-permute-done | bytes 65568 | tf_op jit(solution)/shard_map/ppermute | solution.py:380
  49.6 0.7 %fold_columns.1 = f32[256,256]{1,0:T(8,128)} custom-call(f32[256,256]{1,0:T(8,128)S(1)} %get-tuple-element.42.center_ref, bf16[256,128]{1,0:T(8,128)(2,1)S(1)} %collective-permute-done.11.outer_ref, bf16[256,128]{1,0:T(8,128)(2,1)S(1)} %collective-permute-done.12.inner_ref), custom_call_target="tpu_custom_call" | custom-call | bytes 1048576 | tf_op jit(solution)/shard_map/fold_columns/pallas_call | solution.py:506
  (30 shorter events, 0.3 us)
Async XLA Ops:
  0.0 1.1 %copy-start = (bf16[6,256,256]{2,1,0:T(8,128)(2,1)S(1)}, bf16[6,256,256]{2,1,0:T(8,128)(2,1)}, u32[]{:S(2)}) copy-start(bf16[6,256,256]{2,1,0:T(8,128)(2,1)} %core_ref.1) | copy-start | bytes 2359300
  2.0 11.2 %collective-permute-start.1 = (bf16[2,128,256]{2,1,0:T(8,128)(2,1)S(1)}, bf16[2,128,256]{2,1,0:T(8,128)(2,1)S(1)}, u32[]{:S(2)}, u32[]{:S(2)}) collective-permute-start(bf16[2,128,256]{2,1,0:T(8,128)(2,1)S(1)} %get-tuple-element.26), channel_id=1, source_target_pairs={{0,1},{1,0},{2,3},{3,2},{4,5},{5,4},{6,7},{7,6},{8,9},{9,8},{10,11... | collective-permute-start | bytes 393224 | tf_op jit(solution)/shard_map/ppermute | solution.py:374
  3.2 15.9 %collective-permute-start.4 = (bf16[6,128,128]{2,1,0:T(8,128)(2,1)}, bf16[6,128,128]{2,1,0:T(8,128)(2,1)S(1)}, u32[]{:S(2)}, u32[]{:S(2)}) collective-permute-start(bf16[6,128,128]{2,1,0:T(8,128)(2,1)} %get-tuple-element.28), channel_id=1, source_target_pairs={{0,15},{1,2},{2,1},{3,4},{4,3},{5,6},{6,5},{7,8},{8,7},{9,10},{10,... | collective-permute-start | bytes 589832 | tf_op jit(solution)/shard_map/ppermute | solution.py:380
  5.7 16.1 %collective-permute-start.5 = (bf16[6,128,128]{2,1,0:T(8,128)(2,1)}, bf16[6,128,128]{2,1,0:T(8,128)(2,1)S(1)}, u32[]{:S(2)}, u32[]{:S(2)}) collective-permute-start(bf16[6,128,128]{2,1,0:T(8,128)(2,1)} %get-tuple-element.29), channel_id=1, source_target_pairs={{0,15},{1,2},{2,1},{3,4},{4,3},{5,6},{6,5},{7,8},{8,7},{9,10},{10,... | collective-permute-start | bytes 589832 | tf_op jit(solution)/shard_map/ppermute | solution.py:380
  7.1 14.7 %collective-permute-start.3 = (bf16[6,128,256]{2,1,0:T(8,128)(2,1)S(1)}, bf16[6,128,256]{2,1,0:T(8,128)(2,1)S(1)}, u32[]{:S(2)}, u32[]{:S(2)}) collective-permute-start(bf16[6,128,256]{2,1,0:T(8,128)(2,1)S(1)} %get-tuple-element.27), channel_id=1, source_target_pairs={{0,16},{1,17},{2,18},{3,19},{4,20},{5,21},{6,22},{7,23},{8,24},{9,... | collective-permute-start | bytes 1179656 | tf_op jit(solution)/shard_map/ppermute | solution.py:365
  7.8 14.0 %collective-permute-start = (bf16[4,128,256]{2,1,0:T(8,128)(2,1)}, bf16[4,128,256]{2,1,0:T(8,128)(2,1)S(1)}, u32[]{:S(2)}, u32[]{:S(2)}) collective-permute-start(bf16[4,128,256]{2,1,0:T(8,128)(2,1)} %get-tuple-element.25), channel_id=1, source_target_pairs={{0,1},{1,0},{2,3},{3,2},{4,5},{5,4},{6,7},{7,6},{8,9},{9,8},{10,11... | collective-permute-start | bytes 786440 | tf_op jit(solution)/shard_map/ppermute | solution.py:365
  13.9 5.1 %copy-start.1 = (bf16[6,256,256]{2,1,0:T(8,128)(2,1)S(1)}, bf16[6,256,256]{2,1,0:T(8,128)(2,1)}, u32[]{:S(2)}) copy-start(bf16[6,256,256]{2,1,0:T(8,128)(2,1)} %core_ref.1) | copy-start | bytes 2359300
  13.9 8.0 %collective-permute-start.2 = (bf16[2,128,256]{2,1,0:T(8,128)(2,1)}, bf16[2,128,256]{2,1,0:T(8,128)(2,1)S(1)}, u32[]{:S(2)}, u32[]{:S(2)}) collective-permute-start(bf16[2,128,256]{2,1,0:T(8,128)(2,1)} %broadcast_select_fusion), channel_id=1, source_target_pairs={{0,1},{1,0},{2,3},{3,2},{4,5},{5,4},{6,7},{7,6},{8,9},{9,8},{10,11... | collective-permute-start | bytes 393224 | tf_op jit(solution)/shard_map/ppermute | solution.py:365
  14.9 1.0 %copy-start.3 = (bf16[528,512]{1,0:T(8,128)(2,1)S(1)}, bf16[528,512]{1,0:T(8,128)(2,1)}, u32[]{:S(2)}) copy-start(bf16[528,512]{1,0:T(8,128)(2,1)} %constant.44.clone.left_ref) | copy-start | bytes 1622020
  16.0 1.0 %copy-start.5 = (bf16[512,512]{1,0:T(8,128)(2,1)S(1)}, bf16[512,512]{1,0:T(8,128)(2,1)}, u32[]{:S(2)}) copy-start(bf16[512,512]{1,0:T(8,128)(2,1)} %constant.45.clone.right_ref) | copy-start | bytes 1572868
  17.0 1.0 %copy-start.11 = (bf16[512,512]{1,0:T(8,128)(2,1)S(1)}, bf16[512,512]{1,0:T(8,128)(2,1)}, u32[]{:S(2)}) copy-start(bf16[512,512]{1,0:T(8,128)(2,1)} %noise_ref.1) | copy-start | bytes 1572868
  19.0 3.4 %copy-start.2 = (f32[512,128]{1,0:T(8,128)S(1)}, f32[512,128]{1,0:T(8,128)}, u32[]{:S(2)}) copy-start(f32[512,128]{1,0:T(8,128)} %constant.49.clone.rows_ref) | copy-start | bytes 786436
  19.0 3.4 %copy-start.4 = (bf16[528,512]{1,0:T(8,128)(2,1)S(1)}, bf16[528,512]{1,0:T(8,128)(2,1)}, u32[]{:S(2)}) copy-start(bf16[528,512]{1,0:T(8,128)(2,1)} %constant.44.clone.left_ref) | copy-start | bytes 1622020
  19.0 3.4 %copy-start.6 = (bf16[512,512]{1,0:T(8,128)(2,1)S(1)}, bf16[512,512]{1,0:T(8,128)(2,1)}, u32[]{:S(2)}) copy-start(bf16[512,512]{1,0:T(8,128)(2,1)} %constant.45.clone.right_ref) | copy-start | bytes 1572868
  19.0 3.4 %copy-start.10 = (f32[8,512]{1,0:T(8,128)S(1)}, f32[8,512]{1,0:T(8,128)}, u32[]{:S(2)}) copy-start(f32[8,512]{1,0:T(8,128)} %constant.50.clone.cols_ref) | copy-start | bytes 49156
  19.1 9.4 %collective-permute-start.6 = (bf16[6,128,128]{2,1,0:T(8,128)(2,1)S(1)}, bf16[6,128,128]{2,1,0:T(8,128)(2,1)S(1)}, u32[]{:S(2)}, u32[]{:S(2)}) collective-permute-start(bf16[6,128,128]{2,1,0:T(8,128)(2,1)S(1)} %collective-permute-done.4.outer_first_ref), channel_id=1, source_target_pairs={{0,1},{1,0},{2,3},{3,2},{4,5},{5,4},{6,7},{7,6},{8,9},{9,8},{10,11... | collective-permute-start | bytes 589832 | tf_op jit(solution)/shard_map/ppermute | solution.py:365
  21.8 7.1 %collective-permute-start.7 = (bf16[6,128,128]{2,1,0:T(8,128)(2,1)S(1)}, bf16[6,128,128]{2,1,0:T(8,128)(2,1)S(1)}, u32[]{:S(2)}, u32[]{:S(2)}) collective-permute-start(bf16[6,128,128]{2,1,0:T(8,128)(2,1)S(1)} %collective-permute-done.5.outer_second_ref), channel_id=1, source_target_pairs={{0,16},{1,17},{2,18},{3,19},{4,20},{5,21},{6,22},{7,23},{8,24},{9,... | collective-permute-start | bytes 589832 | tf_op jit(solution)/shard_map/ppermute | solution.py:365
  22.0 7.7 %collective-permute-start.8 = (bf16[6,512,128]{2,1,0:T(8,128)(2,1)S(1)}, bf16[6,512,128]{2,1,0:T(8,128)(2,1)S(1)}, u32[]{:S(2)}, u32[]{:S(2)}) collective-permute-start(bf16[6,512,128]{2,1,0:T(8,128)(2,1)S(1)} %pad_maximum_fusion), channel_id=1, source_target_pairs={{0,1},{1,0},{2,3},{3,2},{4,5},{5,4},{6,7},{7,6},{8,9},{9,8},{10,11... | collective-permute-start | bytes 2359304 | tf_op jit(solution)/shard_map/ppermute | solution.py:380
  29.7 1.0 %copy-start.7 = (bf16[512,512]{1,0:T(8,128)(2,1)S(1)}, bf16[512,512]{1,0:T(8,128)(2,1)}, u32[]{:S(2)}) copy-start(bf16[512,512]{1,0:T(8,128)(2,1)} %constant.46.clone.inverse_right_ref) | copy-start | bytes 1572868
  29.7 1.2 %copy-start.8 = (bf16[512,512]{1,0:T(8,128)(2,1)S(1)}, bf16[512,512]{1,0:T(8,128)(2,1)}, u32[]{:S(2)}) copy-start(bf16[512,512]{1,0:T(8,128)(2,1)} %constant.47.clone.band_columns_ref) | copy-start | bytes 1572868
  29.7 1.2 %copy-start.9 = (bf16[272,384]{1,0:T(8,128)(2,1)S(1)}, bf16[272,384]{1,0:T(8,128)(2,1)}, u32[]{:S(2)}) copy-start(bf16[272,384]{1,0:T(8,128)(2,1)} %constant.48.clone.band_rows_ref) | copy-start | bytes 626692
  34.5 5.1 %collective-permute-start.10 = (bf16[128,512]{1,0:T(8,128)(2,1)S(1)}, bf16[128,512]{1,0:T(8,128)(2,1)S(1)}, u32[]{:S(2)}, u32[]{:S(2)}) collective-permute-start(bf16[128,512]{1,0:T(8,128)(2,1)S(1)} %get-tuple-element.41), channel_id=1, source_target_pairs={{0,16},{1,17},{2,18},{3,19},{4,20},{5,21},{6,22},{7,23},{8,24},{9,... | collective-permute-start | bytes 393224 | tf_op jit(solution)/shard_map/ppermute | solution.py:365
  34.9 8.6 %collective-permute-start.9 = (bf16[128,512]{1,0:T(8,128)(2,1)S(1)}, bf16[128,512]{1,0:T(8,128)(2,1)S(1)}, u32[]{:S(2)}, u32[]{:S(2)}) collective-permute-start(bf16[128,512]{1,0:T(8,128)(2,1)S(1)} %get-tuple-element.40), channel_id=1, source_target_pairs={{0,1},{1,0},{2,3},{3,2},{4,5},{5,4},{6,7},{7,6},{8,9},{9,8},{10,11... | collective-permute-start | bytes 393224 | tf_op jit(solution)/shard_map/ppermute | solution.py:365
  43.7 6.0 %collective-permute-start.11 = (bf16[256,128]{1,0:T(8,128)(2,1)S(1)}, bf16[256,128]{1,0:T(8,128)(2,1)S(1)}, u32[]{:S(2)}, u32[]{:S(2)}) collective-permute-start(bf16[256,128]{1,0:T(8,128)(2,1)S(1)} %get-tuple-element.43), channel_id=1, source_target_pairs={{0,15},{1,2},{2,1},{3,4},{4,3},{5,6},{6,5},{7,8},{8,7},{9,10},{10,... | collective-permute-start | bytes 196616 | tf_op jit(solution)/shard_map/ppermute | solution.py:380
  44.9 4.7 %collective-permute-start.12 = (bf16[256,128]{1,0:T(8,128)(2,1)S(1)}, bf16[256,128]{1,0:T(8,128)(2,1)S(1)}, u32[]{:S(2)}, u32[]{:S(2)}) collective-permute-start(bf16[256,128]{1,0:T(8,128)(2,1)S(1)} %get-tuple-element.44), channel_id=1, source_target_pairs={{0,1},{1,0},{2,3},{3,2},{4,5},{5,4},{6,7},{7,6},{8,9},{9,8},{10,11... | collective-permute-start | bytes 196616 | tf_op jit(solution)/shard_map/ppermute | solution.py:380

commit v13 on v12

--- a/solution.py
+++ b/solution.py
@@ -412,7 +412,7 @@
 
     piece = jax.ShapeDtypeStruct((splits, margin, margin), BF16)
     strip = jax.ShapeDtypeStruct((splits, margin, half), BF16)
-    aside = splits // 3
+    aside = 2 * splits // 3
     direct = jax.ShapeDtypeStruct((splits - aside, margin, half), BF16)
     aside = jax.ShapeDtypeStruct((aside, margin, half), BF16)
     outer_first, outer_second, near, far, second = kernel_call(

time: 50.6 us -> 52.1 us (1.030)
  the two profiles are of different devices: /device:TPU:4 before, /device:TPU:15 now
where the time goes in v13:
time: 52.1 us; the launch traced here: 51.9 us
  starting transfers between devices  22.1 us (42%)
  Pallas kernels  12.7 us (24%)
  waiting for transfers between devices  12.6 us (24%)
  local copies, waits for them, and re-layouts  3.48 us (7%)
  other arithmetic  0.85 us (2%)
    ppermute x7, starting transfers between devices, swap_rows(): return lax.ppermute(values, ('dec', 'ra'), partners(offset, side))  16.2 us
    ppermute x7, waiting for transfers between devices, swap_rows(): return lax.ppermute(values, ('dec', 'ra'), partners(offset, side))  8.48 us
    ppermute x5, starting transfers between devices, swap_columns(): return lax.ppermute(values, 'ra', pairs)  5.27 us
    pallas_call x1, Pallas kernels, shards(): kernel_call(functools.partial(core_kernel, half), 'core_columns', (jax.Sh...  4.64 us
    ppermute x5, waiting for transfers between devices, swap_columns(): return lax.ppermute(values, 'ra', pairs)  4.14 us
    pallas_call x1, Pallas kernels, shards(): kernel_call(functools.partial(main_kernel, half, scale), 'tile_model', (s...  3.57 us
    unnamed x24, local copies, waits for them, and re-layouts  3.42 us
  transfers between devices with their start and end apart: 13, of which 4 were waited for; matrix products, arithmetic and copies ran while one was open for 2% of the time, Pallas kernels for 12%

profile of v13, /device:TPU:15, one launch (start us, length us, event | category | flops | bytes accessed | tf_op | source)
XLA Modules:
  0.0 51.9 jit_solution(6479447904954311234)
XLA Ops:
  0.0 1.1 %copy-done = bf16[6,256,256]{2,1,0:T(8,128)(2,1)S(1)} copy-done((bf16[6,256,256]{2,1,0:T(8,128)(2,1)S(1)}, bf16[6,256,256]{2,1,0:T(8,128)(2,1)}, u32[]{:S(2)}) %copy-start) | copy-done | bytes 786456
  1.1 1.0 %cut.1 = (bf16[6,128,128]{2,1,0:T(8,128)(2,1)}, bf16[6,128,128]{2,1,0:T(8,128)(2,1)}, bf16[2,128,256]{2,1,0:T(8,128)(2,1)S(1)}, bf16[4,128,256]{2,1,0:T(8,128)(2,1)S(1)}, bf16[6,128,256]{2,1,0:T(8,128)(2,1)}) custom-call(bf16[6,256,256]{2,1,0:T(8,128)(2,1)S(1)} %copy-done), custom_call_target="tpu_custom_call" | custom-call | bytes 1048576 | tf_op jit(solution)/shard_map/cut/pallas_call | solution.py:418
  2.1 0.5 %collective-permute-start.1 = (bf16[4,128,256]{2,1,0:T(8,128)(2,1)S(1)}, bf16[4,128,256]{2,1,0:T(8,128)(2,1)S(1)}, u32[]{:S(2)}, u32[]{:S(2)}) collective-permute-start(bf16[4,128,256]{2,1,0:T(8,128)(2,1)S(1)} %get-tuple-element.26), channel_id=1, source_target_pairs={{0,1},{1,0},{2,3},{3,2},{4,5},{5,4},{6,7},{7,6},{8,9},{9,8},{10,11... | collective-permute-start | bytes 786440 | tf_op jit(solution)/shard_map/ppermute | solution.py:374
  2.7 2.8 %collective-permute-start.4 = (bf16[6,128,128]{2,1,0:T(8,128)(2,1)}, bf16[6,128,128]{2,1,0:T(8,128)(2,1)S(1)}, u32[]{:S(2)}, u32[]{:S(2)}) collective-permute-start(bf16[6,128,128]{2,1,0:T(8,128)(2,1)} %get-tuple-element.28), channel_id=1, source_target_pairs={{0,15},{1,2},{2,1},{3,4},{4,3},{5,6},{6,5},{7,8},{8,7},{9,10},{10,... | collective-permute-start | bytes 589832 | tf_op jit(solution)/shard_map/ppermute | solution.py:380
  5.5 1.6 %collective-permute-start.3 = (bf16[6,128,256]{2,1,0:T(8,128)(2,1)}, bf16[6,128,256]{2,1,0:T(8,128)(2,1)S(1)}, u32[]{:S(2)}, u32[]{:S(2)}) collective-permute-start(bf16[6,128,256]{2,1,0:T(8,128)(2,1)} %get-tuple-element.27), channel_id=1, source_target_pairs={{0,16},{1,17},{2,18},{3,19},{4,20},{5,21},{6,22},{7,23},{8,24},{9,... | collective-permute-start | bytes 1179656 | tf_op jit(solution)/shard_map/ppermute | solution.py:365
  7.1 5.5 %collective-permute-start = (bf16[2,128,256]{2,1,0:T(8,128)(2,1)S(1)}, bf16[2,128,256]{2,1,0:T(8,128)(2,1)S(1)}, u32[]{:S(2)}, u32[]{:S(2)}) collective-permute-start(bf16[2,128,256]{2,1,0:T(8,128)(2,1)S(1)} %get-tuple-element.25), channel_id=1, source_target_pairs={{0,1},{1,0},{2,3},{3,2},{4,5},{5,4},{6,7},{7,6},{8,9},{9,8},{10,11... | collective-permute-start | bytes 393224 | tf_op jit(solution)/shard_map/ppermute | solution.py:365
  12.6 0.7 %broadcast_select_fusion = bf16[4,128,256]{2,1,0:T(8,128)(2,1)} fusion(bf16[4,128,256]{2,1,0:T(8,128)(2,1)S(1)} %collective-permute-done.1, bf16[4,128,256]{2,1,0:T(8,128)(2,1)S(1)} %get-tuple-element.26, pred[]{:T(512)S(6)} %or.3), kind=kLoop, calls=%fused_computation.3 | loop fusion | flops 131072 | bytes 786433 | tf_op jit(solution)/shard_map/jit(_where)/select_n | solution.py:427
  13.3 2.2 %collective-permute-start.2 = (bf16[4,128,256]{2,1,0:T(8,128)(2,1)}, bf16[4,128,256]{2,1,0:T(8,128)(2,1)S(1)}, u32[]{:S(2)}, u32[]{:S(2)}) collective-permute-start(bf16[4,128,256]{2,1,0:T(8,128)(2,1)} %broadcast_select_fusion), channel_id=1, source_target_pairs={{0,1},{1,0},{2,3},{3,2},{4,5},{5,4},{6,7},{7,6},{8,9},{9,8},{10,11... | collective-permute-start | bytes 786440 | tf_op jit(solution)/shard_map/ppermute | solution.py:365
  15.5 1.0 %copy-done.11 = bf16[512,512]{1,0:T(8,128)(2,1)S(1)} copy-done((bf16[512,512]{1,0:T(8,128)(2,1)S(1)}, bf16[512,512]{1,0:T(8,128)(2,1)}, u32[]{:S(2)}) %copy-start.11) | copy-done | bytes 524312
  16.6 0.9 %noise_spectrum.1 = (f32[264,512]{1,0:T(8,128)S(1)}, f32[264,512]{1,0:T(8,128)S(1)}) custom-call(bf16[512,512]{1,0:T(8,128)(2,1)S(1)} %copy-done.11, bf16[528,512]{1,0:T(8,128)(2,1)S(1)} %copy-done.3, bf16[512,512]{1,0:T(8,128)(2,1)S(1)} %copy-done.4), custom_call_target="tpu_custom_call" | custom-call | flops 6710886400 | bytes 1048576 | tf_op jit(solution)/shard_map/noise_spectrum/pallas_call | solution.py:431
  17.5 0.8 %copy-done.5 = f32[264,512]{1,0:T(8,128)} copy-done((f32[264,512]{1,0:T(8,128)}, f32[264,512]{1,0:T(8,128)S(1)}, u32[]{:S(2)}) %copy-start.5) | copy-done | bytes 540696
  18.3 0.1 constant_dynamic-slice_fusion.1
  18.4 4.6 %collective-permute-start.6 = (bf16[6,128,128]{2,1,0:T(8,128)(2,1)S(1)}, bf16[6,128,128]{2,1,0:T(8,128)(2,1)S(1)}, u32[]{:S(2)}, u32[]{:S(2)}) collective-permute-start(bf16[6,128,128]{2,1,0:T(8,128)(2,1)S(1)} %collective-permute-done.4.outer_first_ref), channel_id=1, source_target_pairs={{0,1},{1,0},{2,3},{3,2},{4,5},{5,4},{6,7},{7,6},{8,9},{9,8},{10,11... | collective-permute-start | bytes 589832 | tf_op jit(solution)/shard_map/ppermute | solution.py:365
  23.0 1.9 %collective-permute-done.2.far_ref = bf16[4,128,256]{2,1,0:T(8,128)(2,1)S(1)} collective-permute-done((bf16[4,128,256]{2,1,0:T(8,128)(2,1)}, bf16[4,128,256]{2,1,0:T(8,128)(2,1)S(1)}, u32[]{:S(2)}, u32[]{:S(2)}) %collective-permute-start.2) | collective-permute-done | bytes 262176 | tf_op jit(solution)/shard_map/ppermute | solution.py:365
  24.9 0.1 fusion
  25.0 0.1 pad_maximum_fusion
  25.0 1.5 %collective-permute-start.8 = (bf16[6,512,128]{2,1,0:T(8,128)(2,1)S(1)}, bf16[6,512,128]{2,1,0:T(8,128)(2,1)S(1)}, u32[]{:S(2)}, u32[]{:S(2)}) collective-permute-start(bf16[6,512,128]{2,1,0:T(8,128)(2,1)S(1)} %pad_maximum_fusion), channel_id=1, source_target_pairs={{0,1},{1,0},{2,3},{3,2},{4,5},{5,4},{6,7},{7,6},{8,9},{9,8},{10,11... | collective-permute-start | bytes 2359304 | tf_op jit(solution)/shard_map/ppermute | solution.py:380
  26.5 4.6 %core_columns.1 = (f32[6,528,512]{2,1,0:T(8,128)S(1)}, bf16[6,512,128]{2,1,0:T(8,128)(2,1)S(1)}) custom-call(bf16[6,256,256]{2,1,0:T(8,128)(2,1)S(1)} %copy-done.1, bf16[2,128,256]{2,1,0:T(8,128)(2,1)S(1)} %collective-permute-done.near_ref, bf16[4,128,256]{2,1,0:T(8,128)(2,1)S(1)} %collective-permute-done.2.far_ref, ...), custom_call_target="tpu_custom_call" | custom-call | flops 134217728 | bytes 1048576 | tf_op jit(solution)/shard_map/core_columns/pallas_call | solution.py:461
  31.2 0.8 %outer_columns.1.after_ref.outer_ref = bf16[6,528,128]{2,1,0:T(8,128)(2,1)S(1)} custom-call(f32[6,528,512]{2,1,0:T(8,128)S(1)} %get-tuple-element.35.after_ref.core_ref, bf16[6,512,128]{2,1,0:T(8,128)(2,1)S(1)} %get-tuple-element.36.tile, bf16[6,128,128]{2,1,0:T(8,128)(2,1)S(1)} %collective-permute-done.6.first_ref, ...), custom_call_target="tpu_custom_call" | custom-call | flops 53687091200 | bytes 1048576 | tf_op jit(solution)/shard_map/outer_columns/pallas_call | solution.py:472
  32.0 1.0 %inner_columns.1.inner_ref = bf16[6,528,128]{2,1,0:T(8,128)(2,1)S(1)} custom-call(bf16[6,528,128]{2,1,0:T(8,128)(2,1)S(1)} %outer_columns.1.after_ref.outer_ref, bf16[6,512,128]{2,1,0:T(8,128)(2,1)S(1)} %collective-permute-done.8.inner_ref, f32[512,128]{1,0:T(8,128)S(1)} %copy-done.2, f32[8,512]{1,0:T(8,128)S(1)} %copy-done.10, bf16[528,512]{1,0:T(8,128)(2,1)S(1)} %copy-done.3), custom_call_target="tpu_custom_call" | custom-call | flops 134217728 | bytes 1048576 | tf_op jit(solution)/shard_map/inner_columns/pallas_call | solution.py:475
  33.0 0.2 copy-done.7
  33.2 0.2 copy-done.8
  33.3 0.0 copy-done.9
  33.4 3.6 %tile_model.1 = (bf16[128,512]{1,0:T(8,128)(2,1)S(1)}, bf16[128,512]{1,0:T(8,128)(2,1)S(1)}, f32[256,512]{1,0:T(8,128)S(1)}) custom-call(f32[6,528,512]{2,1,0:T(8,128)S(1)} %get-tuple-element.35.after_ref.core_ref, bf16[6,528,128]{2,1,0:T(8,128)(2,1)S(1)} %inner_columns.1.inner_ref, bf16[6,528,128]{2,1,0:T(8,128)(2,1)S(1)} %outer_columns.1.after_ref.outer_ref, ...), custom_call_target="tpu_custom_call" | custom-call | flops 2684354560 | bytes 1048576 | tf_op jit(solution)/shard_map/tile_model/pallas_call | solution.py:478
  37.0 0.1 collective-permute-start.10
  37.1 2.3 %collective-permute-start.9 = (bf16[128,512]{1,0:T(8,128)(2,1)S(1)}, bf16[128,512]{1,0:T(8,128)(2,1)S(1)}, u32[]{:S(2)}, u32[]{:S(2)}) collective-permute-start(bf16[128,512]{1,0:T(8,128)(2,1)S(1)} %get-tuple-element.40), channel_id=1, source_target_pairs={{0,1},{1,0},{2,3},{3,2},{4,5},{5,4},{6,7},{7,6},{8,9},{9,8},{10,11... | collective-permute-start | bytes 393224 | tf_op jit(solution)/shard_map/ppermute | solution.py:365
  39.3 2.8 %collective-permute-done.10.second_ref = bf16[128,512]{1,0:T(8,128)(2,1)S(1)} collective-permute-done((bf16[128,512]{1,0:T(8,128)(2,1)S(1)}, bf16[128,512]{1,0:T(8,128)(2,1)S(1)}, u32[]{:S(2)}, u32[]{:S(2)}) %collective-permute-start.10) | collective-permute-done | bytes 131104 | tf_op jit(solution)/shard_map/ppermute | solution.py:365
  42.1 3.7 %collective-permute-done.9.first_ref = bf16[128,512]{1,0:T(8,128)(2,1)S(1)} collective-permute-done((bf16[128,512]{1,0:T(8,128)(2,1)S(1)}, bf16[128,512]{1,0:T(8,128)(2,1)S(1)}, u32[]{:S(2)}, u32[]{:S(2)}) %collective-permute-start.9) | collective-permute-done | bytes 131104 | tf_op jit(solution)/shard_map/ppermute | solution.py:365
  45.9 0.1 fold_rows.1
  46.0 1.0 %collective-permute-start.11 = (bf16[256,128]{1,0:T(8,128)(2,1)S(1)}, bf16[256,128]{1,0:T(8,128)(2,1)S(1)}, u32[]{:S(2)}, u32[]{:S(2)}) collective-permute-start(bf16[256,128]{1,0:T(8,128)(2,1)S(1)} %get-tuple-element.43), channel_id=1, source_target_pairs={{0,15},{1,2},{2,1},{3,4},{4,3},{5,6},{6,5},{7,8},{8,7},{9,10},{10,... | collective-permute-start | bytes 196616 | tf_op jit(solution)/shard_map/ppermute | solution.py:380
  47.0 4.1 %collective-permute-done.11.outer_ref = bf16[256,128]{1,0:T(8,128)(2,1)S(1)} collective-permute-done((bf16[256,128]{1,0:T(8,128)(2,1)S(1)}, bf16[256,128]{1,0:T(8,128)(2,1)S(1)}, u32[]{:S(2)}, u32[]{:S(2)}) %collective-permute-start.11) | collective-permute-done | bytes 65568 | tf_op jit(solution)/shard_map/ppermute | solution.py:380
  51.1 0.7 %fold_columns.1 = f32[256,256]{1,0:T(8,128)} custom-call(f32[256,256]{1,0:T(8,128)S(1)} %get-tuple-element.42.center_ref, bf16[256,128]{1,0:T(8,128)(2,1)S(1)} %collective-permute-done.11.outer_ref, bf16[256,128]{1,0:T(8,128)(2,1)S(1)} %collective-permute-done.12.inner_ref), custom_call_target="tpu_custom_call" | custom-call | bytes 1048576 | tf_op jit(solution)/shard_map/fold_columns/pallas_call | solution.py:506
  (30 shorter events, 0.1 us)
Async XLA Ops:
  0.0 1.1 %copy-start = (bf16[6,256,256]{2,1,0:T(8,128)(2,1)S(1)}, bf16[6,256,256]{2,1,0:T(8,128)(2,1)}, u32[]{:S(2)}) copy-start(bf16[6,256,256]{2,1,0:T(8,128)(2,1)} %core_ref.1) | copy-start | bytes 2359300
  1.1 14.4 %copy-start.3 = (bf16[528,512]{1,0:T(8,128)(2,1)S(1)}, bf16[528,512]{1,0:T(8,128)(2,1)}, u32[]{:S(2)}) copy-start(bf16[528,512]{1,0:T(8,128)(2,1)} %constant.44.clone.left_ref) | copy-start | bytes 1622020
  1.1 14.4 %copy-start.4 = (bf16[512,512]{1,0:T(8,128)(2,1)S(1)}, bf16[512,512]{1,0:T(8,128)(2,1)}, u32[]{:S(2)}) copy-start(bf16[512,512]{1,0:T(8,128)(2,1)} %constant.45.clone.right_ref) | copy-start | bytes 1572868
  2.1 10.5 %collective-permute-start.1 = (bf16[4,128,256]{2,1,0:T(8,128)(2,1)S(1)}, bf16[4,128,256]{2,1,0:T(8,128)(2,1)S(1)}, u32[]{:S(2)}, u32[]{:S(2)}) collective-permute-start(bf16[4,128,256]{2,1,0:T(8,128)(2,1)S(1)} %get-tuple-element.26), channel_id=1, source_target_pairs={{0,1},{1,0},{2,3},{3,2},{4,5},{5,4},{6,7},{7,6},{8,9},{9,8},{10,11... | collective-permute-start | bytes 786440 | tf_op jit(solution)/shard_map/ppermute | solution.py:374
  2.7 15.7 %collective-permute-start.4 = (bf16[6,128,128]{2,1,0:T(8,128)(2,1)}, bf16[6,128,128]{2,1,0:T(8,128)(2,1)S(1)}, u32[]{:S(2)}, u32[]{:S(2)}) collective-permute-start(bf16[6,128,128]{2,1,0:T(8,128)(2,1)} %get-tuple-element.28), channel_id=1, source_target_pairs={{0,15},{1,2},{2,1},{3,4},{4,3},{5,6},{6,5},{7,8},{8,7},{9,10},{10,... | collective-permute-start | bytes 589832 | tf_op jit(solution)/shard_map/ppermute | solution.py:380
  5.4 17.5 %collective-permute-start.5 = (bf16[6,128,128]{2,1,0:T(8,128)(2,1)}, bf16[6,128,128]{2,1,0:T(8,128)(2,1)}, u32[]{:S(2)}, u32[]{:S(2)}) collective-permute-start(bf16[6,128,128]{2,1,0:T(8,128)(2,1)} %get-tuple-element.29), channel_id=1, source_target_pairs={{0,15},{1,2},{2,1},{3,4},{4,3},{5,6},{6,5},{7,8},{8,7},{9,10},{10,... | collective-permute-start | bytes 589832 | tf_op jit(solution)/shard_map/ppermute | solution.py:380
  5.5 17.5 %collective-permute-start.3 = (bf16[6,128,256]{2,1,0:T(8,128)(2,1)}, bf16[6,128,256]{2,1,0:T(8,128)(2,1)S(1)}, u32[]{:S(2)}, u32[]{:S(2)}) collective-permute-start(bf16[6,128,256]{2,1,0:T(8,128)(2,1)} %get-tuple-element.27), channel_id=1, source_target_pairs={{0,16},{1,17},{2,18},{3,19},{4,20},{5,21},{6,22},{7,23},{8,24},{9,... | collective-permute-start | bytes 1179656 | tf_op jit(solution)/shard_map/ppermute | solution.py:365
  7.1 15.9 %collective-permute-start = (bf16[2,128,256]{2,1,0:T(8,128)(2,1)S(1)}, bf16[2,128,256]{2,1,0:T(8,128)(2,1)S(1)}, u32[]{:S(2)}, u32[]{:S(2)}) collective-permute-start(bf16[2,128,256]{2,1,0:T(8,128)(2,1)S(1)} %get-tuple-element.25), channel_id=1, source_target_pairs={{0,1},{1,0},{2,3},{3,2},{4,5},{5,4},{6,7},{7,6},{8,9},{9,8},{10,11... | collective-permute-start | bytes 393224 | tf_op jit(solution)/shard_map/ppermute | solution.py:365
  13.3 4.9 %copy-start.1 = (bf16[6,256,256]{2,1,0:T(8,128)(2,1)S(1)}, bf16[6,256,256]{2,1,0:T(8,128)(2,1)}, u32[]{:S(2)}) copy-start(bf16[6,256,256]{2,1,0:T(8,128)(2,1)} %core_ref.1) | copy-start | bytes 2359300
  13.3 11.6 %collective-permute-start.2 = (bf16[4,128,256]{2,1,0:T(8,128)(2,1)}, bf16[4,128,256]{2,1,0:T(8,128)(2,1)S(1)}, u32[]{:S(2)}, u32[]{:S(2)}) collective-permute-start(bf16[4,128,256]{2,1,0:T(8,128)(2,1)} %broadcast_select_fusion), channel_id=1, source_target_pairs={{0,1},{1,0},{2,3},{3,2},{4,5},{5,4},{6,7},{7,6},{8,9},{9,8},{10,11... | collective-permute-start | bytes 786440 | tf_op jit(solution)/shard_map/ppermute | solution.py:365
  15.5 1.0 %copy-start.11 = (bf16[512,512]{1,0:T(8,128)(2,1)S(1)}, bf16[512,512]{1,0:T(8,128)(2,1)}, u32[]{:S(2)}) copy-start(bf16[512,512]{1,0:T(8,128)(2,1)} %noise_ref.1) | copy-start | bytes 1572868
  17.4 0.8 %copy-start.5 = (f32[264,512]{1,0:T(8,128)}, f32[264,512]{1,0:T(8,128)S(1)}, u32[]{:S(2)}) copy-start(f32[264,512]{1,0:T(8,128)S(1)} %get-tuple-element.38.im_ref) | copy-start | bytes 1622020
  18.3 8.2 %copy-start.2 = (f32[512,128]{1,0:T(8,128)S(1)}, f32[512,128]{1,0:T(8,128)}, u32[]{:S(2)}) copy-start(f32[512,128]{1,0:T(8,128)} %constant.49.clone.rows_ref) | copy-start | bytes 786436
  18.3 8.2 %copy-start.10 = (f32[8,512]{1,0:T(8,128)S(1)}, f32[8,512]{1,0:T(8,128)}, u32[]{:S(2)}) copy-start(f32[8,512]{1,0:T(8,128)} %constant.50.clone.cols_ref) | copy-start | bytes 49156
  18.4 12.8 %collective-permute-start.6 = (bf16[6,128,128]{2,1,0:T(8,128)(2,1)S(1)}, bf16[6,128,128]{2,1,0:T(8,128)(2,1)S(1)}, u32[]{:S(2)}, u32[]{:S(2)}) collective-permute-start(bf16[6,128,128]{2,1,0:T(8,128)(2,1)S(1)} %collective-permute-done.4.outer_first_ref), channel_id=1, source_target_pairs={{0,1},{1,0},{2,3},{3,2},{4,5},{5,4},{6,7},{7,6},{8,9},{9,8},{10,11... | collective-permute-start | bytes 589832 | tf_op jit(solution)/shard_map/ppermute | solution.py:365
  23.0 8.2 %collective-permute-start.7 = (bf16[6,128,128]{2,1,0:T(8,128)(2,1)}, bf16[6,128,128]{2,1,0:T(8,128)(2,1)S(1)}, u32[]{:S(2)}, u32[]{:S(2)}) collective-permute-start(bf16[6,128,128]{2,1,0:T(8,128)(2,1)} %collective-permute-done.5.outer_second_ref), channel_id=1, source_target_pairs={{0,16},{1,17},{2,18},{3,19},{4,20},{5,21},{6,22},{7,23},{8,24},{9,... | collective-permute-start | bytes 589832 | tf_op jit(solution)/shard_map/ppermute | solution.py:365
  25.0 7.0 %collective-permute-start.8 = (bf16[6,512,128]{2,1,0:T(8,128)(2,1)S(1)}, bf16[6,512,128]{2,1,0:T(8,128)(2,1)S(1)}, u32[]{:S(2)}, u32[]{:S(2)}) collective-permute-start(bf16[6,512,128]{2,1,0:T(8,128)(2,1)S(1)} %pad_maximum_fusion), channel_id=1, source_target_pairs={{0,1},{1,0},{2,3},{3,2},{4,5},{5,4},{6,7},{7,6},{8,9},{9,8},{10,11... | collective-permute-start | bytes 2359304 | tf_op jit(solution)/shard_map/ppermute | solution.py:380
  32.0 1.0 %copy-start.6 = (f32[264,512]{1,0:T(8,128)S(1)}, f32[264,512]{1,0:T(8,128)}, u32[]{:S(2)}) copy-start(f32[264,512]{1,0:T(8,128)} %copy-done.5) | copy-start | bytes 1622020
  32.0 1.2 %copy-start.7 = (bf16[512,512]{1,0:T(8,128)(2,1)S(1)}, bf16[512,512]{1,0:T(8,128)(2,1)}, u32[]{:S(2)}) copy-start(bf16[512,512]{1,0:T(8,128)(2,1)} %constant.46.clone.inverse_right_ref) | copy-start | bytes 1572868
  32.0 1.3 %copy-start.8 = (bf16[512,512]{1,0:T(8,128)(2,1)S(1)}, bf16[512,512]{1,0:T(8,128)(2,1)}, u32[]{:S(2)}) copy-start(bf16[512,512]{1,0:T(8,128)(2,1)} %constant.47.clone.band_columns_ref) | copy-start | bytes 1572868
  32.0 1.4 %copy-start.9 = (bf16[272,384]{1,0:T(8,128)(2,1)S(1)}, bf16[272,384]{1,0:T(8,128)(2,1)}, u32[]{:S(2)}) copy-start(bf16[272,384]{1,0:T(8,128)(2,1)} %constant.48.clone.band_rows_ref) | copy-start | bytes 626692
  37.0 5.2 %collective-permute-start.10 = (bf16[128,512]{1,0:T(8,128)(2,1)S(1)}, bf16[128,512]{1,0:T(8,128)(2,1)S(1)}, u32[]{:S(2)}, u32[]{:S(2)}) collective-permute-start(bf16[128,512]{1,0:T(8,128)(2,1)S(1)} %get-tuple-element.41), channel_id=1, source_target_pairs={{0,16},{1,17},{2,18},{3,19},{4,20},{5,21},{6,22},{7,23},{8,24},{9,... | collective-permute-start | bytes 393224 | tf_op jit(solution)/shard_map/ppermute | solution.py:365
  37.1 8.8 %collective-permute-start.9 = (bf16[128,512]{1,0:T(8,128)(2,1)S(1)}, bf16[128,512]{1,0:T(8,128)(2,1)S(1)}, u32[]{:S(2)}, u32[]{:S(2)}) collective-permute-start(bf16[128,512]{1,0:T(8,128)(2,1)S(1)} %get-tuple-element.40), channel_id=1, source_target_pairs={{0,1},{1,0},{2,3},{3,2},{4,5},{5,4},{6,7},{7,6},{8,9},{9,8},{10,11... | collective-permute-start | bytes 393224 | tf_op jit(solution)/shard_map/ppermute | solution.py:365
  46.0 5.1 %collective-permute-start.11 = (bf16[256,128]{1,0:T(8,128)(2,1)S(1)}, bf16[256,128]{1,0:T(8,128)(2,1)S(1)}, u32[]{:S(2)}, u32[]{:S(2)}) collective-permute-start(bf16[256,128]{1,0:T(8,128)(2,1)S(1)} %get-tuple-element.43), channel_id=1, source_target_pairs={{0,15},{1,2},{2,1},{3,4},{4,3},{5,6},{6,5},{7,8},{8,7},{9,10},{10,... | collective-permute-start | bytes 196616 | tf_op jit(solution)/shard_map/ppermute | solution.py:380
  47.0 4.1 %collective-permute-start.12 = (bf16[256,128]{1,0:T(8,128)(2,1)S(1)}, bf16[256,128]{1,0:T(8,128)(2,1)S(1)}, u32[]{:S(2)}, u32[]{:S(2)}) collective-permute-start(bf16[256,128]{1,0:T(8,128)(2,1)S(1)} %get-tuple-element.44), channel_id=1, source_target_pairs={{0,1},{1,0},{2,3},{3,2},{4,5},{5,4},{6,7},{7,6},{8,9},{9,8},{10,11... | collective-permute-start | bytes 196616 | tf_op jit(solution)/shard_map/ppermute | solution.py:380

commit v14 on v12

--- a/solution.py
+++ b/solution.py
@@ -425,6 +425,7 @@
     beside = swap_beside(far)
     near = swap_rows(near, 1)
     far = swap_rows(jnp.where(jnp.logical_or(row == middle - 1, row == middle), beside, far), 1, side=True)
+    outer_second, outer_first = lax.optimization_barrier((outer_second, outer_first))
     outer_second = swap_columns(outer_second, 1)
 
     spectrum = jax.ShapeDtypeStruct((half + 8, length), F32)

time: 50.6 us -> 53.3 us (1.053)
  starting transfers between devices: 21.5 us -> 23.8 us
    ppermute x7, starting transfers between devices: 13.9 us -> 17.4 us  [swap_rows(): return lax.ppermute(values, ('dec', 'ra'), partners(offset, side))]
    ppermute x5, starting transfers between devices: 6.34 us -> 5.2 us  [swap_columns(): return lax.ppermute(values, 'ra', pairs)]
  transfers between devices with their start and end apart: 13 -> 13, of which waited for: 5 -> 5; matrix products, arithmetic and copies ran while one was open for 2% -> 2% of each run, Pallas kernels for 11% -> 10%
where the time goes in v14:
time: 53.3 us; the launch traced here: 53 us
  starting transfers between devices  23.8 us (45%)
  waiting for transfers between devices  11.9 us (22%)
  Pallas kernels  11.6 us (22%)
  local copies, waits for them, and re-layouts  4.62 us (9%)
  other arithmetic  0.79 us (1%)
    ppermute x7, starting transfers between devices, swap_rows(): return lax.ppermute(values, ('dec', 'ra'), partners(offset, side))  17.4 us
    ppermute x7, waiting for transfers between devices, swap_rows(): return lax.ppermute(values, ('dec', 'ra'), partners(offset, side))  7.73 us
    ppermute x5, starting transfers between devices, swap_columns(): return lax.ppermute(values, 'ra', pairs)  5.2 us
    unnamed x24, local copies, waits for them, and re-layouts  4.54 us
    ppermute x5, waiting for transfers between devices, swap_columns(): return lax.ppermute(values, 'ra', pairs)  4.17 us
    pallas_call x1, Pallas kernels, shards(): kernel_call(functools.partial(core_kernel, half), 'core_columns', (jax.Sh...  3.73 us
    pallas_call x1, Pallas kernels, shards(): kernel_call(functools.partial(main_kernel, half, scale), 'tile_model', (s...  3.56 us
    ppermute x1, starting transfers between devices, swap_beside(): return lax.ppermute(values, ('dec', 'ra'), pairs)  1.2 us
  transfers between devices with their start and end apart: 13, of which 5 were waited for; matrix products, arithmetic and copies ran while one was open for 2% of the time, Pallas kernels for 10%

profile of v14, /device:TPU:4, one launch (start us, length us, event | category | flops | bytes accessed | tf_op | source)
XLA Modules:
  0.0 53.0 jit_solution(11699037432907736541)
XLA Ops:
  0.0 1.1 %copy-done = bf16[6,256,256]{2,1,0:T(8,128)(2,1)S(1)} copy-done((bf16[6,256,256]{2,1,0:T(8,128)(2,1)S(1)}, bf16[6,256,256]{2,1,0:T(8,128)(2,1)}, u32[]{:S(2)}) %copy-start) | copy-done | bytes 786456
  1.1 0.9 %cut.1 = (bf16[6,128,128]{2,1,0:T(8,128)(2,1)S(1)}, bf16[6,128,128]{2,1,0:T(8,128)(2,1)}, bf16[4,128,256]{2,1,0:T(8,128)(2,1)}, bf16[2,128,256]{2,1,0:T(8,128)(2,1)S(1)}, bf16[6,128,256]{2,1,0:T(8,128)(2,1)S(1)}) custom-call(bf16[6,256,256]{2,1,0:T(8,128)(2,1)S(1)} %copy-done), custom_call_target="tpu_custom_call" | custom-call | bytes 1048576 | tf_op jit(solution)/shard_map/cut/pallas_call | solution.py:418
  2.0 1.2 %collective-permute-start.1 = (bf16[2,128,256]{2,1,0:T(8,128)(2,1)S(1)}, bf16[2,128,256]{2,1,0:T(8,128)(2,1)S(1)}, u32[]{:S(2)}, u32[]{:S(2)}) collective-permute-start(bf16[2,128,256]{2,1,0:T(8,128)(2,1)S(1)} %get-tuple-element.28), channel_id=1, source_target_pairs={{0,1},{1,0},{2,3},{3,2},{4,5},{5,4},{6,7},{7,6},{8,9},{9,8},{10,11... | collective-permute-start | bytes 393224 | tf_op jit(solution)/shard_map/ppermute | solution.py:374
  3.2 2.4 %collective-permute-start.4 = (bf16[6,128,128]{2,1,0:T(8,128)(2,1)S(1)}, bf16[6,128,128]{2,1,0:T(8,128)(2,1)S(1)}, u32[]{:S(2)}, u32[]{:S(2)}) collective-permute-start(bf16[6,128,128]{2,1,0:T(8,128)(2,1)S(1)} %get-tuple-element.31), channel_id=1, source_target_pairs={{0,15},{1,2},{2,1},{3,4},{4,3},{5,6},{6,5},{7,8},{8,7},{9,10},{10,... | collective-permute-start | bytes 589832 | tf_op jit(solution)/shard_map/ppermute | solution.py:380
  5.7 2.0 %collective-permute-start.3 = (bf16[6,128,256]{2,1,0:T(8,128)(2,1)S(1)}, bf16[6,128,256]{2,1,0:T(8,128)(2,1)S(1)}, u32[]{:S(2)}, u32[]{:S(2)}) collective-permute-start(bf16[6,128,256]{2,1,0:T(8,128)(2,1)S(1)} %get-tuple-element.29), channel_id=1, source_target_pairs={{0,16},{1,17},{2,18},{3,19},{4,20},{5,21},{6,22},{7,23},{8,24},{9,... | collective-permute-start | bytes 1179656 | tf_op jit(solution)/shard_map/ppermute | solution.py:365
  7.7 5.2 %collective-permute-start = (bf16[4,128,256]{2,1,0:T(8,128)(2,1)}, bf16[4,128,256]{2,1,0:T(8,128)(2,1)S(1)}, u32[]{:S(2)}, u32[]{:S(2)}) collective-permute-start(bf16[4,128,256]{2,1,0:T(8,128)(2,1)} %get-tuple-element.27), channel_id=1, source_target_pairs={{0,1},{1,0},{2,3},{3,2},{4,5},{5,4},{6,7},{7,6},{8,9},{9,8},{10,11... | collective-permute-start | bytes 786440 | tf_op jit(solution)/shard_map/ppermute | solution.py:365
  12.9 0.7 %broadcast_select_fusion = bf16[2,128,256]{2,1,0:T(8,128)(2,1)} fusion(bf16[2,128,256]{2,1,0:T(8,128)(2,1)S(1)} %collective-permute-done.1, bf16[2,128,256]{2,1,0:T(8,128)(2,1)S(1)} %get-tuple-element.28, pred[]{:T(512)S(6)} %or.3), kind=kLoop, calls=%fused_computation.4 | loop fusion | flops 65536 | bytes 393217 | tf_op jit(solution)/shard_map/jit(_where)/select_n | solution.py:427
  13.5 1.3 %collective-permute-start.2 = (bf16[2,128,256]{2,1,0:T(8,128)(2,1)}, bf16[2,128,256]{2,1,0:T(8,128)(2,1)S(1)}, u32[]{:S(2)}, u32[]{:S(2)}) collective-permute-start(bf16[2,128,256]{2,1,0:T(8,128)(2,1)} %broadcast_select_fusion), channel_id=1, source_target_pairs={{0,1},{1,0},{2,3},{3,2},{4,5},{5,4},{6,7},{7,6},{8,9},{9,8},{10,11... | collective-permute-start | bytes 393224 | tf_op jit(solution)/shard_map/ppermute | solution.py:365
  14.9 0.7 %collective-permute-start.5 = (bf16[6,128,128]{2,1,0:T(8,128)(2,1)}, bf16[6,128,128]{2,1,0:T(8,128)(2,1)S(1)}, u32[]{:S(2)}, u32[]{:S(2)}) collective-permute-start(bf16[6,128,128]{2,1,0:T(8,128)(2,1)} %get-tuple-element.33), channel_id=1, source_target_pairs={{0,15},{1,2},{2,1},{3,4},{4,3},{5,6},{6,5},{7,8},{8,7},{9,10},{10,... | collective-permute-start | bytes 589832 | tf_op jit(solution)/shard_map/ppermute | solution.py:380
  15.6 1.0 %copy-done.3 = bf16[528,512]{1,0:T(8,128)(2,1)S(1)} copy-done((bf16[528,512]{1,0:T(8,128)(2,1)S(1)}, bf16[528,512]{1,0:T(8,128)(2,1)}, u32[]{:S(2)}) %copy-start.3) | copy-done | bytes 540696
  16.7 1.0 %copy-done.5 = bf16[512,512]{1,0:T(8,128)(2,1)S(1)} copy-done((bf16[512,512]{1,0:T(8,128)(2,1)S(1)}, bf16[512,512]{1,0:T(8,128)(2,1)}, u32[]{:S(2)}) %copy-start.5) | copy-done | bytes 524312
  17.7 1.0 %copy-done.11 = bf16[512,512]{1,0:T(8,128)(2,1)S(1)} copy-done((bf16[512,512]{1,0:T(8,128)(2,1)S(1)}, bf16[512,512]{1,0:T(8,128)(2,1)}, u32[]{:S(2)}) %copy-start.11) | copy-done | bytes 524312
  18.8 0.9 %noise_spectrum.1 = (f32[264,512]{1,0:T(8,128)S(1)}, f32[264,512]{1,0:T(8,128)S(1)}) custom-call(bf16[512,512]{1,0:T(8,128)(2,1)S(1)} %copy-done.11, bf16[528,512]{1,0:T(8,128)(2,1)S(1)} %copy-done.3, bf16[512,512]{1,0:T(8,128)(2,1)S(1)} %copy-done.5), custom_call_target="tpu_custom_call" | custom-call | flops 6710886400 | bytes 1048576 | tf_op jit(solution)/shard_map/noise_spectrum/pallas_call | solution.py:432
  19.8 5.1 %collective-permute-start.6 = (bf16[6,128,128]{2,1,0:T(8,128)(2,1)S(1)}, bf16[6,128,128]{2,1,0:T(8,128)(2,1)S(1)}, u32[]{:S(2)}, u32[]{:S(2)}) collective-permute-start(bf16[6,128,128]{2,1,0:T(8,128)(2,1)S(1)} %collective-permute-done.4.outer_first_ref), channel_id=1, source_target_pairs={{0,1},{1,0},{2,3},{3,2},{4,5},{5,4},{6,7},{7,6},{8,9},{9,8},{10,11... | collective-permute-start | bytes 589832 | tf_op jit(solution)/shard_map/ppermute | solution.py:365
  24.9 0.1 collective-permute-start.7
  25.0 0.1 fusion
  25.1 0.1 collective-permute-start.8
  25.3 3.7 %core_columns.1 = (f32[6,528,512]{2,1,0:T(8,128)S(1)}, bf16[6,512,128]{2,1,0:T(8,128)(2,1)S(1)}) custom-call(bf16[6,256,256]{2,1,0:T(8,128)(2,1)S(1)} %copy-done.1, bf16[4,128,256]{2,1,0:T(8,128)(2,1)S(1)} %collective-permute-done.near_ref, bf16[2,128,256]{2,1,0:T(8,128)(2,1)S(1)} %collective-permute-done.2.far_ref, ...), custom_call_target="tpu_custom_call" | custom-call | flops 134217728 | bytes 1048576 | tf_op jit(solution)/shard_map/core_columns/pallas_call | solution.py:462
  29.0 1.0 %collective-permute-done.6.first_ref = bf16[6,128,128]{2,1,0:T(8,128)(2,1)S(1)} collective-permute-done((bf16[6,128,128]{2,1,0:T(8,128)(2,1)S(1)}, bf16[6,128,128]{2,1,0:T(8,128)(2,1)S(1)}, u32[]{:S(2)}, u32[]{:S(2)}) %collective-permute-start.6) | collective-permute-done | bytes 196640 | tf_op jit(solution)/shard_map/ppermute | solution.py:365
  30.0 0.7 %collective-permute-done.7.second_ref = bf16[6,128,128]{2,1,0:T(8,128)(2,1)S(1)} collective-permute-done((bf16[6,128,128]{2,1,0:T(8,128)(2,1)S(1)}, bf16[6,128,128]{2,1,0:T(8,128)(2,1)S(1)}, u32[]{:S(2)}, u32[]{:S(2)}) %collective-permute-start.7) | collective-permute-done | bytes 196640 | tf_op jit(solution)/shard_map/ppermute | solution.py:365
  30.6 0.8 %outer_columns.1.after_ref.outer_ref = bf16[6,528,128]{2,1,0:T(8,128)(2,1)S(1)} custom-call(f32[6,528,512]{2,1,0:T(8,128)S(1)} %get-tuple-element.39.after_ref.core_ref, bf16[6,512,128]{2,1,0:T(8,128)(2,1)S(1)} %get-tuple-element.40.tile, bf16[6,128,128]{2,1,0:T(8,128)(2,1)S(1)} %collective-permute-done.6.first_ref, ...), custom_call_target="tpu_custom_call" | custom-call | flops 53687091200 | bytes 1048576 | tf_op jit(solution)/shard_map/outer_columns/pallas_call | solution.py:473
  31.5 1.0 %inner_columns.1.inner_ref = bf16[6,528,128]{2,1,0:T(8,128)(2,1)S(1)} custom-call(bf16[6,528,128]{2,1,0:T(8,128)(2,1)S(1)} %outer_columns.1.after_ref.outer_ref, bf16[6,512,128]{2,1,0:T(8,128)(2,1)S(1)} %collective-permute-done.8.inner_ref, f32[512,128]{1,0:T(8,128)S(1)} %copy-done.2, f32[8,512]{1,0:T(8,128)S(1)} %copy-done.10, bf16[528,512]{1,0:T(8,128)(2,1)S(1)} %copy-done.4), custom_call_target="tpu_custom_call" | custom-call | flops 134217728 | bytes 1048576 | tf_op jit(solution)/shard_map/inner_columns/pallas_call | solution.py:476
  32.5 0.2 copy-done.8
  32.7 3.6 %tile_model.1 = (bf16[128,512]{1,0:T(8,128)(2,1)S(1)}, bf16[128,512]{1,0:T(8,128)(2,1)S(1)}, f32[256,512]{1,0:T(8,128)S(1)}) custom-call(f32[6,528,512]{2,1,0:T(8,128)S(1)} %get-tuple-element.39.after_ref.core_ref, bf16[6,528,128]{2,1,0:T(8,128)(2,1)S(1)} %inner_columns.1.inner_ref, bf16[6,528,128]{2,1,0:T(8,128)(2,1)S(1)} %outer_columns.1.after_ref.outer_ref, ...), custom_call_target="tpu_custom_call" | custom-call | flops 2684354560 | bytes 1048576 | tf_op jit(solution)/shard_map/tile_model/pallas_call | solution.py:479
  36.2 0.5 collective-permute-start.10
  36.7 3.2 %collective-permute-start.9 = (bf16[128,512]{1,0:T(8,128)(2,1)S(1)}, bf16[128,512]{1,0:T(8,128)(2,1)S(1)}, u32[]{:S(2)}, u32[]{:S(2)}) collective-permute-start(bf16[128,512]{1,0:T(8,128)(2,1)S(1)} %get-tuple-element.44), channel_id=1, source_target_pairs={{0,1},{1,0},{2,3},{3,2},{4,5},{5,4},{6,7},{7,6},{8,9},{9,8},{10,11... | collective-permute-start | bytes 393224 | tf_op jit(solution)/shard_map/ppermute | solution.py:365
  39.9 1.4 %collective-permute-done.10.second_ref = bf16[128,512]{1,0:T(8,128)(2,1)S(1)} collective-permute-done((bf16[128,512]{1,0:T(8,128)(2,1)S(1)}, bf16[128,512]{1,0:T(8,128)(2,1)S(1)}, u32[]{:S(2)}, u32[]{:S(2)}) %collective-permute-start.10) | collective-permute-done | bytes 131104 | tf_op jit(solution)/shard_map/ppermute | solution.py:365
  41.3 4.7 %collective-permute-done.9.first_ref = bf16[128,512]{1,0:T(8,128)(2,1)S(1)} collective-permute-done((bf16[128,512]{1,0:T(8,128)(2,1)S(1)}, bf16[128,512]{1,0:T(8,128)(2,1)S(1)}, u32[]{:S(2)}, u32[]{:S(2)}) %collective-permute-start.9) | collective-permute-done | bytes 131104 | tf_op jit(solution)/shard_map/ppermute | solution.py:365
  46.0 0.1 fold_rows.1
  46.2 1.9 %collective-permute-start.11 = (bf16[256,128]{1,0:T(8,128)(2,1)S(1)}, bf16[256,128]{1,0:T(8,128)(2,1)S(1)}, u32[]{:S(2)}, u32[]{:S(2)}) collective-permute-start(bf16[256,128]{1,0:T(8,128)(2,1)S(1)} %get-tuple-element.47), channel_id=1, source_target_pairs={{0,15},{1,2},{2,1},{3,4},{4,3},{5,6},{6,5},{7,8},{8,7},{9,10},{10,... | collective-permute-start | bytes 196616 | tf_op jit(solution)/shard_map/ppermute | solution.py:380
  48.1 4.2 %collective-permute-done.11.outer_ref = bf16[256,128]{1,0:T(8,128)(2,1)S(1)} collective-permute-done((bf16[256,128]{1,0:T(8,128)(2,1)S(1)}, bf16[256,128]{1,0:T(8,128)(2,1)S(1)}, u32[]{:S(2)}, u32[]{:S(2)}) %collective-permute-start.11) | collective-permute-done | bytes 65568 | tf_op jit(solution)/shard_map/ppermute | solution.py:380
  52.3 0.7 %fold_columns.1 = f32[256,256]{1,0:T(8,128)} custom-call(f32[256,256]{1,0:T(8,128)S(1)} %get-tuple-element.46.center_ref, bf16[256,128]{1,0:T(8,128)(2,1)S(1)} %collective-permute-done.11.outer_ref, bf16[256,128]{1,0:T(8,128)(2,1)S(1)} %collective-permute-done.12.inner_ref), custom_call_target="tpu_custom_call" | custom-call | bytes 1048576 | tf_op jit(solution)/shard_map/fold_columns/pallas_call | solution.py:507
  (30 shorter events, 0.3 us)
Async XLA Ops:
  0.0 1.1 %copy-start = (bf16[6,256,256]{2,1,0:T(8,128)(2,1)S(1)}, bf16[6,256,256]{2,1,0:T(8,128)(2,1)}, u32[]{:S(2)}) copy-start(bf16[6,256,256]{2,1,0:T(8,128)(2,1)} %core_ref.1) | copy-start | bytes 2359300
  2.0 10.9 %collective-permute-start.1 = (bf16[2,128,256]{2,1,0:T(8,128)(2,1)S(1)}, bf16[2,128,256]{2,1,0:T(8,128)(2,1)S(1)}, u32[]{:S(2)}, u32[]{:S(2)}) collective-permute-start(bf16[2,128,256]{2,1,0:T(8,128)(2,1)S(1)} %get-tuple-element.28), channel_id=1, source_target_pairs={{0,1},{1,0},{2,3},{3,2},{4,5},{5,4},{6,7},{7,6},{8,9},{9,8},{10,11... | collective-permute-start | bytes 393224 | tf_op jit(solution)/shard_map/ppermute | solution.py:374
  3.2 11.7 %collective-permute-start.4 = (bf16[6,128,128]{2,1,0:T(8,128)(2,1)S(1)}, bf16[6,128,128]{2,1,0:T(8,128)(2,1)S(1)}, u32[]{:S(2)}, u32[]{:S(2)}) collective-permute-start(bf16[6,128,128]{2,1,0:T(8,128)(2,1)S(1)} %get-tuple-element.31), channel_id=1, source_target_pairs={{0,15},{1,2},{2,1},{3,4},{4,3},{5,6},{6,5},{7,8},{8,7},{9,10},{10,... | collective-permute-start | bytes 589832 | tf_op jit(solution)/shard_map/ppermute | solution.py:380
  5.7 19.2 %collective-permute-start.3 = (bf16[6,128,256]{2,1,0:T(8,128)(2,1)S(1)}, bf16[6,128,256]{2,1,0:T(8,128)(2,1)S(1)}, u32[]{:S(2)}, u32[]{:S(2)}) collective-permute-start(bf16[6,128,256]{2,1,0:T(8,128)(2,1)S(1)} %get-tuple-element.29), channel_id=1, source_target_pairs={{0,16},{1,17},{2,18},{3,19},{4,20},{5,21},{6,22},{7,23},{8,24},{9,... | collective-permute-start | bytes 1179656 | tf_op jit(solution)/shard_map/ppermute | solution.py:365
  7.7 17.2 %collective-permute-start = (bf16[4,128,256]{2,1,0:T(8,128)(2,1)}, bf16[4,128,256]{2,1,0:T(8,128)(2,1)S(1)}, u32[]{:S(2)}, u32[]{:S(2)}) collective-permute-start(bf16[4,128,256]{2,1,0:T(8,128)(2,1)} %get-tuple-element.27), channel_id=1, source_target_pairs={{0,1},{1,0},{2,3},{3,2},{4,5},{5,4},{6,7},{7,6},{8,9},{9,8},{10,11... | collective-permute-start | bytes 786440 | tf_op jit(solution)/shard_map/ppermute | solution.py:365
  13.5 11.3 %collective-permute-start.2 = (bf16[2,128,256]{2,1,0:T(8,128)(2,1)}, bf16[2,128,256]{2,1,0:T(8,128)(2,1)S(1)}, u32[]{:S(2)}, u32[]{:S(2)}) collective-permute-start(bf16[2,128,256]{2,1,0:T(8,128)(2,1)} %broadcast_select_fusion), channel_id=1, source_target_pairs={{0,1},{1,0},{2,3},{3,2},{4,5},{5,4},{6,7},{7,6},{8,9},{9,8},{10,11... | collective-permute-start | bytes 393224 | tf_op jit(solution)/shard_map/ppermute | solution.py:365
  14.9 4.8 %copy-start.1 = (bf16[6,256,256]{2,1,0:T(8,128)(2,1)S(1)}, bf16[6,256,256]{2,1,0:T(8,128)(2,1)}, u32[]{:S(2)}) copy-start(bf16[6,256,256]{2,1,0:T(8,128)(2,1)} %core_ref.1) | copy-start | bytes 2359300
  14.9 10.0 %collective-permute-start.5 = (bf16[6,128,128]{2,1,0:T(8,128)(2,1)}, bf16[6,128,128]{2,1,0:T(8,128)(2,1)S(1)}, u32[]{:S(2)}, u32[]{:S(2)}) collective-permute-start(bf16[6,128,128]{2,1,0:T(8,128)(2,1)} %get-tuple-element.33), channel_id=1, source_target_pairs={{0,15},{1,2},{2,1},{3,4},{4,3},{5,6},{6,5},{7,8},{8,7},{9,10},{10,... | collective-permute-start | bytes 589832 | tf_op jit(solution)/shard_map/ppermute | solution.py:380
  15.6 1.0 %copy-start.3 = (bf16[528,512]{1,0:T(8,128)(2,1)S(1)}, bf16[528,512]{1,0:T(8,128)(2,1)}, u32[]{:S(2)}) copy-start(bf16[528,512]{1,0:T(8,128)(2,1)} %constant.44.clone.left_ref) | copy-start | bytes 1622020
  16.7 1.0 %copy-start.5 = (bf16[512,512]{1,0:T(8,128)(2,1)S(1)}, bf16[512,512]{1,0:T(8,128)(2,1)}, u32[]{:S(2)}) copy-start(bf16[512,512]{1,0:T(8,128)(2,1)} %constant.45.clone.right_ref) | copy-start | bytes 1572868
  17.7 1.0 %copy-start.11 = (bf16[512,512]{1,0:T(8,128)(2,1)S(1)}, bf16[512,512]{1,0:T(8,128)(2,1)}, u32[]{:S(2)}) copy-start(bf16[512,512]{1,0:T(8,128)(2,1)} %noise_ref.1) | copy-start | bytes 1572868
  19.7 5.6 %copy-start.2 = (f32[512,128]{1,0:T(8,128)S(1)}, f32[512,128]{1,0:T(8,128)}, u32[]{:S(2)}) copy-start(f32[512,128]{1,0:T(8,128)} %constant.49.clone.rows_ref) | copy-start | bytes 786436
  19.7 5.6 %copy-start.4 = (bf16[528,512]{1,0:T(8,128)(2,1)S(1)}, bf16[528,512]{1,0:T(8,128)(2,1)}, u32[]{:S(2)}) copy-start(bf16[528,512]{1,0:T(8,128)(2,1)} %constant.44.clone.left_ref) | copy-start | bytes 1622020
  19.7 5.6 %copy-start.6 = (bf16[512,512]{1,0:T(8,128)(2,1)S(1)}, bf16[512,512]{1,0:T(8,128)(2,1)}, u32[]{:S(2)}) copy-start(bf16[512,512]{1,0:T(8,128)(2,1)} %constant.45.clone.right_ref) | copy-start | bytes 1572868
  19.7 5.6 %copy-start.10 = (f32[8,512]{1,0:T(8,128)S(1)}, f32[8,512]{1,0:T(8,128)}, u32[]{:S(2)}) copy-start(f32[8,512]{1,0:T(8,128)} %constant.50.clone.cols_ref) | copy-start | bytes 49156
  19.8 10.2 %collective-permute-start.6 = (bf16[6,128,128]{2,1,0:T(8,128)(2,1)S(1)}, bf16[6,128,128]{2,1,0:T(8,128)(2,1)S(1)}, u32[]{:S(2)}, u32[]{:S(2)}) collective-permute-start(bf16[6,128,128]{2,1,0:T(8,128)(2,1)S(1)} %collective-permute-done.4.outer_first_ref), channel_id=1, source_target_pairs={{0,1},{1,0},{2,3},{3,2},{4,5},{5,4},{6,7},{7,6},{8,9},{9,8},{10,11... | collective-permute-start | bytes 589832 | tf_op jit(solution)/shard_map/ppermute | solution.py:365
  24.9 5.8 %collective-permute-start.7 = (bf16[6,128,128]{2,1,0:T(8,128)(2,1)S(1)}, bf16[6,128,128]{2,1,0:T(8,128)(2,1)S(1)}, u32[]{:S(2)}, u32[]{:S(2)}) collective-permute-start(bf16[6,128,128]{2,1,0:T(8,128)(2,1)S(1)} %collective-permute-done.5.outer_second_ref), channel_id=1, source_target_pairs={{0,16},{1,17},{2,18},{3,19},{4,20},{5,21},{6,22},{7,23},{8,24},{9,... | collective-permute-start | bytes 589832 | tf_op jit(solution)/shard_map/ppermute | solution.py:365
  25.1 6.3 %collective-permute-start.8 = (bf16[6,512,128]{2,1,0:T(8,128)(2,1)S(1)}, bf16[6,512,128]{2,1,0:T(8,128)(2,1)S(1)}, u32[]{:S(2)}, u32[]{:S(2)}) collective-permute-start(bf16[6,512,128]{2,1,0:T(8,128)(2,1)S(1)} %pad_maximum_fusion), channel_id=1, source_target_pairs={{0,1},{1,0},{2,3},{3,2},{4,5},{5,4},{6,7},{7,6},{8,9},{9,8},{10,11... | collective-permute-start | bytes 2359304 | tf_op jit(solution)/shard_map/ppermute | solution.py:380
  31.4 1.0 %copy-start.7 = (bf16[512,512]{1,0:T(8,128)(2,1)S(1)}, bf16[512,512]{1,0:T(8,128)(2,1)}, u32[]{:S(2)}) copy-start(bf16[512,512]{1,0:T(8,128)(2,1)} %constant.46.clone.inverse_right_ref) | copy-start | bytes 1572868
  31.4 1.2 %copy-start.8 = (bf16[512,512]{1,0:T(8,128)(2,1)S(1)}, bf16[512,512]{1,0:T(8,128)(2,1)}, u32[]{:S(2)}) copy-start(bf16[512,512]{1,0:T(8,128)(2,1)} %constant.47.clone.band_columns_ref) | copy-start | bytes 1572868
  31.4 1.2 %copy-start.9 = (bf16[272,384]{1,0:T(8,128)(2,1)S(1)}, bf16[272,384]{1,0:T(8,128)(2,1)}, u32[]{:S(2)}) copy-start(bf16[272,384]{1,0:T(8,128)(2,1)} %constant.48.clone.band_rows_ref) | copy-start | bytes 626692
  36.2 5.1 %collective-permute-start.10 = (bf16[128,512]{1,0:T(8,128)(2,1)S(1)}, bf16[128,512]{1,0:T(8,128)(2,1)S(1)}, u32[]{:S(2)}, u32[]{:S(2)}) collective-permute-start(bf16[128,512]{1,0:T(8,128)(2,1)S(1)} %get-tuple-element.45), channel_id=1, source_target_pairs={{0,16},{1,17},{2,18},{3,19},{4,20},{5,21},{6,22},{7,23},{8,24},{9,... | collective-permute-start | bytes 393224 | tf_op jit(solution)/shard_map/ppermute | solution.py:365
  36.7 9.3 %collective-permute-start.9 = (bf16[128,512]{1,0:T(8,128)(2,1)S(1)}, bf16[128,512]{1,0:T(8,128)(2,1)S(1)}, u32[]{:S(2)}, u32[]{:S(2)}) collective-permute-start(bf16[128,512]{1,0:T(8,128)(2,1)S(1)} %get-tuple-element.44), channel_id=1, source_target_pairs={{0,1},{1,0},{2,3},{3,2},{4,5},{5,4},{6,7},{7,6},{8,9},{9,8},{10,11... | collective-permute-start | bytes 393224 | tf_op jit(solution)/shard_map/ppermute | solution.py:365
  46.2 6.1 %collective-permute-start.11 = (bf16[256,128]{1,0:T(8,128)(2,1)S(1)}, bf16[256,128]{1,0:T(8,128)(2,1)S(1)}, u32[]{:S(2)}, u32[]{:S(2)}) collective-permute-start(bf16[256,128]{1,0:T(8,128)(2,1)S(1)} %get-tuple-element.47), channel_id=1, source_target_pairs={{0,15},{1,2},{2,1},{3,4},{4,3},{5,6},{6,5},{7,8},{8,7},{9,10},{10,... | collective-permute-start | bytes 196616 | tf_op jit(solution)/shard_map/ppermute | solution.py:380
  48.1 4.2 %collective-permute-start.12 = (bf16[256,128]{1,0:T(8,128)(2,1)S(1)}, bf16[256,128]{1,0:T(8,128)(2,1)S(1)}, u32[]{:S(2)}, u32[]{:S(2)}) collective-permute-start(bf16[256,128]{1,0:T(8,128)(2,1)S(1)} %get-tuple-element.48), channel_id=1, source_target_pairs={{0,1},{1,0},{2,3},{3,2},{4,5},{5,4},{6,7},{7,6},{8,9},{9,8},{10,11... | collective-permute-start | bytes 196616 | tf_op jit(solution)/shard_map/ppermute | solution.py:380

commit v15 on v12

--- a/solution.py
+++ b/solution.py
@@ -327,7 +327,7 @@
     second_out_ref[...] = strips[pl.ds(pl.multiple_of(margin - place, margin), margin), :]
 
 
-def fold_rows_kernel(half, inside_ref, first_ref, second_ref, center_ref, outer_ref, inner_ref, total):
+def fold_rows_kernel(half, inside_ref, second_ref, first_ref, center_ref, outer_ref, inner_ref, total):
     margin = half // 2
     first, second, outer, inner = sides(half)
     has_first, _ = inside_sky()
@@ -493,14 +493,14 @@
         constant["inverse_right"],
     )
 
+    first = swap_rows(first, 1)
     second = swap_rows(second, 0)
-    first = swap_rows(first, 1)
     column = jax.ShapeDtypeStruct((half, margin), BF16)
     block = jax.ShapeDtypeStruct((half, half), F32)
     center, outer, inner = kernel_call(
         functools.partial(fold_rows_kernel, half), "fold_rows", (block, column, column), 3,
         [pltpu.VMEM((half, length), F32)],
-    )(inside, first, second)
+    )(inside, second, first)
     outer = swap_columns(outer, 1)
     inner = swap_columns(inner, 0)
     return kernel_call(functools.partial(fold_columns_kernel, half), "fold_columns", block, 3)(

time: 50.6 us -> 50.8 us (level)
  waiting for transfers between devices: 11.6 us -> 12.6 us
  starting transfers between devices: 21.5 us -> 20.6 us
    ppermute x5, waiting for transfers between devices: 3.85 us -> 4.76 us  [swap_columns(): return lax.ppermute(values, 'ra', pairs)]
    ppermute x5, starting transfers between devices: 6.34 us -> 5.59 us  [swap_columns(): return lax.ppermute(values, 'ra', pairs)]
where the time goes in v15:
time: 50.8 us; the launch traced here: 50.6 us
  starting transfers between devices  20.6 us (41%)
  waiting for transfers between devices  12.6 us (25%)
  Pallas kernels  11.7 us (23%)
  local copies, waits for them, and re-layouts  4.62 us (9%)
  other arithmetic  0.8 us (2%)
    ppermute x7, starting transfers between devices, swap_rows(): return lax.ppermute(values, ('dec', 'ra'), partners(offset, side))  13.8 us
    ppermute x7, waiting for transfers between devices, swap_rows(): return lax.ppermute(values, ('dec', 'ra'), partners(offset, side))  7.86 us
    ppermute x5, starting transfers between devices, swap_columns(): return lax.ppermute(values, 'ra', pairs)  5.59 us
    ppermute x5, waiting for transfers between devices, swap_columns(): return lax.ppermute(values, 'ra', pairs)  4.76 us
    unnamed x24, local copies, waits for them, and re-layouts  4.54 us
    pallas_call x1, Pallas kernels, shards(): kernel_call(functools.partial(core_kernel, half), 'core_columns', (jax.Sh...  3.73 us
    pallas_call x1, Pallas kernels, shards(): kernel_call(functools.partial(main_kernel, half, scale), 'tile_model', (s...  3.56 us
    ppermute x1, starting transfers between devices, swap_beside(): return lax.ppermute(values, ('dec', 'ra'), pairs)  1.2 us
  transfers between devices with their start and end apart: 13, of which 5 were waited for; matrix products, arithmetic and copies ran while one was open for 2% of the time, Pallas kernels for 11%

profile of v15, /device:TPU:4, one launch (start us, length us, event | category | flops | bytes accessed | tf_op | source)
XLA Modules:
  0.0 50.6 jit_solution(17236381914405817307)
XLA Ops:
  0.0 1.1 %copy-done = bf16[6,256,256]{2,1,0:T(8,128)(2,1)S(1)} copy-done((bf16[6,256,256]{2,1,0:T(8,128)(2,1)S(1)}, bf16[6,256,256]{2,1,0:T(8,128)(2,1)}, u32[]{:S(2)}) %copy-start) | copy-done | bytes 786456
  1.1 0.9 %cut.1 = (bf16[6,128,128]{2,1,0:T(8,128)(2,1)}, bf16[6,128,128]{2,1,0:T(8,128)(2,1)}, bf16[4,128,256]{2,1,0:T(8,128)(2,1)}, bf16[2,128,256]{2,1,0:T(8,128)(2,1)S(1)}, bf16[6,128,256]{2,1,0:T(8,128)(2,1)S(1)}) custom-call(bf16[6,256,256]{2,1,0:T(8,128)(2,1)S(1)} %copy-done), custom_call_target="tpu_custom_call" | custom-call | bytes 1048576 | tf_op jit(solution)/shard_map/cut/pallas_call | solution.py:418
  2.0 1.2 %collective-permute-start.1 = (bf16[2,128,256]{2,1,0:T(8,128)(2,1)S(1)}, bf16[2,128,256]{2,1,0:T(8,128)(2,1)S(1)}, u32[]{:S(2)}, u32[]{:S(2)}) collective-permute-start(bf16[2,128,256]{2,1,0:T(8,128)(2,1)S(1)} %get-tuple-element.26), channel_id=1, source_target_pairs={{0,1},{1,0},{2,3},{3,2},{4,5},{5,4},{6,7},{7,6},{8,9},{9,8},{10,11... | collective-permute-start | bytes 393224 | tf_op jit(solution)/shard_map/ppermute | solution.py:374
  3.2 2.4 %collective-permute-start.4 = (bf16[6,128,128]{2,1,0:T(8,128)(2,1)}, bf16[6,128,128]{2,1,0:T(8,128)(2,1)S(1)}, u32[]{:S(2)}, u32[]{:S(2)}) collective-permute-start(bf16[6,128,128]{2,1,0:T(8,128)(2,1)} %get-tuple-element.28), channel_id=1, source_target_pairs={{0,15},{1,2},{2,1},{3,4},{4,3},{5,6},{6,5},{7,8},{8,7},{9,10},{10,... | collective-permute-start | bytes 589832 | tf_op jit(solution)/shard_map/ppermute | solution.py:380
  5.7 1.4 %collective-permute-start.5 = (bf16[6,128,128]{2,1,0:T(8,128)(2,1)}, bf16[6,128,128]{2,1,0:T(8,128)(2,1)S(1)}, u32[]{:S(2)}, u32[]{:S(2)}) collective-permute-start(bf16[6,128,128]{2,1,0:T(8,128)(2,1)} %get-tuple-element.29), channel_id=1, source_target_pairs={{0,15},{1,2},{2,1},{3,4},{4,3},{5,6},{6,5},{7,8},{8,7},{9,10},{10,... | collective-permute-start | bytes 589832 | tf_op jit(solution)/shard_map/ppermute | solution.py:380
  7.1 0.7 %collective-permute-start.3 = (bf16[6,128,256]{2,1,0:T(8,128)(2,1)S(1)}, bf16[6,128,256]{2,1,0:T(8,128)(2,1)S(1)}, u32[]{:S(2)}, u32[]{:S(2)}) collective-permute-start(bf16[6,128,256]{2,1,0:T(8,128)(2,1)S(1)} %get-tuple-element.27), channel_id=1, source_target_pairs={{0,16},{1,17},{2,18},{3,19},{4,20},{5,21},{6,22},{7,23},{8,24},{9,... | collective-permute-start | bytes 1179656 | tf_op jit(solution)/shard_map/ppermute | solution.py:365
  7.8 5.4 %collective-permute-start = (bf16[4,128,256]{2,1,0:T(8,128)(2,1)}, bf16[4,128,256]{2,1,0:T(8,128)(2,1)S(1)}, u32[]{:S(2)}, u32[]{:S(2)}) collective-permute-start(bf16[4,128,256]{2,1,0:T(8,128)(2,1)} %get-tuple-element.25), channel_id=1, source_target_pairs={{0,1},{1,0},{2,3},{3,2},{4,5},{5,4},{6,7},{7,6},{8,9},{9,8},{10,11... | collective-permute-start | bytes 786440 | tf_op jit(solution)/shard_map/ppermute | solution.py:365
  13.2 0.7 %broadcast_select_fusion = bf16[2,128,256]{2,1,0:T(8,128)(2,1)} fusion(bf16[2,128,256]{2,1,0:T(8,128)(2,1)S(1)} %collective-permute-done.1, bf16[2,128,256]{2,1,0:T(8,128)(2,1)S(1)} %get-tuple-element.26, pred[]{:T(512)S(6)} %or.3), kind=kLoop, calls=%fused_computation.4 | loop fusion | flops 65536 | bytes 393217 | tf_op jit(solution)/shard_map/jit(_where)/select_n | solution.py:427
  13.9 1.1 %collective-permute-start.2 = (bf16[2,128,256]{2,1,0:T(8,128)(2,1)}, bf16[2,128,256]{2,1,0:T(8,128)(2,1)S(1)}, u32[]{:S(2)}, u32[]{:S(2)}) collective-permute-start(bf16[2,128,256]{2,1,0:T(8,128)(2,1)} %broadcast_select_fusion), channel_id=1, source_target_pairs={{0,1},{1,0},{2,3},{3,2},{4,5},{5,4},{6,7},{7,6},{8,9},{9,8},{10,11... | collective-permute-start | bytes 393224 | tf_op jit(solution)/shard_map/ppermute | solution.py:365
  14.9 1.0 %copy-done.3 = bf16[528,512]{1,0:T(8,128)(2,1)S(1)} copy-done((bf16[528,512]{1,0:T(8,128)(2,1)S(1)}, bf16[528,512]{1,0:T(8,128)(2,1)}, u32[]{:S(2)}) %copy-start.3) | copy-done | bytes 540696
  16.0 1.0 %copy-done.5 = bf16[512,512]{1,0:T(8,128)(2,1)S(1)} copy-done((bf16[512,512]{1,0:T(8,128)(2,1)S(1)}, bf16[512,512]{1,0:T(8,128)(2,1)}, u32[]{:S(2)}) %copy-start.5) | copy-done | bytes 524312
  17.0 1.0 %copy-done.11 = bf16[512,512]{1,0:T(8,128)(2,1)S(1)} copy-done((bf16[512,512]{1,0:T(8,128)(2,1)S(1)}, bf16[512,512]{1,0:T(8,128)(2,1)}, u32[]{:S(2)}) %copy-start.11) | copy-done | bytes 524312
  18.1 0.9 %noise_spectrum.1 = (f32[264,512]{1,0:T(8,128)S(1)}, f32[264,512]{1,0:T(8,128)S(1)}) custom-call(bf16[512,512]{1,0:T(8,128)(2,1)S(1)} %copy-done.11, bf16[528,512]{1,0:T(8,128)(2,1)S(1)} %copy-done.3, bf16[512,512]{1,0:T(8,128)(2,1)S(1)} %copy-done.5), custom_call_target="tpu_custom_call" | custom-call | flops 6710886400 | bytes 1048576 | tf_op jit(solution)/shard_map/noise_spectrum/pallas_call | solution.py:431
  19.0 0.1 constant_dynamic-slice_fusion.1
  19.1 2.7 %collective-permute-start.6 = (bf16[6,128,128]{2,1,0:T(8,128)(2,1)S(1)}, bf16[6,128,128]{2,1,0:T(8,128)(2,1)S(1)}, u32[]{:S(2)}, u32[]{:S(2)}) collective-permute-start(bf16[6,128,128]{2,1,0:T(8,128)(2,1)S(1)} %collective-permute-done.4.outer_first_ref), channel_id=1, source_target_pairs={{0,1},{1,0},{2,3},{3,2},{4,5},{5,4},{6,7},{7,6},{8,9},{9,8},{10,11... | collective-permute-start | bytes 589832 | tf_op jit(solution)/shard_map/ppermute | solution.py:365
  21.9 0.1 fusion
  22.0 0.4 collective-permute-start.8
  22.4 3.7 %core_columns.1 = (f32[6,528,512]{2,1,0:T(8,128)S(1)}, bf16[6,512,128]{2,1,0:T(8,128)(2,1)S(1)}) custom-call(bf16[6,256,256]{2,1,0:T(8,128)(2,1)S(1)} %copy-done.1, bf16[4,128,256]{2,1,0:T(8,128)(2,1)S(1)} %collective-permute-done.near_ref, bf16[2,128,256]{2,1,0:T(8,128)(2,1)S(1)} %collective-permute-done.2.far_ref, ...), custom_call_target="tpu_custom_call" | custom-call | flops 134217728 | bytes 1048576 | tf_op jit(solution)/shard_map/core_columns/pallas_call | solution.py:461
  26.1 2.4 %collective-permute-done.6.first_ref = bf16[6,128,128]{2,1,0:T(8,128)(2,1)S(1)} collective-permute-done((bf16[6,128,128]{2,1,0:T(8,128)(2,1)S(1)}, bf16[6,128,128]{2,1,0:T(8,128)(2,1)S(1)}, u32[]{:S(2)}, u32[]{:S(2)}) %collective-permute-start.6) | collective-permute-done | bytes 196640 | tf_op jit(solution)/shard_map/ppermute | solution.py:365
  28.5 0.4 collective-permute-done.7.second_ref
  28.9 0.8 %outer_columns.1.after_ref.outer_ref = bf16[6,528,128]{2,1,0:T(8,128)(2,1)S(1)} custom-call(f32[6,528,512]{2,1,0:T(8,128)S(1)} %get-tuple-element.35.after_ref.core_ref, bf16[6,512,128]{2,1,0:T(8,128)(2,1)S(1)} %get-tuple-element.36.tile, bf16[6,128,128]{2,1,0:T(8,128)(2,1)S(1)} %collective-permute-done.6.first_ref, ...), custom_call_target="tpu_custom_call" | custom-call | flops 53687091200 | bytes 1048576 | tf_op jit(solution)/shard_map/outer_columns/pallas_call | solution.py:472
  29.8 1.0 %inner_columns.1.inner_ref = bf16[6,528,128]{2,1,0:T(8,128)(2,1)S(1)} custom-call(bf16[6,528,128]{2,1,0:T(8,128)(2,1)S(1)} %outer_columns.1.after_ref.outer_ref, bf16[6,512,128]{2,1,0:T(8,128)(2,1)S(1)} %collective-permute-done.8.inner_ref, f32[512,128]{1,0:T(8,128)S(1)} %copy-done.2, f32[8,512]{1,0:T(8,128)S(1)} %copy-done.10, bf16[528,512]{1,0:T(8,128)(2,1)S(1)} %copy-done.4), custom_call_target="tpu_custom_call" | custom-call | flops 134217728 | bytes 1048576 | tf_op jit(solution)/shard_map/inner_columns/pallas_call | solution.py:475
  30.8 0.2 copy-done.8
  31.0 3.6 %tile_model.1 = (bf16[128,512]{1,0:T(8,128)(2,1)S(1)}, bf16[128,512]{1,0:T(8,128)(2,1)S(1)}, f32[256,512]{1,0:T(8,128)S(1)}) custom-call(f32[6,528,512]{2,1,0:T(8,128)S(1)} %get-tuple-element.35.after_ref.core_ref, bf16[6,528,128]{2,1,0:T(8,128)(2,1)S(1)} %inner_columns.1.inner_ref, bf16[6,528,128]{2,1,0:T(8,128)(2,1)S(1)} %outer_columns.1.after_ref.outer_ref, ...), custom_call_target="tpu_custom_call" | custom-call | flops 2684354560 | bytes 1048576 | tf_op jit(solution)/shard_map/tile_model/pallas_call | solution.py:478
  34.5 4.0 %collective-permute-start.10 = (bf16[128,512]{1,0:T(8,128)(2,1)S(1)}, bf16[128,512]{1,0:T(8,128)(2,1)S(1)}, u32[]{:S(2)}, u32[]{:S(2)}) collective-permute-start(bf16[128,512]{1,0:T(8,128)(2,1)S(1)} %get-tuple-element.41), channel_id=1, source_target_pairs={{0,1},{1,0},{2,3},{3,2},{4,5},{5,4},{6,7},{7,6},{8,9},{9,8},{10,11... | collective-permute-start | bytes 393224 | tf_op jit(solution)/shard_map/ppermute | solution.py:365
  38.5 4.7 %collective-permute-done.10.first_ref = bf16[128,512]{1,0:T(8,128)(2,1)S(1)} collective-permute-done((bf16[128,512]{1,0:T(8,128)(2,1)S(1)}, bf16[128,512]{1,0:T(8,128)(2,1)S(1)}, u32[]{:S(2)}, u32[]{:S(2)}) %collective-permute-start.10) | collective-permute-done | bytes 131104 | tf_op jit(solution)/shard_map/ppermute | solution.py:365
  43.2 0.3 collective-permute-done.9.second_ref
  43.6 0.1 fold_rows.1
  43.7 0.7 %collective-permute-start.11 = (bf16[256,128]{1,0:T(8,128)(2,1)S(1)}, bf16[256,128]{1,0:T(8,128)(2,1)S(1)}, u32[]{:S(2)}, u32[]{:S(2)}) collective-permute-start(bf16[256,128]{1,0:T(8,128)(2,1)S(1)} %get-tuple-element.43), channel_id=1, source_target_pairs={{0,15},{1,2},{2,1},{3,4},{4,3},{5,6},{6,5},{7,8},{8,7},{9,10},{10,... | collective-permute-start | bytes 196616 | tf_op jit(solution)/shard_map/ppermute | solution.py:380
  44.4 0.7 %collective-permute-start.12 = (bf16[256,128]{1,0:T(8,128)(2,1)S(1)}, bf16[256,128]{1,0:T(8,128)(2,1)S(1)}, u32[]{:S(2)}, u32[]{:S(2)}) collective-permute-start(bf16[256,128]{1,0:T(8,128)(2,1)S(1)} %get-tuple-element.44), channel_id=1, source_target_pairs={{0,1},{1,0},{2,3},{3,2},{4,5},{5,4},{6,7},{7,6},{8,9},{9,8},{10,11... | collective-permute-start | bytes 196616 | tf_op jit(solution)/shard_map/ppermute | solution.py:380
  45.1 4.7 %collective-permute-done.11.outer_ref = bf16[256,128]{1,0:T(8,128)(2,1)S(1)} collective-permute-done((bf16[256,128]{1,0:T(8,128)(2,1)S(1)}, bf16[256,128]{1,0:T(8,128)(2,1)S(1)}, u32[]{:S(2)}, u32[]{:S(2)}) %collective-permute-start.11) | collective-permute-done | bytes 65568 | tf_op jit(solution)/shard_map/ppermute | solution.py:380
  49.8 0.7 %fold_columns.1 = f32[256,256]{1,0:T(8,128)} custom-call(f32[256,256]{1,0:T(8,128)S(1)} %get-tuple-element.42.center_ref, bf16[256,128]{1,0:T(8,128)(2,1)S(1)} %collective-permute-done.11.outer_ref, bf16[256,128]{1,0:T(8,128)(2,1)S(1)} %collective-permute-done.12.inner_ref), custom_call_target="tpu_custom_call" | custom-call | bytes 1048576 | tf_op jit(solution)/shard_map/fold_columns/pallas_call | solution.py:506
  (30 shorter events, 0.2 us)
Async XLA Ops:
  0.0 1.1 %copy-start = (bf16[6,256,256]{2,1,0:T(8,128)(2,1)S(1)}, bf16[6,256,256]{2,1,0:T(8,128)(2,1)}, u32[]{:S(2)}) copy-start(bf16[6,256,256]{2,1,0:T(8,128)(2,1)} %core_ref.1) | copy-start | bytes 2359300
  2.0 11.2 %collective-permute-start.1 = (bf16[2,128,256]{2,1,0:T(8,128)(2,1)S(1)}, bf16[2,128,256]{2,1,0:T(8,128)(2,1)S(1)}, u32[]{:S(2)}, u32[]{:S(2)}) collective-permute-start(bf16[2,128,256]{2,1,0:T(8,128)(2,1)S(1)} %get-tuple-element.26), channel_id=1, source_target_pairs={{0,1},{1,0},{2,3},{3,2},{4,5},{5,4},{6,7},{7,6},{8,9},{9,8},{10,11... | collective-permute-start | bytes 393224 | tf_op jit(solution)/shard_map/ppermute | solution.py:374
  3.2 15.9 %collective-permute-start.4 = (bf16[6,128,128]{2,1,0:T(8,128)(2,1)}, bf16[6,128,128]{2,1,0:T(8,128)(2,1)S(1)}, u32[]{:S(2)}, u32[]{:S(2)}) collective-permute-start(bf16[6,128,128]{2,1,0:T(8,128)(2,1)} %get-tuple-element.28), channel_id=1, source_target_pairs={{0,15},{1,2},{2,1},{3,4},{4,3},{5,6},{6,5},{7,8},{8,7},{9,10},{10,... | collective-permute-start | bytes 589832 | tf_op jit(solution)/shard_map/ppermute | solution.py:380
  5.7 16.1 %collective-permute-start.5 = (bf16[6,128,128]{2,1,0:T(8,128)(2,1)}, bf16[6,128,128]{2,1,0:T(8,128)(2,1)S(1)}, u32[]{:S(2)}, u32[]{:S(2)}) collective-permute-start(bf16[6,128,128]{2,1,0:T(8,128)(2,1)} %get-tuple-element.29), channel_id=1, source_target_pairs={{0,15},{1,2},{2,1},{3,4},{4,3},{5,6},{6,5},{7,8},{8,7},{9,10},{10,... | collective-permute-start | bytes 589832 | tf_op jit(solution)/shard_map/ppermute | solution.py:380
  7.1 14.7 %collective-permute-start.3 = (bf16[6,128,256]{2,1,0:T(8,128)(2,1)S(1)}, bf16[6,128,256]{2,1,0:T(8,128)(2,1)S(1)}, u32[]{:S(2)}, u32[]{:S(2)}) collective-permute-start(bf16[6,128,256]{2,1,0:T(8,128)(2,1)S(1)} %get-tuple-element.27), channel_id=1, source_target_pairs={{0,16},{1,17},{2,18},{3,19},{4,20},{5,21},{6,22},{7,23},{8,24},{9,... | collective-permute-start | bytes 1179656 | tf_op jit(solution)/shard_map/ppermute | solution.py:365
  7.8 14.0 %collective-permute-start = (bf16[4,128,256]{2,1,0:T(8,128)(2,1)}, bf16[4,128,256]{2,1,0:T(8,128)(2,1)S(1)}, u32[]{:S(2)}, u32[]{:S(2)}) collective-permute-start(bf16[4,128,256]{2,1,0:T(8,128)(2,1)} %get-tuple-element.25), channel_id=1, source_target_pairs={{0,1},{1,0},{2,3},{3,2},{4,5},{5,4},{6,7},{7,6},{8,9},{9,8},{10,11... | collective-permute-start | bytes 786440 | tf_op jit(solution)/shard_map/ppermute | solution.py:365
  13.9 5.1 %copy-start.1 = (bf16[6,256,256]{2,1,0:T(8,128)(2,1)S(1)}, bf16[6,256,256]{2,1,0:T(8,128)(2,1)}, u32[]{:S(2)}) copy-start(bf16[6,256,256]{2,1,0:T(8,128)(2,1)} %core_ref.1) | copy-start | bytes 2359300
  13.9 8.0 %collective-permute-start.2 = (bf16[2,128,256]{2,1,0:T(8,128)(2,1)}, bf16[2,128,256]{2,1,0:T(8,128)(2,1)S(1)}, u32[]{:S(2)}, u32[]{:S(2)}) collective-permute-start(bf16[2,128,256]{2,1,0:T(8,128)(2,1)} %broadcast_select_fusion), channel_id=1, source_target_pairs={{0,1},{1,0},{2,3},{3,2},{4,5},{5,4},{6,7},{7,6},{8,9},{9,8},{10,11... | collective-permute-start | bytes 393224 | tf_op jit(solution)/shard_map/ppermute | solution.py:365
  14.9 1.0 %copy-start.3 = (bf16[528,512]{1,0:T(8,128)(2,1)S(1)}, bf16[528,512]{1,0:T(8,128)(2,1)}, u32[]{:S(2)}) copy-start(bf16[528,512]{1,0:T(8,128)(2,1)} %constant.44.clone.left_ref) | copy-start | bytes 1622020
  16.0 1.0 %copy-start.5 = (bf16[512,512]{1,0:T(8,128)(2,1)S(1)}, bf16[512,512]{1,0:T(8,128)(2,1)}, u32[]{:S(2)}) copy-start(bf16[512,512]{1,0:T(8,128)(2,1)} %constant.45.clone.right_ref) | copy-start | bytes 1572868
  17.0 1.0 %copy-start.11 = (bf16[512,512]{1,0:T(8,128)(2,1)S(1)}, bf16[512,512]{1,0:T(8,128)(2,1)}, u32[]{:S(2)}) copy-start(bf16[512,512]{1,0:T(8,128)(2,1)} %noise_ref.1) | copy-start | bytes 1572868
  19.0 3.4 %copy-start.2 = (f32[512,128]{1,0:T(8,128)S(1)}, f32[512,128]{1,0:T(8,128)}, u32[]{:S(2)}) copy-start(f32[512,128]{1,0:T(8,128)} %constant.49.clone.rows_ref) | copy-start | bytes 786436
  19.0 3.4 %copy-start.4 = (bf16[528,512]{1,0:T(8,128)(2,1)S(1)}, bf16[528,512]{1,0:T(8,128)(2,1)}, u32[]{:S(2)}) copy-start(bf16[528,512]{1,0:T(8,128)(2,1)} %constant.44.clone.left_ref) | copy-start | bytes 1622020
  19.0 3.4 %copy-start.6 = (bf16[512,512]{1,0:T(8,128)(2,1)S(1)}, bf16[512,512]{1,0:T(8,128)(2,1)}, u32[]{:S(2)}) copy-start(bf16[512,512]{1,0:T(8,128)(2,1)} %constant.45.clone.right_ref) | copy-start | bytes 1572868
  19.0 3.4 %copy-start.10 = (f32[8,512]{1,0:T(8,128)S(1)}, f32[8,512]{1,0:T(8,128)}, u32[]{:S(2)}) copy-start(f32[8,512]{1,0:T(8,128)} %constant.50.clone.cols_ref) | copy-start | bytes 49156
  19.1 9.4 %collective-permute-start.6 = (bf16[6,128,128]{2,1,0:T(8,128)(2,1)S(1)}, bf16[6,128,128]{2,1,0:T(8,128)(2,1)S(1)}, u32[]{:S(2)}, u32[]{:S(2)}) collective-permute-start(bf16[6,128,128]{2,1,0:T(8,128)(2,1)S(1)} %collective-permute-done.4.outer_first_ref), channel_id=1, source_target_pairs={{0,1},{1,0},{2,3},{3,2},{4,5},{5,4},{6,7},{7,6},{8,9},{9,8},{10,11... | collective-permute-start | bytes 589832 | tf_op jit(solution)/shard_map/ppermute | solution.py:365
  21.8 7.1 %collective-permute-start.7 = (bf16[6,128,128]{2,1,0:T(8,128)(2,1)S(1)}, bf16[6,128,128]{2,1,0:T(8,128)(2,1)S(1)}, u32[]{:S(2)}, u32[]{:S(2)}) collective-permute-start(bf16[6,128,128]{2,1,0:T(8,128)(2,1)S(1)} %collective-permute-done.5.outer_second_ref), channel_id=1, source_target_pairs={{0,16},{1,17},{2,18},{3,19},{4,20},{5,21},{6,22},{7,23},{8,24},{9,... | collective-permute-start | bytes 589832 | tf_op jit(solution)/shard_map/ppermute | solution.py:365
  22.0 7.7 %collective-permute-start.8 = (bf16[6,512,128]{2,1,0:T(8,128)(2,1)S(1)}, bf16[6,512,128]{2,1,0:T(8,128)(2,1)S(1)}, u32[]{:S(2)}, u32[]{:S(2)}) collective-permute-start(bf16[6,512,128]{2,1,0:T(8,128)(2,1)S(1)} %pad_maximum_fusion), channel_id=1, source_target_pairs={{0,1},{1,0},{2,3},{3,2},{4,5},{5,4},{6,7},{7,6},{8,9},{9,8},{10,11... | collective-permute-start | bytes 2359304 | tf_op jit(solution)/shard_map/ppermute | solution.py:380
  29.7 1.0 %copy-start.7 = (bf16[512,512]{1,0:T(8,128)(2,1)S(1)}, bf16[512,512]{1,0:T(8,128)(2,1)}, u32[]{:S(2)}) copy-start(bf16[512,512]{1,0:T(8,128)(2,1)} %constant.46.clone.inverse_right_ref) | copy-start | bytes 1572868
  29.7 1.2 %copy-start.8 = (bf16[512,512]{1,0:T(8,128)(2,1)S(1)}, bf16[512,512]{1,0:T(8,128)(2,1)}, u32[]{:S(2)}) copy-start(bf16[512,512]{1,0:T(8,128)(2,1)} %constant.47.clone.band_columns_ref) | copy-start | bytes 1572868
  29.7 1.2 %copy-start.9 = (bf16[272,384]{1,0:T(8,128)(2,1)S(1)}, bf16[272,384]{1,0:T(8,128)(2,1)}, u32[]{:S(2)}) copy-start(bf16[272,384]{1,0:T(8,128)(2,1)} %constant.48.clone.band_rows_ref) | copy-start | bytes 626692
  34.5 8.7 %collective-permute-start.10 = (bf16[128,512]{1,0:T(8,128)(2,1)S(1)}, bf16[128,512]{1,0:T(8,128)(2,1)S(1)}, u32[]{:S(2)}, u32[]{:S(2)}) collective-permute-start(bf16[128,512]{1,0:T(8,128)(2,1)S(1)} %get-tuple-element.41), channel_id=1, source_target_pairs={{0,1},{1,0},{2,3},{3,2},{4,5},{5,4},{6,7},{7,6},{8,9},{9,8},{10,11... | collective-permute-start | bytes 393224 | tf_op jit(solution)/shard_map/ppermute | solution.py:365
  38.5 5.1 %collective-permute-start.9 = (bf16[128,512]{1,0:T(8,128)(2,1)S(1)}, bf16[128,512]{1,0:T(8,128)(2,1)S(1)}, u32[]{:S(2)}, u32[]{:S(2)}) collective-permute-start(bf16[128,512]{1,0:T(8,128)(2,1)S(1)} %get-tuple-element.40), channel_id=1, source_target_pairs={{0,16},{1,17},{2,18},{3,19},{4,20},{5,21},{6,22},{7,23},{8,24},{9,... | collective-permute-start | bytes 393224 | tf_op jit(solution)/shard_map/ppermute | solution.py:365
  43.7 6.1 %collective-permute-start.11 = (bf16[256,128]{1,0:T(8,128)(2,1)S(1)}, bf16[256,128]{1,0:T(8,128)(2,1)S(1)}, u32[]{:S(2)}, u32[]{:S(2)}) collective-permute-start(bf16[256,128]{1,0:T(8,128)(2,1)S(1)} %get-tuple-element.43), channel_id=1, source_target_pairs={{0,15},{1,2},{2,1},{3,4},{4,3},{5,6},{6,5},{7,8},{8,7},{9,10},{10,... | collective-permute-start | bytes 196616 | tf_op jit(solution)/shard_map/ppermute | solution.py:380
  44.4 5.4 %collective-permute-start.12 = (bf16[256,128]{1,0:T(8,128)(2,1)S(1)}, bf16[256,128]{1,0:T(8,128)(2,1)S(1)}, u32[]{:S(2)}, u32[]{:S(2)}) collective-permute-start(bf16[256,128]{1,0:T(8,128)(2,1)S(1)} %get-tuple-element.44), channel_id=1, source_target_pairs={{0,1},{1,0},{2,3},{3,2},{4,5},{5,4},{6,7},{7,6},{8,9},{9,8},{10,11... | collective-permute-start | bytes 196616 | tf_op jit(solution)/shard_map/ppermute | solution.py:380
